TPU v7x, 128 devices: a whole 4x4x4 slice. The times are simulated.
128 devices in a mesh: req: 8 (over y, core), unit: 16 (over x, z).
Axes of the slice: x: 4, y: 4, z: 4, core: 2. Of those that a mesh axis runs over, the one named last changes fastest.
Arguments:
- hidden: bfloat16 [6144, 2048], P(('req', 'unit')), may hold values from -6 to 6
- tree_q: bfloat16 [6144, 2048], P(('req', 'unit')), may hold values from -1.5 to 1.5
- tree_kv: bfloat16 [6144, 2, 512], P(('req', 'unit')), may hold values from -1.5 to 1.5
- kv_cache: bfloat16 [128, 2, 2, 2048, 256], P(('req', 'unit')), may hold values from -1.5 to 1.5
- cache_lengths: int32 [128], P(('req', 'unit')), may hold values from 1 to 2048, as said below
- tree_parents: int32 [128, 48], P(('req', 'unit')), may hold values from 0 to 46, as said below
- accepted: int32 [128, 4], P(('req', 'unit')), may hold values from 0 to 47, as said below
- tenant_ranges: int32 [128, 2], replicated, may hold values from 0 to 262144, as said below
- out_weight: bfloat16 [2048, 2048], P(None, 'unit'), may hold values from -0.125 to 0.125
- mlp_weights: bfloat16 [3, 2048, 8192], P(None, None, ('req', 'unit')), may hold values from -0.125 to 0.125
- draft_weights: bfloat16 [4, 2048, 2048], P(None, None, 'unit'), may hold values from -0.125 to 0.125
- embedding: bfloat16 [262144, 2048], P(('req', 'unit')), may hold values from -1.1269514 to 1.1269514
- attn_post_gain: bfloat16 [2048], replicated, may hold values from 0.25 to 1.75
- ff_pre_gain: bfloat16 [2048], replicated, may hold values from 0.25 to 1.75
- ff_post_gain: bfloat16 [2048], replicated, may hold values from 0.25 to 1.75
- final_gain: bfloat16 [2048], replicated, may hold values from 0.25 to 1.75
Outputs:
- tree_out: bfloat16 [6144, 2048], P(('req', 'unit'))
- draft_logprobs: bfloat16 [4, 512, 262144], P(None, None, ('req', 'unit'))
Inputs may be any that keep to these rules, and one draw needn't show every extreme that they name: A request's cache holds live entries in its first cache_lengths slots; some request fills all 2048. `tree_parents`: node 0 is the root and its own parent; every other node's parent has a smaller index. `accepted`: rising nodes starting at the root 0, each the parent of the next. `tenant_ranges`: column 0 is the first allowed id, column 1 one past the last; each request allows 262144 // 2 ids or more; some request allows all.
All inputs are finite; a program needn't handle non-finite values.
Results may differ from a plain program's by a relative error of at most 0.008.
Values may be sent and summed in bfloat16 or wider, within the bound.
No kernel may reach another device: no remote copies, remote signals or barrier semaphores. Data moves between devices by JAX's collectives and lax.ppermute only.
A program may use at most 128 MiB of HBM per device.

v0:
```python
import jax
import jax.numpy as jnp
from jax import lax
from jax.sharding import PartitionSpec as P

QH = 8
KVH = 2
HD = 256
HEADS = 4
ACC = 4


EPS = 1e-06
SOFTCAP = 30.0
BLOCK_SLOTS = 512


def rms_scale(values, gain):
    floats = values.astype(jnp.float32)
    return (
        floats
        * lax.rsqrt(jnp.mean(floats * floats, axis=-1, keepdims=True) + EPS)
        * gain.astype(jnp.float32)
    )


def ancestor_table(parents):
    tree_size = parents.shape[-1]
    node_ids = jnp.arange(tree_size, dtype=jnp.int32)
    reachable = jnp.maximum(
        (parents[:, None] == node_ids[None, :]).astype(jnp.float32),
        (node_ids[:, None] == node_ids[None, :]).astype(jnp.float32),
    )
    for doubling in range(max(1, (tree_size - 1).bit_length())):
        reachable = jnp.minimum(jnp.dot(reachable, reachable, precision=lax.Precision.HIGHEST), 1.0)
    return reachable


def cache_attention(queries, cache, length):
    slots_total = cache.shape[2]
    block_width = min(BLOCK_SLOTS, slots_total)
    blocks = slots_total // block_width
    score_scale = HD ** (-0.5)
    tree_size = queries.shape[0]
    group_size = queries.shape[2]

    def add_block(block_index, running):
        numerator, denominator = running
        offset = block_index * block_width
        key_block = lax.dynamic_slice_in_dim(cache[0], offset, block_width, 1)
        value_block = lax.dynamic_slice_in_dim(cache[1], offset, block_width, 1)
        scores = jnp.exp(
            jnp.einsum("tkgd,ksd->kgts", queries, key_block, preferred_element_type=jnp.float32)
            * score_scale
        )
        slot_ids = offset + jnp.arange(block_width, dtype=jnp.int32)
        weights_now = jnp.where(slot_ids < length, scores, 0.0)
        numerator = numerator + jnp.einsum(
            "kgts,ksd->tkgd",
            weights_now.astype(jnp.bfloat16),
            value_block,
            preferred_element_type=jnp.float32,
        )
        return (numerator, denominator + jnp.sum(weights_now, axis=3))

    start_state = (
        jnp.zeros((tree_size, KVH, group_size, HD), jnp.float32),
        jnp.zeros((KVH, group_size, tree_size), jnp.float32),
    )
    return lax.fori_loop(0, blocks, add_block, start_state)


def unit_terms(mlp_rows, weight_part):
    gate_part = jnp.dot(mlp_rows, weight_part[0], preferred_element_type=jnp.float32)
    upward = jnp.dot(mlp_rows, weight_part[1], preferred_element_type=jnp.float32)
    active = (jax.nn.gelu(gate_part, approximate=True) * upward).astype(jnp.bfloat16)
    return lax.dot_general(
        active, weight_part[2], (((1,), (1,)), ((), ())), preferred_element_type=jnp.float32
    )


def per_device(
    hidden,
    tree_q,
    tree_kv,
    kv_cache,
    cache_lengths,
    tree_parents,
    accepted,
    tenant_ranges,
    out_weight,
    mlp_weights,
    draft_weights,
    embedding,
    attn_post_gain,
    ff_pre_gain,
    ff_post_gain,
    final_gain,
):
    tree_size = tree_q.shape[0]
    group_size = QH // KVH
    queries = tree_q.reshape(tree_size, KVH, group_size, HD)
    numerator, denominator = cache_attention(queries, kv_cache[0], cache_lengths[0])
    tree_keys = tree_kv[:, 0].reshape(tree_size, KVH, HD)
    tree_values = tree_kv[:, 1].reshape(tree_size, KVH, HD)
    tree_scores = jnp.exp(
        jnp.einsum("tkgd,skd->kgts", queries, tree_keys, preferred_element_type=jnp.float32)
        * HD ** (-0.5)
    )
    tree_weights = tree_scores * ancestor_table(tree_parents[0])
    numerator = numerator + jnp.einsum(
        "kgts,skd->tkgd",
        tree_weights.astype(jnp.bfloat16),
        tree_values,
        preferred_element_type=jnp.float32,
    )
    denominator = denominator + jnp.sum(tree_weights, axis=3)
    attended = numerator / jnp.transpose(denominator, (2, 0, 1))[..., None]
    attended = attended.reshape(tree_size, QH * HD).astype(jnp.bfloat16)
    projected_cols = jnp.dot(
        lax.all_gather(attended, "unit", axis=0, tiled=True),
        out_weight,
        preferred_element_type=jnp.float32,
    ).astype(jnp.bfloat16)
    projected = lax.all_to_all(projected_cols, "unit", split_axis=0, concat_axis=1, tiled=True)
    first = (hidden.astype(jnp.float32) + rms_scale(projected, attn_post_gain)).astype(jnp.bfloat16)
    normed = rms_scale(first, ff_pre_gain).astype(jnp.bfloat16)
    mlp_rows = lax.all_gather(normed, "unit", axis=0, tiled=True)
    partial_sums = unit_terms(mlp_rows, lax.all_gather(mlp_weights, "req", axis=2, tiled=True))
    mlp_sum = lax.psum_scatter(partial_sums, "unit", scatter_dimension=0, tiled=True)
    tree_out = (first.astype(jnp.float32) + rms_scale(mlp_sum, ff_post_gain)).astype(jnp.bfloat16)
    path_rows = jnp.take(tree_out, accepted[0], axis=0)
    path_normed = rms_scale(path_rows, final_gain).astype(jnp.bfloat16)
    column_width = draft_weights.shape[2]
    column_start = lax.axis_index("unit") * column_width
    every_row = lax.all_gather(path_normed, ("req", "unit"), axis=0, tiled=True)
    before = jnp.einsum("rd,hde->rhe", every_row, draft_weights, preferred_element_type=jnp.float32)
    own_columns = lax.dynamic_slice_in_dim(every_row, column_start, column_width, 1).astype(
        jnp.float32
    )
    drafts = lax.all_gather(
        (own_columns[:, None, :] + jax.nn.silu(before)).astype(jnp.bfloat16),
        "unit",
        axis=2,
        tiled=True,
    )
    vocab_width = embedding.shape[0]
    vocab_ids = lax.axis_index(("req", "unit")) * vocab_width + jnp.arange(
        vocab_width, dtype=jnp.int32
    )
    starts = jnp.repeat(tenant_ranges[:, 0], ACC)
    range_ends = jnp.repeat(tenant_ranges[:, 1], ACC)
    allowed = (vocab_ids[None, :] >= starts[:, None]) & (vocab_ids[None, :] < range_ends[:, None])
    head_logits = []
    head_totals = []
    for head_index in range(HEADS):
        products = lax.dot_general(
            drafts[:, head_index],
            embedding,
            (((1,), (1,)), ((), ())),
            preferred_element_type=jnp.float32,
        )
        logits = SOFTCAP * jnp.tanh(products / SOFTCAP)
        head_logits.append(logits)
        head_totals.append(jnp.sum(jnp.where(allowed, jnp.exp(logits), 0.0), axis=1))
    totals = lax.psum(jnp.stack(head_totals), ("req", "unit"))
    draft_logprobs = jnp.stack(
        [
            jnp.where(allowed, head_logits[head_index] - jnp.log(totals[head_index])[:, None], 0.0)
            for head_index in range(HEADS)
        ]
    ).astype(jnp.bfloat16)
    return (tree_out, draft_logprobs)


def solution(mesh):
    return jax.shard_map(
        per_device,
        mesh=mesh,
        in_specs=(
            P(("req", "unit"), None),
            P(("req", "unit"), None),
            P(("req", "unit"), None, None),
            P(("req", "unit"), None, None, None, None),
            P(("req", "unit")),
            P(("req", "unit"), None),
            P(("req", "unit"), None),
            P(),
            P(None, "unit"),
            P(None, None, ("req", "unit")),
            P(None, None, "unit"),
            P(("req", "unit"), None),
            P(),
            P(),
            P(),
            P(),
        ),
        out_specs=(P(("req", "unit"), None), P(None, None, ("req", "unit"))),
        check_vma=False,
    )
```

profile of v0, /device:TPU:1, one launch (start us, length us, event | category | flops | bytes accessed | tf_op | source)
XLA Modules:
  0.0 548.7 jit_solution(7113160795114602746)
XLA Ops:
  7.2 1.0 convolution_minimum_fusion.5
  8.3 0.2 convolution_minimum_fusion.4
  8.4 0.2 convolution_minimum_fusion.3
  8.6 0.2 convolution_minimum_fusion.2
  8.8 0.2 convolution_minimum_fusion.1
  8.9 0.2 convolution_minimum_fusion
  9.2 1.4 slice_reduce_fusion
  10.6 1.1 reshape.124
  11.7 16.0 %while.16 = (s32[]{:T(128)}, f32[48,2,4,256]{3,0,2,1:T(8,128)S(1)}, f32[2,4,48]{2,1,0:T(4,128)S(1)}, bf16[2,2,2048,256]{3,2,1,0:T(8,128)(2,1)}, s32[]{:T(128)}, ...) while((s32[]{:T(128)}, f32[48,2,4,256]{3,0,2,1:T(8,128)S(1)}, ...), condition=%wide.region_2.3_spmd.clone, body=%wide.region_0.2_spmd.clone.sunk | while | flops 202311040 | bytes 11214006 | solution.py:70
  11.8 0.7 add_compare_fusion.2
  12.5 2.5 fusion.102
  15.0 0.4 fusion.103
  15.4 0.3 fusion.104
  15.8 0.7 add_compare_fusion.2
  16.5 2.5 fusion.102
  19.0 0.4 fusion.103
  19.4 0.3 fusion.104
  19.8 0.7 add_compare_fusion.2
  20.4 2.5 fusion.102
  22.9 0.4 fusion.103
  23.4 0.3 fusion.104
  23.8 0.7 add_compare_fusion.2
  24.4 2.5 fusion.102
  26.9 0.4 fusion.103
  27.4 0.3 fusion.104
  27.8 0.3 fusion.69
  28.1 0.3 fusion.33
  28.3 0.1 copy.35
  28.4 0.8 convert_element_type.87
  29.3 0.7 all-gather.11.cloned.1.call-update
  30.0 50.4 %all-gather.7.cloned.1.call-done = bf16[768,2048]{1,0:T(8,128)(2,1)} async-done(((bf16[48,2048]{1,0:T(8,128)(2,1)}), bf16[768,2048]{1,0:T(8,128)(2,1)}) %all-gather.7.cloned.1.call-update) | async-done | bytes 3145744 | tf_op jit(solution)/shard_map/all_gather | solution.py:121
  80.4 3.5 convolution_convert_fusion
  84.0 4.1 all-to-all-start
  88.1 6.8 %all-to-all-done = bf16[16,48,128]{2,1,0:T(8,128)(2,1)S(1)} async-done(((bf16[16,48,128]{2,1,0:T(8,128)(2,1)}), bf16[16,48,128]{2,1,0:T(8,128)(2,1)S(1)}, u32[]{:S(2)}, u32[]{:S(2)}) %all-to-all-start) | async-done | bytes 196640 | tf_op jit(solution)/shard_map/all_to_all | solution.py:125
  95.0 0.1 fusion.41
  95.1 0.3 fusion.42
  95.4 0.8 fusion.44
  96.3 26.3 %all-gather.11.cloned.1.call-done = bf16[3,2048,512]{1,2,0:T(8,128)(2,1)} async-done(((bf16[3,2048,64]{1,2,0:T(8,128)(2,1)}), bf16[3,2048,512]{1,2,0:T(8,128)(2,1)}) %all-gather.11.cloned.1.call-update) | async-done | bytes 6291472 | tf_op jit(solution)/shard_map/all_gather | solution.py:129
  122.6 50.2 %all-gather.9.cloned.1.call-done = bf16[768,2048]{1,0:T(8,128)(2,1)} async-done(((bf16[48,2048]{1,0:T(8,128)(2,1)}), bf16[768,2048]{1,0:T(8,128)(2,1)}) %all-gather.9.cloned.1.call-update) | async-done | bytes 3145744 | tf_op jit(solution)/shard_map/all_gather | solution.py:128
  172.8 5.5 %fusion.21 = f32[768,512]{1,0:T(8,128)} fusion(bf16[768,2048]{1,0:T(8,128)(2,1)} %all-gather.9.cloned.1.call-done, bf16[3,2048,512]{1,2,0:T(8,128)(2,1)} %all-gather.11.cloned.1.call-done), kind=kOutput, calls=%fused_computation.48 | convolution fusion | flops 1610612736 | bytes 6815744 | tf_op jit(solution)/shard_map/dot_general | solution.py:74
  178.3 10.0 %fusion.19 = f32[768,2048]{1,0:T(8,128)} fusion(bf16[3,2048,512]{1,2,0:T(8,128)(2,1)} %all-gather.11.cloned.1.call-done, f32[768,512]{1,0:T(8,128)} %fusion.21, bf16[768,2048]{1,0:T(8,128)(2,1)} %all-gather.9.cloned.1.call-done), kind=kOutput, calls=%fused_computation.44 | convolution fusion | flops 3225157632 | bytes 15204352 | tf_op jit(solution)/shard_map/dot_general | solution.py:77
  188.4 0.6 copy-done.8
  189.1 78.9 %reduce-scatter.2.cloned.1.call-done = f32[48,2048]{1,0:T(8,128)} async-done(((f32[768,2048]{1,0:T(8,128)}), f32[48,2048]{1,0:T(8,128)}) %reduce-scatter.2.cloned.1.call-update) | async-done | bytes 393232 | tf_op jit(solution)/shard_map/reduce_scatter | solution.py:130
  268.0 1.1 multiply_reduce_fusion
  269.1 1.1 fusion.45
  270.3 0.6 gather_fusion
  270.9 0.2 fusion.52
  271.1 0.7 fusion.58
  271.8 0.2 all-gather.13.cloned.1.call-start
  272.0 65.9 %all-gather.15.cloned.1.call-done = bf16[128,4,2048]{2,1,0:T(4,128)(2,1)} async-done(((bf16[1,4,2048]{2,1,0:T(4,128)(2,1)}), bf16[128,4,2048]{2,1,0:T(4,128)(2,1)}) %all-gather.15.cloned.1.call-update) | async-done | bytes 2097168 | tf_op jit(solution)/shard_map/all_gather | solution.py:136
  337.9 3.9 reshape.135
  341.8 0.9 dynamic-slice_convert_fusion
  342.8 3.9 reshape.140
  346.7 3.9 add_convert_fusion
  350.7 0.1 ge.23
  350.9 0.1 lt.58
  351.0 74.3 %all-gather.13.cloned.1.call-done = bf16[512,4,2048]{2,0,1:T(8,128)(2,1)} async-done(((bf16[512,4,128]{2,0,1:T(8,128)(2,1)}), bf16[512,4,2048]{2,0,1:T(8,128)(2,1)}) %all-gather.13.cloned.1.call-update) | async-done | bytes 8388624 | tf_op jit(solution)/shard_map/all_gather | solution.py:141
  425.4 7.8 %fusion.15 = f32[512,2048]{1,0:T(8,128)S(1)} fusion(bf16[2048,2048]{1,0:T(8,128)(2,1)} %param.29, bf16[512,4,2048]{2,0,1:T(8,128)(2,1)} %all-gather.13.cloned.1.call-done), kind=kOutput, calls=%fused_computation.36 | convolution fusion | flops 4294967296 | bytes 14680064 | tf_op jit(solution)/shard_map/dot_general | solution.py:157
  433.2 9.2 %fusion.16 = f32[512,2048]{1,0:T(8,128)S(1)} fusion(bf16[2048,2048]{1,0:T(8,128)(2,1)} %param.29, bf16[512,4,2048]{2,0,1:T(8,128)(2,1)} %all-gather.13.cloned.1.call-done), kind=kOutput, calls=%fused_computation.38 | convolution fusion | flops 4294967296 | bytes 14680064 | tf_op jit(solution)/shard_map/dot_general | solution.py:157
  442.4 9.4 %fusion.17 = f32[512,2048]{1,0:T(8,128)} fusion(bf16[2048,2048]{1,0:T(8,128)(2,1)S(1)} %bitcast.153, bf16[512,4,2048]{2,0,1:T(8,128)(2,1)} %all-gather.13.cloned.1.call-done), kind=kOutput, calls=%fused_computation.40 | convolution fusion | flops 4294967296 | bytes 14680064 | tf_op jit(solution)/shard_map/dot_general | solution.py:157
  451.9 13.0 %select_reduce_fusion.3 = (f32[512]{0:T(512)S(1)}, f32[512]{0:T(512)S(1)}, f32[512]{0:T(512)S(1)}, f32[512]{0:T(512)S(1)}, f32[512,2048]{1,0:T(8,128)}) fusion(s32[512]{0:T(512)S(1)} %lt.58, s32[512]{0:T(512)S(1)} %ge.23, s32[2048]{0:T(1024)S(1)} %iota_add_fusion, f32[512,2048]{1,0:T(8,128)} %fusion.17, f32[512,2048]{1,0:T(8,128)S(1)} %fusion.16, ...), kind=kOutput, calls=%fused_computation.27 | convolution fusion | flops 4314888192 | bytes 27283456 | tf_op jit(solution)/shard_map/dot_general | solution.py:157
  464.9 65.4 %psum.7 = f32[4,512]{1,0:T(4,128)S(1)} all-reduce(f32[4,512]{1,0:T(4,128)S(1)} %pad_maximum_fusion.1), channel_id=1, replica_groups=mesh['req'=8,'unit'=16] {'req','unit'}, use_global_device_ids=true, to_apply=%region_13.14 | all-reduce | flops 2048 | bytes 16384 | tf_op jit(solution)/shard_map/psum | solution.py:166
  530.4 7.6 %fusion.11 = (bf16[1,512,2048]{2,1,0:T(8,128)(2,1)S(1)}, bf16[1,512,2048]{2,1,0:T(8,128)(2,1)S(1)}, bf16[1,512,2048]{2,1,0:T(8,128)(2,1)S(1)}, bf16[1,512,2048]{2,1,0:T(8,128)(2,1)S(1)}) fusion(f32[512,2048]{1,0:T(8,128)} %get-tuple-element.183, f32[512]{0:T(512)S(1)} %bitcast.144, s32[512]{0:T(512)S(1)} %lt.58, s32[512]{0:T(512)S(1)} %ge.23, ...), kind=kLoop, calls=%fused_computation.31 | loop fusion | flops 24117248 | bytes 25186304 | tf_op jit(solution)/shard_map/stack | solution.py:167
  538.0 3.9 pad_maximum_fusion
  (68 shorter events, 0.8 us)
Async XLA Ops:
  7.2 339.6 %copy-start = (bf16[4,2048,128]{2,1,0:T(8,128)(2,1)S(1)}, bf16[4,2048,128]{2,1,0:T(8,128)(2,1)}, u32[]{:S(2)}) copy-start(bf16[4,2048,128]{2,1,0:T(8,128)(2,1)} %param.28) | copy-start | bytes 6291460
  7.2 73.2 %all-gather.7.cloned.1.call-start = ((), (), s32[]{:S(2)}) async-start(), calls=%async_computation.2 | async-start | bytes 3342336 | tf_op jit(solution)/shard_map/all_gather | solution.py:121
  11.7 68.7 %copy-start.11 = (bf16[2048,128]{1,0:T(8,128)(2,1)S(1)}, bf16[2048,128]{1,0:T(8,128)(2,1)}, u32[]{:S(2)}) copy-start(bf16[2048,128]{1,0:T(8,128)(2,1)} %param.26) | copy-start | bytes 1572868
  28.0 60.0 %copy-start.6 = (bf16[2048]{0:T(1024)(128)(2,1)S(1)}, bf16[2048]{0:T(1024)(128)(2,1)}, u32[]{:S(2)}) copy-start(bf16[2048]{0:T(1024)(128)(2,1)} %param.30) | copy-start | bytes 12292
  28.1 60.1 %copy-start.7 = (bf16[2048]{0:T(1024)(128)(2,1)S(1)}, bf16[2048]{0:T(1024)(128)(2,1)}, u32[]{:S(2)}) copy-start(bf16[2048]{0:T(1024)(128)(2,1)} %param.31) | copy-start | bytes 12292
  28.1 67.1 %copy-start.5 = (bf16[48,2048]{1,0:T(8,128)(2,1)S(1)}, bf16[48,2048]{1,0:T(8,128)(2,1)}, u32[]{:S(2)}) copy-start(bf16[48,2048]{1,0:T(8,128)(2,1)} %param.18) | copy-start | bytes 589828
  29.3 93.3 %all-gather.11.cloned.1.call-start = ((), (), s32[]{:S(2)}) async-start(), calls=%async_computation.4 | async-start | bytes 7077888 | tf_op jit(solution)/shard_map/all_gather | solution.py:129
  84.0 11.0 %all-to-all-start = ((bf16[16,48,128]{2,1,0:T(8,128)(2,1)}), bf16[16,48,128]{2,1,0:T(8,128)(2,1)S(1)}, u32[]{:S(2)}, u32[]{:S(2)}) async-start(bf16[16,48,128]{2,1,0:T(8,128)(2,1)} %bitcast.8), calls=%async_computation | async-start | bytes 393216 | tf_op jit(solution)/shard_map/all_to_all | solution.py:125
  88.0 84.8 %all-gather.9.cloned.1.call-start = ((), (), s32[]{:S(2)}) async-start(), calls=%async_computation.3 | async-start | bytes 3342336 | tf_op jit(solution)/shard_map/all_gather | solution.py:128
  96.2 171.8 %reduce-scatter.2.cloned.1.call-start = ((), (), s32[]{:S(2)}) async-start(), calls=%async_computation.5 | async-start | bytes 6684672 | tf_op jit(solution)/shard_map/reduce_scatter | solution.py:130
  188.3 0.7 copy-start.8
  188.3 0.7 copy-start.9
  188.3 0.7 copy-start.12
  188.4 149.5 %all-gather.15.cloned.1.call-start = ((), (), s32[]{:S(2)}) async-start(), calls=%async_computation.7 | async-start | bytes 2113536 | tf_op jit(solution)/shard_map/all_gather | solution.py:136
  270.3 76.5 %copy-start.4 = (bf16[48,2048]{1,0:T(8,128)(2,1)}, bf16[48,2048]{1,0:T(8,128)(2,1)S(1)}, u32[]{:S(2)}) copy-start(bf16[48,2048]{1,0:T(8,128)(2,1)S(1)} %fusion.45) | copy-start | bytes 589828
  271.8 153.6 %all-gather.13.cloned.1.call-start = ((), (), s32[]{:S(2)}) async-start(), calls=%async_computation.6 | async-start | bytes 8912896 | tf_op jit(solution)/shard_map/all_gather | solution.py:141
  346.7 3.9 copy-start.10
  425.4 17.0 %slice-start = ((s8[8388608]{0:T(1024)(128)(4,1)}), s8[4194304]{0:T(1024)(128)(4,1)S(1)}, s32[]{:S(2)}) async-start(s8[8388608]{0:T(1024)(128)(4,1)} %bitcast.152), calls=%async_computation.8 | async-start | bytes 8388608
  433.2 18.7 %copy-start.2 = (f32[512,2048]{1,0:T(8,128)}, f32[512,2048]{1,0:T(8,128)S(1)}, u32[]{:S(2)}) copy-start(f32[512,2048]{1,0:T(8,128)S(1)} %fusion.15) | copy-start | bytes 12582916
  433.2 9.2 %slice-start.1 = ((s8[8388608]{0:T(1024)(128)(4,1)}), s8[4194304]{0:T(1024)(128)(4,1)S(1)}, s32[]{:S(2)}) async-start(s8[8388608]{0:T(1024)(128)(4,1)} %bitcast.152), calls=%async_computation.9 | async-start | bytes 8388608
  442.4 9.5 %copy-start.3 = (f32[512,2048]{1,0:T(8,128)}, f32[512,2048]{1,0:T(8,128)S(1)}, u32[]{:S(2)}) copy-start(f32[512,2048]{1,0:T(8,128)S(1)} %fusion.16) | copy-start | bytes 12582916
  538.0 3.9 copy-start.1
Sparse Core Ops, SparseCore 0:
  29.4 50.9 all-gather.6
  82.1 40.4 all-gather.10
  125.4 47.3 all-gather.8
  188.5 79.4 reduce-scatter.1
  271.9 65.9 all-gather.14
  350.7 74.6 all-gather.12
where the time goes:
time: 549 us
  waiting for transfers between devices  354 us (64%)
  matrix products  67.8 us (12%)
  blocking collectives  65.4 us (12%)
  local copies, waits for them, and re-layouts  23.1 us (4%)
  other arithmetic  19.6 us (4%)
  between operations  14.5 us (3%)
    reduce_scatter x1, waiting for transfers between devices, per_device(): lax.psum_scatter(partial_sums, 'unit', scatter_dimension=0, tiled=True)  78.9 us
    all_gather x1, waiting for transfers between devices, per_device(): lax.all_gather((own_columns[:, None, :] + jax.nn.silu(before)).astype(jnp...  74.3 us
    all_gather x1, waiting for transfers between devices, per_device(): every_row = lax.all_gather(path_normed, ('req', 'unit'), axis=0, tiled=True)  65.9 us
    psum x1, blocking collectives, per_device(): totals = lax.psum(jnp.stack(head_totals), ('req', 'unit'))  65.4 us
    all_gather x1, waiting for transfers between devices, per_device(): lax.all_gather(attended, 'unit', axis=0, tiled=True)  50.4 us
    all_gather x1, waiting for transfers between devices, per_device(): mlp_rows = lax.all_gather(normed, 'unit', axis=0, tiled=True)  50.2 us
    dot_general x4, matrix products, per_device(): lax.dot_general(drafts[:, head_index], embedding, (((1,), (1,)), ((), ())...  39.4 us
    all_gather x1, waiting for transfers between devices, per_device(): lax.all_gather(mlp_weights, 'req', axis=2, tiled=True)  26.3 us
  transfers between devices with their start and end apart: 7, of which 7 were waited for; matrix products, arithmetic and copies ran while one was open for 1% of the time, Pallas kernels for 0%

commit v1 on v0

v1 whole, which is shorter than its diff:
```python
import jax
import jax.numpy as jnp
from jax import lax
from jax.sharding import Mesh, PartitionSpec as P

QH = 8
KVH = 2
HD = 256
HEADS = 4
ACC = 4

EPS = 1e-06
SOFTCAP = 30.0
BLOCK_SLOTS = 512

Y, CORE, X, Z = 4, 2, 4, 4
XZ = ("x", "z")
YC = ("y", "core")
ALL = ("y", "core", "x", "z")
BF = jnp.bfloat16
F32 = jnp.float32


def rms_scale(values, gain):
    floats = values.astype(F32)
    return (
        floats
        * lax.rsqrt(jnp.mean(floats * floats, axis=-1, keepdims=True) + EPS)
        * gain.astype(F32)
    )


def ancestor_table(parents):
    tree_size = parents.shape[-1]
    node_ids = jnp.arange(tree_size, dtype=jnp.int32)
    reachable = jnp.maximum(
        (parents[:, None] == node_ids[None, :]).astype(BF),
        (node_ids[:, None] == node_ids[None, :]).astype(BF),
    )
    for doubling in range(max(1, (tree_size - 1).bit_length())):
        reachable = jnp.minimum(
            jnp.dot(reachable, reachable, preferred_element_type=F32), 1.0
        ).astype(BF)
    return reachable.astype(F32)


def cache_attention(queries, cache, length):
    slots_total = cache.shape[2]
    block_width = min(BLOCK_SLOTS, slots_total)
    blocks = slots_total // block_width
    score_scale = HD ** (-0.5)
    tree_size = queries.shape[0]
    group_size = queries.shape[2]

    def add_block(block_index, running):
        numerator, denominator = running
        offset = block_index * block_width
        key_block = lax.dynamic_slice_in_dim(cache[0], offset, block_width, 1)
        value_block = lax.dynamic_slice_in_dim(cache[1], offset, block_width, 1)
        scores = jnp.exp(
            jnp.einsum("tkgd,ksd->kgts", queries, key_block, preferred_element_type=F32)
            * score_scale
        )
        slot_ids = offset + jnp.arange(block_width, dtype=jnp.int32)
        weights_now = jnp.where(slot_ids < length, scores, 0.0)
        numerator = numerator + jnp.einsum(
            "kgts,ksd->tkgd",
            weights_now.astype(BF),
            value_block,
            preferred_element_type=F32,
        )
        return (numerator, denominator + jnp.sum(weights_now, axis=3))

    start_state = (
        jnp.zeros((tree_size, KVH, group_size, HD), F32),
        jnp.zeros((KVH, group_size, tree_size), F32),
    )
    return lax.fori_loop(0, blocks, add_block, start_state)


def attention(tree_q, tree_kv, kv_cache, cache_lengths, tree_parents):
    tree_size = tree_q.shape[0]
    group_size = QH // KVH
    queries = tree_q.reshape(tree_size, KVH, group_size, HD)
    numerator, denominator = cache_attention(queries, kv_cache[0], cache_lengths[0])
    tree_keys = tree_kv[:, 0].reshape(tree_size, KVH, HD)
    tree_values = tree_kv[:, 1].reshape(tree_size, KVH, HD)
    tree_scores = jnp.exp(
        jnp.einsum("tkgd,skd->kgts", queries, tree_keys, preferred_element_type=F32)
        * HD ** (-0.5)
    )
    tree_weights = tree_scores * ancestor_table(tree_parents[0])
    numerator = numerator + jnp.einsum(
        "kgts,skd->tkgd", tree_weights.astype(BF), tree_values, preferred_element_type=F32
    )
    denominator = denominator + jnp.sum(tree_weights, axis=3)
    attended = numerator / jnp.transpose(denominator, (2, 0, 1))[..., None]
    return attended.reshape(tree_size, QH * HD).astype(BF)


def ring(values, axis, size, shift):
    return lax.ppermute(values, axis, [((i + shift) % size, i) for i in range(size)])


def spread(values, axes, size):
    copies = lax.optimization_barrier(jnp.broadcast_to(values[None], (size,) + values.shape))
    return lax.all_to_all(copies, axes, split_axis=0, concat_axis=0, tiled=True)


def out_projection(attended, out_weight):
    rows, depth = attended.shape
    width = out_weight.shape[1]
    half = depth // 2
    core, x = lax.axis_index("core"), lax.axis_index("x")
    own_half = lax.dynamic_slice_in_dim(out_weight, core * half, half, 0)
    halves = [own_half] + [ring(own_half, "x", X, shift) for shift in range(1, X)]
    own_weight = jnp.concatenate(halves, axis=1)
    other_weight = ring(own_weight, "core", CORE, 1)
    group = lax.all_gather(attended, "z", axis=0, tiled=True)
    own_part = lax.dynamic_slice_in_dim(group, core * half, half, 1)
    other_part = lax.dynamic_slice_in_dim(group, (1 - core) * half, half, 1)
    columns = (
        jnp.dot(own_part, own_weight, preferred_element_type=F32)
        + jnp.dot(other_part, other_weight, preferred_element_type=F32)
    ).astype(BF)
    back = lax.all_to_all(
        columns.reshape(Z, rows, X * width), "z", split_axis=0, concat_axis=0, tiled=True
    )
    back = back.reshape(Z, rows, X, width)
    placed = []
    for column_x in range(X):
        shift = (column_x - x) % X
        piece = back[:, :, 0]
        for candidate in range(1, X):
            piece = jnp.where(shift == candidate, back[:, :, candidate], piece)
        placed.append(piece)
    return jnp.concatenate([p[z] for p in placed for z in range(Z)], axis=1)


def unit_terms(mlp_rows, weights):
    gate_part = jnp.dot(mlp_rows, weights[0], preferred_element_type=F32)
    upward = jnp.dot(mlp_rows, weights[1], preferred_element_type=F32)
    active = (jax.nn.gelu(gate_part, approximate=True) * upward).astype(BF)
    return lax.dot_general(
        active, weights[2], (((1,), (1,)), ((), ())), preferred_element_type=F32
    ).astype(BF)


def shared_sum(partial, size):
    rows = partial.shape[0] // size
    pieces = lax.all_to_all(
        partial.reshape(size, rows, -1), XZ, split_axis=0, concat_axis=0, tiled=True
    )
    return jnp.sum(pieces.astype(F32), axis=0)


def per_device(
    hidden,
    tree_q,
    tree_kv,
    kv_cache,
    cache_lengths,
    tree_parents,
    accepted,
    tenant_ranges,
    out_weight,
    mlp_weights,
    draft_weights,
    embedding,
    attn_post_gain,
    ff_pre_gain,
    ff_post_gain,
    final_gain,
):
    units = X * Z
    core = lax.axis_index("core")
    unit = lax.axis_index(XZ)
    weights = lax.all_gather(mlp_weights, YC, axis=2, tiled=True)
    attended = attention(tree_q, tree_kv, kv_cache, cache_lengths, tree_parents)
    projected = out_projection(attended, out_weight)
    first = (hidden.astype(F32) + rms_scale(projected, attn_post_gain)).astype(BF)
    normed = rms_scale(first, ff_pre_gain).astype(BF)

    chosen = (
        accepted[0][:, None] == jnp.arange(first.shape[0], dtype=jnp.int32)[None, :]
    ).astype(BF)
    first_path = jnp.dot(chosen, first, preferred_element_type=F32)
    normed_path = jnp.dot(chosen, normed, preferred_element_type=F32).astype(BF)
    path_rows = spread(normed_path, XZ, units).reshape(units * ACC, -1)
    path_sum = shared_sum(unit_terms(path_rows, weights), units)
    path = (first_path + rms_scale(path_sum, ff_post_gain)).astype(BF)
    path_normed = rms_scale(path, final_gain).astype(BF)
    group_path = spread(path_normed, XZ, units).reshape(units * ACC, -1)

    column_width = draft_weights.shape[2]
    before = jnp.einsum("rd,hde->hre", group_path, draft_weights, preferred_element_type=F32)
    own_columns = lax.dynamic_slice_in_dim(group_path, unit * column_width, column_width, 1)
    drafts = (own_columns.astype(F32)[None] + jax.nn.silu(before)).astype(BF)
    drafts = spread(drafts, "y", Y)
    drafts = jnp.transpose(drafts, (1, 0, 2, 3)).reshape(HEADS, Y * units * ACC, column_width)
    own_drafts = lax.all_gather(drafts, XZ, axis=2, tiled=True)
    other_drafts = ring(own_drafts, "core", CORE, 1)

    mlp_rows = lax.all_gather(normed, XZ, axis=0, tiled=True)
    partial = unit_terms(mlp_rows, weights)
    partial, own_drafts = lax.optimization_barrier((partial, own_drafts))
    mlp_sum = shared_sum(partial, units)
    tree_out = (first.astype(F32) + rms_scale(mlp_sum, ff_post_gain)).astype(BF)

    low = jnp.where(core == 0, own_drafts, other_drafts)
    high = jnp.where(core == 0, other_drafts, own_drafts)
    rows = units * ACC
    every = jnp.stack(
        [low.reshape(HEADS, Y, rows, -1), high.reshape(HEADS, Y, rows, -1)], axis=2
    ).reshape(HEADS, Y * CORE * rows, -1)

    vocab_width = embedding.shape[0]
    vocab_ids = lax.axis_index(ALL) * vocab_width + jnp.arange(vocab_width, dtype=jnp.int32)
    starts = jnp.repeat(tenant_ranges[:, 0], ACC)
    range_ends = jnp.repeat(tenant_ranges[:, 1], ACC)
    allowed = (vocab_ids[None, :] >= starts[:, None]) & (vocab_ids[None, :] < range_ends[:, None])
    head_logits = []
    head_totals = []
    for head_index in range(HEADS):
        products = lax.dot_general(
            every[head_index], embedding, (((1,), (1,)), ((), ())), preferred_element_type=F32
        )
        logits = SOFTCAP * jnp.tanh(products / SOFTCAP)
        head_logits.append(logits)
        head_totals.append(jnp.sum(jnp.where(allowed, jnp.exp(logits), 0.0), axis=1))
    totals = jnp.stack(head_totals)
    totals = jnp.sum(spread(totals, YC, Y * CORE), axis=0)
    totals = jnp.sum(spread(totals, XZ, units), axis=0)
    draft_logprobs = jnp.stack(
        [
            jnp.where(allowed, head_logits[head_index] - jnp.log(totals[head_index])[:, None], 0.0)
            for head_index in range(HEADS)
        ]
    ).astype(BF)
    return (tree_out, draft_logprobs)


def solution(mesh):
    fine = Mesh(mesh.devices.reshape(Y, CORE, X, Z), ALL)
    return jax.shard_map(
        per_device,
        mesh=fine,
        in_specs=(
            P(ALL, None),
            P(ALL, None),
            P(ALL, None, None),
            P(ALL, None, None, None, None),
            P(ALL),
            P(ALL, None),
            P(ALL, None),
            P(),
            P(None, XZ),
            P(None, None, ALL),
            P(None, None, XZ),
            P(ALL, None),
            P(),
            P(),
            P(),
            P(),
        ),
        out_specs=(P(ALL, None), P(None, None, ALL)),
        check_vma=False,
    )
```

time: 549 us -> 341 us (0.62)
  waiting for transfers between devices: 354 us -> 132 us
  starting transfers between devices: 4.48 us -> 40.9 us
  blocking collectives: 65.4 us -> 32.7 us
  other arithmetic: 19.6 us -> 27.8 us
    all_gather x5 -> x3, waiting for transfers between devices: 267 us -> 58.5 us  [the longest x1 58.5 us: per_device(): own_drafts = lax.all_gather(drafts, XZ, axis=2, tiled=True)]
    reduce_scatter x1 -> x0, waiting for transfers between devices: 78.9 us -> none  [per_device(): lax.psum_scatter(partial_sums, 'unit', scatter_dimension=0, tiled=True)]
    all_to_all x1 -> x6, waiting for transfers between devices: 6.83 us -> 73.4 us  [the longest x2 48.5 us: shared_sum(): lax.all_to_all(partial.reshape(size, rows, -1), XZ, split_axis=0, concat_...]
    psum x1 -> x0, blocking collectives: 65.4 us -> none  [per_device(): totals = lax.psum(jnp.stack(head_totals), ('req', 'unit'))]
    all_to_all x1 -> x6, starting transfers between devices: 4.05 us -> 32.1 us  [the longest x3 20.4 us: spread(): return lax.all_to_all(copies, axes, split_axis=0, concat_axis=0, tiled=True)]
    all_to_all x0 -> x2, blocking collectives: none -> 19.3 us  [spread(): return lax.all_to_all(copies, axes, split_axis=0, concat_axis=0, tiled=True)]
    all_gather x0 -> x1, blocking collectives: none -> 13.5 us  [out_projection(): group = lax.all_gather(attended, 'z', axis=0, tiled=True)]
    ppermute x0 -> x5, starting transfers between devices: none -> 8.63 us  [ring(): lax.ppermute(values, axis, [((i + shift) % size, i) for i in range(size)])]
  transfers between devices with their start and end apart: 7 -> 14, of which waited for: 7 -> 7; matrix products, arithmetic and copies ran while one was open for 1% -> 19% of each run, Pallas kernels for 0% -> 0%
where the time goes in v1:
time: 341 us; the launch traced here: 339 us
  waiting for transfers between devices  132 us (39%)
  matrix products  65 us (19%)
  starting transfers between devices  40.9 us (12%)
  blocking collectives  32.7 us (10%)
  other arithmetic  27.8 us (8%)
  local copies, waits for them, and re-layouts  26.1 us (8%)
  between operations  14.5 us (4%)
    all_gather x1, waiting for transfers between devices, per_device(): own_drafts = lax.all_gather(drafts, XZ, axis=2, tiled=True)  58.5 us
    all_to_all x2, waiting for transfers between devices, shared_sum(): lax.all_to_all(partial.reshape(size, rows, -1), XZ, split_axis=0, concat_...  48.5 us
    dot_general x4, matrix products, per_device(): lax.dot_general(every[head_index], embedding, (((1,), (1,)), ((), ())), p...  34.8 us
    all_to_all x3, starting transfers between devices, spread(): return lax.all_to_all(copies, axes, split_axis=0, concat_axis=0, tiled=True)  20.4 us
    all_to_all x3, waiting for transfers between devices, spread(): return lax.all_to_all(copies, axes, split_axis=0, concat_axis=0, tiled=True)  19.9 us
    all_to_all x2, blocking collectives, spread(): return lax.all_to_all(copies, axes, split_axis=0, concat_axis=0, tiled=True)  19.3 us
    all_gather x1, blocking collectives, out_projection(): group = lax.all_gather(attended, 'z', axis=0, tiled=True)  13.5 us
    dot_general x2, matrix products, unit_terms(): lax.dot_general(active, weights[2], (((1,), (1,)), ((), ())), preferred_e...  11.9 us
  transfers between devices with their start and end apart: 14, of which 7 were waited for; matrix products, arithmetic and copies ran while one was open for 19% of the time, Pallas kernels for 0%

profile of v1, /device:TPU:1, one launch (start us, length us, event | category | flops | bytes accessed | tf_op | source)
XLA Modules:
  0.0 339.1 jit_solution(7296813015388025201)
XLA Ops:
  7.2 1.1 constant_dynamic-slice_fusion
  8.4 2.1 collective-permute-start.2
  10.5 2.5 collective-permute-start.1
  12.9 1.2 collective-permute-start
  14.1 1.1 reshape.185
  15.2 0.7 copy.321
  15.9 16.8 %while.16 = (s32[]{:T(128)}, f32[48,2,4,256]{3,0,2,1:T(8,128)S(1)}, f32[2,4,48]{2,1,0:T(4,128)S(1)}, bf16[2,2,2048,256]{3,2,1,0:T(8,128)(2,1)}, s32[]{:T(128)}, ...) while((s32[]{:T(128)}, f32[48,2,4,256]{3,0,2,1:T(8,128)S(1)}, ...), condition=%wide.region_2.3_spmd.clone, body=%wide.region_0.2_spmd.clone.sunk | while | flops 202311040 | bytes 12000466 | solution.py:78
  15.9 0.7 add_compare_fusion.2
  16.6 2.5 fusion.142
  20.0 0.7 add_compare_fusion.2
  20.7 2.5 fusion.142
  24.0 0.7 add_compare_fusion.2
  24.7 3.1 fusion.142
  28.7 0.7 add_compare_fusion.2
  29.4 2.5 fusion.142
  33.3 0.9 fusion.48
  34.3 0.7 copy-done.6
  35.0 2.0 pad_maximum_fusion.2
  37.0 1.4 collective-permute-start.3
  38.4 2.0 slice_reduce_fusion
  40.4 1.4 copy.324
  41.9 1.4 reshape_squeeze.7
  43.3 1.4 reshape_squeeze.6
  44.7 1.2 fusion.105
  45.9 1.1 fusion.36
  47.3 13.5 %all_gather.12 = bf16[192,2048]{1,0:T(8,128)(2,1)S(1)} all-gather(bf16[48,2048]{1,0:T(8,128)(2,1)S(1)} %convert_element_type.128), channel_id=1, replica_groups=mesh['y'=4,'core'=2,'x'=4,'z'=4] {'z'}, dimensions={0}, use_global_device_ids=true | all-gather | bytes 983040 | tf_op jit(solution)/shard_map/all_gather | solution.py:119
  61.1 2.3 fusion.35
  63.4 3.4 all-to-all-start
  67.0 5.0 %all-to-all-done = bf16[4,48,512]{2,1,0:T(8,128)(2,1)S(1)} async-done(((bf16[4,48,512]{2,1,0:T(8,128)(2,1)}), bf16[4,48,512]{2,1,0:T(8,128)(2,1)S(1)}, u32[]{:S(2)}, u32[]{:S(2)}) %all-to-all-start) | async-done | bytes 196640 | tf_op jit(solution)/shard_map/all_to_all | solution.py:126
  74.0 0.8 fusion.59
  74.8 1.1 convolution_convert_fusion.2
  76.0 9.9 %all_to_all.40 = bf16[16,4,2048]{2,1,0:T(4,128)(2,1)S(1)} all-to-all(bf16[16,4,2048]{2,1,0:T(4,128)(2,1)S(1)} %broadcast_in_dim.47), channel_id=1, replica_groups=mesh['y'=4,'core'=2,'x'=4,'z'=4] {'x','z'}, dimensions={0} | all-to-all | bytes 524288 | tf_op jit(solution)/shard_map/all_to_all | solution.py:107
  86.1 2.4 fusion.70
  88.5 3.4 %convolution_convert_fusion.1 = bf16[64,2048]{1,0:T(8,128)(2,1)S(1)} fusion(bf16[3,2048,512]{1,2,0:T(8,128)(2,1)} %all-gather.6.cloned.1.call-done, f32[64,512]{1,0:T(8,128)S(1)} %fusion.70, bf16[64,2048]{1,0:T(8,128)(2,1)S(1)} %reshape.188), kind=kOutput, calls=%fused_computation.40 | convolution fusion | flops 268632064 | bytes 4849664 | tf_op jit(solution)/shard_map/dot_general | solution.py:144
  91.9 0.8 reshape.189
  92.7 3.5 %all-to-all-start.2 = ((bf16[16,4,2048]{2,1,0:T(4,128)(2,1)}), bf16[16,4,2048]{2,1,0:T(4,128)(2,1)S(1)}, u32[]{:S(2)}, u32[]{:S(2)}) async-start(bf16[16,4,2048]{2,1,0:T(4,128)(2,1)} %reshape.189), calls=%async_computation.2 | async-start | bytes 524288 | tf_op jit(solution)/shard_map/all_to_all | solution.py:151
  96.3 7.2 %all-to-all-done.2 = bf16[16,4,2048]{2,1,0:T(4,128)(2,1)S(1)} async-done(((bf16[16,4,2048]{2,1,0:T(4,128)(2,1)}), bf16[16,4,2048]{2,1,0:T(4,128)(2,1)S(1)}, u32[]{:S(2)}, u32[]{:S(2)}) %all-to-all-start.2) | async-done | bytes 262176 | tf_op jit(solution)/shard_map/all_to_all | solution.py:151
  104.2 0.8 broadcast_in_dim.48
  105.1 3.5 %all-to-all-start.3 = ((bf16[16,4,2048]{2,1,0:T(4,128)(2,1)}), bf16[16,4,2048]{2,1,0:T(4,128)(2,1)S(1)}, u32[]{:S(2)}, u32[]{:S(2)}) async-start(bf16[16,4,2048]{2,1,0:T(4,128)(2,1)} %broadcast_in_dim.48), calls=%async_computation.3 | async-start | bytes 524288 | tf_op jit(solution)/shard_map/all_to_all | solution.py:107
  108.7 9.2 %all-to-all-done.3 = bf16[16,4,2048]{2,1,0:T(4,128)(2,1)S(1)} async-done(((bf16[16,4,2048]{2,1,0:T(4,128)(2,1)}), bf16[16,4,2048]{2,1,0:T(4,128)(2,1)S(1)}, u32[]{:S(2)}, u32[]{:S(2)}) %all-to-all-start.3) | async-done | bytes 262176 | tf_op jit(solution)/shard_map/all_to_all | solution.py:107
  118.6 9.3 %all_to_all.41 = bf16[4,4,64,128]{3,2,1,0:T(8,128)(2,1)S(1)} all-to-all(bf16[4,4,64,128]{3,2,1,0:T(8,128)(2,1)S(1)} %broadcast_in_dim.49), channel_id=1, replica_groups=mesh['y'=4,'core'=2,'x'=4,'z'=4] {'y'}, dimensions={0} | all-to-all | bytes 524288 | tf_op jit(solution)/shard_map/all_to_all | solution.py:107
  127.9 0.7 copy.328
  128.7 4.4 %fusion.21 = f32[768,512]{1,0:T(8,128)S(1)} fusion(bf16[768,2048]{1,0:T(8,128)(2,1)} %all-gather.4.cloned.1.call-done, bf16[3,2048,512]{1,2,0:T(8,128)(2,1)} %all-gather.6.cloned.1.call-done), kind=kOutput, calls=%fused_computation.57 | convolution fusion | flops 1610612736 | bytes 6815744 | tf_op jit(solution)/shard_map/dot_general | solution.py:141
  133.0 58.5 %all-gather.8.cloned.1.call-done = bf16[4,256,2048]{2,1,0:T(8,128)(2,1)} async-done(((bf16[4,256,128]{2,1,0:T(8,128)(2,1)}), bf16[4,256,2048]{2,1,0:T(8,128)(2,1)}) %all-gather.8.cloned.1.call-update) | async-done | bytes 4194320 | tf_op jit(solution)/shard_map/all_gather | solution.py:201
  191.5 1.5 collective-permute-start.4
  193.1 8.5 %convolution_convert_fusion = bf16[768,2048]{1,0:T(8,128)(2,1)} fusion(bf16[3,2048,512]{1,2,0:T(8,128)(2,1)} %all-gather.6.cloned.1.call-done, f32[768,512]{1,0:T(8,128)S(1)} %fusion.21, bf16[768,2048]{1,0:T(8,128)(2,1)} %all-gather.4.cloned.1.call-done), kind=kOutput, calls=%fused_computation.38 | convolution fusion | flops 3226730496 | bytes 12058624 | tf_op jit(solution)/shard_map/dot_general | solution.py:144
  201.6 4.8 %all-to-all-start.5 = ((bf16[16,48,2048]{2,1,0:T(8,128)(2,1)}), bf16[16,48,2048]{2,1,0:T(8,128)(2,1)}, u32[]{:S(2)}, u32[]{:S(2)}) async-start(bf16[16,48,2048]{2,1,0:T(8,128)(2,1)} %bitcast.172), calls=%async_computation.5 | async-start | bytes 6291456 | tf_op jit(solution)/shard_map/all_to_all | solution.py:151
  206.9 41.3 %all-to-all-done.5 = bf16[16,48,2048]{2,1,0:T(8,128)(2,1)} async-done(((bf16[16,48,2048]{2,1,0:T(8,128)(2,1)}), bf16[16,48,2048]{2,1,0:T(8,128)(2,1)}, u32[]{:S(2)}, u32[]{:S(2)}) %all-to-all-start.5) | async-done | bytes 3145760 | tf_op jit(solution)/shard_map/all_to_all | solution.py:151
  248.1 2.5 convert_reduce_fusion
  250.8 3.8 %broadcast_select_fusion.1 = (bf16[4,256,2048]{2,1,0:T(8,128)(2,1)S(1)}, bf16[4,256,2048]{2,1,0:T(8,128)(2,1)S(1)}) fusion(bf16[4,256,2048]{2,1,0:T(8,128)(2,1)} %all-gather.8.cloned.1.call-done, bf16[4,256,2048]{2,1,0:T(8,128)(2,1)} %collective-permute-done.4, pred[]{:T(512)S(6)} %eq.111), kind=kLoop, calls=%fused_computation.36 | loop fusion | flops 4194304 | bytes 16777216 | tf_op jit(solution)/shard_map/jit(_where)/select_n | solution.py:210
  254.6 1.8 fusion.17
  256.3 7.1 %fusion.107 = f32[512,2048]{1,0:T(8,128)S(1)} fusion(bf16[512,2048]{1,0:T(8,128)(2,1)S(1)} %bitcast.176, bf16[2048,2048]{1,0:T(8,128)(2,1)} %param.29), kind=kOutput, calls=%fused_computation.209 | convolution fusion | flops 4294967296 | bytes 14680064 | tf_op jit(solution)/shard_map/dot_general | solution.py:225
  263.5 8.5 %fusion.106 = f32[512,2048]{1,0:T(8,128)S(1)} fusion(bf16[512,2048]{1,0:T(8,128)(2,1)S(1)} %bitcast.175, bf16[2048,2048]{1,0:T(8,128)(2,1)} %param.29), kind=kOutput, calls=%fused_computation.208 | convolution fusion | flops 4294967296 | bytes 14680064 | tf_op jit(solution)/shard_map/dot_general | solution.py:225
  272.0 6.1 %fusion.108 = f32[512,2048]{1,0:T(8,128)} fusion(bf16[512,2048]{1,0:T(8,128)(2,1)S(1)} %bitcast.174, bf16[2048,2048]{1,0:T(8,128)(2,1)S(1)} %bitcast.189), kind=kOutput, calls=%fused_computation.210 | convolution fusion | flops 4294967296 | bytes 14680064 | tf_op jit(solution)/shard_map/dot_general | solution.py:225
  278.1 13.1 %select_reduce_fusion.3 = (f32[512]{0:T(512)S(1)}, f32[512]{0:T(512)S(1)}, f32[512]{0:T(512)S(1)}, f32[512]{0:T(512)S(1)}, f32[512,2048]{1,0:T(8,128)}) fusion(s32[512]{0:T(512)S(1)} %lt.75, s32[512]{0:T(512)S(1)} %ge.16, s32[2048]{0:T(1024)S(1)} %iota_add_fusion, f32[512,2048]{1,0:T(8,128)S(1)} %fusion.106, f32[512,2048]{1,0:T(8,128)S(1)} %fusion.107, ...), kind=kOutput, calls=%fused_computation.33 | convolution fusion | flops 4314888192 | bytes 27283456 | tf_op jit(solution)/shard_map/dot_general | solution.py:225
  291.2 0.6 broadcast_in_dim.100
  291.9 6.2 %all-to-all-start.6 = ((f32[8,4,512]{2,1,0:T(4,128)}), f32[8,4,512]{2,1,0:T(4,128)S(1)}, u32[]{:S(2)}, u32[]{:S(2)}) async-start(f32[8,4,512]{2,1,0:T(4,128)} %broadcast_in_dim.100), calls=%async_computation.6 | async-start | bytes 131072 | tf_op jit(solution)/shard_map/all_to_all | solution.py:107
  298.1 4.8 %all-to-all-done.6 = f32[8,4,512]{2,1,0:T(4,128)S(1)} async-done(((f32[8,4,512]{2,1,0:T(4,128)}), f32[8,4,512]{2,1,0:T(4,128)S(1)}, u32[]{:S(2)}, u32[]{:S(2)}) %all-to-all-start.6) | async-done | bytes 65568 | tf_op jit(solution)/shard_map/all_to_all | solution.py:107
  302.9 0.7 broadcast_in_dim.101
  303.6 10.7 %all-to-all-start.7 = ((f32[16,4,512]{2,1,0:T(4,128)}), f32[16,4,512]{2,1,0:T(4,128)S(1)}, u32[]{:S(2)}, u32[]{:S(2)}) async-start(f32[16,4,512]{2,1,0:T(4,128)} %broadcast_in_dim.101), calls=%async_computation.7 | async-start | bytes 262144 | tf_op jit(solution)/shard_map/all_to_all | solution.py:107
  314.3 0.8 fusion.60
  315.1 5.9 %all-to-all-done.7 = f32[16,4,512]{2,1,0:T(4,128)S(1)} async-done(((f32[16,4,512]{2,1,0:T(4,128)}), f32[16,4,512]{2,1,0:T(4,128)S(1)}, u32[]{:S(2)}, u32[]{:S(2)}) %all-to-all-start.7) | async-done | bytes 131104 | tf_op jit(solution)/shard_map/all_to_all | solution.py:107
  321.1 7.6 %fusion.13 = (bf16[1,512,2048]{2,1,0:T(8,128)(2,1)S(1)}, bf16[1,512,2048]{2,1,0:T(8,128)(2,1)S(1)}, bf16[1,512,2048]{2,1,0:T(8,128)(2,1)S(1)}, bf16[1,512,2048]{2,1,0:T(8,128)(2,1)S(1)}) fusion(f32[512,2048]{1,0:T(8,128)} %get-tuple-element.323, f32[512]{0:T(512)S(1)} %bitcast.180, s32[512]{0:T(512)S(1)} %lt.75, s32[512]{0:T(512)S(1)} %ge.16, ...), kind=kLoop, calls=%fused_computation.45 | loop fusion | flops 24117248 | bytes 25186304 | tf_op jit(solution)/shard_map/stack | solution.py:234
  328.7 3.9 %pad_maximum_fusion = bf16[4,512,2048]{2,1,0:T(8,128)(2,1)} fusion(bf16[1,512,2048]{2,1,0:T(8,128)(2,1)S(1)} %get-tuple-element.312, bf16[1,512,2048]{2,1,0:T(8,128)(2,1)S(1)} %get-tuple-element.311, bf16[1,512,2048]{2,1,0:T(8,128)(2,1)S(1)} %get-tuple-element.310, bf16[1,512,2048]{2,1,0:T(8,128)(2,1)S(1)} %get-tuple-element.309), kind=kLoop, calls=%fused_computation.21 | loop fusion | flops 12582912 | bytes 16777216 | tf_op jit(solution)/shard_map/stack | solution.py:234
  (131 shorter events, 8.9 us)
Async XLA Ops:
  7.2 110.8 %copy-start = (bf16[4,2048,128]{2,1,0:T(8,128)(2,1)S(1)}, bf16[4,2048,128]{2,1,0:T(8,128)(2,1)}, u32[]{:S(2)}) copy-start(bf16[4,2048,128]{2,1,0:T(8,128)(2,1)} %param.28) | copy-start | bytes 6291460
  7.2 78.9 %all-gather.6.cloned.1.call-start = ((), (), s32[]{:S(2)}) async-start(), calls=%async_computation.9 | async-start | bytes 7077888 | tf_op jit(solution)/shard_map/all_gather | solution.py:178
  8.3 25.9 %copy-start.4 = (bf16[1024,128]{1,0:T(8,128)(2,1)}, bf16[1024,128]{1,0:T(8,128)(2,1)S(1)}, u32[]{:S(2)}) copy-start(bf16[1024,128]{1,0:T(8,128)(2,1)S(1)} %constant_dynamic-slice_fusion) | copy-start | bytes 786436
  8.4 25.9 %collective-permute-start.2 = (bf16[1024,128]{1,0:T(8,128)(2,1)S(1)}, bf16[1024,128]{1,0:T(8,128)(2,1)S(1)}, u32[]{:S(2)}, u32[]{:S(2)}) collective-permute-start(bf16[1024,128]{1,0:T(8,128)(2,1)S(1)} %constant_dynamic-slice_fusion), channel_id=1, source_target_pairs={{12,0},{0,4},{4,8},{8,12},{13,1},{1,5},{5,9},{9,13},{14,2},{2,6},{... | collective-permute-start | bytes 786440 | tf_op jit(solution)/shard_map/ppermute | solution.py:102
  10.5 23.8 %collective-permute-start.1 = (bf16[1024,128]{1,0:T(8,128)(2,1)S(1)}, bf16[1024,128]{1,0:T(8,128)(2,1)S(1)}, u32[]{:S(2)}, u32[]{:S(2)}) collective-permute-start(bf16[1024,128]{1,0:T(8,128)(2,1)S(1)} %constant_dynamic-slice_fusion), channel_id=1, source_target_pairs={{8,0},{12,4},{0,8},{4,12},{9,1},{13,5},{1,9},{5,13},{10,2},{14,6},... | collective-permute-start | bytes 786440 | tf_op jit(solution)/shard_map/ppermute | solution.py:102
  12.9 21.3 %collective-permute-start = (bf16[1024,128]{1,0:T(8,128)(2,1)S(1)}, bf16[1024,128]{1,0:T(8,128)(2,1)}, u32[]{:S(2)}, u32[]{:S(2)}) collective-permute-start(bf16[1024,128]{1,0:T(8,128)(2,1)S(1)} %constant_dynamic-slice_fusion), channel_id=1, source_target_pairs={{4,0},{8,4},{12,8},{0,12},{5,1},{9,5},{13,9},{1,13},{6,2},{10,6},{... | collective-permute-start | bytes 786440 | tf_op jit(solution)/shard_map/ppermute | solution.py:102
  15.2 0.7 copy-start.5
  15.9 16.8 %copy-start.15 = (s32[1,48]{1,0:T(1,128)S(1)}, s32[1,48]{1,0:T(1,128)}, u32[]{:S(2)}) copy-start(s32[1,48]{1,0:T(1,128)} %param.23) | copy-start | bytes 580
  16.6 2.6 copy-start.8
  20.6 2.6 copy-start.8
  24.7 3.1 copy-start.8
  29.3 2.6 copy-start.8
  34.2 0.7 copy-start.6
  34.2 0.8 copy-start.7
  37.0 23.7 %collective-permute-start.3 = (bf16[1024,512]{1,0:T(8,128)(2,1)}, bf16[1024,512]{1,0:T(8,128)(2,1)S(1)}, u32[]{:S(2)}, u32[]{:S(2)}) collective-permute-start(bf16[1024,512]{1,0:T(8,128)(2,1)} %pad_maximum_fusion.2), channel_id=1, source_target_pairs={{16,0},{0,16},{17,1},{1,17},{18,2},{2,18},{19,3},{3,19},{20,4},{4,... | collective-permute-start | bytes 3145736 | tf_op jit(solution)/shard_map/ppermute | solution.py:102
  47.1 19.8 %copy-start.10 = (bf16[2048]{0:T(1024)(128)(2,1)S(1)}, bf16[2048]{0:T(1024)(128)(2,1)}, u32[]{:S(2)}) copy-start(bf16[2048]{0:T(1024)(128)(2,1)} %param.30) | copy-start | bytes 12292
  47.1 19.8 %copy-start.11 = (bf16[2048]{0:T(1024)(128)(2,1)S(1)}, bf16[2048]{0:T(1024)(128)(2,1)}, u32[]{:S(2)}) copy-start(bf16[2048]{0:T(1024)(128)(2,1)} %param.31) | copy-start | bytes 12292
  61.1 12.6 %copy-start.9 = (bf16[48,2048]{1,0:T(8,128)(2,1)S(1)}, bf16[48,2048]{1,0:T(8,128)(2,1)}, u32[]{:S(2)}) copy-start(bf16[48,2048]{1,0:T(8,128)(2,1)} %param.18) | copy-start | bytes 589828
  61.1 13.7 %copy-start.16 = (s32[1,4]{1,0:T(1,128)S(1)}, s32[1,4]{1,0:T(1,128)}, u32[]{:S(2)}) copy-start(s32[1,4]{1,0:T(1,128)} %param.24) | copy-start | bytes 52
  63.4 8.5 %all-to-all-start = ((bf16[4,48,512]{2,1,0:T(8,128)(2,1)}), bf16[4,48,512]{2,1,0:T(8,128)(2,1)S(1)}, u32[]{:S(2)}, u32[]{:S(2)}) async-start(bf16[4,48,512]{2,1,0:T(8,128)(2,1)} %bitcast.8), calls=%async_computation | async-start | bytes 393216 | tf_op jit(solution)/shard_map/all_to_all | solution.py:126
  66.8 61.9 %all-gather.4.cloned.1.call-start = ((), (), s32[]{:S(2)}) async-start(), calls=%async_computation.8 | async-start | bytes 3342336 | tf_op jit(solution)/shard_map/all_gather | solution.py:204
  86.0 10.2 %copy-start.12 = (bf16[2048]{0:T(1024)(128)(2,1)S(1)}, bf16[2048]{0:T(1024)(128)(2,1)}, u32[]{:S(2)}) copy-start(bf16[2048]{0:T(1024)(128)(2,1)} %param.32) | copy-start | bytes 12292
  86.1 10.2 %copy-start.13 = (bf16[2048]{0:T(1024)(128)(2,1)S(1)}, bf16[2048]{0:T(1024)(128)(2,1)}, u32[]{:S(2)}) copy-start(bf16[2048]{0:T(1024)(128)(2,1)} %param.33) | copy-start | bytes 12292
  92.7 10.8 %all-to-all-start.2 = ((bf16[16,4,2048]{2,1,0:T(4,128)(2,1)}), bf16[16,4,2048]{2,1,0:T(4,128)(2,1)S(1)}, u32[]{:S(2)}, u32[]{:S(2)}) async-start(bf16[16,4,2048]{2,1,0:T(4,128)(2,1)} %reshape.189), calls=%async_computation.2 | async-start | bytes 524288 | tf_op jit(solution)/shard_map/all_to_all | solution.py:151
  105.1 12.8 %all-to-all-start.3 = ((bf16[16,4,2048]{2,1,0:T(4,128)(2,1)}), bf16[16,4,2048]{2,1,0:T(4,128)(2,1)S(1)}, u32[]{:S(2)}, u32[]{:S(2)}) async-start(bf16[16,4,2048]{2,1,0:T(4,128)(2,1)} %broadcast_in_dim.48), calls=%async_computation.3 | async-start | bytes 524288 | tf_op jit(solution)/shard_map/all_to_all | solution.py:107
  108.6 82.9 %all-gather.8.cloned.1.call-start = ((), (), s32[]{:S(2)}) async-start(), calls=%async_computation.10 | async-start | bytes 4456448 | tf_op jit(solution)/shard_map/all_gather | solution.py:201
  191.5 59.3 %collective-permute-start.4 = (bf16[4,256,2048]{2,1,0:T(8,128)(2,1)}, bf16[4,256,2048]{2,1,0:T(8,128)(2,1)}, u32[]{:S(2)}, u32[]{:S(2)}) collective-permute-start(bf16[4,256,2048]{2,1,0:T(8,128)(2,1)} %all-gather.8.cloned.1.call-done), channel_id=1, source_target_pairs={{16,0},{0,16},{17,1},{1,17},{18,2},{2,18},{19,3},{3,19},{20,4},{4,... | collective-permute-start | bytes 12582920 | tf_op jit(solution)/shard_map/ppermute | solution.py:102
  201.6 4.9 %copy-start.14 = (s32[128,2]{0,1:T(2,128)S(1)}, s32[128,2]{0,1:T(2,128)}, u32[]{:S(2)}) copy-start(s32[128,2]{0,1:T(2,128)} %param.25) | copy-start | bytes 3076
  201.6 46.6 %all-to-all-start.5 = ((bf16[16,48,2048]{2,1,0:T(8,128)(2,1)}), bf16[16,48,2048]{2,1,0:T(8,128)(2,1)}, u32[]{:S(2)}, u32[]{:S(2)}) async-start(bf16[16,48,2048]{2,1,0:T(8,128)(2,1)} %bitcast.172), calls=%async_computation.5 | async-start | bytes 6291456 | tf_op jit(solution)/shard_map/all_to_all | solution.py:151
  256.3 15.6 %slice-start = ((s8[8388608]{0:T(1024)(128)(4,1)}), s8[4194304]{0:T(1024)(128)(4,1)S(1)}, s32[]{:S(2)}) async-start(s8[8388608]{0:T(1024)(128)(4,1)} %bitcast.188), calls=%async_computation.11 | async-start | bytes 8388608
  263.4 14.7 %copy-start.2 = (f32[512,2048]{1,0:T(8,128)}, f32[512,2048]{1,0:T(8,128)S(1)}, u32[]{:S(2)}) copy-start(f32[512,2048]{1,0:T(8,128)S(1)} %fusion.107) | copy-start | bytes 12582916
  263.5 8.5 %slice-start.1 = ((s8[8388608]{0:T(1024)(128)(4,1)}), s8[4194304]{0:T(1024)(128)(4,1)S(1)}, s32[]{:S(2)}) async-start(s8[8388608]{0:T(1024)(128)(4,1)} %bitcast.188), calls=%async_computation.12 | async-start | bytes 8388608
  272.0 6.2 %copy-start.3 = (f32[512,2048]{1,0:T(8,128)}, f32[512,2048]{1,0:T(8,128)S(1)}, u32[]{:S(2)}) copy-start(f32[512,2048]{1,0:T(8,128)S(1)} %fusion.106) | copy-start | bytes 12582916
  291.9 11.0 %all-to-all-start.6 = ((f32[8,4,512]{2,1,0:T(4,128)}), f32[8,4,512]{2,1,0:T(4,128)S(1)}, u32[]{:S(2)}, u32[]{:S(2)}) async-start(f32[8,4,512]{2,1,0:T(4,128)} %broadcast_in_dim.100), calls=%async_computation.6 | async-start | bytes 131072 | tf_op jit(solution)/shard_map/all_to_all | solution.py:107
  303.6 17.4 %all-to-all-start.7 = ((f32[16,4,512]{2,1,0:T(4,128)}), f32[16,4,512]{2,1,0:T(4,128)S(1)}, u32[]{:S(2)}, u32[]{:S(2)}) async-start(f32[16,4,512]{2,1,0:T(4,128)} %broadcast_in_dim.101), calls=%async_computation.7 | async-start | bytes 262144 | tf_op jit(solution)/shard_map/all_to_all | solution.py:107
  328.7 3.9 %copy-start.1 = (bf16[4,2048,128]{2,1,0:T(8,128)(2,1)S(1)}, bf16[4,2048,128]{2,1,0:T(8,128)(2,1)}, u32[]{:S(2)}) copy-start(bf16[4,2048,128]{2,1,0:T(8,128)(2,1)} %param.28) | copy-start | bytes 6291460
Sparse Core Ops, SparseCore 0:
  14.2 42.1 all-gather.5
  74.9 50.8 all-gather.3
  128.8 62.7 all-gather.7

commit v2 on v1

v2 whole, which is shorter than its diff:
```python
import jax
import jax.numpy as jnp
from jax import lax
from jax.experimental import pallas as pl
from jax.experimental.pallas import tpu as pltpu
from jax.sharding import Mesh, PartitionSpec as P

BF = jnp.bfloat16
F32 = jnp.float32
QH = 8
KVH = 2
HD = 256
HEADS = 4
SOFTCAP = 30.0
Y, CORE, X, Z = 4, 2, 4, 4
EPS = 1e-06
ACC = 4
XZ = ("x", "z")
YC = ("y", "core")
ALL = ("y", "core", "x", "z")
PIECE_PLACES = tuple(
    place
    for kind in range(2)
    for place in (
        (kind, 0, 2 * kind, 2 * kind + 2),
        (kind, 1, 2 * kind, 2 * kind + 2),
        (kind, 3, 2 * kind, 2 * kind + 2),
        (kind, 2, 2 * kind, 2 * kind + 1),
        (kind, 2, 2 * kind + 1, 2 * kind + 2),
    )
)
PIECES = len(PIECE_PLACES)
CONTRACT_LAST = (((1,), (1,)), ((), ()))


def attention_kernel(length_ref, q_ref, kv_ref, parents_ref, keys_ref, values_ref, out_ref, top, bottom, tree):
    rows = q_ref.shape[0]
    group = QH // KVH
    head, block = pl.program_id(0), pl.program_id(1)
    width = keys_ref.shape[0]
    queries = jnp.concatenate([q_ref[:, g * HD : (g + 1) * HD] for g in range(group)], axis=0)
    scale = HD ** (-0.5)

    @pl.when((head == 0) & (block == 0))
    def _():
        lanes = lax.broadcasted_iota(jnp.int32, (rows, rows), 1)
        subs = lax.broadcasted_iota(jnp.int32, (rows, rows), 0)
        reach = jnp.where((parents_ref[...] == lanes) | (subs == lanes), 1.0, 0.0)
        for _ in range(max(1, (rows - 1).bit_length())):
            half = reach.astype(BF)
            reach = jnp.minimum(jnp.dot(half, half, preferred_element_type=F32), 1.0)
        tree[...] = reach

    @pl.when(block == 0)
    def _():
        keys = kv_ref[0]
        scores = lax.dot_general(queries, keys, CONTRACT_LAST, preferred_element_type=F32)
        reach = tree[...]
        weights = jnp.exp(scores * scale) * jnp.concatenate([reach] * group, axis=0)
        bottom[...] = jnp.sum(weights, axis=1, keepdims=True)
        top[...] = jnp.dot(weights.astype(BF), kv_ref[1], preferred_element_type=F32)

    scores = lax.dot_general(queries, keys_ref[...], CONTRACT_LAST, preferred_element_type=F32)
    slots = block * width + lax.broadcasted_iota(jnp.int32, scores.shape, 1)
    weights = jnp.where(slots < length_ref[0], jnp.exp(scores * scale), 0.0)
    bottom[...] += jnp.sum(weights, axis=1, keepdims=True)
    top[...] += jnp.dot(weights.astype(BF), values_ref[...], preferred_element_type=F32)

    @pl.when(block == pl.num_programs(1) - 1)
    def _():
        attended = (top[...] / bottom[...]).astype(BF)
        for g in range(group):
            out_ref[:, g * HD : (g + 1) * HD] = attended[g * rows : (g + 1) * rows]


def attention(tree_q, tree_kv, kv_cache, cache_lengths, tree_parents):
    rows = tree_q.shape[0]
    group = QH // KVH
    slots = kv_cache.shape[3]
    block = min(1024, slots)
    kv = jnp.transpose(tree_kv, (1, 0, 2))
    spec = pl.BlockSpec
    return pl.pallas_call(
        attention_kernel,
        out_shape=jax.ShapeDtypeStruct((rows, QH * HD), BF),
        grid_spec=pltpu.PrefetchScalarGridSpec(
            num_scalar_prefetch=1,
            grid=(KVH, slots // block),
            in_specs=[
                spec((rows, group * HD), lambda k, b, n: (0, k)),
                spec((2, rows, HD), lambda k, b, n: (0, 0, k)),
                spec((rows, 1), lambda k, b, n: (0, 0)),
                spec((None, None, None, block, HD), lambda k, b, n: (0, 0, k, b, 0)),
                spec((None, None, None, block, HD), lambda k, b, n: (0, 1, k, b, 0)),
            ],
            out_specs=spec((rows, group * HD), lambda k, b, n: (0, k)),
            scratch_shapes=[
                pltpu.VMEM((group * rows, HD), F32),
                pltpu.VMEM((group * rows, 1), F32),
                pltpu.VMEM((rows, rows), F32),
            ],
        ),
        compiler_params=pltpu.CompilerParams(
            dimension_semantics=("arbitrary", "arbitrary"), vmem_limit_bytes=24 << 20
        ),
        cost_estimate=pl.CostEstimate(
            flops=4 * rows * QH * HD * slots,
            bytes_accessed=4 * KVH * slots * HD,
            transcendentals=rows * QH * slots,
        ),
    )(cache_lengths, tree_q, kv, tree_parents.reshape(rows, 1), kv_cache, kv_cache)


def logits_kernel(place_ref, *refs):
    pieces = refs[:PIECES]
    bounds_ref, embedding_ref = refs[PIECES : PIECES + 2]
    out_ref, totals_ref, rows_ref, running, sems = refs[-5:]
    step, steps = pl.program_id(0), pl.num_programs(0)
    heads, depth = rows_ref.shape[0], rows_ref.shape[2]
    count = rows_ref.shape[1]
    width = depth // (X * Z)
    x, z, start = place_ref[1], place_ref[2], place_ref[3]
    vocab = embedding_ref.shape[0]

    def copies():
        found = []
        for piece, (kind, d, first, last) in zip(pieces, PIECE_PLACES):
            for e in range(Z):
                dx, dz = (d, e) if kind == 0 else (e, d)
                column = (lax.rem(x + dx, X) * Z + lax.rem(z + dz, Z)) * width
                column = pl.multiple_of(column, width)
                found.append(
                    pltpu.make_async_copy(
                        piece.at[:, :, e * width : (e + 1) * width],
                        rows_ref.at[first:last, :, pl.ds(column, width)],
                        sems.at[len(found)],
                    )
                )
        return found

    @pl.when(step == 0)
    def _():
        started = copies()
        for copy in started:
            copy.start()
        for copy in started:
            copy.wait()
        running[...] = jnp.zeros_like(running)

    ids = start + step * vocab + lax.broadcasted_iota(jnp.int32, (count, vocab), 1)
    allowed = (ids >= bounds_ref[:, 0:1]) & (ids < bounds_ref[:, 1:2])
    for head in range(heads):
        products = lax.dot_general(
            rows_ref[head], embedding_ref[...], CONTRACT_LAST, preferred_element_type=F32
        )
        logits = SOFTCAP * jnp.tanh(products * (1.0 / SOFTCAP))
        out_ref[head] = logits.reshape(out_ref.shape[1:])
        terms = jnp.where(allowed, jnp.exp(logits), 0.0)
        part = terms[:, :128]
        for lane in range(128, vocab, 128):
            part = part + terms[:, lane : lane + 128]
        running[head] += part

    @pl.when(step == steps - 1)
    def _():
        for head in range(heads):
            totals_ref[head : head + 1, :] = jnp.sum(
                jnp.transpose(running[head]), axis=0, keepdims=True
            )


def some_logits(place, pieces, bounds, embedding, table):
    heads = HEADS
    count = pieces[0].shape[1]
    vocab_width, depth = embedding.shape
    vocab = min(256, vocab_width)
    spec = pl.BlockSpec
    out_shape = jax.ShapeDtypeStruct((heads, Y, CORE, count // Y, vocab_width), F32)
    given = [place, *pieces, bounds, embedding]
    aliases = {}
    extra_specs = []
    if table is not None:
        given.append(table)
        aliases = {len(given) - 1: 0}
        extra_specs = [spec(memory_space=pl.ANY)]
    return pl.pallas_call(
        logits_kernel,
        out_shape=(out_shape, jax.ShapeDtypeStruct((heads, count), F32)),
        grid_spec=pltpu.PrefetchScalarGridSpec(
            num_scalar_prefetch=1,
            grid=(vocab_width // vocab,),
            in_specs=[spec(memory_space=pl.ANY)] * len(pieces)
            + [
                spec((count, 2), lambda j, p: (0, 0)),
                spec((vocab, depth), lambda j, p: (j, 0)),
            ]
            + extra_specs,
            out_specs=(
                spec((heads, Y, None, count // Y, vocab), lambda j, p: (0, 0, p[0], 0, j)),
                spec((heads, count), lambda j, p: (0, 0)),
            ),
            scratch_shapes=[
                pltpu.VMEM((heads, count, depth), BF),
                pltpu.VMEM((heads, count, 128), F32),
                pltpu.SemaphoreType.DMA((PIECES * Z,)),
            ],
        ),
        input_output_aliases=aliases,
        compiler_params=pltpu.CompilerParams(
            dimension_semantics=("arbitrary",), vmem_limit_bytes=32 << 20
        ),
        cost_estimate=pl.CostEstimate(
            flops=2 * heads * count * vocab_width * depth,
            bytes_accessed=2 * vocab_width * depth + 4 * heads * count * vocab_width,
            transcendentals=2 * heads * count * vocab_width,
        ),
    )(*given)


def finish_kernel(place_ref, table_ref, logs_ref, bounds_ref, out_ref):
    step = pl.program_id(0)
    heads, count, vocab = table_ref.shape
    ids = place_ref[3] + step * vocab + lax.broadcasted_iota(jnp.int32, (count, vocab), 1)
    allowed = (ids >= bounds_ref[:, 0:1]) & (ids < bounds_ref[:, 1:2])
    for head in range(heads):
        values = table_ref[head] - logs_ref[:, head : head + 1]
        out_ref[head] = jnp.where(allowed, values, 0.0).astype(BF)


def finish(place, table, logs, bounds):
    heads, count, vocab_width = table.shape
    vocab = min(256, vocab_width)
    spec = pl.BlockSpec
    return pl.pallas_call(
        finish_kernel,
        out_shape=jax.ShapeDtypeStruct(table.shape, BF),
        grid_spec=pltpu.PrefetchScalarGridSpec(
            num_scalar_prefetch=1,
            grid=(vocab_width // vocab,),
            in_specs=[
                spec((heads, count, vocab), lambda j, p: (0, 0, j)),
                spec((count, heads), lambda j, p: (0, 0)),
                spec((count, 2), lambda j, p: (0, 0)),
            ],
            out_specs=spec((heads, count, vocab), lambda j, p: (0, 0, j)),
        ),
        compiler_params=pltpu.CompilerParams(
            dimension_semantics=("arbitrary",), vmem_limit_bytes=32 << 20
        ),
        cost_estimate=pl.CostEstimate(
            flops=4 * heads * count * vocab_width,
            bytes_accessed=6 * heads * count * vocab_width,
            transcendentals=0,
        ),
    )(place, table, logs, bounds)


def rms_scale(values, gain):
    floats = values.astype(F32)
    return (
        floats
        * lax.rsqrt(jnp.mean(floats * floats, axis=-1, keepdims=True) + EPS)
        * gain.astype(F32)
    )


def after(values, *earlier):
    return lax.optimization_barrier((values, *earlier))[0]


def ring(values, axis, size, shift):
    return lax.ppermute(values, axis, [((i + shift) % size, i) for i in range(size)])


def spread(values, axes, size):
    copies = lax.optimization_barrier(jnp.broadcast_to(values[None], (size,) + values.shape))
    return lax.all_to_all(copies, axes, split_axis=0, concat_axis=0, tiled=True)


def in_order(blocks, index):
    size = len(blocks)
    ordered = []
    for position in range(size):
        shift = (position - index) % size
        block = blocks[0]
        for candidate in range(1, size):
            block = jnp.where(shift == candidate, blocks[candidate], block)
        ordered.append(block)
    return ordered


def out_weights(out_weight):
    half = out_weight.shape[0] // 2
    own = lax.dynamic_slice_in_dim(out_weight, lax.axis_index("core") * half, half, 0)
    own = jnp.concatenate([own] + [ring(own, "x", X, shift) for shift in range(1, X)], axis=1)
    return own, ring(own, "core", CORE, 1)


def out_projection(attended, own_weight, other_weight):
    rows, depth = attended.shape
    half = depth // 2
    core = lax.axis_index("core")
    group = jnp.concatenate(
        [attended] + [ring(attended, "z", Z, shift) for shift in range(1, Z)], axis=0
    )
    own_part = lax.dynamic_slice_in_dim(group, core * half, half, 1)
    other_part = lax.dynamic_slice_in_dim(group, (1 - core) * half, half, 1)
    columns = (
        jnp.dot(own_part, own_weight, preferred_element_type=F32)
        + jnp.dot(other_part, other_weight, preferred_element_type=F32)
    ).astype(BF)
    width = columns.shape[1] // X
    back = [columns[:rows]]
    for shift in range(1, Z):
        slot = (Z - shift) % Z
        back.append(ring(columns[slot * rows : (slot + 1) * rows], "z", Z, shift))
    by_z = in_order(back, lax.axis_index("z"))
    by_x = in_order(
        [
            jnp.concatenate([b[:, d * width : (d + 1) * width] for b in by_z], axis=1)
            for d in range(X)
        ],
        lax.axis_index("x"),
    )
    return jnp.concatenate(by_x, axis=1)


def unit_terms(mlp_rows, weights):
    gate_part = jnp.dot(mlp_rows, weights[0], preferred_element_type=F32)
    upward = jnp.dot(mlp_rows, weights[1], preferred_element_type=F32)
    active = (jax.nn.gelu(gate_part, approximate=True) * upward).astype(BF)
    return lax.dot_general(
        active, weights[2], (((1,), (1,)), ((), ())), preferred_element_type=F32
    ).astype(BF)


def gather_drafts(drafts):
    pieces = []
    firsts = []
    for kind, near in ((0, "z"), (1, "x")):
        part = drafts[2 * kind : 2 * kind + 2]
        ahead, behind = ring(part, near, X, 1), ring(part, near, X, 3)
        firsts.append((part, ahead, behind))
    joined = []
    for (kind, near), (part, ahead, behind) in zip(((0, "z"), (1, "x")), firsts):
        across = ring(ahead, near, X, 1)
        joined.append(jnp.concatenate([part, ahead, across, behind], axis=2))
    seconds = []
    for far, part in zip(("x", "z"), joined):
        seconds.append((part, ring(part, far, X, 1), ring(part, far, X, 3)))
    for far, (part, ahead, behind) in zip(("x", "z"), seconds):
        pieces += [part, ahead, behind, ring(ahead[:1], far, X, 1), ring(behind[1:], far, X, 3)]
    return pieces


def per_device(
    hidden,
    tree_q,
    tree_kv,
    kv_cache,
    cache_lengths,
    tree_parents,
    accepted,
    tenant_ranges,
    out_weight,
    mlp_weights,
    draft_weights,
    embedding,
    attn_post_gain,
    ff_pre_gain,
    ff_post_gain,
    final_gain,
):
    units = X * Z
    rows = units * ACC
    core = lax.axis_index("core")
    y = lax.axis_index("y")
    unit = lax.axis_index(XZ)
    weights = lax.all_gather(mlp_weights, YC, axis=2, tiled=True)
    chosen = (
        accepted[0][:, None] == jnp.arange(hidden.shape[0], dtype=jnp.int32)[None, :]
    ).astype(BF)

    def pick(values):
        return jnp.dot(chosen, values, preferred_element_type=F32).astype(BF)

    path_hidden = spread(pick(hidden), XZ, units).reshape(rows, -1)
    own_weight, other_weight = out_weights(out_weight)
    attended = attention(tree_q, tree_kv, kv_cache, cache_lengths, tree_parents)

    path_attended = spread(pick(attended), XZ, units).reshape(rows, -1)
    path_columns = jnp.dot(path_attended, out_weight, preferred_element_type=F32).astype(BF)
    path_columns = spread(path_columns, XZ, units)
    path_projected = jnp.transpose(path_columns, (1, 0, 2)).reshape(rows, -1)
    path_first = (path_hidden.astype(F32) + rms_scale(path_projected, attn_post_gain)).astype(BF)
    path_rows = rms_scale(path_first, ff_pre_gain).astype(BF)
    path_terms = unit_terms(path_rows, weights)
    path_terms = lax.all_to_all(
        path_terms.reshape(units, ACC, -1), XZ, split_axis=0, concat_axis=0, tiled=True
    )
    path_sum = jnp.sum(path_terms.astype(F32), axis=0)
    own_first = lax.dynamic_slice_in_dim(path_first, unit * ACC, ACC, 0)
    path = (own_first.astype(F32) + rms_scale(path_sum, ff_post_gain)).astype(BF)
    path_normed = rms_scale(path, final_gain).astype(BF)
    group_path = spread(path_normed, XZ, units).reshape(rows, -1)

    width = draft_weights.shape[2]
    before = jnp.einsum("rd,hde->hre", group_path, draft_weights, preferred_element_type=F32)
    own_columns = lax.dynamic_slice_in_dim(group_path, unit * width, width, 1)
    drafts = (own_columns.astype(F32)[None] + jax.nn.silu(before)).astype(BF)
    drafts = in_order([drafts] + [ring(drafts, "y", Y, shift) for shift in range(1, Y)], y)
    drafts = jnp.concatenate(drafts, axis=1)
    pieces = gather_drafts(drafts)

    projected = out_projection(after(attended, path_attended), own_weight, other_weight)
    first = (hidden.astype(F32) + rms_scale(projected, attn_post_gain)).astype(BF)
    normed = rms_scale(first, ff_pre_gain).astype(BF)
    mlp_rows = lax.all_gather(normed, XZ, axis=0, tiled=True)
    partial = unit_terms(after(mlp_rows, drafts), weights)
    mlp_sum = lax.psum_scatter(partial, XZ, scatter_dimension=0, tiled=True).astype(F32)

    vocab_width = embedding.shape[0]
    start = lax.axis_index(ALL) * vocab_width
    bounds = jnp.repeat(tenant_ranges, ACC, axis=0)
    by_core = bounds.reshape(Y, CORE, rows, 2)

    def place_of(which):
        return jnp.stack([which, lax.axis_index("x"), lax.axis_index("z"), start]).astype(jnp.int32)

    def bounds_of(which):
        return lax.dynamic_index_in_dim(by_core, which, 1, keepdims=False).reshape(Y * rows, 2)

    table, own_totals = some_logits(place_of(core), pieces, bounds_of(core), embedding, None)
    other_pieces = [ring(piece, "core", CORE, 1) for piece in pieces]
    table, other_totals = some_logits(
        place_of(1 - core), other_pieces, bounds_of(1 - core), embedding, table
    )
    sums = jnp.stack(
        [
            jnp.sum(spread(own_totals, XZ, units), axis=0),
            jnp.sum(spread(other_totals, XZ, units), axis=0),
        ]
    )
    sums = sums + ring(sums, "y", Y, 1) + ring(sums, "y", Y, 2) + ring(sums, "y", Y, 3)
    swapped = ring(sums, "core", CORE, 1)
    logs = jnp.log(sums + swapped[::-1])
    logs = jnp.where(core == 0, logs, logs[::-1]).reshape(CORE, HEADS, Y, rows)
    logs = jnp.transpose(logs, (2, 0, 3, 1)).reshape(Y * CORE * rows, HEADS)
    draft_logprobs = finish(
        place_of(core), table.reshape(HEADS, Y * CORE * rows, vocab_width), logs, bounds
    )
    mlp_sum = after(mlp_sum, sums)
    tree_out = (first.astype(F32) + rms_scale(mlp_sum, ff_post_gain)).astype(BF)
    return (tree_out, draft_logprobs)


def solution(mesh):
    fine = Mesh(mesh.devices.reshape(Y, CORE, X, Z), ALL)
    return jax.shard_map(
        per_device,
        mesh=fine,
        in_specs=(
            P(ALL, None),
            P(ALL, None),
            P(ALL, None, None),
            P(ALL, None, None, None, None),
            P(ALL),
            P(ALL, None),
            P(ALL, None),
            P(),
            P(None, XZ),
            P(None, None, ALL),
            P(None, None, XZ),
            P(ALL, None),
            P(),
            P(),
            P(),
            P(),
        ),
        out_specs=(P(ALL, None), P(None, None, ALL)),
        check_vma=False,
    )
```

time: 341 us -> 297 us (0.87)
  waiting for transfers between devices: 132 us -> 68.2 us
  starting transfers between devices: 40.9 us -> 103 us
  Pallas kernels: 0 us -> 44.5 us
  matrix products: 65 us -> 23.6 us
  blocking collectives: 32.7 us -> 0 us
  other arithmetic: 27.8 us -> 9.05 us
  local copies, waits for them, and re-layouts: 26.1 us -> 32.1 us
    ppermute x5 -> x41, starting transfers between devices: 8.63 us -> 72 us  [ring(): lax.ppermute(values, axis, [((i + shift) % size, i) for i in range(size)])]
    all_gather x1 -> x0, waiting for transfers between devices: 58.5 us -> none  [per_device(): own_drafts = lax.all_gather(drafts, XZ, axis=2, tiled=True)]
    all_to_all x3 -> x1, waiting for transfers between devices: 53.5 us -> 7.4 us  [per_device(): lax.all_to_all(path_terms.reshape(units, ACC, -1), XZ, split_axis=0, conc...]
    pallas_call x0 -> x4, Pallas kernels: none -> 44.5 us  [the longest x2 32.5 us: some_logits(): pl.pallas_call(logits_kernel, out_shape=(out_shape, jax.ShapeDtypeStruct(...]
    dot_general x19 -> x3, matrix products: 43.1 us -> 0.62 us  [the longest x2 0.4 us: pick(): return jnp.dot(chosen, values, preferred_element_type=F32).astype(BF)]
    ppermute x5 -> x41, waiting for transfers between devices: 0.01 us -> 32.4 us  [ring(): lax.ppermute(values, axis, [((i + shift) % size, i) for i in range(size)])]
    all_to_all x2 -> x0, blocking collectives: 19.3 us -> none  [spread(): return lax.all_to_all(copies, axes, split_axis=0, concat_axis=0, tiled=True)]
    unnamed x52 -> x39, local copies, waits for them, and re-layouts: 1.74 us -> 17.4 us
  transfers between devices with their start and end apart: 14 -> 51, of which waited for: 7 -> 20; matrix products, arithmetic and copies ran while one was open for 19% -> 11% of each run, Pallas kernels for 0% -> 15%
where the time goes in v2:
time: 297 us; the launch traced here: 295 us
  starting transfers between devices  103 us (35%)
  waiting for transfers between devices  68.2 us (23%)
  Pallas kernels  44.5 us (15%)
  local copies, waits for them, and re-layouts  32.1 us (11%)
  matrix products  23.6 us (8%)
  between operations  15 us (5%)
  other arithmetic  9.05 us (3%)
    ppermute x41, starting transfers between devices, ring(): lax.ppermute(values, axis, [((i + shift) % size, i) for i in range(size)])  72 us
    pallas_call x2, Pallas kernels, some_logits(): pl.pallas_call(logits_kernel, out_shape=(out_shape, jax.ShapeDtypeStruct(...  32.5 us
    ppermute x41, waiting for transfers between devices, ring(): lax.ppermute(values, axis, [((i + shift) % size, i) for i in range(size)])  32.4 us
    all_to_all x6, waiting for transfers between devices, spread(): return lax.all_to_all(copies, axes, split_axis=0, concat_axis=0, tiled=True)  27.6 us
    all_to_all x6, starting transfers between devices, spread(): return lax.all_to_all(copies, axes, split_axis=0, concat_axis=0, tiled=True)  27.3 us
    unnamed x39, local copies, waits for them, and re-layouts  17.4 us
    dot_general x2, matrix products, unit_terms(): lax.dot_general(active, weights[2], (((1,), (1,)), ((), ())), preferred_e...  12 us
    pallas_call x1, Pallas kernels, finish(): pl.pallas_call(finish_kernel, out_shape=jax.ShapeDtypeStruct(table.shape,...  8.04 us
  transfers between devices with their start and end apart: 51, of which 20 were waited for; matrix products, arithmetic and copies ran while one was open for 11% of the time, Pallas kernels for 15%

profile of v2, /device:TPU:1, one launch (start us, length us, event | category | flops | bytes accessed | tf_op | source)
XLA Modules:
  0.0 295.4 jit_solution(2632072773710016641)
XLA Ops:
  7.9 1.0 constant_dynamic-slice_fusion.2
  8.9 2.1 collective-permute-start.5
  11.0 2.5 collective-permute-start.4
  13.5 1.2 collective-permute-start.3
  16.0 0.9 copy.70
  16.9 2.2 copy-done.3
  19.1 0.9 copy-done.4
  20.0 3.9 %shard_map.167 = bf16[48,2048]{1,0:T(8,128)(2,1)S(1)} custom-call(s32[1]{0:T(128)S(6)} %copy.75.length_ref, bf16[48,2048]{1,0:T(8,128)(2,1)S(1)} %copy-done.4, bf16[2,48,512]{2,1,0:T(8,128)(2,1)S(1)} %bitcast.73, s32[48,1]{1,0:T(8,128)S(1)} %copy.53.parents_ref, bf16[1,2,2,2048,256]{4,3,2,1,0:T(8,128)(2,1)S(1)} %copy-done.3, ...), custom_call_target="tpu_custom_call" | custom-call | flops 805306368 | bytes 4194304 | tf_op jit(solution)/shard_map/pallas_call | solution.py:83
  25.0 5.2 %all-to-all-start = ((bf16[16,4,2048]{2,1,0:T(4,128)(2,1)}), bf16[16,4,2048]{2,1,0:T(4,128)(2,1)S(1)}, u32[]{:S(2)}, u32[]{:S(2)}) async-start(bf16[16,4,2048]{2,1,0:T(4,128)(2,1)} %broadcast_in_dim.14), calls=%async_computation | async-start | bytes 524288 | tf_op jit(solution)/shard_map/all_to_all | solution.py:277
  30.3 2.1 pad_maximum_fusion
  32.4 1.8 collective-permute-start.6
  34.2 3.3 %all-to-all-done = bf16[16,4,2048]{2,1,0:T(4,128)(2,1)S(1)} async-done(((bf16[16,4,2048]{2,1,0:T(4,128)(2,1)}), bf16[16,4,2048]{2,1,0:T(4,128)(2,1)S(1)}, u32[]{:S(2)}, u32[]{:S(2)}) %all-to-all-start) | async-done | bytes 262176 | tf_op jit(solution)/shard_map/all_to_all | solution.py:277
  37.8 1.9 collective-permute-start.1
  39.7 1.4 collective-permute-start
  41.1 5.9 %collective-permute-done = bf16[48,2048]{1,0:T(8,128)(2,1)S(1)} collective-permute-done((bf16[48,2048]{1,0:T(8,128)(2,1)S(1)}, bf16[48,2048]{1,0:T(8,128)(2,1)S(1)}, u32[]{:S(2)}, u32[]{:S(2)}) %collective-permute-start) | collective-permute-done | bytes 196640 | tf_op jit(solution)/shard_map/ppermute | solution.py:272
  47.1 1.6 fusion.32
  48.7 1.5 fusion.13
  50.9 4.1 %collective-permute-start.9 = (bf16[48,512]{1,0:T(8,128)(2,1)}, bf16[48,512]{1,0:T(8,128)(2,1)S(1)}, u32[]{:S(2)}, u32[]{:S(2)}) collective-permute-start(bf16[48,512]{1,0:T(8,128)(2,1)} %get-tuple-element.36), channel_id=1, source_target_pairs={{1,0},{2,1},{3,2},{0,3},{5,4},{6,5},{7,6},{4,7},{9,8},{10,9},{11,1... | collective-permute-start | bytes 147464 | tf_op jit(solution)/shard_map/ppermute | solution.py:272
  55.5 0.9 collective-permute-done.9
  56.4 3.2 %collective-permute-done.8 = bf16[48,512]{1,0:T(8,128)(2,1)S(1)} collective-permute-done((bf16[48,512]{1,0:T(8,128)(2,1)}, bf16[48,512]{1,0:T(8,128)(2,1)S(1)}, u32[]{:S(2)}, u32[]{:S(2)}) %collective-permute-start.8) | collective-permute-done | bytes 49184 | tf_op jit(solution)/shard_map/ppermute | solution.py:272
  62.8 3.5 %all-to-all-start.2 = ((bf16[16,64,128]{2,1,0:T(8,128)(2,1)}), bf16[16,64,128]{2,1,0:T(8,128)(2,1)S(1)}, u32[]{:S(2)}, u32[]{:S(2)}) async-start(bf16[16,64,128]{2,1,0:T(8,128)(2,1)} %broadcast_in_dim.16), calls=%async_computation.2 | async-start | bytes 524288 | tf_op jit(solution)/shard_map/all_to_all | solution.py:277
  67.4 6.3 %all-to-all-done.2 = bf16[16,64,128]{2,1,0:T(8,128)(2,1)S(1)} async-done(((bf16[16,64,128]{2,1,0:T(8,128)(2,1)}), bf16[16,64,128]{2,1,0:T(8,128)(2,1)S(1)}, u32[]{:S(2)}, u32[]{:S(2)}) %all-to-all-start.2) | async-done | bytes 262176 | tf_op jit(solution)/shard_map/all_to_all | solution.py:277
  73.6 3.5 %all-to-all-start.1 = ((bf16[16,4,2048]{2,1,0:T(4,128)(2,1)}), bf16[16,4,2048]{2,1,0:T(4,128)(2,1)S(1)}, u32[]{:S(2)}, u32[]{:S(2)}) async-start(bf16[16,4,2048]{2,1,0:T(4,128)(2,1)} %broadcast_in_dim.15), calls=%async_computation.1 | async-start | bytes 524288 | tf_op jit(solution)/shard_map/all_to_all | solution.py:277
  77.5 1.1 copy.54
  78.6 1.2 reshape.183
  79.8 5.1 %all-to-all-done.1 = bf16[16,4,2048]{2,1,0:T(4,128)(2,1)S(1)} async-done(((bf16[16,4,2048]{2,1,0:T(4,128)(2,1)}), bf16[16,4,2048]{2,1,0:T(4,128)(2,1)S(1)}, u32[]{:S(2)}, u32[]{:S(2)}) %all-to-all-start.1) | async-done | bytes 262176 | tf_op jit(solution)/shard_map/all_to_all | solution.py:277
  85.7 3.0 %fusion.41 = f32[64,512]{1,0:T(8,128)} fusion(bf16[64,2048]{1,0:T(8,128)(2,1)S(1)} %convert_element_type.162, bf16[3,2048,512]{1,2,0:T(8,128)(2,1)} %all-gather.5.cloned.1.call-done), kind=kOutput, calls=%fused_computation.72 | convolution fusion | flops 134479872 | bytes 2490368 | tf_op jit(solution)/shard_map/dot_general | solution.py:329
  88.7 3.5 %convolution_convert_fusion.1 = bf16[64,2048]{1,0:T(8,128)(2,1)S(1)} fusion(bf16[3,2048,512]{1,2,0:T(8,128)(2,1)} %all-gather.5.cloned.1.call-done, f32[64,512]{1,0:T(8,128)} %fusion.41, bf16[64,2048]{1,0:T(8,128)(2,1)S(1)} %convert_element_type.162), kind=kOutput, calls=%fused_computation.2 | convolution fusion | flops 268632064 | bytes 4849664 | tf_op jit(solution)/shard_map/dot_general | solution.py:332
  93.1 3.5 %all-to-all-start.3 = ((bf16[16,4,2048]{2,1,0:T(4,128)(2,1)}), bf16[16,4,2048]{2,1,0:T(4,128)(2,1)S(1)}, u32[]{:S(2)}, u32[]{:S(2)}) async-start(bf16[16,4,2048]{2,1,0:T(4,128)(2,1)} %reshape.173), calls=%async_computation.3 | async-start | bytes 524288 | tf_op jit(solution)/shard_map/all_to_all | solution.py:398
  98.4 7.4 %all-to-all-done.3 = bf16[16,4,2048]{2,1,0:T(4,128)(2,1)S(1)} async-done(((bf16[16,4,2048]{2,1,0:T(4,128)(2,1)}), bf16[16,4,2048]{2,1,0:T(4,128)(2,1)S(1)}, u32[]{:S(2)}, u32[]{:S(2)}) %all-to-all-start.3) | async-done | bytes 262176 | tf_op jit(solution)/shard_map/all_to_all | solution.py:398
  106.1 1.1 fusion.42
  108.1 4.3 %all-to-all-start.4 = ((bf16[16,4,2048]{2,1,0:T(4,128)(2,1)}), bf16[16,4,2048]{2,1,0:T(4,128)(2,1)S(1)}, u32[]{:S(2)}, u32[]{:S(2)}) async-start(bf16[16,4,2048]{2,1,0:T(4,128)(2,1)} %broadcast_in_dim.17), calls=%async_computation.4 | async-start | bytes 524288 | tf_op jit(solution)/shard_map/all_to_all | solution.py:277
  112.4 7.3 %all-to-all-done.4 = bf16[16,4,2048]{2,1,0:T(4,128)(2,1)S(1)} async-done(((bf16[16,4,2048]{2,1,0:T(4,128)(2,1)}), bf16[16,4,2048]{2,1,0:T(4,128)(2,1)S(1)}, u32[]{:S(2)}, u32[]{:S(2)}) %all-to-all-start.4) | async-done | bytes 262176 | tf_op jit(solution)/shard_map/all_to_all | solution.py:277
  120.4 2.7 collective-permute-start.12
  124.4 3.6 %collective-permute-done.11 = bf16[4,64,128]{2,1,0:T(8,128)(2,1)S(1)} collective-permute-done((bf16[4,64,128]{2,1,0:T(8,128)(2,1)S(1)}, bf16[4,64,128]{2,1,0:T(8,128)(2,1)S(1)}, u32[]{:S(2)}, u32[]{:S(2)}) %collective-permute-start.11) | collective-permute-done | bytes 65568 | tf_op jit(solution)/shard_map/ppermute | solution.py:272
  128.5 4.4 %fusion = f32[768,512]{1,0:T(8,128)S(1)} fusion(bf16[768,2048]{1,0:T(8,128)(2,1)} %all-gather.3.cloned.1.call-done, bf16[3,2048,512]{1,2,0:T(8,128)(2,1)} %all-gather.5.cloned.1.call-done), kind=kOutput, calls=%fused_computation.8 | convolution fusion | flops 1610612736 | bytes 6815744 | tf_op jit(solution)/shard_map/dot_general | solution.py:329
  132.9 8.4 %convolution_convert_fusion = bf16[768,2048]{1,0:T(8,128)(2,1)} fusion(bf16[3,2048,512]{1,2,0:T(8,128)(2,1)} %all-gather.5.cloned.1.call-done, f32[768,512]{1,0:T(8,128)S(1)} %fusion, bf16[768,2048]{1,0:T(8,128)(2,1)} %all-gather.3.cloned.1.call-done), kind=kOutput, calls=%fused_computation | convolution fusion | flops 3226730496 | bytes 12058624 | tf_op jit(solution)/shard_map/dot_general | solution.py:332
  142.9 2.4 collective-permute-done.13
  145.3 2.0 collective-permute-start.14
  147.8 1.4 collective-permute-done.14
  150.0 1.1 collective-permute-done.20
  151.1 1.8 collective-permute-start.21
  153.5 6.6 %collective-permute-done.22 = bf16[2,256,128]{2,1,0:T(8,128)(2,1)S(1)} collective-permute-done((bf16[2,256,128]{2,1,0:T(8,128)(2,1)S(1)}, bf16[2,256,128]{2,1,0:T(8,128)(2,1)S(1)}, u32[]{:S(2)}, u32[]{:S(2)}) %collective-permute-start.22) | collective-permute-done | bytes 131104 | tf_op jit(solution)/shard_map/ppermute | solution.py:272
  160.2 4.5 %collective-permute-start.23 = (bf16[2,256,512]{2,1,0:T(8,128)(2,1)S(1)}, bf16[2,256,512]{2,1,0:T(8,128)(2,1)S(1)}, u32[]{:S(2)}, u32[]{:S(2)}) collective-permute-start(bf16[2,256,512]{2,1,0:T(8,128)(2,1)S(1)} %pad_maximum_fusion.2.refs_5_), channel_id=1, source_target_pairs={{1,0},{2,1},{3,2},{0,3},{5,4},{6,5},{7,6},{4,7},{9,8},{10,9},{11,1... | collective-permute-start | bytes 1572872 | tf_op jit(solution)/shard_map/ppermute | solution.py:272
  164.6 16.4 %collective-permute-start.27 = (bf16[2,256,512]{2,1,0:T(8,128)(2,1)S(1)}, bf16[2,256,512]{2,1,0:T(8,128)(2,1)}, u32[]{:S(2)}, u32[]{:S(2)}) collective-permute-start(bf16[2,256,512]{2,1,0:T(8,128)(2,1)S(1)} %pad_maximum_fusion.1.refs_0_), channel_id=1, source_target_pairs={{16,0},{0,16},{17,1},{1,17},{18,2},{2,18},{19,3},{3,19},{20,4},{4,... | collective-permute-start | bytes 1572872 | tf_op jit(solution)/shard_map/ppermute | solution.py:272
  181.9 2.7 collective-permute-start.18
  184.6 6.9 %collective-permute-start.29 = (bf16[2,256,512]{2,1,0:T(8,128)(2,1)S(1)}, bf16[2,256,512]{2,1,0:T(8,128)(2,1)}, u32[]{:S(2)}, u32[]{:S(2)}) collective-permute-start(bf16[2,256,512]{2,1,0:T(8,128)(2,1)S(1)} %collective-permute-done.17.refs_2_), channel_id=1, source_target_pairs={{16,0},{0,16},{17,1},{1,17},{18,2},{2,18},{19,3},{3,19},{20,4},{4,... | collective-permute-start | bytes 1572872 | tf_op jit(solution)/shard_map/ppermute | solution.py:272
  193.1 2.5 collective-permute-start.25
  196.1 2.1 collective-permute-start.30
  198.6 4.7 %collective-permute-done.26.refs_9_ = bf16[1,256,512]{2,1,0:T(8,128)(2,1)} collective-permute-done((bf16[1,256,512]{2,1,0:T(8,128)(2,1)}, bf16[1,256,512]{2,1,0:T(8,128)(2,1)}, u32[]{:S(2)}, u32[]{:S(2)}) %collective-permute-start.26) | collective-permute-done | bytes 262176 | tf_op jit(solution)/shard_map/ppermute | solution.py:272
  203.3 0.9 collective-permute-start.28
  205.2 3.4 %copy-done.5 = bf16[2048,2048]{1,0:T(8,128)(2,1)S(1)} copy-done((bf16[2048,2048]{1,0:T(8,128)(2,1)S(1)}, bf16[2048,2048]{1,0:T(8,128)(2,1)}, u32[]{:S(2)}) %copy-start.5) | copy-done | bytes 8388632
  208.6 16.2 %shard_map.168 = (f32[4,4,2,64,2048]{4,3,2,1,0:T(8,128)}, f32[4,256]{1,0:T(4,128)S(1)}) custom-call(s32[4]{0:T(128)S(1)} %add_add_fusion.1.place_ref, bf16[2,256,512]{2,1,0:T(8,128)(2,1)S(1)} %pad_maximum_fusion.1.refs_0_, bf16[2,256,512]{2,1,0:T(8,128)(2,1)S(1)} %collective-permute-done.16.refs_1_, ...), custom_call_target="tpu_custom_call" | custom-call | flops 8589934592 | bytes 16777216 | tf_op jit(solution)/shard_map/pallas_call | solution.py:186
  225.4 4.2 %all-to-all-start.5 = ((f32[16,4,256]{2,1,0:T(4,128)}), f32[16,4,256]{2,1,0:T(4,128)}, u32[]{:S(2)}, u32[]{:S(2)}) async-start(f32[16,4,256]{2,1,0:T(4,128)} %broadcast_in_dim.19), calls=%async_computation.6 | async-start | bytes 131072 | tf_op jit(solution)/shard_map/all_to_all | solution.py:277
  229.7 3.4 %copy-done.6 = bf16[2048,2048]{1,0:T(8,128)(2,1)S(1)} copy-done((bf16[2048,2048]{1,0:T(8,128)(2,1)S(1)}, bf16[2048,2048]{1,0:T(8,128)(2,1)}, u32[]{:S(2)}) %copy-start.6) | copy-done | bytes 8388632
  233.1 16.4 %shard_map.169 = (f32[4,4,2,64,2048]{4,3,2,1,0:T(8,128)}, f32[4,256]{1,0:T(4,128)S(1)}) custom-call(s32[4]{0:T(128)S(1)} %add_add_fusion.2.place_ref, bf16[2,256,512]{2,1,0:T(8,128)(2,1)} %collective-permute-done.27.refs_0_, bf16[2,256,512]{2,1,0:T(8,128)(2,1)} %collective-permute-done.28.refs_1_, ...), custom_call_target="tpu_custom_call", output_to_operand_aliasing={{0}: (13, {})} | custom-call | flops 8589934592 | bytes 16777216 | tf_op jit(solution)/shard_map/pallas_call | solution.py:186
  250.1 6.6 %all-to-all-start.6 = ((f32[16,4,256]{2,1,0:T(4,128)}), f32[16,4,256]{2,1,0:T(4,128)S(1)}, u32[]{:S(2)}, u32[]{:S(2)}) async-start(f32[16,4,256]{2,1,0:T(4,128)} %broadcast_in_dim.20), calls=%async_computation.7 | async-start | bytes 131072 | tf_op jit(solution)/shard_map/all_to_all | solution.py:277
  257.6 5.6 %all-to-all-done.6 = f32[16,4,256]{2,1,0:T(4,128)S(1)} async-done(((f32[16,4,256]{2,1,0:T(4,128)}), f32[16,4,256]{2,1,0:T(4,128)S(1)}, u32[]{:S(2)}, u32[]{:S(2)}) %all-to-all-start.6) | async-done | bytes 65568 | tf_op jit(solution)/shard_map/all_to_all | solution.py:277
  263.3 1.1 collective-permute-start.38
  264.3 2.7 collective-permute-start.37
  268.1 4.0 %collective-permute-start.40 = (f32[2,4,256]{2,1,0:T(4,128)S(1)}, f32[2,4,256]{2,1,0:T(4,128)S(1)}, u32[]{:S(2)}, u32[]{:S(2)}) collective-permute-start(f32[2,4,256]{2,1,0:T(4,128)S(1)} %add_add_fusion), channel_id=1, source_target_pairs={{16,0},{0,16},{17,1},{1,17},{18,2},{2,18},{19,3},{3,19},{20,4},{4,... | collective-permute-start | bytes 24584 | tf_op jit(solution)/shard_map/ppermute | solution.py:272
  273.1 5.8 %copy-done.2 = f32[4,4,2,64,2048]{4,3,2,1,0:T(8,128)S(1)} copy-done((f32[4,4,2,64,2048]{4,3,2,1,0:T(8,128)S(1)}, f32[4,4,2,64,2048]{4,3,2,1,0:T(8,128)}, u32[]{:S(2)}) %copy-start.2) | copy-done | bytes 16777240
  278.9 8.0 %shard_map.170 = bf16[4,512,2048]{2,1,0:T(8,128)(2,1)} custom-call(s32[4]{0:T(128)S(1)} %add_add_fusion.1.place_ref, f32[4,512,2048]{2,1,0:T(8,128)S(1)} %bitcast.69, f32[512,4]{1,0:T(8,128)S(1)} %bitcast.72, s32[512,2]{1,0:T(8,128)S(1)} %bitcast.71), custom_call_target="tpu_custom_call" | custom-call | flops 16777216 | bytes 25165824 | tf_op jit(solution)/shard_map/pallas_call | solution.py:234
  286.9 1.0 convert_element_type.175
  (170 shorter events, 29.0 us)
Async XLA Ops:
  7.2 112.7 %copy-start = (bf16[4,2048,128]{2,1,0:T(8,128)(2,1)S(1)}, bf16[4,2048,128]{2,1,0:T(8,128)(2,1)}, u32[]{:S(2)}) copy-start(bf16[4,2048,128]{2,1,0:T(8,128)(2,1)} %param.26) | copy-start | bytes 6291460
  7.2 78.5 %all-gather.5.cloned.1.call-start = ((), (), s32[]{:S(2)}) async-start(), calls=%async_computation.9 | async-start | bytes 7077888 | tf_op jit(solution)/shard_map/all_gather | solution.py:379
  8.9 21.4 %collective-permute-start.5 = (bf16[1024,128]{1,0:T(8,128)(2,1)S(1)}, bf16[1024,128]{1,0:T(8,128)(2,1)S(1)}, u32[]{:S(2)}, u32[]{:S(2)}) collective-permute-start(bf16[1024,128]{1,0:T(8,128)(2,1)S(1)} %constant_dynamic-slice_fusion.2), channel_id=1, source_target_pairs={{12,0},{0,4},{4,8},{8,12},{13,1},{1,5},{5,9},{9,13},{14,2},{2,6},{... | collective-permute-start | bytes 786440 | tf_op jit(solution)/shard_map/ppermute | solution.py:272
  11.0 19.3 %collective-permute-start.4 = (bf16[1024,128]{1,0:T(8,128)(2,1)S(1)}, bf16[1024,128]{1,0:T(8,128)(2,1)}, u32[]{:S(2)}, u32[]{:S(2)}) collective-permute-start(bf16[1024,128]{1,0:T(8,128)(2,1)S(1)} %constant_dynamic-slice_fusion.2), channel_id=1, source_target_pairs={{8,0},{12,4},{0,8},{4,12},{9,1},{13,5},{1,9},{5,13},{10,2},{14,6},... | collective-permute-start | bytes 786440 | tf_op jit(solution)/shard_map/ppermute | solution.py:272
  13.5 16.8 %collective-permute-start.3 = (bf16[1024,128]{1,0:T(8,128)(2,1)S(1)}, bf16[1024,128]{1,0:T(8,128)(2,1)}, u32[]{:S(2)}, u32[]{:S(2)}) collective-permute-start(bf16[1024,128]{1,0:T(8,128)(2,1)S(1)} %constant_dynamic-slice_fusion.2), channel_id=1, source_target_pairs={{4,0},{8,4},{12,8},{0,12},{5,1},{9,5},{13,9},{1,13},{6,2},{10,6},{... | collective-permute-start | bytes 786440 | tf_op jit(solution)/shard_map/ppermute | solution.py:272
  20.0 3.9 %copy-start.16 = (s32[1,4]{1,0:T(1,128)S(1)}, s32[1,4]{1,0:T(1,128)}, u32[]{:S(2)}) copy-start(s32[1,4]{1,0:T(1,128)} %param.22) | copy-start | bytes 52
  25.0 12.5 %all-to-all-start = ((bf16[16,4,2048]{2,1,0:T(4,128)(2,1)}), bf16[16,4,2048]{2,1,0:T(4,128)(2,1)S(1)}, u32[]{:S(2)}, u32[]{:S(2)}) async-start(bf16[16,4,2048]{2,1,0:T(4,128)(2,1)} %broadcast_in_dim.14), calls=%async_computation | async-start | bytes 524288 | tf_op jit(solution)/shard_map/all_to_all | solution.py:277
  30.2 98.3 %all-gather.3.cloned.1.call-start = ((), (), s32[]{:S(2)}) async-start(), calls=%async_computation.8 | async-start | bytes 3342336 | tf_op jit(solution)/shard_map/all_gather | solution.py:418
  32.4 14.6 %collective-permute-start.6 = (bf16[1024,512]{1,0:T(8,128)(2,1)}, bf16[1024,512]{1,0:T(8,128)(2,1)}, u32[]{:S(2)}, u32[]{:S(2)}) collective-permute-start(bf16[1024,512]{1,0:T(8,128)(2,1)} %pad_maximum_fusion), channel_id=1, source_target_pairs={{16,0},{0,16},{17,1},{1,17},{18,2},{2,18},{19,3},{3,19},{20,4},{4,... | collective-permute-start | bytes 3145736 | tf_op jit(solution)/shard_map/ppermute | solution.py:272
  37.6 9.4 %collective-permute-start.2 = (bf16[48,2048]{1,0:T(8,128)(2,1)S(1)}, bf16[48,2048]{1,0:T(8,128)(2,1)S(1)}, u32[]{:S(2)}, u32[]{:S(2)}) collective-permute-start(bf16[48,2048]{1,0:T(8,128)(2,1)S(1)} %shard_map.167), channel_id=1, source_target_pairs={{3,0},{0,1},{1,2},{2,3},{7,4},{4,5},{5,6},{6,7},{11,8},{8,9},{9,10... | collective-permute-start | bytes 589832 | tf_op jit(solution)/shard_map/ppermute | solution.py:272
  37.8 9.2 %collective-permute-start.1 = (bf16[48,2048]{1,0:T(8,128)(2,1)S(1)}, bf16[48,2048]{1,0:T(8,128)(2,1)S(1)}, u32[]{:S(2)}, u32[]{:S(2)}) collective-permute-start(bf16[48,2048]{1,0:T(8,128)(2,1)S(1)} %shard_map.167), channel_id=1, source_target_pairs={{2,0},{3,1},{0,2},{1,3},{6,4},{7,5},{4,6},{5,7},{10,8},{11,9},{8,1... | collective-permute-start | bytes 589832 | tf_op jit(solution)/shard_map/ppermute | solution.py:272
  39.7 7.3 %collective-permute-start = (bf16[48,2048]{1,0:T(8,128)(2,1)S(1)}, bf16[48,2048]{1,0:T(8,128)(2,1)S(1)}, u32[]{:S(2)}, u32[]{:S(2)}) collective-permute-start(bf16[48,2048]{1,0:T(8,128)(2,1)S(1)} %shard_map.167), channel_id=1, source_target_pairs={{1,0},{2,1},{3,2},{0,3},{5,4},{6,5},{7,6},{4,7},{9,8},{10,9},{11,1... | collective-permute-start | bytes 589832 | tf_op jit(solution)/shard_map/ppermute | solution.py:272
  48.7 6.8 %copy-start.11 = (bf16[2048]{0:T(1024)(128)(2,1)S(1)}, bf16[2048]{0:T(1024)(128)(2,1)}, u32[]{:S(2)}) copy-start(bf16[2048]{0:T(1024)(128)(2,1)} %param.28) | copy-start | bytes 12292
  48.7 6.8 %copy-start.12 = (bf16[2048]{0:T(1024)(128)(2,1)S(1)}, bf16[2048]{0:T(1024)(128)(2,1)}, u32[]{:S(2)}) copy-start(bf16[2048]{0:T(1024)(128)(2,1)} %param.29) | copy-start | bytes 12292
  50.2 9.9 %copy-start.10 = (bf16[48,2048]{1,0:T(8,128)(2,1)S(1)}, bf16[48,2048]{1,0:T(8,128)(2,1)}, u32[]{:S(2)}) copy-start(bf16[48,2048]{1,0:T(8,128)(2,1)} %param.16) | copy-start | bytes 589828
  50.2 11.6 %copy-start.9 = (bf16[2048,128]{1,0:T(8,128)(2,1)S(1)}, bf16[2048,128]{1,0:T(8,128)(2,1)}, u32[]{:S(2)}) copy-start(bf16[2048,128]{1,0:T(8,128)(2,1)} %param.24) | copy-start | bytes 1572868
  50.9 5.6 %collective-permute-start.9 = (bf16[48,512]{1,0:T(8,128)(2,1)}, bf16[48,512]{1,0:T(8,128)(2,1)S(1)}, u32[]{:S(2)}, u32[]{:S(2)}) collective-permute-start(bf16[48,512]{1,0:T(8,128)(2,1)} %get-tuple-element.36), channel_id=1, source_target_pairs={{1,0},{2,1},{3,2},{0,3},{5,4},{6,5},{7,6},{4,7},{9,8},{10,9},{11,1... | collective-permute-start | bytes 147464 | tf_op jit(solution)/shard_map/ppermute | solution.py:272
  54.9 4.7 %collective-permute-start.8 = (bf16[48,512]{1,0:T(8,128)(2,1)}, bf16[48,512]{1,0:T(8,128)(2,1)S(1)}, u32[]{:S(2)}, u32[]{:S(2)}) collective-permute-start(bf16[48,512]{1,0:T(8,128)(2,1)} %get-tuple-element.37), channel_id=1, source_target_pairs={{2,0},{3,1},{0,2},{1,3},{6,4},{7,5},{4,6},{5,7},{10,8},{11,9},{8,1... | collective-permute-start | bytes 147464 | tf_op jit(solution)/shard_map/ppermute | solution.py:272
  54.9 4.7 %collective-permute-start.7 = (bf16[48,512]{1,0:T(8,128)(2,1)S(1)}, bf16[48,512]{1,0:T(8,128)(2,1)S(1)}, u32[]{:S(2)}, u32[]{:S(2)}) collective-permute-start(bf16[48,512]{1,0:T(8,128)(2,1)S(1)} %get-tuple-element.38), channel_id=1, source_target_pairs={{3,0},{0,1},{1,2},{2,3},{7,4},{4,5},{5,6},{6,7},{11,8},{8,9},{9,10... | collective-permute-start | bytes 147464 | tf_op jit(solution)/shard_map/ppermute | solution.py:272
  62.8 10.8 %all-to-all-start.2 = ((bf16[16,64,128]{2,1,0:T(8,128)(2,1)}), bf16[16,64,128]{2,1,0:T(8,128)(2,1)S(1)}, u32[]{:S(2)}, u32[]{:S(2)}) async-start(bf16[16,64,128]{2,1,0:T(8,128)(2,1)} %broadcast_in_dim.16), calls=%async_computation.2 | async-start | bytes 524288 | tf_op jit(solution)/shard_map/all_to_all | solution.py:277
  73.6 11.3 %all-to-all-start.1 = ((bf16[16,4,2048]{2,1,0:T(4,128)(2,1)}), bf16[16,4,2048]{2,1,0:T(4,128)(2,1)S(1)}, u32[]{:S(2)}, u32[]{:S(2)}) async-start(bf16[16,4,2048]{2,1,0:T(4,128)(2,1)} %broadcast_in_dim.15), calls=%async_computation.1 | async-start | bytes 524288 | tf_op jit(solution)/shard_map/all_to_all | solution.py:277
  88.7 7.9 %copy-start.13 = (bf16[2048]{0:T(1024)(128)(2,1)S(1)}, bf16[2048]{0:T(1024)(128)(2,1)}, u32[]{:S(2)}) copy-start(bf16[2048]{0:T(1024)(128)(2,1)} %param.30) | copy-start | bytes 12292
  88.7 7.9 %copy-start.14 = (bf16[2048]{0:T(1024)(128)(2,1)S(1)}, bf16[2048]{0:T(1024)(128)(2,1)}, u32[]{:S(2)}) copy-start(bf16[2048]{0:T(1024)(128)(2,1)} %param.31) | copy-start | bytes 12292
  93.1 12.8 %all-to-all-start.3 = ((bf16[16,4,2048]{2,1,0:T(4,128)(2,1)}), bf16[16,4,2048]{2,1,0:T(4,128)(2,1)S(1)}, u32[]{:S(2)}, u32[]{:S(2)}) async-start(bf16[16,4,2048]{2,1,0:T(4,128)(2,1)} %reshape.173), calls=%async_computation.3 | async-start | bytes 524288 | tf_op jit(solution)/shard_map/all_to_all | solution.py:398
  108.1 11.6 %all-to-all-start.4 = ((bf16[16,4,2048]{2,1,0:T(4,128)(2,1)}), bf16[16,4,2048]{2,1,0:T(4,128)(2,1)S(1)}, u32[]{:S(2)}, u32[]{:S(2)}) async-start(bf16[16,4,2048]{2,1,0:T(4,128)(2,1)} %broadcast_in_dim.17), calls=%async_computation.4 | async-start | bytes 524288 | tf_op jit(solution)/shard_map/all_to_all | solution.py:277
  112.4 174.6 %reduce-scatter.2.cloned.1.call-start = ((), (), s32[]{:S(2)}) async-start(), calls=%async_computation.10 | async-start | bytes 3342336 | tf_op jit(solution)/shard_map/reduce_scatter | solution.py:420
  120.4 4.0 %collective-permute-start.12 = (bf16[4,64,128]{2,1,0:T(8,128)(2,1)S(1)}, bf16[4,64,128]{2,1,0:T(8,128)(2,1)S(1)}, u32[]{:S(2)}, u32[]{:S(2)}) collective-permute-start(bf16[4,64,128]{2,1,0:T(8,128)(2,1)S(1)} %add_convert_fusion.1), channel_id=1, source_target_pairs={{32,0},{64,32},{96,64},{0,96},{33,1},{65,33},{97,65},{1,97},{34,2}... | collective-permute-start | bytes 196616 | tf_op jit(solution)/shard_map/ppermute | solution.py:272
  123.1 4.9 %collective-permute-start.11 = (bf16[4,64,128]{2,1,0:T(8,128)(2,1)S(1)}, bf16[4,64,128]{2,1,0:T(8,128)(2,1)S(1)}, u32[]{:S(2)}, u32[]{:S(2)}) collective-permute-start(bf16[4,64,128]{2,1,0:T(8,128)(2,1)S(1)} %add_convert_fusion.1), channel_id=1, source_target_pairs={{64,0},{96,32},{0,64},{32,96},{65,1},{97,33},{1,65},{33,97},{66,2}... | collective-permute-start | bytes 196616 | tf_op jit(solution)/shard_map/ppermute | solution.py:272
  123.5 5.0 %collective-permute-start.10 = (bf16[4,64,128]{2,1,0:T(8,128)(2,1)S(1)}, bf16[4,64,128]{2,1,0:T(8,128)(2,1)S(1)}, u32[]{:S(2)}, u32[]{:S(2)}) collective-permute-start(bf16[4,64,128]{2,1,0:T(8,128)(2,1)S(1)} %add_convert_fusion.1), channel_id=1, source_target_pairs={{96,0},{0,32},{32,64},{64,96},{97,1},{1,33},{33,65},{65,97},{98,2}... | collective-permute-start | bytes 196616 | tf_op jit(solution)/shard_map/ppermute | solution.py:272
  141.4 3.9 %collective-permute-start.13 = (bf16[2,256,128]{2,1,0:T(8,128)(2,1)S(1)}, bf16[2,256,128]{2,1,0:T(8,128)(2,1)S(1)}, u32[]{:S(2)}, u32[]{:S(2)}) collective-permute-start(bf16[2,256,128]{2,1,0:T(8,128)(2,1)S(1)} %get-tuple-element.29), channel_id=1, source_target_pairs={{1,0},{2,1},{3,2},{0,3},{5,4},{6,5},{7,6},{4,7},{9,8},{10,9},{11,1... | collective-permute-start | bytes 393224 | tf_op jit(solution)/shard_map/ppermute | solution.py:272
  142.2 5.6 %collective-permute-start.15 = (bf16[2,256,128]{2,1,0:T(8,128)(2,1)S(1)}, bf16[2,256,128]{2,1,0:T(8,128)(2,1)S(1)}, u32[]{:S(2)}, u32[]{:S(2)}) collective-permute-start(bf16[2,256,128]{2,1,0:T(8,128)(2,1)S(1)} %get-tuple-element.29), channel_id=1, source_target_pairs={{3,0},{0,1},{1,2},{2,3},{7,4},{4,5},{5,6},{6,7},{11,8},{8,9},{9,10... | collective-permute-start | bytes 393224 | tf_op jit(solution)/shard_map/ppermute | solution.py:272
  145.3 3.9 %collective-permute-start.14 = (bf16[2,256,128]{2,1,0:T(8,128)(2,1)S(1)}, bf16[2,256,128]{2,1,0:T(8,128)(2,1)S(1)}, u32[]{:S(2)}, u32[]{:S(2)}) collective-permute-start(bf16[2,256,128]{2,1,0:T(8,128)(2,1)S(1)} %collective-permute-done.13), channel_id=1, source_target_pairs={{1,0},{2,1},{3,2},{0,3},{5,4},{6,5},{7,6},{4,7},{9,8},{10,9},{11,1... | collective-permute-start | bytes 393224 | tf_op jit(solution)/shard_map/ppermute | solution.py:272
  147.2 51.1 %copy-start.15 = (s32[128,2]{0,1:T(2,128)S(1)}, s32[128,2]{0,1:T(2,128)}, u32[]{:S(2)}) copy-start(s32[128,2]{0,1:T(2,128)} %param.23) | copy-start | bytes 3076
  147.2 3.8 %collective-permute-start.20 = (bf16[2,256,128]{2,1,0:T(8,128)(2,1)S(1)}, bf16[2,256,128]{2,1,0:T(8,128)(2,1)S(1)}, u32[]{:S(2)}, u32[]{:S(2)}) collective-permute-start(bf16[2,256,128]{2,1,0:T(8,128)(2,1)S(1)} %get-tuple-element.28), channel_id=1, source_target_pairs={{4,0},{8,4},{12,8},{0,12},{5,1},{9,5},{13,9},{1,13},{6,2},{10,6},{... | collective-permute-start | bytes 393224 | tf_op jit(solution)/shard_map/ppermute | solution.py:272
  149.2 31.8 %collective-permute-start.17 = (bf16[2,256,512]{2,1,0:T(8,128)(2,1)S(1)}, bf16[2,256,512]{2,1,0:T(8,128)(2,1)S(1)}, u32[]{:S(2)}, u32[]{:S(2)}) collective-permute-start(bf16[2,256,512]{2,1,0:T(8,128)(2,1)S(1)} %pad_maximum_fusion.1.refs_0_), channel_id=1, source_target_pairs={{12,0},{0,4},{4,8},{8,12},{13,1},{1,5},{5,9},{9,13},{14,2},{2,6},{... | collective-permute-start | bytes 1572872 | tf_op jit(solution)/shard_map/ppermute | solution.py:272
  149.3 10.7 %collective-permute-start.22 = (bf16[2,256,128]{2,1,0:T(8,128)(2,1)S(1)}, bf16[2,256,128]{2,1,0:T(8,128)(2,1)S(1)}, u32[]{:S(2)}, u32[]{:S(2)}) collective-permute-start(bf16[2,256,128]{2,1,0:T(8,128)(2,1)S(1)} %get-tuple-element.28), channel_id=1, source_target_pairs={{12,0},{0,4},{4,8},{8,12},{13,1},{1,5},{5,9},{9,13},{14,2},{2,6},{... | collective-permute-start | bytes 393224 | tf_op jit(solution)/shard_map/ppermute | solution.py:272
  151.1 9.0 %collective-permute-start.21 = (bf16[2,256,128]{2,1,0:T(8,128)(2,1)S(1)}, bf16[2,256,128]{2,1,0:T(8,128)(2,1)S(1)}, u32[]{:S(2)}, u32[]{:S(2)}) collective-permute-start(bf16[2,256,128]{2,1,0:T(8,128)(2,1)S(1)} %collective-permute-done.20), channel_id=1, source_target_pairs={{4,0},{8,4},{12,8},{0,12},{5,1},{9,5},{13,9},{1,13},{6,2},{10,6},{... | collective-permute-start | bytes 393224 | tf_op jit(solution)/shard_map/ppermute | solution.py:272
  152.8 28.2 %collective-permute-start.16 = (bf16[2,256,512]{2,1,0:T(8,128)(2,1)S(1)}, bf16[2,256,512]{2,1,0:T(8,128)(2,1)S(1)}, u32[]{:S(2)}, u32[]{:S(2)}) collective-permute-start(bf16[2,256,512]{2,1,0:T(8,128)(2,1)S(1)} %pad_maximum_fusion.1.refs_0_), channel_id=1, source_target_pairs={{4,0},{8,4},{12,8},{0,12},{5,1},{9,5},{13,9},{1,13},{6,2},{10,6},{... | collective-permute-start | bytes 1572872 | tf_op jit(solution)/shard_map/ppermute | solution.py:272
  160.1 21.8 %collective-permute-start.24 = (bf16[2,256,512]{2,1,0:T(8,128)(2,1)S(1)}, bf16[2,256,512]{2,1,0:T(8,128)(2,1)S(1)}, u32[]{:S(2)}, u32[]{:S(2)}) collective-permute-start(bf16[2,256,512]{2,1,0:T(8,128)(2,1)S(1)} %pad_maximum_fusion.2.refs_5_), channel_id=1, source_target_pairs={{3,0},{0,1},{1,2},{2,3},{7,4},{4,5},{5,6},{6,7},{11,8},{8,9},{9,10... | collective-permute-start | bytes 1572872 | tf_op jit(solution)/shard_map/ppermute | solution.py:272
  160.2 24.4 %collective-permute-start.23 = (bf16[2,256,512]{2,1,0:T(8,128)(2,1)S(1)}, bf16[2,256,512]{2,1,0:T(8,128)(2,1)S(1)}, u32[]{:S(2)}, u32[]{:S(2)}) collective-permute-start(bf16[2,256,512]{2,1,0:T(8,128)(2,1)S(1)} %pad_maximum_fusion.2.refs_5_), channel_id=1, source_target_pairs={{1,0},{2,1},{3,2},{0,3},{5,4},{6,5},{7,6},{4,7},{9,8},{10,9},{11,1... | collective-permute-start | bytes 1572872 | tf_op jit(solution)/shard_map/ppermute | solution.py:272
  164.6 28.2 %collective-permute-start.27 = (bf16[2,256,512]{2,1,0:T(8,128)(2,1)S(1)}, bf16[2,256,512]{2,1,0:T(8,128)(2,1)}, u32[]{:S(2)}, u32[]{:S(2)}) collective-permute-start(bf16[2,256,512]{2,1,0:T(8,128)(2,1)S(1)} %pad_maximum_fusion.1.refs_0_), channel_id=1, source_target_pairs={{16,0},{0,16},{17,1},{1,17},{18,2},{2,18},{19,3},{3,19},{20,4},{4,... | collective-permute-start | bytes 1572872 | tf_op jit(solution)/shard_map/ppermute | solution.py:272
  181.1 12.0 %collective-permute-start.32 = (bf16[2,256,512]{2,1,0:T(8,128)(2,1)S(1)}, bf16[2,256,512]{2,1,0:T(8,128)(2,1)}, u32[]{:S(2)}, u32[]{:S(2)}) collective-permute-start(bf16[2,256,512]{2,1,0:T(8,128)(2,1)S(1)} %pad_maximum_fusion.2.refs_5_), channel_id=1, source_target_pairs={{16,0},{0,16},{17,1},{1,17},{18,2},{2,18},{19,3},{3,19},{20,4},{4,... | collective-permute-start | bytes 1572872 | tf_op jit(solution)/shard_map/ppermute | solution.py:272
  181.1 14.5 %collective-permute-start.19 = (bf16[1,256,512]{2,1,0:T(8,128)(2,1)S(1)}, bf16[1,256,512]{2,1,0:T(8,128)(2,1)}, u32[]{:S(2)}, u32[]{:S(2)}) collective-permute-start(bf16[1,256,512]{2,1,0:T(8,128)(2,1)S(1)} %slice.144), channel_id=1, source_target_pairs={{12,0},{0,4},{4,8},{8,12},{13,1},{1,5},{5,9},{9,13},{14,2},{2,6},{... | collective-permute-start | bytes 786440 | tf_op jit(solution)/shard_map/ppermute | solution.py:272
  181.9 14.2 %collective-permute-start.18 = (bf16[1,256,512]{2,1,0:T(8,128)(2,1)}, bf16[1,256,512]{2,1,0:T(8,128)(2,1)}, u32[]{:S(2)}, u32[]{:S(2)}) collective-permute-start(bf16[1,256,512]{2,1,0:T(8,128)(2,1)} %slice.143), channel_id=1, source_target_pairs={{4,0},{8,4},{12,8},{0,12},{5,1},{9,5},{13,9},{1,13},{6,2},{10,6},{... | collective-permute-start | bytes 786440 | tf_op jit(solution)/shard_map/ppermute | solution.py:272
  184.6 20.1 %collective-permute-start.29 = (bf16[2,256,512]{2,1,0:T(8,128)(2,1)S(1)}, bf16[2,256,512]{2,1,0:T(8,128)(2,1)}, u32[]{:S(2)}, u32[]{:S(2)}) collective-permute-start(bf16[2,256,512]{2,1,0:T(8,128)(2,1)S(1)} %collective-permute-done.17.refs_2_), channel_id=1, source_target_pairs={{16,0},{0,16},{17,1},{1,17},{18,2},{2,18},{19,3},{3,19},{20,4},{4,... | collective-permute-start | bytes 1572872 | tf_op jit(solution)/shard_map/ppermute | solution.py:272
  192.9 10.4 %collective-permute-start.26 = (bf16[1,256,512]{2,1,0:T(8,128)(2,1)}, bf16[1,256,512]{2,1,0:T(8,128)(2,1)}, u32[]{:S(2)}, u32[]{:S(2)}) collective-permute-start(bf16[1,256,512]{2,1,0:T(8,128)(2,1)} %slice.147), channel_id=1, source_target_pairs={{3,0},{0,1},{1,2},{2,3},{7,4},{4,5},{5,6},{6,7},{11,8},{8,9},{9,10... | collective-permute-start | bytes 786440 | tf_op jit(solution)/shard_map/ppermute | solution.py:272
  193.1 11.1 %collective-permute-start.25 = (bf16[1,256,512]{2,1,0:T(8,128)(2,1)}, bf16[1,256,512]{2,1,0:T(8,128)(2,1)}, u32[]{:S(2)}, u32[]{:S(2)}) collective-permute-start(bf16[1,256,512]{2,1,0:T(8,128)(2,1)} %slice.146), channel_id=1, source_target_pairs={{1,0},{2,1},{3,2},{0,3},{5,4},{6,5},{7,6},{4,7},{9,8},{10,9},{11,1... | collective-permute-start | bytes 786440 | tf_op jit(solution)/shard_map/ppermute | solution.py:272
  195.6 8.6 %collective-permute-start.31 = (bf16[1,256,512]{2,1,0:T(8,128)(2,1)}, bf16[1,256,512]{2,1,0:T(8,128)(2,1)}, u32[]{:S(2)}, u32[]{:S(2)}) collective-permute-start(bf16[1,256,512]{2,1,0:T(8,128)(2,1)} %collective-permute-done.19.refs_4_), channel_id=1, source_target_pairs={{16,0},{0,16},{17,1},{1,17},{18,2},{2,18},{19,3},{3,19},{20,4},{4,... | collective-permute-start | bytes 786440 | tf_op jit(solution)/shard_map/ppermute | solution.py:272
  196.1 8.7 %collective-permute-start.30 = (bf16[1,256,512]{2,1,0:T(8,128)(2,1)}, bf16[1,256,512]{2,1,0:T(8,128)(2,1)}, u32[]{:S(2)}, u32[]{:S(2)}) collective-permute-start(bf16[1,256,512]{2,1,0:T(8,128)(2,1)} %collective-permute-done.18.refs_3_), channel_id=1, source_target_pairs={{16,0},{0,16},{17,1},{1,17},{18,2},{2,18},{19,3},{3,19},{20,4},{4,... | collective-permute-start | bytes 786440 | tf_op jit(solution)/shard_map/ppermute | solution.py:272
  203.3 26.4 %collective-permute-start.28 = (bf16[2,256,512]{2,1,0:T(8,128)(2,1)S(1)}, bf16[2,256,512]{2,1,0:T(8,128)(2,1)}, u32[]{:S(2)}, u32[]{:S(2)}) collective-permute-start(bf16[2,256,512]{2,1,0:T(8,128)(2,1)S(1)} %collective-permute-done.16.refs_1_), channel_id=1, source_target_pairs={{16,0},{0,16},{17,1},{1,17},{18,2},{2,18},{19,3},{3,19},{20,4},{4,... | collective-permute-start | bytes 1572872 | tf_op jit(solution)/shard_map/ppermute | solution.py:272
  204.2 25.5 %collective-permute-start.34 = (bf16[2,256,512]{2,1,0:T(8,128)(2,1)S(1)}, bf16[2,256,512]{2,1,0:T(8,128)(2,1)}, u32[]{:S(2)}, u32[]{:S(2)}) collective-permute-start(bf16[2,256,512]{2,1,0:T(8,128)(2,1)S(1)} %collective-permute-done.24.refs_7_), channel_id=1, source_target_pairs={{16,0},{0,16},{17,1},{1,17},{18,2},{2,18},{19,3},{3,19},{20,4},{4,... | collective-permute-start | bytes 1572872 | tf_op jit(solution)/shard_map/ppermute | solution.py:272
  204.2 25.5 %collective-permute-start.33 = (bf16[2,256,512]{2,1,0:T(8,128)(2,1)S(1)}, bf16[2,256,512]{2,1,0:T(8,128)(2,1)}, u32[]{:S(2)}, u32[]{:S(2)}) collective-permute-start(bf16[2,256,512]{2,1,0:T(8,128)(2,1)S(1)} %collective-permute-done.23.refs_6_), channel_id=1, source_target_pairs={{16,0},{0,16},{17,1},{1,17},{18,2},{2,18},{19,3},{3,19},{20,4},{4,... | collective-permute-start | bytes 1572872 | tf_op jit(solution)/shard_map/ppermute | solution.py:272
  204.7 25.0 %collective-permute-start.36 = (bf16[1,256,512]{2,1,0:T(8,128)(2,1)}, bf16[1,256,512]{2,1,0:T(8,128)(2,1)}, u32[]{:S(2)}, u32[]{:S(2)}) collective-permute-start(bf16[1,256,512]{2,1,0:T(8,128)(2,1)} %collective-permute-done.26.refs_9_), channel_id=1, source_target_pairs={{16,0},{0,16},{17,1},{1,17},{18,2},{2,18},{19,3},{3,19},{20,4},{4,... | collective-permute-start | bytes 786440 | tf_op jit(solution)/shard_map/ppermute | solution.py:272
  204.8 24.9 %collective-permute-start.35 = (bf16[1,256,512]{2,1,0:T(8,128)(2,1)}, bf16[1,256,512]{2,1,0:T(8,128)(2,1)}, u32[]{:S(2)}, u32[]{:S(2)}) collective-permute-start(bf16[1,256,512]{2,1,0:T(8,128)(2,1)} %collective-permute-done.25.refs_8_), channel_id=1, source_target_pairs={{16,0},{0,16},{17,1},{1,17},{18,2},{2,18},{19,3},{3,19},{20,4},{4,... | collective-permute-start | bytes 786440 | tf_op jit(solution)/shard_map/ppermute | solution.py:272
  225.4 24.7 %all-to-all-start.5 = ((f32[16,4,256]{2,1,0:T(4,128)}), f32[16,4,256]{2,1,0:T(4,128)}, u32[]{:S(2)}, u32[]{:S(2)}) async-start(f32[16,4,256]{2,1,0:T(4,128)} %broadcast_in_dim.19), calls=%async_computation.6 | async-start | bytes 131072 | tf_op jit(solution)/shard_map/all_to_all | solution.py:277
  229.7 3.4 %copy-start.6 = (bf16[2048,2048]{1,0:T(8,128)(2,1)S(1)}, bf16[2048,2048]{1,0:T(8,128)(2,1)}, u32[]{:S(2)}) copy-start(bf16[2048,2048]{1,0:T(8,128)(2,1)} %refs_11_.3) | copy-start | bytes 25165828
  250.1 13.1 %all-to-all-start.6 = ((f32[16,4,256]{2,1,0:T(4,128)}), f32[16,4,256]{2,1,0:T(4,128)S(1)}, u32[]{:S(2)}, u32[]{:S(2)}) async-start(f32[16,4,256]{2,1,0:T(4,128)} %broadcast_in_dim.20), calls=%async_computation.7 | async-start | bytes 131072 | tf_op jit(solution)/shard_map/all_to_all | solution.py:277
  263.3 4.1 %collective-permute-start.38 = (f32[2,4,256]{2,1,0:T(4,128)S(1)}, f32[2,4,256]{2,1,0:T(4,128)S(1)}, u32[]{:S(2)}, u32[]{:S(2)}) collective-permute-start(f32[2,4,256]{2,1,0:T(4,128)S(1)} %pad_maximum_fusion.9), channel_id=1, source_target_pairs={{64,0},{96,32},{0,64},{32,96},{65,1},{97,33},{1,65},{33,97},{66,2}... | collective-permute-start | bytes 24584 | tf_op jit(solution)/shard_map/ppermute | solution.py:272
  264.3 3.7 %collective-permute-start.39 = (f32[2,4,256]{2,1,0:T(4,128)S(1)}, f32[2,4,256]{2,1,0:T(4,128)S(1)}, u32[]{:S(2)}, u32[]{:S(2)}) collective-permute-start(f32[2,4,256]{2,1,0:T(4,128)S(1)} %pad_maximum_fusion.9), channel_id=1, source_target_pairs={{96,0},{0,32},{32,64},{64,96},{97,1},{1,33},{33,65},{65,97},{98,2}... | collective-permute-start | bytes 24584 | tf_op jit(solution)/shard_map/ppermute | solution.py:272
  264.3 3.7 %collective-permute-start.37 = (f32[2,4,256]{2,1,0:T(4,128)S(1)}, f32[2,4,256]{2,1,0:T(4,128)S(1)}, u32[]{:S(2)}, u32[]{:S(2)}) collective-permute-start(f32[2,4,256]{2,1,0:T(4,128)S(1)} %pad_maximum_fusion.9), channel_id=1, source_target_pairs={{32,0},{64,32},{96,64},{0,96},{33,1},{65,33},{97,65},{1,97},{34,2}... | collective-permute-start | bytes 24584 | tf_op jit(solution)/shard_map/ppermute | solution.py:272
  268.1 4.8 %collective-permute-start.40 = (f32[2,4,256]{2,1,0:T(4,128)S(1)}, f32[2,4,256]{2,1,0:T(4,128)S(1)}, u32[]{:S(2)}, u32[]{:S(2)}) collective-permute-start(f32[2,4,256]{2,1,0:T(4,128)S(1)} %add_add_fusion), channel_id=1, source_target_pairs={{16,0},{0,16},{17,1},{1,17},{18,2},{2,18},{19,3},{3,19},{20,4},{4,... | collective-permute-start | bytes 24584 | tf_op jit(solution)/shard_map/ppermute | solution.py:272
  273.1 5.8 %copy-start.2 = (f32[4,4,2,64,2048]{4,3,2,1,0:T(8,128)S(1)}, f32[4,4,2,64,2048]{4,3,2,1,0:T(8,128)}, u32[]{:S(2)}) copy-start(f32[4,4,2,64,2048]{4,3,2,1,0:T(8,128)} %get-tuple-element.15) | copy-start | bytes 50331652
  278.9 9.2 %copy-start.8 = (bf16[48,2048]{1,0:T(8,128)(2,1)S(1)}, bf16[48,2048]{1,0:T(8,128)(2,1)}, u32[]{:S(2)}) copy-start(bf16[48,2048]{1,0:T(8,128)(2,1)} %copy-done.7) | copy-start | bytes 589828
  278.9 10.0 %copy-start.1 = (bf16[4,2048,128]{2,1,0:T(8,128)(2,1)S(1)}, bf16[4,2048,128]{2,1,0:T(8,128)(2,1)}, u32[]{:S(2)}) copy-start(bf16[4,2048,128]{2,1,0:T(8,128)(2,1)} %param.26) | copy-start | bytes 6291460
  (4 other events, 7.2 us)
Sparse Core Ops, SparseCore 0:
  9.7 44.7 all-gather.4
  61.9 52.0 all-gather.2
  141.5 82.4 reduce-scatter.1

commit v3 on v2

--- a/solution.py
+++ b/solution.py
@@ -13,22 +13,16 @@
 HEADS = 4
 SOFTCAP = 30.0
 Y, CORE, X, Z = 4, 2, 4, 4
+TILE = 256
+VOCAB_BLOCK = 512
+FINISH_BLOCK = 512
+HIDDEN = -1e30
 EPS = 1e-06
 ACC = 4
 XZ = ("x", "z")
 YC = ("y", "core")
 ALL = ("y", "core", "x", "z")
-PIECE_PLACES = tuple(
-    place
-    for kind in range(2)
-    for place in (
-        (kind, 0, 2 * kind, 2 * kind + 2),
-        (kind, 1, 2 * kind, 2 * kind + 2),
-        (kind, 3, 2 * kind, 2 * kind + 2),
-        (kind, 2, 2 * kind, 2 * kind + 1),
-        (kind, 2, 2 * kind + 1, 2 * kind + 2),
-    )
-)
+PIECE_PLACES = tuple((kind, d) for kind in range(2) for d in range(X))
 PIECES = len(PIECE_PLACES)
 CONTRACT_LAST = (((1,), (1,)), ((), ()))
 
@@ -124,18 +118,23 @@
 
     def copies():
         found = []
-        for piece, (kind, d, first, last) in zip(pieces, PIECE_PLACES):
-            for e in range(Z):
-                dx, dz = (d, e) if kind == 0 else (e, d)
-                column = (lax.rem(x + dx, X) * Z + lax.rem(z + dz, Z)) * width
-                column = pl.multiple_of(column, width)
-                found.append(
-                    pltpu.make_async_copy(
-                        piece.at[:, :, e * width : (e + 1) * width],
-                        rows_ref.at[first:last, :, pl.ds(column, width)],
-                        sems.at[len(found)],
+        for piece, (kind, d) in zip(pieces, PIECE_PLACES):
+            target = rows_ref.at[2 * kind : 2 * kind + 2]
+            if kind == 0:
+                column = pl.multiple_of(lax.rem(x + d, X) * Z * width, width)
+                parts = [(piece, target.at[:, :, pl.ds(column, Z * width)])]
+            else:
+                parts = []
+                for e in range(X):
+                    column = pl.multiple_of((e * Z + lax.rem(z + d, Z)) * width, width)
+                    parts.append(
+                        (
+                            piece.at[:, :, e * width : (e + 1) * width],
+                            target.at[:, :, pl.ds(column, width)],
+                        )
                     )
-                )
+            for source, place in parts:
+                found.append(pltpu.make_async_copy(source, place, sems.at[len(found)]))
         return found
 
     @pl.when(step == 0)
@@ -147,19 +146,25 @@
             copy.wait()
         running[...] = jnp.zeros_like(running)
 
-    ids = start + step * vocab + lax.broadcasted_iota(jnp.int32, (count, vocab), 1)
-    allowed = (ids >= bounds_ref[:, 0:1]) & (ids < bounds_ref[:, 1:2])
-    for head in range(heads):
+    every = rows_ref[...].reshape(heads * count, depth)
+    ids = start + step * vocab + lax.broadcasted_iota(jnp.int32, (count, TILE), 1)
+    for tile in range(0, vocab, TILE):
         products = lax.dot_general(
-            rows_ref[head], embedding_ref[...], CONTRACT_LAST, preferred_element_type=F32
+            every,
+            embedding_ref[tile : tile + TILE],
+            CONTRACT_LAST,
+            preferred_element_type=F32,
         )
-        logits = SOFTCAP * jnp.tanh(products * (1.0 / SOFTCAP))
-        out_ref[head] = logits.reshape(out_ref.shape[1:])
-        terms = jnp.where(allowed, jnp.exp(logits), 0.0)
-        part = terms[:, :128]
-        for lane in range(128, vocab, 128):
-            part = part + terms[:, lane : lane + 128]
-        running[head] += part
+        allowed = (ids >= bounds_ref[:, 0:1] - tile) & (ids < bounds_ref[:, 1:2] - tile)
+        for head in range(heads):
+            bent = jnp.tanh(products[head * count : (head + 1) * count] * (1.0 / SOFTCAP))
+            terms = jnp.where(allowed, jnp.exp(bent * SOFTCAP), 0.0)
+            kept = jnp.where(allowed, bent * SOFTCAP, HIDDEN).astype(BF)
+            out_ref[head, :, :, tile : tile + TILE] = kept.reshape(out_ref.shape[1:3] + (TILE,))
+            part = terms[:, :128]
+            for lane in range(128, TILE, 128):
+                part = part + terms[:, lane : lane + 128]
+            running[head] += part
 
     @pl.when(step == steps - 1)
     def _():
@@ -173,9 +178,9 @@
     heads = HEADS
     count = pieces[0].shape[1]
     vocab_width, depth = embedding.shape
-    vocab = min(256, vocab_width)
+    vocab = min(VOCAB_BLOCK, vocab_width)
     spec = pl.BlockSpec
-    out_shape = jax.ShapeDtypeStruct((heads, Y, CORE, count // Y, vocab_width), F32)
+    out_shape = jax.ShapeDtypeStruct((heads, Y, CORE, count // Y, vocab_width), BF)
     given = [place, *pieces, bounds, embedding]
     aliases = {}
     extra_specs = []
@@ -202,57 +207,50 @@
             scratch_shapes=[
                 pltpu.VMEM((heads, count, depth), BF),
                 pltpu.VMEM((heads, count, 128), F32),
-                pltpu.SemaphoreType.DMA((PIECES * Z,)),
+                pltpu.SemaphoreType.DMA((X + X * Z,)),
             ],
         ),
         input_output_aliases=aliases,
         compiler_params=pltpu.CompilerParams(
-            dimension_semantics=("arbitrary",), vmem_limit_bytes=32 << 20
+            dimension_semantics=("arbitrary",), vmem_limit_bytes=56 << 20
         ),
         cost_estimate=pl.CostEstimate(
             flops=2 * heads * count * vocab_width * depth,
-            bytes_accessed=2 * vocab_width * depth + 4 * heads * count * vocab_width,
+            bytes_accessed=2 * vocab_width * depth + 2 * heads * count * vocab_width,
             transcendentals=2 * heads * count * vocab_width,
         ),
     )(*given)
 
 
-def finish_kernel(place_ref, table_ref, logs_ref, bounds_ref, out_ref):
-    step = pl.program_id(0)
-    heads, count, vocab = table_ref.shape
-    ids = place_ref[3] + step * vocab + lax.broadcasted_iota(jnp.int32, (count, vocab), 1)
-    allowed = (ids >= bounds_ref[:, 0:1]) & (ids < bounds_ref[:, 1:2])
-    for head in range(heads):
-        values = table_ref[head] - logs_ref[:, head : head + 1]
-        out_ref[head] = jnp.where(allowed, values, 0.0).astype(BF)
-
-
-def finish(place, table, logs, bounds):
+def finish_kernel(table_ref, logs_ref, out_ref):
+    for head in range(table_ref.shape[0]):
+        values = table_ref[head].astype(F32)
+        shifted = values - logs_ref[:, head : head + 1]
+        out_ref[head] = jnp.where(values > 0.5 * HIDDEN, shifted, 0.0).astype(BF)
+
+
+def finish(table, logs):
     heads, count, vocab_width = table.shape
-    vocab = min(256, vocab_width)
+    vocab = min(FINISH_BLOCK, vocab_width)
     spec = pl.BlockSpec
     return pl.pallas_call(
         finish_kernel,
         out_shape=jax.ShapeDtypeStruct(table.shape, BF),
-        grid_spec=pltpu.PrefetchScalarGridSpec(
-            num_scalar_prefetch=1,
-            grid=(vocab_width // vocab,),
-            in_specs=[
-                spec((heads, count, vocab), lambda j, p: (0, 0, j)),
-                spec((count, heads), lambda j, p: (0, 0)),
-                spec((count, 2), lambda j, p: (0, 0)),
-            ],
-            out_specs=spec((heads, count, vocab), lambda j, p: (0, 0, j)),
-        ),
+        grid=(vocab_width // vocab,),
+        in_specs=[
+            spec((heads, count, vocab), lambda j: (0, 0, j)),
+            spec((count, heads), lambda j: (0, 0)),
+        ],
+        out_specs=spec((heads, count, vocab), lambda j: (0, 0, j)),
         compiler_params=pltpu.CompilerParams(
-            dimension_semantics=("arbitrary",), vmem_limit_bytes=32 << 20
+            dimension_semantics=("arbitrary",), vmem_limit_bytes=56 << 20
         ),
         cost_estimate=pl.CostEstimate(
-            flops=4 * heads * count * vocab_width,
-            bytes_accessed=6 * heads * count * vocab_width,
+            flops=3 * heads * count * vocab_width,
+            bytes_accessed=4 * heads * count * vocab_width,
             transcendentals=0,
         ),
-    )(place, table, logs, bounds)
+    )(table, logs)
 
 
 def rms_scale(values, gain):
@@ -265,16 +263,23 @@
 
 
 def after(values, *earlier):
-    return lax.optimization_barrier((values, *earlier))[0]
+    return lax.optimization_barrier((values, earlier))[0]
 
 
 def ring(values, axis, size, shift):
     return lax.ppermute(values, axis, [((i + shift) % size, i) for i in range(size)])
 
 
+def copies_of(values, size):
+    return lax.optimization_barrier(jnp.broadcast_to(values[None], (size,) + values.shape))
+
+
+def swap(copies, axes):
+    return lax.all_to_all(copies, axes, split_axis=0, concat_axis=0, tiled=True)
+
+
 def spread(values, axes, size):
-    copies = lax.optimization_barrier(jnp.broadcast_to(values[None], (size,) + values.shape))
-    return lax.all_to_all(copies, axes, split_axis=0, concat_axis=0, tiled=True)
+    return swap(copies_of(values, size), axes)
 
 
 def in_order(blocks, index):
@@ -289,20 +294,25 @@
     return ordered
 
 
-def out_weights(out_weight):
+def own_half_of(out_weight):
     half = out_weight.shape[0] // 2
-    own = lax.dynamic_slice_in_dim(out_weight, lax.axis_index("core") * half, half, 0)
+    return lax.dynamic_slice_in_dim(out_weight, lax.axis_index("core") * half, half, 0)
+
+
+def out_weights(own):
     own = jnp.concatenate([own] + [ring(own, "x", X, shift) for shift in range(1, X)], axis=1)
     return own, ring(own, "core", CORE, 1)
 
 
-def out_projection(attended, own_weight, other_weight):
-    rows, depth = attended.shape
+def gather_group(attended):
+    return [attended] + [ring(attended, "z", Z, shift) for shift in range(1, Z)]
+
+
+def out_projection(group, own_weight, other_weight, earlier):
+    rows, depth = group[0].shape
     half = depth // 2
     core = lax.axis_index("core")
-    group = jnp.concatenate(
-        [attended] + [ring(attended, "z", Z, shift) for shift in range(1, Z)], axis=0
-    )
+    group = jnp.concatenate(group, axis=0)
     own_part = lax.dynamic_slice_in_dim(group, core * half, half, 1)
     other_part = lax.dynamic_slice_in_dim(group, (1 - core) * half, half, 1)
     columns = (
@@ -314,6 +324,7 @@
     for shift in range(1, Z):
         slot = (Z - shift) % Z
         back.append(ring(columns[slot * rows : (slot + 1) * rows], "z", Z, shift))
+    back = after(back, earlier)
     by_z = in_order(back, lax.axis_index("z"))
     by_x = in_order(
         [
@@ -335,21 +346,22 @@
 
 
 def gather_drafts(drafts):
+    nears, fars = ("z", "x"), ("x", "z")
+    parts = [drafts[:2], drafts[2:]]
+    near = [
+        [part] + [ring(part, axis, X, shift) for shift in (1, 3, 2)]
+        for part, axis in zip(parts, nears)
+    ]
+    near = lax.optimization_barrier(near)
+    joined = [
+        jnp.concatenate(in_order([b[0], b[1], b[3], b[2]], lax.axis_index(axis)), axis=2)
+        for b, axis in zip(near, nears)
+    ]
+    joined = lax.optimization_barrier(joined)
     pieces = []
-    firsts = []
-    for kind, near in ((0, "z"), (1, "x")):
-        part = drafts[2 * kind : 2 * kind + 2]
-        ahead, behind = ring(part, near, X, 1), ring(part, near, X, 3)
-        firsts.append((part, ahead, behind))
-    joined = []
-    for (kind, near), (part, ahead, behind) in zip(((0, "z"), (1, "x")), firsts):
-        across = ring(ahead, near, X, 1)
-        joined.append(jnp.concatenate([part, ahead, across, behind], axis=2))
-    seconds = []
-    for far, part in zip(("x", "z"), joined):
-        seconds.append((part, ring(part, far, X, 1), ring(part, far, X, 3)))
-    for far, (part, ahead, behind) in zip(("x", "z"), seconds):
-        pieces += [part, ahead, behind, ring(ahead[:1], far, X, 1), ring(behind[1:], far, X, 3)]
+    for part, axis in zip(joined, fars):
+        moved = {shift: ring(part, axis, X, shift) for shift in (1, 3, 2)}
+        pieces += [part, moved[1], moved[2], moved[3]]
     return pieces
 
 
@@ -384,19 +396,22 @@
     def pick(values):
         return jnp.dot(chosen, values, preferred_element_type=F32).astype(BF)
 
-    path_hidden = spread(pick(hidden), XZ, units).reshape(rows, -1)
-    own_weight, other_weight = out_weights(out_weight)
-    attended = attention(tree_q, tree_kv, kv_cache, cache_lengths, tree_parents)
-
-    path_attended = spread(pick(attended), XZ, units).reshape(rows, -1)
+    own_half = own_half_of(out_weight)
+    own_weight, other_weight = out_weights(own_half)
+    attended = attention(after(tree_q, own_half), tree_kv, kv_cache, cache_lengths, tree_parents)
+
+    ahead = copies_of(jnp.concatenate([pick(attended), pick(hidden)], axis=1), units)
+    depth = attended.shape[1]
+    arrived = swap(ahead, XZ).reshape(rows, -1)
+    path_attended, path_hidden = arrived[:, :depth], arrived[:, depth:]
     path_columns = jnp.dot(path_attended, out_weight, preferred_element_type=F32).astype(BF)
-    path_columns = spread(path_columns, XZ, units)
-    path_projected = jnp.transpose(path_columns, (1, 0, 2)).reshape(rows, -1)
+    path_copies = copies_of(path_columns, units)
+    path_projected = jnp.transpose(swap(path_copies, XZ), (1, 0, 2)).reshape(rows, -1)
     path_first = (path_hidden.astype(F32) + rms_scale(path_projected, attn_post_gain)).astype(BF)
     path_rows = rms_scale(path_first, ff_pre_gain).astype(BF)
-    path_terms = unit_terms(path_rows, weights)
+    path_partial = unit_terms(path_rows, weights)
     path_terms = lax.all_to_all(
-        path_terms.reshape(units, ACC, -1), XZ, split_axis=0, concat_axis=0, tiled=True
+        path_partial.reshape(units, ACC, -1), XZ, split_axis=0, concat_axis=0, tiled=True
     )
     path_sum = jnp.sum(path_terms.astype(F32), axis=0)
     own_first = lax.dynamic_slice_in_dim(path_first, unit * ACC, ACC, 0)
@@ -412,12 +427,18 @@
     drafts = jnp.concatenate(drafts, axis=1)
     pieces = gather_drafts(drafts)
 
-    projected = out_projection(after(attended, path_attended), own_weight, other_weight)
+    group = gather_group(after(attended, ahead))
+    projected = out_projection(
+        after(group, path_copies), own_weight, other_weight, path_partial
+    )
     first = (hidden.astype(F32) + rms_scale(projected, attn_post_gain)).astype(BF)
     normed = rms_scale(first, ff_pre_gain).astype(BF)
     mlp_rows = lax.all_gather(normed, XZ, axis=0, tiled=True)
-    partial = unit_terms(after(mlp_rows, drafts), weights)
-    mlp_sum = lax.psum_scatter(partial, XZ, scatter_dimension=0, tiled=True).astype(F32)
+    other_pieces = [ring(piece, "core", CORE, 1) for piece in pieces]
+    mlp_rows = after(mlp_rows, other_pieces[0], other_pieces[X])
+    mlp_partial = unit_terms(mlp_rows, weights)
+    pieces = after(pieces, mlp_partial)
+    mlp_sum = lax.psum_scatter(mlp_partial, XZ, scatter_dimension=0, tiled=True)
 
     vocab_width = embedding.shape[0]
     start = lax.axis_index(ALL) * vocab_width
@@ -431,24 +452,16 @@
         return lax.dynamic_index_in_dim(by_core, which, 1, keepdims=False).reshape(Y * rows, 2)
 
     table, own_totals = some_logits(place_of(core), pieces, bounds_of(core), embedding, None)
-    other_pieces = [ring(piece, "core", CORE, 1) for piece in pieces]
     table, other_totals = some_logits(
         place_of(1 - core), other_pieces, bounds_of(1 - core), embedding, table
     )
-    sums = jnp.stack(
-        [
-            jnp.sum(spread(own_totals, XZ, units), axis=0),
-            jnp.sum(spread(other_totals, XZ, units), axis=0),
-        ]
-    )
-    sums = sums + ring(sums, "y", Y, 1) + ring(sums, "y", Y, 2) + ring(sums, "y", Y, 3)
-    swapped = ring(sums, "core", CORE, 1)
-    logs = jnp.log(sums + swapped[::-1])
+    sums = jnp.sum(spread(jnp.stack([own_totals, other_totals]), XZ, units), axis=0)
+    whole = sums + ring(sums, "y", Y, 1) + ring(sums, "y", Y, 2) + ring(sums, "y", Y, 3)
+    swapped = ring(whole, "core", CORE, 1)
+    logs = jnp.log(whole + swapped[::-1])
     logs = jnp.where(core == 0, logs, logs[::-1]).reshape(CORE, HEADS, Y, rows)
     logs = jnp.transpose(logs, (2, 0, 3, 1)).reshape(Y * CORE * rows, HEADS)
-    draft_logprobs = finish(
-        place_of(core), table.reshape(HEADS, Y * CORE * rows, vocab_width), logs, bounds
-    )
+    draft_logprobs = finish(table.reshape(HEADS, Y * CORE * rows, vocab_width), logs)
     mlp_sum = after(mlp_sum, sums)
     tree_out = (first.astype(F32) + rms_scale(mlp_sum, ff_post_gain)).astype(BF)
     return (tree_out, draft_logprobs)

time: 297 us -> 270 us (0.909)
  starting transfers between devices: 103 us -> 72.9 us
  blocking collectives: 0 us -> 12.3 us
  local copies, waits for them, and re-layouts: 32.1 us -> 20 us
  Pallas kernels: 44.5 us -> 47.6 us
    ppermute x41 -> x37, starting transfers between devices: 72 us -> 50.5 us  [ring(): lax.ppermute(values, axis, [((i + shift) % size, i) for i in range(size)])]
    all_to_all x7 -> x4, waiting for transfers between devices: 35 us -> 17.8 us  [the longest x3 10.4 us: swap(): return lax.all_to_all(copies, axes, split_axis=0, concat_axis=0, tiled=True)]
    ppermute x41 -> x37, waiting for transfers between devices: 32.4 us -> 47.4 us  [ring(): lax.ppermute(values, axis, [((i + shift) % size, i) for i in range(size)])]
    all_to_all x0 -> x1, blocking collectives: none -> 12.3 us  [swap(): return lax.all_to_all(copies, axes, split_axis=0, concat_axis=0, tiled=True)]
    all_to_all x7 -> x4, starting transfers between devices: 30.9 us -> 22.2 us  [the longest x3 16.9 us: swap(): return lax.all_to_all(copies, axes, split_axis=0, concat_axis=0, tiled=True)]
    unnamed x39 -> x60, local copies, waits for them, and re-layouts: 17.4 us -> 9.08 us
    convert_element_type x5 -> x0, local copies, waits for them, and re-layouts: 4.06 us -> none  [the longest x3 3.14 us: rms_scale(): floats = values.astype(F32)]
  transfers between devices with their start and end apart: 51 -> 44, of which waited for: 20 -> 20; matrix products, arithmetic and copies ran while one was open for 11% -> 12% of each run, Pallas kernels for 15% -> 18%
where the time goes in v3:
time: 270 us; the launch traced here: 269 us
  starting transfers between devices  72.9 us (27%)
  waiting for transfers between devices  65.9 us (24%)
  Pallas kernels  47.6 us (18%)
  matrix products  24.9 us (9%)
  local copies, waits for them, and re-layouts  20 us (7%)
  between operations  15 us (6%)
  blocking collectives  12.3 us (5%)
  other arithmetic  10.6 us (4%)
    ppermute x37, starting transfers between devices, ring(): lax.ppermute(values, axis, [((i + shift) % size, i) for i in range(size)])  50.5 us
    ppermute x37, waiting for transfers between devices, ring(): lax.ppermute(values, axis, [((i + shift) % size, i) for i in range(size)])  47.4 us
    pallas_call x2, Pallas kernels, some_logits(): pl.pallas_call(logits_kernel, out_shape=(out_shape, jax.ShapeDtypeStruct(...  35.3 us
    all_to_all x3, starting transfers between devices, swap(): return lax.all_to_all(copies, axes, split_axis=0, concat_axis=0, tiled=True)  16.9 us
    dot_general x2, matrix products, unit_terms(): lax.dot_general(active, weights[2], (((1,), (1,)), ((), ())), preferred_e...  12.3 us
    all_to_all x1, blocking collectives, swap(): return lax.all_to_all(copies, axes, split_axis=0, concat_axis=0, tiled=True)  12.3 us
    all_to_all x3, waiting for transfers between devices, swap(): return lax.all_to_all(copies, axes, split_axis=0, concat_axis=0, tiled=True)  10.4 us
    unnamed x60, local copies, waits for them, and re-layouts  9.08 us
  transfers between devices with their start and end apart: 44, of which 20 were waited for; matrix products, arithmetic and copies ran while one was open for 12% of the time, Pallas kernels for 18%

profile of v3, /device:TPU:1, one launch (start us, length us, event | category | flops | bytes accessed | tf_op | source)
XLA Modules:
  0.0 269.2 jit_solution(9552410962990217767)
XLA Ops:
  8.6 1.0 constant_dynamic-slice_fusion.2
  9.6 1.0 copy.56
  11.3 2.2 copy-done.2
  14.4 3.9 %shard_map.167 = bf16[48,2048]{1,0:T(8,128)(2,1)S(1)} custom-call(s32[1]{0:T(128)S(6)} %copy.61.length_ref, bf16[48,2048]{1,0:T(8,128)(2,1)S(1)} %copy-done.3, bf16[2,48,512]{2,1,0:T(8,128)(2,1)S(1)} %bitcast.73, s32[48,1]{1,0:T(8,128)S(1)} %copy.45.parents_ref, bf16[1,2,2,2048,256]{4,3,2,1,0:T(8,128)(2,1)S(1)} %copy-done.2, ...), custom_call_target="tpu_custom_call" | custom-call | flops 805306368 | bytes 4194304 | tf_op jit(solution)/shard_map/pallas_call | solution.py:77
  18.9 1.1 broadcast_in_dim.10
  19.9 8.6 %all-to-all-start = ((bf16[16,4,4096]{2,1,0:T(4,128)(2,1)}), bf16[16,4,4096]{2,1,0:T(4,128)(2,1)}, u32[]{:S(2)}, u32[]{:S(2)}) async-start(bf16[16,4,4096]{2,1,0:T(4,128)(2,1)} %broadcast_in_dim.10), calls=%async_computation | async-start | bytes 1048576 | tf_op jit(solution)/shard_map/all_to_all | solution.py:278
  28.5 1.3 collective-permute-start.5
  29.8 2.4 collective-permute-start.4
  32.2 1.2 collective-permute-start.3
  33.4 2.4 collective-permute-start
  36.4 6.3 %collective-permute-done.5 = bf16[1024,128]{1,0:T(8,128)(2,1)} collective-permute-done((bf16[1024,128]{1,0:T(8,128)(2,1)S(1)}, bf16[1024,128]{1,0:T(8,128)(2,1)}, u32[]{:S(2)}, u32[]{:S(2)}) %collective-permute-start.5) | collective-permute-done | bytes 262176 | tf_op jit(solution)/shard_map/ppermute | solution.py:270
  42.7 1.2 collective-permute-start.2
  43.9 4.5 %collective-permute-done.4 = bf16[1024,128]{1,0:T(8,128)(2,1)} collective-permute-done((bf16[1024,128]{1,0:T(8,128)(2,1)S(1)}, bf16[1024,128]{1,0:T(8,128)(2,1)}, u32[]{:S(2)}, u32[]{:S(2)}) %collective-permute-start.4) | collective-permute-done | bytes 262176 | tf_op jit(solution)/shard_map/ppermute | solution.py:270
  48.3 2.2 pad_maximum_fusion
  50.6 1.8 collective-permute-start.6
  52.4 1.2 reshape.103
  54.6 4.7 %all-to-all-start.1 = ((bf16[16,64,128]{2,1,0:T(8,128)(2,1)}), bf16[16,64,128]{2,1,0:T(8,128)(2,1)S(1)}, u32[]{:S(2)}, u32[]{:S(2)}) async-start(bf16[16,64,128]{2,1,0:T(8,128)(2,1)} %broadcast_in_dim.11), calls=%async_computation.1 | async-start | bytes 524288 | tf_op jit(solution)/shard_map/all_to_all | solution.py:278
  60.8 1.6 constant_dynamic-update-slice_fusion.1
  62.4 1.6 constant_dynamic-update-slice_fusion
  64.1 3.2 %all-to-all-done.1 = bf16[16,64,128]{2,1,0:T(8,128)(2,1)S(1)} async-done(((bf16[16,64,128]{2,1,0:T(8,128)(2,1)}), bf16[16,64,128]{2,1,0:T(8,128)(2,1)S(1)}, u32[]{:S(2)}, u32[]{:S(2)}) %all-to-all-start.1) | async-done | bytes 262176 | tf_op jit(solution)/shard_map/all_to_all | solution.py:278
  67.4 1.0 fusion.21
  68.4 1.7 fusion.38
  70.2 1.6 fusion.13
  71.9 1.0 collective-permute-start.7
  72.9 0.9 collective-permute-start.8
  74.0 2.4 fusion.48
  76.4 3.4 %convolution_convert_fusion.1 = bf16[64,2048]{1,0:T(8,128)(2,1)S(1)} fusion(bf16[3,2048,512]{1,2,0:T(8,128)(2,1)} %all-gather.3.cloned.1.call-done, f32[64,512]{1,0:T(8,128)S(1)} %fusion.48, bf16[64,2048]{1,0:T(8,128)(2,1)S(1)} %copy-done.9, f32[2048]{0:T(1024)S(1)} %convert_element_type.121, f32[64]{0:T(128)S(1)} %add_rsqrt_fusion.5), kind=kOutput, calls=%fused_computation.2 | convolution fusion | flops 269156352 | bytes 4858112 | tf_op jit(solution)/shard_map/dot_general | solution.py:343
  82.7 5.3 %all-to-all-start.2 = ((bf16[16,4,2048]{2,1,0:T(4,128)(2,1)}), bf16[16,4,2048]{2,1,0:T(4,128)(2,1)S(1)}, u32[]{:S(2)}, u32[]{:S(2)}) async-start(bf16[16,4,2048]{2,1,0:T(4,128)(2,1)} %reshape.104), calls=%async_computation.2 | async-start | bytes 524288 | tf_op jit(solution)/shard_map/all_to_all | solution.py:413
  88.1 7.4 %all-to-all-done.2 = bf16[16,4,2048]{2,1,0:T(4,128)(2,1)S(1)} async-done(((bf16[16,4,2048]{2,1,0:T(4,128)(2,1)}), bf16[16,4,2048]{2,1,0:T(4,128)(2,1)S(1)}, u32[]{:S(2)}, u32[]{:S(2)}) %all-to-all-start.2) | async-done | bytes 262176 | tf_op jit(solution)/shard_map/all_to_all | solution.py:413
  96.8 3.6 %all-to-all-start.3 = ((bf16[16,4,2048]{2,1,0:T(4,128)(2,1)}), bf16[16,4,2048]{2,1,0:T(4,128)(2,1)S(1)}, u32[]{:S(2)}, u32[]{:S(2)}) async-start(bf16[16,4,2048]{2,1,0:T(4,128)(2,1)} %broadcast_in_dim.12), calls=%async_computation.3 | async-start | bytes 524288 | tf_op jit(solution)/shard_map/all_to_all | solution.py:278
  100.5 7.2 %all-to-all-done.3 = bf16[16,4,2048]{2,1,0:T(4,128)(2,1)S(1)} async-done(((bf16[16,4,2048]{2,1,0:T(4,128)(2,1)}), bf16[16,4,2048]{2,1,0:T(4,128)(2,1)S(1)}, u32[]{:S(2)}, u32[]{:S(2)}) %all-to-all-start.3) | async-done | bytes 262176 | tf_op jit(solution)/shard_map/all_to_all | solution.py:278
  108.4 1.3 collective-permute-start.10
  109.7 2.8 %collective-permute-start.11 = (bf16[4,64,128]{2,1,0:T(8,128)(2,1)S(1)}, bf16[4,64,128]{2,1,0:T(8,128)(2,1)S(1)}, u32[]{:S(2)}, u32[]{:S(2)}) collective-permute-start(bf16[4,64,128]{2,1,0:T(8,128)(2,1)S(1)} %add_convert_fusion), channel_id=1, source_target_pairs={{64,0},{96,32},{0,64},{32,96},{65,1},{97,33},{1,65},{33,97},{66,2}... | collective-permute-start | bytes 196616 | tf_op jit(solution)/shard_map/ppermute | solution.py:270
  112.5 1.0 collective-permute-start.12
  113.4 1.4 collective-permute-done.11
  115.7 1.0 collective-permute-start.13
  117.2 1.5 collective-permute-start.15
  118.8 0.9 collective-permute-start.16
  120.2 2.5 collective-permute-done.13
  122.7 1.2 collective-permute-start.18
  123.9 1.4 collective-permute-done.14
  125.3 3.3 %collective-permute-done.15 = bf16[2,256,128]{2,1,0:T(8,128)(2,1)S(1)} collective-permute-done((bf16[2,256,128]{2,1,0:T(8,128)(2,1)S(1)}, bf16[2,256,128]{2,1,0:T(8,128)(2,1)S(1)}, u32[]{:S(2)}, u32[]{:S(2)}) %collective-permute-start.15) | collective-permute-done | bytes 131104 | tf_op jit(solution)/shard_map/ppermute | solution.py:270
  129.5 8.8 %collective-permute-start.19 = (bf16[2,256,512]{2,1,0:T(8,128)(2,1)S(1)}, bf16[2,256,512]{2,1,0:T(8,128)(2,1)S(1)}, u32[]{:S(2)}, u32[]{:S(2)}) collective-permute-start(bf16[2,256,512]{2,1,0:T(8,128)(2,1)S(1)} %get-tuple-element.57.refs_0_), channel_id=1, source_target_pairs={{16,0},{0,16},{17,1},{1,17},{18,2},{2,18},{19,3},{3,19},{20,4},{4,... | collective-permute-start | bytes 1572872 | tf_op jit(solution)/shard_map/ppermute | solution.py:270
  138.4 1.4 collective-permute-done.19.refs_0_
  140.6 5.7 %fusion = f32[768,512]{1,0:T(8,128)} fusion(bf16[768,2048]{1,0:T(8,128)(2,1)} %all-gather.5.cloned.1.call-done, bf16[3,2048,512]{1,2,0:T(8,128)(2,1)} %all-gather.3.cloned.1.call-done), kind=kOutput, calls=%fused_computation.8 | convolution fusion | flops 1610612736 | bytes 6815744 | tf_op jit(solution)/shard_map/dot_general | solution.py:340
  146.3 8.9 %convolution_convert_fusion = bf16[768,2048]{1,0:T(8,128)(2,1)} fusion(bf16[3,2048,512]{1,2,0:T(8,128)(2,1)} %all-gather.3.cloned.1.call-done, f32[768,512]{1,0:T(8,128)} %fusion, bf16[768,2048]{1,0:T(8,128)(2,1)} %all-gather.5.cloned.1.call-done), kind=kOutput, calls=%fused_computation | convolution fusion | flops 3226730496 | bytes 12058624 | tf_op jit(solution)/shard_map/dot_general | solution.py:343
  156.0 1.5 collective-permute-start.22
  157.4 1.5 collective-permute-start.24
  159.5 10.1 %collective-permute-done.21.refs_1_ = bf16[2,256,512]{2,1,0:T(8,128)(2,1)S(1)} collective-permute-done((bf16[2,256,512]{2,1,0:T(8,128)(2,1)S(1)}, bf16[2,256,512]{2,1,0:T(8,128)(2,1)S(1)}, u32[]{:S(2)}, u32[]{:S(2)}) %collective-permute-start.21) | collective-permute-done | bytes 524320 | tf_op jit(solution)/shard_map/ppermute | solution.py:270
  170.3 1.4 collective-permute-done.22.refs_2_
  171.6 2.8 %collective-permute-start.27 = (bf16[2,256,512]{2,1,0:T(8,128)(2,1)S(1)}, bf16[2,256,512]{2,1,0:T(8,128)(2,1)}, u32[]{:S(2)}, u32[]{:S(2)}) collective-permute-start(bf16[2,256,512]{2,1,0:T(8,128)(2,1)S(1)} %collective-permute-done.21.refs_1_), channel_id=1, source_target_pairs={{16,0},{0,16},{17,1},{1,17},{18,2},{2,18},{19,3},{3,19},{20,4},{4,... | collective-permute-start | bytes 1572872 | tf_op jit(solution)/shard_map/ppermute | solution.py:270
  177.4 8.8 %collective-permute-done.23.refs_3_ = bf16[2,256,512]{2,1,0:T(8,128)(2,1)} collective-permute-done((bf16[2,256,512]{2,1,0:T(8,128)(2,1)S(1)}, bf16[2,256,512]{2,1,0:T(8,128)(2,1)}, u32[]{:S(2)}, u32[]{:S(2)}) %collective-permute-start.23) | collective-permute-done | bytes 524320 | tf_op jit(solution)/shard_map/ppermute | solution.py:270
  187.2 1.4 collective-permute-done.26.refs_7_
  188.6 1.7 collective-permute-start.31
  190.3 17.5 %shard_map.168 = (bf16[4,4,2,64,2048]{4,3,2,1,0:T(8,128)(2,1)}, f32[4,256]{1,0:T(4,128)}) custom-call(s32[4]{0:T(128)} %add_add_fusion.1.place_ref, bf16[2,256,512]{2,1,0:T(8,128)(2,1)} %copy-done.7, bf16[2,256,512]{2,1,0:T(8,128)(2,1)} %copy-done.20, bf16[2,256,512]{2,1,0:T(8,128)(2,1)} %copy-done.21, bf16[2,256,512]{2,1,0:T(8,128)(2,1)} %collective-permute-done.23.refs_3_, ...), custom_call_target="tpu_custom_call" | custom-call | flops 8589934592 | bytes 12582912 | tf_op jit(solution)/shard_map/pallas_call | solution.py:191
  209.4 17.7 %shard_map.169 = (bf16[4,4,2,64,2048]{4,3,2,1,0:T(8,128)(2,1)}, f32[4,256]{1,0:T(4,128)}) custom-call(s32[4]{0:T(128)} %add_add_fusion.2.place_ref, bf16[2,256,512]{2,1,0:T(8,128)(2,1)} %copy-done.18, bf16[2,256,512]{2,1,0:T(8,128)(2,1)} %collective-permute-done.27.refs_1_, bf16[2,256,512]{2,1,0:T(8,128)(2,1)} %copy-done.22, ...), custom_call_target="tpu_custom_call", output_to_operand_aliasing={{0}: (11, {})} | custom-call | flops 8589934592 | bytes 12582912 | tf_op jit(solution)/shard_map/pallas_call | solution.py:191
  227.9 12.3 %all_to_all.25 = f32[16,2,4,256]{3,2,1,0:T(4,128)S(1)} all-to-all(f32[16,2,4,256]{3,2,1,0:T(4,128)S(1)} %broadcast_in_dim.14), channel_id=1, replica_groups=mesh['y'=4,'core'=2,'x'=4,'z'=4] {'x','z'}, dimensions={0} | all-to-all | bytes 262144 | tf_op jit(solution)/shard_map/all_to_all | solution.py:278
  240.2 1.0 collective-permute-start.35
  241.2 2.7 collective-permute-start.34
  245.2 1.4 collective-permute-done.33
  246.7 3.0 %collective-permute-start.36 = (f32[2,4,256]{2,1,0:T(4,128)S(1)}, f32[2,4,256]{2,1,0:T(4,128)S(1)}, u32[]{:S(2)}, u32[]{:S(2)}) collective-permute-start(f32[2,4,256]{2,1,0:T(4,128)S(1)} %bitcast.80), channel_id=1, source_target_pairs={{16,0},{0,16},{17,1},{1,17},{18,2},{2,18},{19,3},{3,19},{20,4},{4,... | collective-permute-start | bytes 24584 | tf_op jit(solution)/shard_map/ppermute | solution.py:270
  251.5 8.4 %shard_map.170 = bf16[4,512,2048]{2,1,0:T(8,128)(2,1)} custom-call(bf16[4,512,2048]{2,1,0:T(8,128)(2,1)} %bitcast.74, f32[512,4]{1,0:T(8,128)} %bitcast.75), custom_call_target="tpu_custom_call" | custom-call | flops 12582912 | bytes 16777216 | tf_op jit(solution)/shard_map/pallas_call | solution.py:236
  259.9 1.1 fusion.32
  260.9 1.8 fusion.37
  (166 shorter events, 26.1 us)
Async XLA Ops:
  7.2 100.7 %copy-start = (bf16[4,2048,128]{2,1,0:T(8,128)(2,1)S(1)}, bf16[4,2048,128]{2,1,0:T(8,128)(2,1)}, u32[]{:S(2)}) copy-start(bf16[4,2048,128]{2,1,0:T(8,128)(2,1)} %param.26) | copy-start | bytes 6291460
  7.2 66.9 %all-gather.3.cloned.1.call-start = ((), (), s32[]{:S(2)}) async-start(), calls=%async_computation.6 | async-start | bytes 7077888 | tf_op jit(solution)/shard_map/all_gather | solution.py:391
  9.5 38.8 %copy-start.5 = (bf16[1024,128]{1,0:T(8,128)(2,1)}, bf16[1024,128]{1,0:T(8,128)(2,1)S(1)}, u32[]{:S(2)}) copy-start(bf16[1024,128]{1,0:T(8,128)(2,1)S(1)} %constant_dynamic-slice_fusion.2) | copy-start | bytes 786436
  14.4 4.0 %copy-start.10 = (bf16[48,2048]{1,0:T(8,128)(2,1)S(1)}, bf16[48,2048]{1,0:T(8,128)(2,1)}, u32[]{:S(2)}) copy-start(bf16[48,2048]{1,0:T(8,128)(2,1)} %param.16) | copy-start | bytes 589828
  14.4 4.0 %copy-start.27 = (s32[1,4]{1,0:T(1,128)S(1)}, s32[1,4]{1,0:T(1,128)}, u32[]{:S(2)}) copy-start(s32[1,4]{1,0:T(1,128)} %param.22) | copy-start | bytes 52
  18.4 18.0 %copy-start.12 = (bf16[2048]{0:T(1024)(128)(2,1)S(1)}, bf16[2048]{0:T(1024)(128)(2,1)}, u32[]{:S(2)}) copy-start(bf16[2048]{0:T(1024)(128)(2,1)} %param.28) | copy-start | bytes 12292
  18.4 18.0 %copy-start.13 = (bf16[2048]{0:T(1024)(128)(2,1)S(1)}, bf16[2048]{0:T(1024)(128)(2,1)}, u32[]{:S(2)}) copy-start(bf16[2048]{0:T(1024)(128)(2,1)} %param.29) | copy-start | bytes 12292
  19.9 33.7 %copy-start.4 = (bf16[2048,128]{1,0:T(8,128)(2,1)S(1)}, bf16[2048,128]{1,0:T(8,128)(2,1)}, u32[]{:S(2)}) copy-start(bf16[2048,128]{1,0:T(8,128)(2,1)} %param.24) | copy-start | bytes 1572868
  19.9 32.5 %all-to-all-start = ((bf16[16,4,4096]{2,1,0:T(4,128)(2,1)}), bf16[16,4,4096]{2,1,0:T(4,128)(2,1)}, u32[]{:S(2)}, u32[]{:S(2)}) async-start(bf16[16,4,4096]{2,1,0:T(4,128)(2,1)} %broadcast_in_dim.10), calls=%async_computation | async-start | bytes 1048576 | tf_op jit(solution)/shard_map/all_to_all | solution.py:278
  28.5 14.2 %collective-permute-start.5 = (bf16[1024,128]{1,0:T(8,128)(2,1)S(1)}, bf16[1024,128]{1,0:T(8,128)(2,1)}, u32[]{:S(2)}, u32[]{:S(2)}) collective-permute-start(bf16[1024,128]{1,0:T(8,128)(2,1)S(1)} %constant_dynamic-slice_fusion.2), channel_id=1, source_target_pairs={{12,0},{0,4},{4,8},{8,12},{13,1},{1,5},{5,9},{9,13},{14,2},{2,6},{... | collective-permute-start | bytes 786440 | tf_op jit(solution)/shard_map/ppermute | solution.py:270
  29.8 18.5 %collective-permute-start.4 = (bf16[1024,128]{1,0:T(8,128)(2,1)S(1)}, bf16[1024,128]{1,0:T(8,128)(2,1)}, u32[]{:S(2)}, u32[]{:S(2)}) collective-permute-start(bf16[1024,128]{1,0:T(8,128)(2,1)S(1)} %constant_dynamic-slice_fusion.2), channel_id=1, source_target_pairs={{8,0},{12,4},{0,8},{4,12},{9,1},{13,5},{1,9},{5,13},{10,2},{14,6},... | collective-permute-start | bytes 786440 | tf_op jit(solution)/shard_map/ppermute | solution.py:270
  32.2 16.1 %collective-permute-start.3 = (bf16[1024,128]{1,0:T(8,128)(2,1)S(1)}, bf16[1024,128]{1,0:T(8,128)(2,1)}, u32[]{:S(2)}, u32[]{:S(2)}) collective-permute-start(bf16[1024,128]{1,0:T(8,128)(2,1)S(1)} %constant_dynamic-slice_fusion.2), channel_id=1, source_target_pairs={{4,0},{8,4},{12,8},{0,12},{5,1},{9,5},{13,9},{1,13},{6,2},{10,6},{... | collective-permute-start | bytes 786440 | tf_op jit(solution)/shard_map/ppermute | solution.py:270
  33.4 26.0 %collective-permute-start = (bf16[48,2048]{1,0:T(8,128)(2,1)S(1)}, bf16[48,2048]{1,0:T(8,128)(2,1)S(1)}, u32[]{:S(2)}, u32[]{:S(2)}) collective-permute-start(bf16[48,2048]{1,0:T(8,128)(2,1)S(1)} %shard_map.167), channel_id=1, source_target_pairs={{1,0},{2,1},{3,2},{0,3},{5,4},{6,5},{7,6},{4,7},{9,8},{10,9},{11,1... | collective-permute-start | bytes 589832 | tf_op jit(solution)/shard_map/ppermute | solution.py:270
  35.8 23.6 %collective-permute-start.1 = (bf16[48,2048]{1,0:T(8,128)(2,1)S(1)}, bf16[48,2048]{1,0:T(8,128)(2,1)}, u32[]{:S(2)}, u32[]{:S(2)}) collective-permute-start(bf16[48,2048]{1,0:T(8,128)(2,1)S(1)} %shard_map.167), channel_id=1, source_target_pairs={{2,0},{3,1},{0,2},{1,3},{6,4},{7,5},{4,6},{5,7},{10,8},{11,9},{8,1... | collective-permute-start | bytes 589832 | tf_op jit(solution)/shard_map/ppermute | solution.py:270
  42.7 16.7 %collective-permute-start.2 = (bf16[48,2048]{1,0:T(8,128)(2,1)S(1)}, bf16[48,2048]{1,0:T(8,128)(2,1)}, u32[]{:S(2)}, u32[]{:S(2)}) collective-permute-start(bf16[48,2048]{1,0:T(8,128)(2,1)S(1)} %shard_map.167), channel_id=1, source_target_pairs={{3,0},{0,1},{1,2},{2,3},{7,4},{4,5},{5,6},{6,7},{11,8},{8,9},{9,10... | collective-permute-start | bytes 589832 | tf_op jit(solution)/shard_map/ppermute | solution.py:270
  50.6 17.8 %collective-permute-start.6 = (bf16[1024,512]{1,0:T(8,128)(2,1)}, bf16[1024,512]{1,0:T(8,128)(2,1)}, u32[]{:S(2)}, u32[]{:S(2)}) collective-permute-start(bf16[1024,512]{1,0:T(8,128)(2,1)} %pad_maximum_fusion), channel_id=1, source_target_pairs={{16,0},{0,16},{17,1},{1,17},{18,2},{2,18},{19,3},{3,19},{20,4},{4,... | collective-permute-start | bytes 3145736 | tf_op jit(solution)/shard_map/ppermute | solution.py:270
  54.6 12.6 %all-to-all-start.1 = ((bf16[16,64,128]{2,1,0:T(8,128)(2,1)}), bf16[16,64,128]{2,1,0:T(8,128)(2,1)S(1)}, u32[]{:S(2)}, u32[]{:S(2)}) async-start(bf16[16,64,128]{2,1,0:T(8,128)(2,1)} %broadcast_in_dim.11), calls=%async_computation.1 | async-start | bytes 524288 | tf_op jit(solution)/shard_map/all_to_all | solution.py:278
  59.3 81.2 %all-gather.5.cloned.1.call-start = ((), (), s32[]{:S(2)}) async-start(), calls=%async_computation.7 | async-start | bytes 3342336 | tf_op jit(solution)/shard_map/all_gather | solution.py:436
  60.1 10.1 %copy-start.6 = (bf16[1024,128]{1,0:T(8,128)(2,1)S(1)}, bf16[1024,128]{1,0:T(8,128)(2,1)}, u32[]{:S(2)}) copy-start(bf16[1024,128]{1,0:T(8,128)(2,1)} %copy-done.5) | copy-start | bytes 786436
  70.2 3.9 %copy-start.9 = (bf16[64,2048]{1,0:T(8,128)(2,1)S(1)}, bf16[64,2048]{1,0:T(8,128)(2,1)}, u32[]{:S(2)}) copy-start(bf16[64,2048]{1,0:T(8,128)(2,1)} %get-tuple-element.75) | copy-start | bytes 786436
  71.9 8.0 %collective-permute-start.7 = (bf16[48,512]{1,0:T(8,128)(2,1)S(1)}, bf16[48,512]{1,0:T(8,128)(2,1)S(1)}, u32[]{:S(2)}, u32[]{:S(2)}) collective-permute-start(bf16[48,512]{1,0:T(8,128)(2,1)S(1)} %get-tuple-element.96), channel_id=1, source_target_pairs={{1,0},{2,1},{3,2},{0,3},{5,4},{6,5},{7,6},{4,7},{9,8},{10,9},{11,1... | collective-permute-start | bytes 147464 | tf_op jit(solution)/shard_map/ppermute | solution.py:270
  72.9 7.0 %collective-permute-start.8 = (bf16[48,512]{1,0:T(8,128)(2,1)S(1)}, bf16[48,512]{1,0:T(8,128)(2,1)S(1)}, u32[]{:S(2)}, u32[]{:S(2)}) collective-permute-start(bf16[48,512]{1,0:T(8,128)(2,1)S(1)} %get-tuple-element.95), channel_id=1, source_target_pairs={{2,0},{3,1},{0,2},{1,3},{6,4},{7,5},{4,6},{5,7},{10,8},{11,9},{8,1... | collective-permute-start | bytes 147464 | tf_op jit(solution)/shard_map/ppermute | solution.py:270
  73.8 6.1 %collective-permute-start.9 = (bf16[48,512]{1,0:T(8,128)(2,1)S(1)}, bf16[48,512]{1,0:T(8,128)(2,1)S(1)}, u32[]{:S(2)}, u32[]{:S(2)}) collective-permute-start(bf16[48,512]{1,0:T(8,128)(2,1)S(1)} %get-tuple-element.94), channel_id=1, source_target_pairs={{3,0},{0,1},{1,2},{2,3},{7,4},{4,5},{5,6},{6,7},{11,8},{8,9},{9,10... | collective-permute-start | bytes 147464 | tf_op jit(solution)/shard_map/ppermute | solution.py:270
  79.9 8.1 %copy-start.14 = (bf16[2048]{0:T(1024)(128)(2,1)S(1)}, bf16[2048]{0:T(1024)(128)(2,1)}, u32[]{:S(2)}) copy-start(bf16[2048]{0:T(1024)(128)(2,1)} %param.30) | copy-start | bytes 12292
  79.9 8.1 %copy-start.15 = (bf16[2048]{0:T(1024)(128)(2,1)S(1)}, bf16[2048]{0:T(1024)(128)(2,1)}, u32[]{:S(2)}) copy-start(bf16[2048]{0:T(1024)(128)(2,1)} %param.31) | copy-start | bytes 12292
  82.7 12.7 %all-to-all-start.2 = ((bf16[16,4,2048]{2,1,0:T(4,128)(2,1)}), bf16[16,4,2048]{2,1,0:T(4,128)(2,1)S(1)}, u32[]{:S(2)}, u32[]{:S(2)}) async-start(bf16[16,4,2048]{2,1,0:T(4,128)(2,1)} %reshape.104), calls=%async_computation.2 | async-start | bytes 524288 | tf_op jit(solution)/shard_map/all_to_all | solution.py:413
  96.8 10.9 %all-to-all-start.3 = ((bf16[16,4,2048]{2,1,0:T(4,128)(2,1)}), bf16[16,4,2048]{2,1,0:T(4,128)(2,1)S(1)}, u32[]{:S(2)}, u32[]{:S(2)}) async-start(bf16[16,4,2048]{2,1,0:T(4,128)(2,1)} %broadcast_in_dim.12), calls=%async_computation.3 | async-start | bytes 524288 | tf_op jit(solution)/shard_map/all_to_all | solution.py:278
  100.4 159.4 %reduce-scatter.2.cloned.1.call-start = ((), (), s32[]{:S(2)}) async-start(), calls=%async_computation.8 | async-start | bytes 3342336 | tf_op jit(solution)/shard_map/reduce_scatter | solution.py:441
  108.4 5.0 %collective-permute-start.10 = (bf16[4,64,128]{2,1,0:T(8,128)(2,1)S(1)}, bf16[4,64,128]{2,1,0:T(8,128)(2,1)S(1)}, u32[]{:S(2)}, u32[]{:S(2)}) collective-permute-start(bf16[4,64,128]{2,1,0:T(8,128)(2,1)S(1)} %add_convert_fusion), channel_id=1, source_target_pairs={{96,0},{0,32},{32,64},{64,96},{97,1},{1,33},{33,65},{65,97},{98,2}... | collective-permute-start | bytes 196616 | tf_op jit(solution)/shard_map/ppermute | solution.py:270
  109.7 5.1 %collective-permute-start.11 = (bf16[4,64,128]{2,1,0:T(8,128)(2,1)S(1)}, bf16[4,64,128]{2,1,0:T(8,128)(2,1)S(1)}, u32[]{:S(2)}, u32[]{:S(2)}) collective-permute-start(bf16[4,64,128]{2,1,0:T(8,128)(2,1)S(1)} %add_convert_fusion), channel_id=1, source_target_pairs={{64,0},{96,32},{0,64},{32,96},{65,1},{97,33},{1,65},{33,97},{66,2}... | collective-permute-start | bytes 196616 | tf_op jit(solution)/shard_map/ppermute | solution.py:270
  112.5 3.1 %collective-permute-start.12 = (bf16[4,64,128]{2,1,0:T(8,128)(2,1)S(1)}, bf16[4,64,128]{2,1,0:T(8,128)(2,1)S(1)}, u32[]{:S(2)}, u32[]{:S(2)}) collective-permute-start(bf16[4,64,128]{2,1,0:T(8,128)(2,1)S(1)} %add_convert_fusion), channel_id=1, source_target_pairs={{32,0},{64,32},{96,64},{0,96},{33,1},{65,33},{97,65},{1,97},{34,2}... | collective-permute-start | bytes 196616 | tf_op jit(solution)/shard_map/ppermute | solution.py:270
  115.7 7.0 %collective-permute-start.13 = (bf16[2,256,128]{2,1,0:T(8,128)(2,1)S(1)}, bf16[2,256,128]{2,1,0:T(8,128)(2,1)S(1)}, u32[]{:S(2)}, u32[]{:S(2)}) collective-permute-start(bf16[2,256,128]{2,1,0:T(8,128)(2,1)S(1)} %get-tuple-element.49), channel_id=1, source_target_pairs={{1,0},{2,1},{3,2},{0,3},{5,4},{6,5},{7,6},{4,7},{9,8},{10,9},{11,1... | collective-permute-start | bytes 393224 | tf_op jit(solution)/shard_map/ppermute | solution.py:270
  116.7 8.6 %collective-permute-start.14 = (bf16[2,256,128]{2,1,0:T(8,128)(2,1)S(1)}, bf16[2,256,128]{2,1,0:T(8,128)(2,1)S(1)}, u32[]{:S(2)}, u32[]{:S(2)}) collective-permute-start(bf16[2,256,128]{2,1,0:T(8,128)(2,1)S(1)} %get-tuple-element.49), channel_id=1, source_target_pairs={{3,0},{0,1},{1,2},{2,3},{7,4},{4,5},{5,6},{6,7},{11,8},{8,9},{9,10... | collective-permute-start | bytes 393224 | tf_op jit(solution)/shard_map/ppermute | solution.py:270
  117.2 11.4 %collective-permute-start.15 = (bf16[2,256,128]{2,1,0:T(8,128)(2,1)S(1)}, bf16[2,256,128]{2,1,0:T(8,128)(2,1)S(1)}, u32[]{:S(2)}, u32[]{:S(2)}) collective-permute-start(bf16[2,256,128]{2,1,0:T(8,128)(2,1)S(1)} %get-tuple-element.49), channel_id=1, source_target_pairs={{2,0},{3,1},{0,2},{1,3},{6,4},{7,5},{4,6},{5,7},{10,8},{11,9},{8,1... | collective-permute-start | bytes 393224 | tf_op jit(solution)/shard_map/ppermute | solution.py:270
  118.8 9.8 %collective-permute-start.16 = (bf16[2,256,128]{2,1,0:T(8,128)(2,1)S(1)}, bf16[2,256,128]{2,1,0:T(8,128)(2,1)S(1)}, u32[]{:S(2)}, u32[]{:S(2)}) collective-permute-start(bf16[2,256,128]{2,1,0:T(8,128)(2,1)S(1)} %get-tuple-element.53), channel_id=1, source_target_pairs={{4,0},{8,4},{12,8},{0,12},{5,1},{9,5},{13,9},{1,13},{6,2},{10,6},{... | collective-permute-start | bytes 393224 | tf_op jit(solution)/shard_map/ppermute | solution.py:270
  119.7 8.9 %collective-permute-start.17 = (bf16[2,256,128]{2,1,0:T(8,128)(2,1)S(1)}, bf16[2,256,128]{2,1,0:T(8,128)(2,1)S(1)}, u32[]{:S(2)}, u32[]{:S(2)}) collective-permute-start(bf16[2,256,128]{2,1,0:T(8,128)(2,1)S(1)} %get-tuple-element.53), channel_id=1, source_target_pairs={{12,0},{0,4},{4,8},{8,12},{13,1},{1,5},{5,9},{9,13},{14,2},{2,6},{... | collective-permute-start | bytes 393224 | tf_op jit(solution)/shard_map/ppermute | solution.py:270
  122.7 6.5 %collective-permute-start.18 = (bf16[2,256,128]{2,1,0:T(8,128)(2,1)S(1)}, bf16[2,256,128]{2,1,0:T(8,128)(2,1)S(1)}, u32[]{:S(2)}, u32[]{:S(2)}) collective-permute-start(bf16[2,256,128]{2,1,0:T(8,128)(2,1)S(1)} %get-tuple-element.53), channel_id=1, source_target_pairs={{8,0},{12,4},{0,8},{4,12},{9,1},{13,5},{1,9},{5,13},{10,2},{14,6},... | collective-permute-start | bytes 393224 | tf_op jit(solution)/shard_map/ppermute | solution.py:270
  129.5 27.9 %copy-start.7 = (bf16[2,256,512]{2,1,0:T(8,128)(2,1)}, bf16[2,256,512]{2,1,0:T(8,128)(2,1)S(1)}, u32[]{:S(2)}) copy-start(bf16[2,256,512]{2,1,0:T(8,128)(2,1)S(1)} %get-tuple-element.57.refs_0_) | copy-start | bytes 1572868
  129.5 40.1 %copy-start.8 = (bf16[2,256,512]{2,1,0:T(8,128)(2,1)}, bf16[2,256,512]{2,1,0:T(8,128)(2,1)S(1)}, u32[]{:S(2)}) copy-start(bf16[2,256,512]{2,1,0:T(8,128)(2,1)S(1)} %get-tuple-element.61.refs_4_) | copy-start | bytes 1572868
  129.5 10.3 %collective-permute-start.19 = (bf16[2,256,512]{2,1,0:T(8,128)(2,1)S(1)}, bf16[2,256,512]{2,1,0:T(8,128)(2,1)S(1)}, u32[]{:S(2)}, u32[]{:S(2)}) collective-permute-start(bf16[2,256,512]{2,1,0:T(8,128)(2,1)S(1)} %get-tuple-element.57.refs_0_), channel_id=1, source_target_pairs={{16,0},{0,16},{17,1},{1,17},{18,2},{2,18},{19,3},{3,19},{20,4},{4,... | collective-permute-start | bytes 1572872 | tf_op jit(solution)/shard_map/ppermute | solution.py:270
  138.3 2.3 collective-permute-start.20
  139.8 6.4 %copy-start.18 = (bf16[2,256,512]{2,1,0:T(8,128)(2,1)}, bf16[2,256,512]{2,1,0:T(8,128)(2,1)S(1)}, u32[]{:S(2)}) copy-start(bf16[2,256,512]{2,1,0:T(8,128)(2,1)S(1)} %collective-permute-done.19.refs_0_) | copy-start | bytes 1572868
  140.6 5.7 %copy-start.19 = (bf16[2,256,512]{2,1,0:T(8,128)(2,1)}, bf16[2,256,512]{2,1,0:T(8,128)(2,1)S(1)}, u32[]{:S(2)}) copy-start(bf16[2,256,512]{2,1,0:T(8,128)(2,1)S(1)} %collective-permute-done.20.refs_4_) | copy-start | bytes 1572868
  155.2 19.2 %copy-start.17 = (s32[128,2]{0,1:T(2,128)S(1)}, s32[128,2]{0,1:T(2,128)}, u32[]{:S(2)}) copy-start(s32[128,2]{0,1:T(2,128)} %param.23) | copy-start | bytes 3076
  155.2 14.4 %collective-permute-start.21 = (bf16[2,256,512]{2,1,0:T(8,128)(2,1)S(1)}, bf16[2,256,512]{2,1,0:T(8,128)(2,1)S(1)}, u32[]{:S(2)}, u32[]{:S(2)}) collective-permute-start(bf16[2,256,512]{2,1,0:T(8,128)(2,1)S(1)} %get-tuple-element.57.refs_0_), channel_id=1, source_target_pairs={{4,0},{8,4},{12,8},{0,12},{5,1},{9,5},{13,9},{1,13},{6,2},{10,6},{... | collective-permute-start | bytes 1572872 | tf_op jit(solution)/shard_map/ppermute | solution.py:270
  156.0 15.7 %collective-permute-start.22 = (bf16[2,256,512]{2,1,0:T(8,128)(2,1)S(1)}, bf16[2,256,512]{2,1,0:T(8,128)(2,1)S(1)}, u32[]{:S(2)}, u32[]{:S(2)}) collective-permute-start(bf16[2,256,512]{2,1,0:T(8,128)(2,1)S(1)} %get-tuple-element.57.refs_0_), channel_id=1, source_target_pairs={{8,0},{12,4},{0,8},{4,12},{9,1},{13,5},{1,9},{5,13},{10,2},{14,6},... | collective-permute-start | bytes 1572872 | tf_op jit(solution)/shard_map/ppermute | solution.py:270
  157.4 28.8 %collective-permute-start.23 = (bf16[2,256,512]{2,1,0:T(8,128)(2,1)S(1)}, bf16[2,256,512]{2,1,0:T(8,128)(2,1)}, u32[]{:S(2)}, u32[]{:S(2)}) collective-permute-start(bf16[2,256,512]{2,1,0:T(8,128)(2,1)S(1)} %get-tuple-element.57.refs_0_), channel_id=1, source_target_pairs={{12,0},{0,4},{4,8},{8,12},{13,1},{1,5},{5,9},{9,13},{14,2},{2,6},{... | collective-permute-start | bytes 1572872 | tf_op jit(solution)/shard_map/ppermute | solution.py:270
  157.4 29.3 %collective-permute-start.24 = (bf16[2,256,512]{2,1,0:T(8,128)(2,1)S(1)}, bf16[2,256,512]{2,1,0:T(8,128)(2,1)}, u32[]{:S(2)}, u32[]{:S(2)}) collective-permute-start(bf16[2,256,512]{2,1,0:T(8,128)(2,1)S(1)} %get-tuple-element.61.refs_4_), channel_id=1, source_target_pairs={{1,0},{2,1},{3,2},{0,3},{5,4},{6,5},{7,6},{4,7},{9,8},{10,9},{11,1... | collective-permute-start | bytes 1572872 | tf_op jit(solution)/shard_map/ppermute | solution.py:270
  158.9 27.8 %collective-permute-start.25 = (bf16[2,256,512]{2,1,0:T(8,128)(2,1)S(1)}, bf16[2,256,512]{2,1,0:T(8,128)(2,1)}, u32[]{:S(2)}, u32[]{:S(2)}) collective-permute-start(bf16[2,256,512]{2,1,0:T(8,128)(2,1)S(1)} %get-tuple-element.61.refs_4_), channel_id=1, source_target_pairs={{2,0},{3,1},{0,2},{1,3},{6,4},{7,5},{4,6},{5,7},{10,8},{11,9},{8,1... | collective-permute-start | bytes 1572872 | tf_op jit(solution)/shard_map/ppermute | solution.py:270
  169.6 20.7 %copy-start.20 = (bf16[2,256,512]{2,1,0:T(8,128)(2,1)}, bf16[2,256,512]{2,1,0:T(8,128)(2,1)S(1)}, u32[]{:S(2)}) copy-start(bf16[2,256,512]{2,1,0:T(8,128)(2,1)S(1)} %collective-permute-done.21.refs_1_) | copy-start | bytes 1572868
  169.6 19.0 %collective-permute-start.26 = (bf16[2,256,512]{2,1,0:T(8,128)(2,1)S(1)}, bf16[2,256,512]{2,1,0:T(8,128)(2,1)}, u32[]{:S(2)}, u32[]{:S(2)}) collective-permute-start(bf16[2,256,512]{2,1,0:T(8,128)(2,1)S(1)} %get-tuple-element.61.refs_4_), channel_id=1, source_target_pairs={{3,0},{0,1},{1,2},{2,3},{7,4},{4,5},{5,6},{6,7},{11,8},{8,9},{9,10... | collective-permute-start | bytes 1572872 | tf_op jit(solution)/shard_map/ppermute | solution.py:270
  171.6 18.7 %copy-start.21 = (bf16[2,256,512]{2,1,0:T(8,128)(2,1)}, bf16[2,256,512]{2,1,0:T(8,128)(2,1)S(1)}, u32[]{:S(2)}) copy-start(bf16[2,256,512]{2,1,0:T(8,128)(2,1)S(1)} %collective-permute-done.22.refs_2_) | copy-start | bytes 1572868
  171.6 18.7 %collective-permute-start.27 = (bf16[2,256,512]{2,1,0:T(8,128)(2,1)S(1)}, bf16[2,256,512]{2,1,0:T(8,128)(2,1)}, u32[]{:S(2)}, u32[]{:S(2)}) collective-permute-start(bf16[2,256,512]{2,1,0:T(8,128)(2,1)S(1)} %collective-permute-done.21.refs_1_), channel_id=1, source_target_pairs={{16,0},{0,16},{17,1},{1,17},{18,2},{2,18},{19,3},{3,19},{20,4},{4,... | collective-permute-start | bytes 1572872 | tf_op jit(solution)/shard_map/ppermute | solution.py:270
  186.2 21.7 %collective-permute-start.28 = (bf16[2,256,512]{2,1,0:T(8,128)(2,1)S(1)}, bf16[2,256,512]{2,1,0:T(8,128)(2,1)S(1)}, u32[]{:S(2)}, u32[]{:S(2)}) collective-permute-start(bf16[2,256,512]{2,1,0:T(8,128)(2,1)S(1)} %collective-permute-done.22.refs_2_), channel_id=1, source_target_pairs={{16,0},{0,16},{17,1},{1,17},{18,2},{2,18},{19,3},{3,19},{20,4},{4,... | collective-permute-start | bytes 1572872 | tf_op jit(solution)/shard_map/ppermute | solution.py:270
  186.7 21.2 %collective-permute-start.29 = (bf16[2,256,512]{2,1,0:T(8,128)(2,1)}, bf16[2,256,512]{2,1,0:T(8,128)(2,1)S(1)}, u32[]{:S(2)}, u32[]{:S(2)}) collective-permute-start(bf16[2,256,512]{2,1,0:T(8,128)(2,1)} %collective-permute-done.23.refs_3_), channel_id=1, source_target_pairs={{16,0},{0,16},{17,1},{1,17},{18,2},{2,18},{19,3},{3,19},{20,4},{4,... | collective-permute-start | bytes 1572872 | tf_op jit(solution)/shard_map/ppermute | solution.py:270
  186.7 21.2 %collective-permute-start.30 = (bf16[2,256,512]{2,1,0:T(8,128)(2,1)}, bf16[2,256,512]{2,1,0:T(8,128)(2,1)S(1)}, u32[]{:S(2)}, u32[]{:S(2)}) collective-permute-start(bf16[2,256,512]{2,1,0:T(8,128)(2,1)} %collective-permute-done.24.refs_5_), channel_id=1, source_target_pairs={{16,0},{0,16},{17,1},{1,17},{18,2},{2,18},{19,3},{3,19},{20,4},{4,... | collective-permute-start | bytes 1572872 | tf_op jit(solution)/shard_map/ppermute | solution.py:270
  188.6 19.4 %collective-permute-start.31 = (bf16[2,256,512]{2,1,0:T(8,128)(2,1)}, bf16[2,256,512]{2,1,0:T(8,128)(2,1)S(1)}, u32[]{:S(2)}, u32[]{:S(2)}) collective-permute-start(bf16[2,256,512]{2,1,0:T(8,128)(2,1)} %collective-permute-done.25.refs_6_), channel_id=1, source_target_pairs={{16,0},{0,16},{17,1},{1,17},{18,2},{2,18},{19,3},{3,19},{20,4},{4,... | collective-permute-start | bytes 1572872 | tf_op jit(solution)/shard_map/ppermute | solution.py:270
  190.3 17.7 %collective-permute-start.32 = (bf16[2,256,512]{2,1,0:T(8,128)(2,1)}, bf16[2,256,512]{2,1,0:T(8,128)(2,1)S(1)}, u32[]{:S(2)}, u32[]{:S(2)}) collective-permute-start(bf16[2,256,512]{2,1,0:T(8,128)(2,1)} %collective-permute-done.26.refs_7_), channel_id=1, source_target_pairs={{16,0},{0,16},{17,1},{1,17},{18,2},{2,18},{19,3},{3,19},{20,4},{4,... | collective-permute-start | bytes 1572872 | tf_op jit(solution)/shard_map/ppermute | solution.py:270
  209.4 17.7 %copy-start.16 = (f32[4,256]{1,0:T(4,128)S(1)}, f32[4,256]{1,0:T(4,128)}, u32[]{:S(2)}) copy-start(f32[4,256]{1,0:T(4,128)} %get-tuple-element.65) | copy-start | bytes 12292
  240.2 4.4 %collective-permute-start.35 = (f32[2,4,256]{2,1,0:T(4,128)S(1)}, f32[2,4,256]{2,1,0:T(4,128)S(1)}, u32[]{:S(2)}, u32[]{:S(2)}) collective-permute-start(f32[2,4,256]{2,1,0:T(4,128)S(1)} %reduce_sum.88), channel_id=1, source_target_pairs={{96,0},{0,32},{32,64},{64,96},{97,1},{1,33},{33,65},{65,97},{98,2}... | collective-permute-start | bytes 24584 | tf_op jit(solution)/shard_map/ppermute | solution.py:270
  241.2 4.0 %collective-permute-start.34 = (f32[2,4,256]{2,1,0:T(4,128)S(1)}, f32[2,4,256]{2,1,0:T(4,128)S(1)}, u32[]{:S(2)}, u32[]{:S(2)}) collective-permute-start(f32[2,4,256]{2,1,0:T(4,128)S(1)} %reduce_sum.88), channel_id=1, source_target_pairs={{64,0},{96,32},{0,64},{32,96},{65,1},{97,33},{1,65},{33,97},{66,2}... | collective-permute-start | bytes 24584 | tf_op jit(solution)/shard_map/ppermute | solution.py:270
  243.9 2.8 %collective-permute-start.33 = (f32[2,4,256]{2,1,0:T(4,128)S(1)}, f32[2,4,256]{2,1,0:T(4,128)S(1)}, u32[]{:S(2)}, u32[]{:S(2)}) collective-permute-start(f32[2,4,256]{2,1,0:T(4,128)S(1)} %reduce_sum.88), channel_id=1, source_target_pairs={{32,0},{64,32},{96,64},{0,96},{33,1},{65,33},{97,65},{1,97},{34,2}... | collective-permute-start | bytes 24584 | tf_op jit(solution)/shard_map/ppermute | solution.py:270
  246.7 3.8 %collective-permute-start.36 = (f32[2,4,256]{2,1,0:T(4,128)S(1)}, f32[2,4,256]{2,1,0:T(4,128)S(1)}, u32[]{:S(2)}, u32[]{:S(2)}) collective-permute-start(f32[2,4,256]{2,1,0:T(4,128)S(1)} %bitcast.80), channel_id=1, source_target_pairs={{16,0},{0,16},{17,1},{1,17},{18,2},{2,18},{19,3},{3,19},{20,4},{4,... | collective-permute-start | bytes 24584 | tf_op jit(solution)/shard_map/ppermute | solution.py:270
  251.5 11.2 %copy-start.1 = (bf16[4,2048,128]{2,1,0:T(8,128)(2,1)S(1)}, bf16[4,2048,128]{2,1,0:T(8,128)(2,1)}, u32[]{:S(2)}) copy-start(bf16[4,2048,128]{2,1,0:T(8,128)(2,1)} %param.26) | copy-start | bytes 6291460
  (8 other events, 9.6 us)
Sparse Core Ops, SparseCore 0:
  9.7 45.3 all-gather.2
  82.0 54.4 all-gather.4
  155.3 84.3 reduce-scatter.1

commit v4 on v3

v4 whole, which is shorter than its diff:
```python
import functools

import jax
import jax.numpy as jnp
from jax import lax
from jax.experimental import pallas as pl
from jax.experimental.pallas import tpu as pltpu
from jax.sharding import Mesh, PartitionSpec as P

BF = jnp.bfloat16
F32 = jnp.float32
QH = 8
KVH = 2
HD = 256
HEADS = 4
SOFTCAP = 30.0
Y, CORE, X, Z = 4, 2, 4, 4
EPS = 1e-06
ACC = 4
XZ = ("x", "z")
YC = ("y", "core")
ALL = ("y", "core", "x", "z")
GROUPS = ((0, 0), (0, 1), (1, 0), (3, 0), (1, 1), (3, 1), (2, 0), (2, 1))
CALLS = ((0, 2), (2, 6), (6, 8))
TILE = 256
VOCAB_BLOCK = 512
HIDDEN = -1e30
CONTRACT_LAST = (((1,), (1,)), ((), ()))


def attention_kernel(length_ref, q_ref, kv_ref, parents_ref, keys_ref, values_ref, out_ref, top, bottom, tree):
    rows = q_ref.shape[0]
    group = QH // KVH
    head, block = pl.program_id(0), pl.program_id(1)
    width = keys_ref.shape[0]
    queries = jnp.concatenate([q_ref[:, g * HD : (g + 1) * HD] for g in range(group)], axis=0)
    scale = HD ** (-0.5)

    @pl.when((head == 0) & (block == 0))
    def _():
        lanes = lax.broadcasted_iota(jnp.int32, (rows, rows), 1)
        subs = lax.broadcasted_iota(jnp.int32, (rows, rows), 0)
        reach = jnp.where((parents_ref[...] == lanes) | (subs == lanes), 1.0, 0.0)
        for _ in range(max(1, (rows - 1).bit_length())):
            half = reach.astype(BF)
            reach = jnp.minimum(jnp.dot(half, half, preferred_element_type=F32), 1.0)
        tree[...] = reach

    @pl.when(block == 0)
    def _():
        keys = kv_ref[0]
        scores = lax.dot_general(queries, keys, CONTRACT_LAST, preferred_element_type=F32)
        reach = tree[...]
        weights = jnp.exp(scores * scale) * jnp.concatenate([reach] * group, axis=0)
        bottom[...] = jnp.sum(weights, axis=1, keepdims=True)
        top[...] = jnp.dot(weights.astype(BF), kv_ref[1], preferred_element_type=F32)

    scores = lax.dot_general(queries, keys_ref[...], CONTRACT_LAST, preferred_element_type=F32)
    slots = block * width + lax.broadcasted_iota(jnp.int32, scores.shape, 1)
    weights = jnp.where(slots < length_ref[0], jnp.exp(scores * scale), 0.0)
    bottom[...] += jnp.sum(weights, axis=1, keepdims=True)
    top[...] += jnp.dot(weights.astype(BF), values_ref[...], preferred_element_type=F32)

    @pl.when(block == pl.num_programs(1) - 1)
    def _():
        attended = (top[...] / bottom[...]).astype(BF)
        for g in range(group):
            out_ref[:, g * HD : (g + 1) * HD] = attended[g * rows : (g + 1) * rows]


def attention(tree_q, tree_kv, kv_cache, cache_lengths, tree_parents):
    rows = tree_q.shape[0]
    group = QH // KVH
    slots = kv_cache.shape[3]
    block = min(1024, slots)
    kv = jnp.transpose(tree_kv, (1, 0, 2))
    spec = pl.BlockSpec
    return pl.pallas_call(
        attention_kernel,
        out_shape=jax.ShapeDtypeStruct((rows, QH * HD), BF),
        grid_spec=pltpu.PrefetchScalarGridSpec(
            num_scalar_prefetch=1,
            grid=(KVH, slots // block),
            in_specs=[
                spec((rows, group * HD), lambda k, b, n: (0, k)),
                spec((2, rows, HD), lambda k, b, n: (0, 0, k)),
                spec((rows, 1), lambda k, b, n: (0, 0)),
                spec((None, None, None, block, HD), lambda k, b, n: (0, 0, k, b, 0)),
                spec((None, None, None, block, HD), lambda k, b, n: (0, 1, k, b, 0)),
            ],
            out_specs=spec((rows, group * HD), lambda k, b, n: (0, k)),
            scratch_shapes=[
                pltpu.VMEM((group * rows, HD), F32),
                pltpu.VMEM((group * rows, 1), F32),
                pltpu.VMEM((rows, rows), F32),
            ],
        ),
        compiler_params=pltpu.CompilerParams(
            dimension_semantics=("arbitrary", "arbitrary"), vmem_limit_bytes=24 << 20
        ),
        cost_estimate=pl.CostEstimate(
            flops=4 * rows * QH * HD * slots,
            bytes_accessed=4 * KVH * slots * HD,
            transcendentals=rows * QH * slots,
        ),
    )(cache_lengths, tree_q, kv, tree_parents.reshape(rows, 1), kv_cache, kv_cache)


def logits_kernel(first, parts, place_ref, *refs):
    pieces = refs[: len(parts)]
    bounds_ref, embedding_ref, out_ref, totals_ref, rows_ref, running, sems = refs[len(parts) :]
    step, steps = pl.program_id(0), pl.num_programs(0)
    groups, heads, count, depth = rows_ref.shape
    vocab = embedding_ref.shape[0]

    @pl.when(step == 0)
    def _():
        copies = [
            pltpu.make_async_copy(
                piece, rows_ref.at[group, low : low + piece.shape[0]], sems.at[number]
            )
            for number, (piece, (group, low)) in enumerate(zip(pieces, parts))
        ]
        for copy in copies:
            copy.start()
        for copy in copies:
            copy.wait()
        running[...] = jnp.zeros_like(running)

    every = rows_ref[...].reshape(groups * heads * count, depth)
    ids = place_ref[0] + step * vocab + lax.broadcasted_iota(jnp.int32, (count, TILE), 1)
    for tile in range(0, vocab, TILE):
        products = lax.dot_general(
            every,
            embedding_ref[tile : tile + TILE],
            CONTRACT_LAST,
            preferred_element_type=F32,
        )
        for group in range(groups):
            bounds = bounds_ref[place_ref[1 + first + group]] - tile
            allowed = (ids >= bounds[:, 0:1]) & (ids < bounds[:, 1:2])
            for head in range(heads):
                low = (group * heads + head) * count
                bent = jnp.tanh(products[low : low + count] * (1.0 / SOFTCAP))
                terms = jnp.where(allowed, jnp.exp(bent * SOFTCAP), 0.0)
                kept = jnp.where(allowed, bent * SOFTCAP, HIDDEN).astype(BF)
                out_ref[group, head, :, tile : tile + TILE] = kept
                part = terms[:, :128]
                for lane in range(128, TILE, 128):
                    part = part + terms[:, lane : lane + 128]
                running[low : low + count] += part

    @pl.when(step == steps - 1)
    def _():
        size = heads * count
        for group in range(groups):
            totals_ref[group : group + 1, :] = jnp.sum(
                jnp.transpose(running[group * size : (group + 1) * size]), axis=0, keepdims=True
            )


def some_logits(call, place, pieces, parts, bounds, embedding):
    first, last = CALLS[call]
    groups = last - first
    count, depth = pieces[0].shape[1:]
    vocab_width = embedding.shape[0]
    vocab = min(VOCAB_BLOCK, vocab_width)
    size = groups * HEADS * count
    spec = pl.BlockSpec
    return pl.pallas_call(
        functools.partial(logits_kernel, first, parts),
        out_shape=(
            jax.ShapeDtypeStruct((groups, HEADS, count, vocab_width), BF),
            jax.ShapeDtypeStruct((groups, HEADS * count), F32),
        ),
        grid_spec=pltpu.PrefetchScalarGridSpec(
            num_scalar_prefetch=1,
            grid=(vocab_width // vocab,),
            in_specs=[spec(memory_space=pl.ANY)] * len(pieces)
            + [
                spec(bounds.shape, lambda j, p: (0, 0, 0)),
                spec((vocab, depth), lambda j, p: (j, 0)),
            ],
            out_specs=(
                spec((groups, HEADS, count, vocab), lambda j, p: (0, 0, 0, j)),
                spec((groups, HEADS * count), lambda j, p: (0, 0)),
            ),
            scratch_shapes=[
                pltpu.VMEM((groups, HEADS, count, depth), BF),
                pltpu.VMEM((size, 128), F32),
                pltpu.SemaphoreType.DMA((len(pieces),)),
            ],
        ),
        compiler_params=pltpu.CompilerParams(
            dimension_semantics=("arbitrary",), vmem_limit_bytes=56 << 20
        ),
        cost_estimate=pl.CostEstimate(
            flops=2 * size * vocab_width * depth,
            bytes_accessed=2 * vocab_width * depth + 2 * size * vocab_width,
            transcendentals=2 * size * vocab_width,
        ),
    )(place, *pieces, bounds, embedding)


def finish_kernel(place_ref, *refs):
    tables, logs_ref, out_ref = refs[: len(CALLS)], refs[-2], refs[-1]
    step = pl.program_id(0)
    for table_ref, (first, last) in zip(tables, CALLS):

        @pl.when((step >= first) & (step < last))
        def _(table_ref=table_ref):
            for head in range(HEADS):
                values = table_ref[head].astype(F32)
                shifted = values - logs_ref[:, head : head + 1]
                out_ref[head] = jnp.where(values > 0.5 * HIDDEN, shifted, 0.0).astype(BF)


def finish(place, tables, logs):
    count, vocab_width = tables[0].shape[2:]
    groups = len(GROUPS)
    spec = pl.BlockSpec

    def table_spec(first, last):
        return spec(
            (None, HEADS, count, vocab_width),
            lambda k, p: (jnp.clip(k - first, 0, last - first - 1), 0, 0, 0),
        )

    return pl.pallas_call(
        finish_kernel,
        out_shape=jax.ShapeDtypeStruct((HEADS, groups, count, vocab_width), BF),
        grid_spec=pltpu.PrefetchScalarGridSpec(
            num_scalar_prefetch=1,
            grid=(groups,),
            in_specs=[table_spec(*call) for call in CALLS]
            + [spec((None, count, HEADS), lambda k, p: (p[1 + k], 0, 0))],
            out_specs=spec((HEADS, None, count, vocab_width), lambda k, p: (0, p[1 + k], 0, 0)),
        ),
        compiler_params=pltpu.CompilerParams(
            dimension_semantics=("arbitrary",), vmem_limit_bytes=56 << 20
        ),
        cost_estimate=pl.CostEstimate(
            flops=3 * groups * HEADS * count * vocab_width,
            bytes_accessed=4 * groups * HEADS * count * vocab_width,
            transcendentals=0,
        ),
    )(place, *tables, logs)


def rms_scale(values, gain):
    floats = values.astype(F32)
    return (
        floats
        * lax.rsqrt(jnp.mean(floats * floats, axis=-1, keepdims=True) + EPS)
        * gain.astype(F32)
    )


def after(values, *earlier):
    return lax.optimization_barrier((values, earlier))[0]


def ring(values, axis, size, shift):
    return lax.ppermute(values, axis, [((i + shift) % size, i) for i in range(size)])


def copies_of(values, size):
    return lax.optimization_barrier(jnp.broadcast_to(values[None], (size,) + values.shape))


def swap(copies, axes):
    return lax.all_to_all(copies, axes, split_axis=0, concat_axis=0, tiled=True)


def spread(values, axes, size):
    return swap(copies_of(values, size), axes)


def in_order(blocks, index):
    size = len(blocks)
    ordered = []
    for position in range(size):
        shift = (position - index) % size
        block = blocks[0]
        for candidate in range(1, size):
            block = jnp.where(shift == candidate, blocks[candidate], block)
        ordered.append(block)
    return ordered


def own_half_of(out_weight):
    half = out_weight.shape[0] // 2
    return lax.dynamic_slice_in_dim(out_weight, lax.axis_index("core") * half, half, 0)


def out_weights(pieces):
    own = jnp.concatenate(pieces, axis=1)
    return own, ring(own, "core", CORE, 1)


def out_projection(attended, own_weight, other_weight):
    rows, depth = attended.shape
    half = depth // 2
    core = lax.axis_index("core")
    group = lax.all_gather(attended, "z", axis=0, tiled=True)
    own_part = lax.dynamic_slice_in_dim(group, core * half, half, 1)
    other_part = lax.dynamic_slice_in_dim(group, (1 - core) * half, half, 1)
    columns = (
        jnp.dot(own_part, own_weight, preferred_element_type=F32)
        + jnp.dot(other_part, other_weight, preferred_element_type=F32)
    ).astype(BF)
    width = columns.shape[1] // X
    back = swap(columns.reshape(Z, rows, X * width), "z")
    by_x = in_order(
        [
            jnp.concatenate([back[z, :, d * width : (d + 1) * width] for z in range(Z)], axis=1)
            for d in range(X)
        ],
        lax.axis_index("x"),
    )
    return jnp.concatenate(by_x, axis=1)


def unit_terms(mlp_rows, weights):
    gate_part = jnp.dot(mlp_rows, weights[0], preferred_element_type=F32)
    upward = jnp.dot(mlp_rows, weights[1], preferred_element_type=F32)
    active = (jax.nn.gelu(gate_part, approximate=True) * upward).astype(BF)
    return lax.dot_general(
        active, weights[2], (((1,), (1,)), ((), ())), preferred_element_type=F32
    ).astype(BF)


def per_device(
    hidden,
    tree_q,
    tree_kv,
    kv_cache,
    cache_lengths,
    tree_parents,
    accepted,
    tenant_ranges,
    out_weight,
    mlp_weights,
    draft_weights,
    embedding,
    attn_post_gain,
    ff_pre_gain,
    ff_post_gain,
    final_gain,
):
    units = X * Z
    rows = units * ACC
    core = lax.axis_index("core")
    y = lax.axis_index("y")
    unit = lax.axis_index(XZ)
    weights = lax.all_gather(mlp_weights, YC, axis=2, tiled=True)
    chosen = (
        accepted[0][:, None] == jnp.arange(hidden.shape[0], dtype=jnp.int32)[None, :]
    ).astype(BF)

    def pick(values):
        return jnp.dot(chosen, values, preferred_element_type=F32).astype(BF)

    own_half = own_half_of(out_weight)
    pieces = [own_half] + [ring(own_half, "x", X, shift) for shift in range(1, X)]
    attended = attention(after(tree_q, own_half), tree_kv, kv_cache, cache_lengths, tree_parents)
    own_weight, other_weight = out_weights(after(pieces, attended))
    projected = out_projection(attended, own_weight, other_weight)
    first = (hidden.astype(F32) + rms_scale(projected, attn_post_gain)).astype(BF)
    normed = rms_scale(first, ff_pre_gain).astype(BF)
    mlp_rows = lax.all_gather(normed, XZ, axis=0, tiled=True)

    path_rows = spread(pick(normed), XZ, units).reshape(rows, -1)
    path_terms = swap(unit_terms(path_rows, weights).reshape(units, ACC, -1), XZ)
    path_sum = jnp.sum(path_terms.astype(F32), axis=0)
    path = (pick(first).astype(F32) + rms_scale(path_sum, ff_post_gain)).astype(BF)
    path_normed = rms_scale(path, final_gain).astype(BF)
    group_path = spread(path_normed, XZ, units).reshape(rows, -1)

    width = draft_weights.shape[2]
    before = jnp.einsum("rd,hde->hre", group_path, draft_weights, preferred_element_type=F32)
    own_columns = lax.dynamic_slice_in_dim(group_path, unit * width, width, 1)
    drafts = (own_columns.astype(F32)[None] + jax.nn.silu(before)).astype(BF)
    draft_copies = copies_of(drafts, units)
    drafts = jnp.transpose(swap(draft_copies, XZ), (1, 2, 0, 3)).reshape(HEADS, rows, -1)

    mlp_partial = unit_terms(after(mlp_rows, drafts), weights)
    mlp_sum = lax.psum_scatter(mlp_partial, XZ, scatter_dimension=0, tiled=True)

    vocab_width = embedding.shape[0]
    start = lax.axis_index(ALL) * vocab_width
    order = [((y + dy) % Y) * CORE + (core + dc) % CORE for dy, dc in GROUPS]
    place = jnp.stack([start] + order).astype(jnp.int32)
    bounds = jnp.repeat(tenant_ranges, ACC, axis=0).reshape(Y * CORE, rows, 2)
    half = HEADS // 2
    next_up, next_down = ring(drafts, "y", Y, 1), ring(drafts, "y", Y, 3)
    beside = ring(drafts, "core", CORE, 1)
    across = [ring(next_up[:half], "y", Y, 1), ring(next_down[half:], "y", Y, 3)]
    beside_up, beside_down = ring(next_up, "core", CORE, 1), ring(next_down, "core", CORE, 1)
    beside_across = [ring(piece, "core", CORE, 1) for piece in across]
    table_a, totals_a = some_logits(
        0, place, [drafts, beside], ((0, 0), (1, 0)), bounds, embedding
    )
    table_b, totals_b = some_logits(
        1,
        place,
        after([next_up, next_down, beside_up, beside_down], totals_a, mlp_partial),
        ((0, 0), (1, 0), (2, 0), (3, 0)),
        bounds,
        embedding,
    )
    table_c, totals_c = some_logits(
        2,
        place,
        after(across + beside_across, totals_b),
        ((0, 0), (0, half), (1, 0), (1, half)),
        bounds,
        embedding,
    )
    sums = jnp.concatenate([totals_a, totals_b, totals_c], axis=0)
    here = place[1:, None] == jnp.arange(Y * CORE, dtype=jnp.int32)[None, :]
    sums = jnp.sum(jnp.where(here[:, :, None], sums[:, None, :], 0.0), axis=0)
    sums = jnp.sum(spread(sums, XZ, units), axis=0)
    whole = sums + ring(sums, "y", Y, 1) + ring(sums, "y", Y, 2) + ring(sums, "y", Y, 3)
    whole = whole + ring(whole, "core", CORE, 1)
    logs = jnp.transpose(jnp.log(whole).reshape(Y * CORE, HEADS, rows), (0, 2, 1))
    draft_logprobs = finish(place, [table_a, table_b, table_c], logs).reshape(
        HEADS, Y * CORE * rows, vocab_width
    )
    mlp_sum = after(mlp_sum, sums)
    tree_out = (first.astype(F32) + rms_scale(mlp_sum, ff_post_gain)).astype(BF)
    return (tree_out, draft_logprobs)


def solution(mesh):
    fine = Mesh(mesh.devices.reshape(Y, CORE, X, Z), ALL)
    return jax.shard_map(
        per_device,
        mesh=fine,
        in_specs=(
            P(ALL, None),
            P(ALL, None),
            P(ALL, None, None),
            P(ALL, None, None, None, None),
            P(ALL),
            P(ALL, None),
            P(ALL, None),
            P(),
            P(None, XZ),
            P(None, None, ALL),
            P(None, None, XZ),
            P(ALL, None),
            P(),
            P(),
            P(),
            P(),
        ),
        out_specs=(P(ALL, None), P(None, None, ALL)),
        check_vma=False,
    )
```

time: 270 us -> 254 us (0.941)
  blocking collectives: 12.3 us -> 49.4 us
  waiting for transfers between devices: 65.9 us -> 32.5 us
  starting transfers between devices: 72.9 us -> 51 us
  Pallas kernels: 47.6 us -> 55.5 us
  other arithmetic: 10.6 us -> 5.5 us
    ppermute x37 -> x17, waiting for transfers between devices: 47.4 us -> 10.2 us  [ring(): lax.ppermute(values, axis, [((i + shift) % size, i) for i in range(size)])]
    all_to_all x1 -> x3, blocking collectives: 12.3 us -> 35.6 us  [swap(): return lax.all_to_all(copies, axes, split_axis=0, concat_axis=0, tiled=True)]
    all_gather x0 -> x1, blocking collectives: none -> 13.8 us  [out_projection(): group = lax.all_gather(attended, 'z', axis=0, tiled=True)]
    all_to_all x3, waiting for transfers between devices: 10.4 us -> 21.5 us  [swap(): return lax.all_to_all(copies, axes, split_axis=0, concat_axis=0, tiled=True)]
    ppermute x37 -> x17, starting transfers between devices: 50.5 us -> 40.2 us  [ring(): lax.ppermute(values, axis, [((i + shift) % size, i) for i in range(size)])]
    pallas_call x3 -> x4, Pallas kernels: 43.6 us -> 51.6 us  [the longest x3 40.3 us: some_logits(): pl.pallas_call(functools.partial(logits_kernel, first, parts), out_shape=...]
    all_to_all x1 -> x0, waiting for transfers between devices: 7.38 us -> none  [per_device(): lax.all_to_all(path_partial.reshape(units, ACC, -1), XZ, split_axis=0, co...]
    all_to_all x3, starting transfers between devices: 16.9 us -> 10.7 us  [swap(): return lax.all_to_all(copies, axes, split_axis=0, concat_axis=0, tiled=True)]
  transfers between devices with their start and end apart: 44 -> 23, of which waited for: 20 -> 9; matrix products, arithmetic and copies ran while one was open for 12% -> 10% of each run, Pallas kernels for 18% -> 22%
where the time goes in v4:
time: 254 us; the launch traced here: 252 us
  Pallas kernels  55.5 us (22%)
  starting transfers between devices  51 us (20%)
  blocking collectives  49.4 us (19%)
  waiting for transfers between devices  32.5 us (13%)
  matrix products  25.3 us (10%)
  local copies, waits for them, and re-layouts  18.2 us (7%)
  between operations  14.9 us (6%)
  other arithmetic  5.5 us (2%)
    pallas_call x3, Pallas kernels, some_logits(): pl.pallas_call(functools.partial(logits_kernel, first, parts), out_shape=...  40.3 us
    ppermute x17, starting transfers between devices, ring(): lax.ppermute(values, axis, [((i + shift) % size, i) for i in range(size)])  40.2 us
    all_to_all x3, blocking collectives, swap(): return lax.all_to_all(copies, axes, split_axis=0, concat_axis=0, tiled=True)  35.6 us
    all_to_all x3, waiting for transfers between devices, swap(): return lax.all_to_all(copies, axes, split_axis=0, concat_axis=0, tiled=True)  21.5 us
    all_gather x1, blocking collectives, out_projection(): group = lax.all_gather(attended, 'z', axis=0, tiled=True)  13.8 us
    dot_general x2, matrix products, unit_terms(): lax.dot_general(active, weights[2], (((1,), (1,)), ((), ())), preferred_e...  12.4 us
    pallas_call x1, Pallas kernels, finish(): pl.pallas_call(finish_kernel, out_shape=jax.ShapeDtypeStruct((HEADS, grou...  11.3 us
    all_to_all x3, starting transfers between devices, swap(): return lax.all_to_all(copies, axes, split_axis=0, concat_axis=0, tiled=True)  10.7 us
  transfers between devices with their start and end apart: 23, of which 9 were waited for; matrix products, arithmetic and copies ran while one was open for 10% of the time, Pallas kernels for 22%

profile of v4, /device:TPU:1, one launch (start us, length us, event | category | flops | bytes accessed | tf_op | source)
XLA Modules:
  0.0 252.4 jit_solution(12116514615672941105)
XLA Ops:
  7.2 0.7 all-gather.5.cloned.1.call-update
  7.9 1.0 constant_dynamic-slice_fusion
  8.9 3.4 %collective-permute-start = (bf16[1024,128]{1,0:T(8,128)(2,1)S(1)}, bf16[1024,128]{1,0:T(8,128)(2,1)S(1)}, u32[]{:S(2)}, u32[]{:S(2)}) collective-permute-start(bf16[1024,128]{1,0:T(8,128)(2,1)S(1)} %constant_dynamic-slice_fusion), channel_id=1, source_target_pairs={{4,0},{8,4},{12,8},{0,12},{5,1},{9,5},{13,9},{1,13},{6,2},{10,6},{... | collective-permute-start | bytes 786440 | tf_op jit(solution)/shard_map/ppermute | solution.py:264
  12.3 0.5 collective-permute-start.1
  12.8 0.6 collective-permute-start.2
  14.1 0.9 copy.38
  15.0 0.7 copy.31.parents_ref
  15.7 2.2 copy-done.2
  17.9 0.9 copy-done.3
  18.8 3.9 %shard_map.167 = bf16[48,2048]{1,0:T(8,128)(2,1)S(1)} custom-call(s32[1]{0:T(128)S(6)} %copy.42.length_ref, bf16[48,2048]{1,0:T(8,128)(2,1)S(1)} %copy-done.3, bf16[2,48,512]{2,1,0:T(8,128)(2,1)S(1)} %bitcast.94, s32[48,1]{1,0:T(8,128)S(1)} %copy.31.parents_ref, bf16[1,2,2,2048,256]{4,3,2,1,0:T(8,128)(2,1)S(1)} %copy-done.2, ...), custom_call_target="tpu_custom_call" | custom-call | flops 805306368 | bytes 4194304 | tf_op jit(solution)/shard_map/pallas_call | solution.py:78
  22.8 0.7 copy-done.7
  23.5 0.7 copy-done.8
  24.2 3.5 %collective-permute-done.2 = bf16[1024,128]{1,0:T(8,128)(2,1)} collective-permute-done((bf16[1024,128]{1,0:T(8,128)(2,1)S(1)}, bf16[1024,128]{1,0:T(8,128)(2,1)}, u32[]{:S(2)}, u32[]{:S(2)}) %collective-permute-start.2) | collective-permute-done | bytes 262176 | tf_op jit(solution)/shard_map/ppermute | solution.py:264
  27.7 1.0 constant_dynamic-update-slice_fusion.3
  28.7 1.0 constant_dynamic-update-slice_fusion.2
  29.8 1.1 constant_dynamic-update-slice_fusion.1
  30.8 1.0 constant_dynamic-update-slice_fusion
  31.8 0.5 collective-permute-start.3
  32.4 13.8 %all_gather.9 = bf16[192,2048]{1,0:T(8,128)(2,1)S(1)} all-gather(bf16[48,2048]{1,0:T(8,128)(2,1)S(1)} %shard_map.167), channel_id=1, replica_groups=mesh['y'=4,'core'=2,'x'=4,'z'=4] {'z'}, dimensions={0}, use_global_device_ids=true | all-gather | bytes 983040 | tf_op jit(solution)/shard_map/all_gather | solution.py:305
  46.2 1.6 fusion.34
  47.8 1.1 fusion.17
  48.9 3.7 %all-to-all-start = ((bf16[4,48,512]{2,1,0:T(8,128)(2,1)}), bf16[4,48,512]{2,1,0:T(8,128)(2,1)S(1)}, u32[]{:S(2)}, u32[]{:S(2)}) async-start(bf16[4,48,512]{2,1,0:T(8,128)(2,1)} %bitcast.2), calls=%async_computation | async-start | bytes 393216 | tf_op jit(solution)/shard_map/all_to_all | solution.py:272
  52.6 5.1 %all-to-all-done = bf16[4,48,512]{2,1,0:T(8,128)(2,1)S(1)} async-done(((bf16[4,48,512]{2,1,0:T(8,128)(2,1)}), bf16[4,48,512]{2,1,0:T(8,128)(2,1)S(1)}, u32[]{:S(2)}, u32[]{:S(2)}) %all-to-all-start) | async-done | bytes 196640 | tf_op jit(solution)/shard_map/all_to_all | solution.py:272
  58.4 0.8 fusion.32
  59.3 1.1 convolution_convert_fusion.2
  60.5 10.1 %all_to_all.30 = bf16[16,4,2048]{2,1,0:T(4,128)(2,1)S(1)} all-to-all(bf16[16,4,2048]{2,1,0:T(4,128)(2,1)S(1)} %broadcast_in_dim.23), channel_id=1, replica_groups=mesh['y'=4,'core'=2,'x'=4,'z'=4] {'x','z'}, dimensions={0} | all-to-all | bytes 524288 | tf_op jit(solution)/shard_map/all_to_all | solution.py:272
  70.7 2.4 fusion.43
  73.2 3.4 %convolution_convert_fusion.1 = bf16[64,2048]{1,0:T(8,128)(2,1)S(1)} fusion(bf16[3,2048,512]{1,2,0:T(8,128)(2,1)} %all-gather.5.cloned.1.call-done, f32[64,512]{1,0:T(8,128)S(1)} %fusion.43, bf16[64,2048]{1,0:T(8,128)(2,1)S(1)} %reshape.102), kind=kOutput, calls=%fused_computation.2 | convolution fusion | flops 268632064 | bytes 4849664 | tf_op jit(solution)/shard_map/dot_general | solution.py:328
  76.6 0.8 reshape.103
  77.4 3.5 %all-to-all-start.2 = ((bf16[16,4,2048]{2,1,0:T(4,128)(2,1)}), bf16[16,4,2048]{2,1,0:T(4,128)(2,1)S(1)}, u32[]{:S(2)}, u32[]{:S(2)}) async-start(bf16[16,4,2048]{2,1,0:T(4,128)(2,1)} %reshape.103), calls=%async_computation.2 | async-start | bytes 524288 | tf_op jit(solution)/shard_map/all_to_all | solution.py:272
  81.0 7.2 %all-to-all-done.2 = bf16[16,4,2048]{2,1,0:T(4,128)(2,1)S(1)} async-done(((bf16[16,4,2048]{2,1,0:T(4,128)(2,1)}), bf16[16,4,2048]{2,1,0:T(4,128)(2,1)S(1)}, u32[]{:S(2)}, u32[]{:S(2)}) %all-to-all-start.2) | async-done | bytes 262176 | tf_op jit(solution)/shard_map/all_to_all | solution.py:272
  88.9 0.8 broadcast_in_dim.24
  89.7 3.5 %all-to-all-start.3 = ((bf16[16,4,2048]{2,1,0:T(4,128)(2,1)}), bf16[16,4,2048]{2,1,0:T(4,128)(2,1)S(1)}, u32[]{:S(2)}, u32[]{:S(2)}) async-start(bf16[16,4,2048]{2,1,0:T(4,128)(2,1)} %broadcast_in_dim.24), calls=%async_computation.3 | async-start | bytes 524288 | tf_op jit(solution)/shard_map/all_to_all | solution.py:272
  93.3 9.2 %all-to-all-done.3 = bf16[16,4,2048]{2,1,0:T(4,128)(2,1)S(1)} async-done(((bf16[16,4,2048]{2,1,0:T(4,128)(2,1)}), bf16[16,4,2048]{2,1,0:T(4,128)(2,1)S(1)}, u32[]{:S(2)}, u32[]{:S(2)}) %all-to-all-start.3) | async-done | bytes 262176 | tf_op jit(solution)/shard_map/all_to_all | solution.py:272
  103.4 15.8 %all_to_all.31 = bf16[16,4,64,128]{3,2,1,0:T(8,128)(2,1)S(1)} all-to-all(bf16[16,4,64,128]{3,2,1,0:T(8,128)(2,1)S(1)} %broadcast_in_dim.25), channel_id=1, replica_groups=mesh['y'=4,'core'=2,'x'=4,'z'=4] {'x','z'}, dimensions={0} | all-to-all | bytes 2097152 | tf_op jit(solution)/shard_map/all_to_all | solution.py:272
  119.5 5.9 %fusion.4 = f32[768,512]{1,0:T(8,128)} fusion(bf16[768,2048]{1,0:T(8,128)(2,1)} %all-gather.3.cloned.1.call-done, bf16[3,2048,512]{1,2,0:T(8,128)(2,1)} %all-gather.5.cloned.1.call-done), kind=kOutput, calls=%fused_computation.12 | convolution fusion | flops 1610612736 | bytes 6815744 | tf_op jit(solution)/shard_map/dot_general | solution.py:325
  125.3 9.0 %convolution_convert_fusion = bf16[768,2048]{1,0:T(8,128)(2,1)} fusion(bf16[3,2048,512]{1,2,0:T(8,128)(2,1)} %all-gather.5.cloned.1.call-done, f32[768,512]{1,0:T(8,128)} %fusion.4, bf16[768,2048]{1,0:T(8,128)(2,1)} %all-gather.3.cloned.1.call-done), kind=kOutput, calls=%fused_computation | convolution fusion | flops 3226730496 | bytes 12058624 | tf_op jit(solution)/shard_map/dot_general | solution.py:328
  134.3 2.8 %collective-permute-start.5 = (bf16[4,64,2048]{2,1,0:T(8,128)(2,1)S(1)}, bf16[4,64,2048]{2,1,0:T(8,128)(2,1)S(1)}, u32[]{:S(2)}, u32[]{:S(2)}) collective-permute-start(bf16[4,64,2048]{2,1,0:T(8,128)(2,1)S(1)} %copy_bitcast_fusion.refs_0_), channel_id=1, source_target_pairs={{32,0},{64,32},{96,64},{0,96},{33,1},{65,33},{97,65},{1,97},{34,2}... | collective-permute-start | bytes 3145736 | tf_op jit(solution)/shard_map/ppermute | solution.py:264
  137.2 9.3 %collective-permute-start.4 = (bf16[4,64,2048]{2,1,0:T(8,128)(2,1)S(1)}, bf16[4,64,2048]{2,1,0:T(8,128)(2,1)}, u32[]{:S(2)}, u32[]{:S(2)}) collective-permute-start(bf16[4,64,2048]{2,1,0:T(8,128)(2,1)S(1)} %copy_bitcast_fusion.refs_0_), channel_id=1, source_target_pairs={{16,0},{0,16},{17,1},{1,17},{18,2},{2,18},{19,3},{3,19},{20,4},{4,... | collective-permute-start | bytes 3145736 | tf_op jit(solution)/shard_map/ppermute | solution.py:264
  146.5 4.1 %collective-permute-done.5.refs_0_ = bf16[4,64,2048]{2,1,0:T(8,128)(2,1)S(1)} collective-permute-done((bf16[4,64,2048]{2,1,0:T(8,128)(2,1)S(1)}, bf16[4,64,2048]{2,1,0:T(8,128)(2,1)S(1)}, u32[]{:S(2)}, u32[]{:S(2)}) %collective-permute-start.5) | collective-permute-done | bytes 1048608 | tf_op jit(solution)/shard_map/ppermute | solution.py:264
  150.6 10.0 %collective-permute-start.7 = (bf16[4,64,2048]{2,1,0:T(8,128)(2,1)S(1)}, bf16[4,64,2048]{2,1,0:T(8,128)(2,1)}, u32[]{:S(2)}, u32[]{:S(2)}) collective-permute-start(bf16[4,64,2048]{2,1,0:T(8,128)(2,1)S(1)} %collective-permute-done.5.refs_0_), channel_id=1, source_target_pairs={{16,0},{0,16},{17,1},{1,17},{18,2},{2,18},{19,3},{3,19},{20,4},{4,... | collective-permute-start | bytes 3145736 | tf_op jit(solution)/shard_map/ppermute | solution.py:264
  160.5 3.5 %collective-permute-start.8 = (bf16[4,64,2048]{2,1,0:T(8,128)(2,1)}, bf16[4,64,2048]{2,1,0:T(8,128)(2,1)}, u32[]{:S(2)}, u32[]{:S(2)}) collective-permute-start(bf16[4,64,2048]{2,1,0:T(8,128)(2,1)} %collective-permute-done.6.refs_1_), channel_id=1, source_target_pairs={{16,0},{0,16},{17,1},{1,17},{18,2},{2,18},{19,3},{3,19},{20,4},{4,... | collective-permute-start | bytes 3145736 | tf_op jit(solution)/shard_map/ppermute | solution.py:264
  164.1 0.6 stack.42.place_ref
  165.0 1.1 slice.109
  166.1 1.5 collective-permute-start.10
  167.7 0.7 broadcast_in_dim.27
  168.5 11.5 %shard_map.168 = (bf16[2,4,64,2048]{3,2,1,0:T(8,128)(2,1)}, f32[2,256]{1,0:T(2,128)}) custom-call(s32[9]{0:T(128)} %stack.42.place_ref, bf16[4,64,2048]{2,1,0:T(8,128)(2,1)} %copy-done.5, bf16[4,64,2048]{2,1,0:T(8,128)(2,1)} %collective-permute-done.4.refs_1_, s32[8,64,2]{2,1,0:T(8,128)} %bitcast.97, bf16[2048,2048]{1,0:T(8,128)(2,1)} %refs_5_.3), custom_call_target="tpu_custom_call" | custom-call | flops 4294967296 | bytes 10485760 | tf_op jit(solution)/shard_map/pallas_call | solution.py:170
  180.0 0.6 collective-permute-start.11
  180.6 1.2 collective-permute-start.12
  181.7 17.3 %shard_map.169 = (bf16[4,4,64,2048]{3,2,1,0:T(8,128)(2,1)}, f32[4,256]{1,0:T(4,128)}) custom-call(s32[9]{0:T(128)} %stack.42.place_ref, bf16[4,64,2048]{2,1,0:T(8,128)(2,1)} %copy-done.6, bf16[4,64,2048]{2,1,0:T(8,128)(2,1)} %collective-permute-done.6.refs_1_, bf16[4,64,2048]{2,1,0:T(8,128)(2,1)} %collective-permute-done.7.refs_2_, ...), custom_call_target="tpu_custom_call" | custom-call | flops 8589934592 | bytes 12582912 | tf_op jit(solution)/shard_map/pallas_call | solution.py:170
  199.1 0.8 copy-done.19
  200.1 11.6 %shard_map.170 = (bf16[2,4,64,2048]{3,2,1,0:T(8,128)(2,1)}, f32[2,256]{1,0:T(2,128)}) custom-call(s32[9]{0:T(128)} %stack.42.place_ref, bf16[2,64,2048]{2,1,0:T(8,128)(2,1)} %copy-done.17, bf16[2,64,2048]{2,1,0:T(8,128)(2,1)} %copy-done.18, bf16[2,64,2048]{2,1,0:T(8,128)(2,1)} %copy-done.19, bf16[2,64,2048]{2,1,0:T(8,128)(2,1)} %copy-done.20, ...), custom_call_target="tpu_custom_call" | custom-call | flops 4294967296 | bytes 10485760 | tf_op jit(solution)/shard_map/pallas_call | solution.py:170
  211.6 0.7 pad_maximum_fusion.5
  212.4 9.6 %all_to_all.32 = f32[16,8,256]{2,1,0:T(8,128)S(1)} all-to-all(f32[16,8,256]{2,1,0:T(8,128)S(1)} %broadcast_in_dim.30), channel_id=1, replica_groups=mesh['y'=4,'core'=2,'x'=4,'z'=4] {'x','z'}, dimensions={0} | all-to-all | bytes 262144 | tf_op jit(solution)/shard_map/all_to_all | solution.py:272
  222.5 1.7 collective-permute-start.14
  224.2 0.8 collective-permute-start.13
  225.0 0.8 collective-permute-done.15
  225.8 0.7 collective-permute-done.14
  226.7 3.2 %collective-permute-start.16 = (f32[8,256]{1,0:T(8,128)S(1)}, f32[8,256]{1,0:T(8,128)S(1)}, u32[]{:S(2)}, u32[]{:S(2)}) collective-permute-start(f32[8,256]{1,0:T(8,128)S(1)} %add_add_fusion), channel_id=1, source_target_pairs={{16,0},{0,16},{17,1},{1,17},{18,2},{2,18},{19,3},{3,19},{20,4},{4,... | collective-permute-start | bytes 24584 | tf_op jit(solution)/shard_map/ppermute | solution.py:264
  230.0 0.8 collective-permute-done.16
  230.9 0.9 copy.34
  231.7 11.3 %shard_map.171 = bf16[4,8,64,2048]{3,2,1,0:T(8,128)(2,1)} custom-call(s32[9]{0:T(128)} %stack.42.place_ref, bf16[2,4,64,2048]{3,2,1,0:T(8,128)(2,1)} %get-tuple-element.41.refs_0_, bf16[4,4,64,2048]{3,2,1,0:T(8,128)(2,1)} %get-tuple-element.42.refs_1_, bf16[2,4,64,2048]{3,2,1,0:T(8,128)(2,1)} %get-tuple-element.43.refs_2_, f32[8,64,4]{2,1,0:T(8,128)} %bitcast.96), custom_call_target="tpu_custom_call" | custom-call | flops 12582912 | bytes 16777216 | tf_op jit(solution)/shard_map/pallas_call | solution.py:229
  243.0 1.1 fusion.28
  244.1 1.8 fusion.33
  (100 shorter events, 4.3 us)
Async XLA Ops:
  7.2 95.5 %copy-start = (bf16[4,2048,128]{2,1,0:T(8,128)(2,1)S(1)}, bf16[4,2048,128]{2,1,0:T(8,128)(2,1)}, u32[]{:S(2)}) copy-start(bf16[4,2048,128]{2,1,0:T(8,128)(2,1)} %param.26) | copy-start | bytes 6291460
  7.2 63.5 %all-gather.5.cloned.1.call-start = ((), (), s32[]{:S(2)}) async-start(), calls=%async_computation.8 | async-start | bytes 7077888 | tf_op jit(solution)/shard_map/all_gather | solution.py:356
  8.9 13.9 %copy-start.4 = (bf16[1024,128]{1,0:T(8,128)(2,1)}, bf16[1024,128]{1,0:T(8,128)(2,1)S(1)}, u32[]{:S(2)}) copy-start(bf16[1024,128]{1,0:T(8,128)(2,1)S(1)} %constant_dynamic-slice_fusion) | copy-start | bytes 786436
  8.9 13.9 %collective-permute-start = (bf16[1024,128]{1,0:T(8,128)(2,1)S(1)}, bf16[1024,128]{1,0:T(8,128)(2,1)S(1)}, u32[]{:S(2)}, u32[]{:S(2)}) collective-permute-start(bf16[1024,128]{1,0:T(8,128)(2,1)S(1)} %constant_dynamic-slice_fusion), channel_id=1, source_target_pairs={{4,0},{8,4},{12,8},{0,12},{5,1},{9,5},{13,9},{1,13},{6,2},{10,6},{... | collective-permute-start | bytes 786440 | tf_op jit(solution)/shard_map/ppermute | solution.py:264
  12.3 10.5 %collective-permute-start.1 = (bf16[1024,128]{1,0:T(8,128)(2,1)S(1)}, bf16[1024,128]{1,0:T(8,128)(2,1)S(1)}, u32[]{:S(2)}, u32[]{:S(2)}) collective-permute-start(bf16[1024,128]{1,0:T(8,128)(2,1)S(1)} %constant_dynamic-slice_fusion), channel_id=1, source_target_pairs={{8,0},{12,4},{0,8},{4,12},{9,1},{13,5},{1,9},{5,13},{10,2},{14,6},... | collective-permute-start | bytes 786440 | tf_op jit(solution)/shard_map/ppermute | solution.py:264
  12.8 14.9 %collective-permute-start.2 = (bf16[1024,128]{1,0:T(8,128)(2,1)S(1)}, bf16[1024,128]{1,0:T(8,128)(2,1)}, u32[]{:S(2)}, u32[]{:S(2)}) collective-permute-start(bf16[1024,128]{1,0:T(8,128)(2,1)S(1)} %constant_dynamic-slice_fusion), channel_id=1, source_target_pairs={{12,0},{0,4},{4,8},{8,12},{13,1},{1,5},{5,9},{9,13},{14,2},{2,6},{... | collective-permute-start | bytes 786440 | tf_op jit(solution)/shard_map/ppermute | solution.py:264
  15.7 2.2 copy-start.2
  17.9 0.9 copy-start.3
  22.8 0.7 copy-start.7
  23.5 0.7 copy-start.8
  31.8 14.3 %collective-permute-start.3 = (bf16[1024,512]{1,0:T(8,128)(2,1)S(1)}, bf16[1024,512]{1,0:T(8,128)(2,1)}, u32[]{:S(2)}, u32[]{:S(2)}) collective-permute-start(bf16[1024,512]{1,0:T(8,128)(2,1)S(1)} %constant_dynamic-update-slice_fusion), channel_id=1, source_target_pairs={{16,0},{0,16},{17,1},{1,17},{18,2},{2,18},{19,3},{3,19},{20,4},{4,... | collective-permute-start | bytes 3145736 | tf_op jit(solution)/shard_map/ppermute | solution.py:264
  46.2 6.4 %copy-start.10 = (bf16[2048]{0:T(1024)(128)(2,1)S(1)}, bf16[2048]{0:T(1024)(128)(2,1)}, u32[]{:S(2)}) copy-start(bf16[2048]{0:T(1024)(128)(2,1)} %param.28) | copy-start | bytes 12292
  46.2 6.4 %copy-start.11 = (bf16[2048]{0:T(1024)(128)(2,1)S(1)}, bf16[2048]{0:T(1024)(128)(2,1)}, u32[]{:S(2)}) copy-start(bf16[2048]{0:T(1024)(128)(2,1)} %param.29) | copy-start | bytes 12292
  47.8 10.3 %copy-start.9 = (bf16[48,2048]{1,0:T(8,128)(2,1)S(1)}, bf16[48,2048]{1,0:T(8,128)(2,1)}, u32[]{:S(2)}) copy-start(bf16[48,2048]{1,0:T(8,128)(2,1)} %param.16) | copy-start | bytes 589828
  48.9 10.4 %copy-start.21 = (s32[1,4]{1,0:T(1,128)S(1)}, s32[1,4]{1,0:T(1,128)}, u32[]{:S(2)}) copy-start(s32[1,4]{1,0:T(1,128)} %param.22) | copy-start | bytes 52
  48.9 8.8 %all-to-all-start = ((bf16[4,48,512]{2,1,0:T(8,128)(2,1)}), bf16[4,48,512]{2,1,0:T(8,128)(2,1)S(1)}, u32[]{:S(2)}, u32[]{:S(2)}) async-start(bf16[4,48,512]{2,1,0:T(8,128)(2,1)} %bitcast.2), calls=%async_computation | async-start | bytes 393216 | tf_op jit(solution)/shard_map/all_to_all | solution.py:272
  52.6 66.9 %all-gather.3.cloned.1.call-start = ((), (), s32[]{:S(2)}) async-start(), calls=%async_computation.7 | async-start | bytes 3342336 | tf_op jit(solution)/shard_map/all_gather | solution.py:371
  73.1 7.8 %copy-start.12 = (bf16[2048]{0:T(1024)(128)(2,1)S(1)}, bf16[2048]{0:T(1024)(128)(2,1)}, u32[]{:S(2)}) copy-start(bf16[2048]{0:T(1024)(128)(2,1)} %param.30) | copy-start | bytes 12292
  73.2 7.8 %copy-start.13 = (bf16[2048]{0:T(1024)(128)(2,1)S(1)}, bf16[2048]{0:T(1024)(128)(2,1)}, u32[]{:S(2)}) copy-start(bf16[2048]{0:T(1024)(128)(2,1)} %param.31) | copy-start | bytes 12292
  77.4 10.8 %all-to-all-start.2 = ((bf16[16,4,2048]{2,1,0:T(4,128)(2,1)}), bf16[16,4,2048]{2,1,0:T(4,128)(2,1)S(1)}, u32[]{:S(2)}, u32[]{:S(2)}) async-start(bf16[16,4,2048]{2,1,0:T(4,128)(2,1)} %reshape.103), calls=%async_computation.2 | async-start | bytes 524288 | tf_op jit(solution)/shard_map/all_to_all | solution.py:272
  89.7 12.8 %all-to-all-start.3 = ((bf16[16,4,2048]{2,1,0:T(4,128)(2,1)}), bf16[16,4,2048]{2,1,0:T(4,128)(2,1)S(1)}, u32[]{:S(2)}, u32[]{:S(2)}) async-start(bf16[16,4,2048]{2,1,0:T(4,128)(2,1)} %broadcast_in_dim.24), calls=%async_computation.3 | async-start | bytes 524288 | tf_op jit(solution)/shard_map/all_to_all | solution.py:272
  93.3 149.7 %reduce-scatter.2.cloned.1.call-start = ((), (), s32[]{:S(2)}) async-start(), calls=%async_computation.9 | async-start | bytes 3342336 | tf_op jit(solution)/shard_map/reduce_scatter | solution.py:388
  119.4 17.7 %copy-start.5 = (bf16[4,64,2048]{2,1,0:T(8,128)(2,1)}, bf16[4,64,2048]{2,1,0:T(8,128)(2,1)S(1)}, u32[]{:S(2)}) copy-start(bf16[4,64,2048]{2,1,0:T(8,128)(2,1)S(1)} %copy_bitcast_fusion.refs_0_) | copy-start | bytes 3145732
  134.3 30.5 %copy-start.16 = (s32[128,2]{0,1:T(2,128)S(1)}, s32[128,2]{0,1:T(2,128)}, u32[]{:S(2)}) copy-start(s32[128,2]{0,1:T(2,128)} %param.23) | copy-start | bytes 3076
  134.3 16.2 %collective-permute-start.5 = (bf16[4,64,2048]{2,1,0:T(8,128)(2,1)S(1)}, bf16[4,64,2048]{2,1,0:T(8,128)(2,1)S(1)}, u32[]{:S(2)}, u32[]{:S(2)}) collective-permute-start(bf16[4,64,2048]{2,1,0:T(8,128)(2,1)S(1)} %copy_bitcast_fusion.refs_0_), channel_id=1, source_target_pairs={{32,0},{64,32},{96,64},{0,96},{33,1},{65,33},{97,65},{1,97},{34,2}... | collective-permute-start | bytes 3145736 | tf_op jit(solution)/shard_map/ppermute | solution.py:264
  137.2 23.4 %collective-permute-start.6 = (bf16[4,64,2048]{2,1,0:T(8,128)(2,1)S(1)}, bf16[4,64,2048]{2,1,0:T(8,128)(2,1)}, u32[]{:S(2)}, u32[]{:S(2)}) collective-permute-start(bf16[4,64,2048]{2,1,0:T(8,128)(2,1)S(1)} %copy_bitcast_fusion.refs_0_), channel_id=1, source_target_pairs={{96,0},{0,32},{32,64},{64,96},{97,1},{1,33},{33,65},{65,97},{98,2}... | collective-permute-start | bytes 3145736 | tf_op jit(solution)/shard_map/ppermute | solution.py:264
  137.2 30.5 %collective-permute-start.4 = (bf16[4,64,2048]{2,1,0:T(8,128)(2,1)S(1)}, bf16[4,64,2048]{2,1,0:T(8,128)(2,1)}, u32[]{:S(2)}, u32[]{:S(2)}) collective-permute-start(bf16[4,64,2048]{2,1,0:T(8,128)(2,1)S(1)} %copy_bitcast_fusion.refs_0_), channel_id=1, source_target_pairs={{16,0},{0,16},{17,1},{1,17},{18,2},{2,18},{19,3},{3,19},{20,4},{4,... | collective-permute-start | bytes 3145736 | tf_op jit(solution)/shard_map/ppermute | solution.py:264
  150.6 29.4 %copy-start.6 = (bf16[4,64,2048]{2,1,0:T(8,128)(2,1)}, bf16[4,64,2048]{2,1,0:T(8,128)(2,1)S(1)}, u32[]{:S(2)}) copy-start(bf16[4,64,2048]{2,1,0:T(8,128)(2,1)S(1)} %collective-permute-done.5.refs_0_) | copy-start | bytes 3145732
  150.6 31.2 %collective-permute-start.7 = (bf16[4,64,2048]{2,1,0:T(8,128)(2,1)S(1)}, bf16[4,64,2048]{2,1,0:T(8,128)(2,1)}, u32[]{:S(2)}, u32[]{:S(2)}) collective-permute-start(bf16[4,64,2048]{2,1,0:T(8,128)(2,1)S(1)} %collective-permute-done.5.refs_0_), channel_id=1, source_target_pairs={{16,0},{0,16},{17,1},{1,17},{18,2},{2,18},{19,3},{3,19},{20,4},{4,... | collective-permute-start | bytes 3145736 | tf_op jit(solution)/shard_map/ppermute | solution.py:264
  160.5 21.2 %collective-permute-start.8 = (bf16[4,64,2048]{2,1,0:T(8,128)(2,1)}, bf16[4,64,2048]{2,1,0:T(8,128)(2,1)}, u32[]{:S(2)}, u32[]{:S(2)}) collective-permute-start(bf16[4,64,2048]{2,1,0:T(8,128)(2,1)} %collective-permute-done.6.refs_1_), channel_id=1, source_target_pairs={{16,0},{0,16},{17,1},{1,17},{18,2},{2,18},{19,3},{3,19},{20,4},{4,... | collective-permute-start | bytes 3145736 | tf_op jit(solution)/shard_map/ppermute | solution.py:264
  164.9 15.0 %collective-permute-start.9 = (bf16[2,64,2048]{2,1,0:T(8,128)(2,1)S(1)}, bf16[2,64,2048]{2,1,0:T(8,128)(2,1)S(1)}, u32[]{:S(2)}, u32[]{:S(2)}) collective-permute-start(bf16[2,64,2048]{2,1,0:T(8,128)(2,1)S(1)} %slice.108), channel_id=1, source_target_pairs={{32,0},{64,32},{96,64},{0,96},{33,1},{65,33},{97,65},{1,97},{34,2}... | collective-permute-start | bytes 1572872 | tf_op jit(solution)/shard_map/ppermute | solution.py:264
  166.1 14.4 %collective-permute-start.10 = (bf16[2,64,2048]{2,1,0:T(8,128)(2,1)S(1)}, bf16[2,64,2048]{2,1,0:T(8,128)(2,1)S(1)}, u32[]{:S(2)}, u32[]{:S(2)}) collective-permute-start(bf16[2,64,2048]{2,1,0:T(8,128)(2,1)S(1)} %slice.109), channel_id=1, source_target_pairs={{96,0},{0,32},{32,64},{64,96},{97,1},{1,33},{33,65},{65,97},{98,2}... | collective-permute-start | bytes 1572872 | tf_op jit(solution)/shard_map/ppermute | solution.py:264
  180.0 19.1 %copy-start.17 = (bf16[2,64,2048]{2,1,0:T(8,128)(2,1)}, bf16[2,64,2048]{2,1,0:T(8,128)(2,1)S(1)}, u32[]{:S(2)}) copy-start(bf16[2,64,2048]{2,1,0:T(8,128)(2,1)S(1)} %collective-permute-done.9.refs_0_) | copy-start | bytes 1572868
  180.0 19.1 %collective-permute-start.11 = (bf16[2,64,2048]{2,1,0:T(8,128)(2,1)S(1)}, bf16[2,64,2048]{2,1,0:T(8,128)(2,1)S(1)}, u32[]{:S(2)}, u32[]{:S(2)}) collective-permute-start(bf16[2,64,2048]{2,1,0:T(8,128)(2,1)S(1)} %collective-permute-done.9.refs_0_), channel_id=1, source_target_pairs={{16,0},{0,16},{17,1},{1,17},{18,2},{2,18},{19,3},{3,19},{20,4},{4,... | collective-permute-start | bytes 1572872 | tf_op jit(solution)/shard_map/ppermute | solution.py:264
  180.5 18.5 %copy-start.18 = (bf16[2,64,2048]{2,1,0:T(8,128)(2,1)}, bf16[2,64,2048]{2,1,0:T(8,128)(2,1)S(1)}, u32[]{:S(2)}) copy-start(bf16[2,64,2048]{2,1,0:T(8,128)(2,1)S(1)} %collective-permute-done.10.refs_1_) | copy-start | bytes 1572868
  180.6 18.5 %collective-permute-start.12 = (bf16[2,64,2048]{2,1,0:T(8,128)(2,1)S(1)}, bf16[2,64,2048]{2,1,0:T(8,128)(2,1)S(1)}, u32[]{:S(2)}, u32[]{:S(2)}) collective-permute-start(bf16[2,64,2048]{2,1,0:T(8,128)(2,1)S(1)} %collective-permute-done.10.refs_1_), channel_id=1, source_target_pairs={{16,0},{0,16},{17,1},{1,17},{18,2},{2,18},{19,3},{3,19},{20,4},{4,... | collective-permute-start | bytes 1572872 | tf_op jit(solution)/shard_map/ppermute | solution.py:264
  199.1 0.8 copy-start.19
  199.1 1.0 copy-start.20
  200.1 11.6 %copy-start.14 = (f32[4,256]{1,0:T(4,128)S(1)}, f32[4,256]{1,0:T(4,128)}, u32[]{:S(2)}) copy-start(f32[4,256]{1,0:T(4,128)} %get-tuple-element.34) | copy-start | bytes 12292
  200.1 11.6 %copy-start.15 = (f32[2,256]{1,0:T(2,128)S(1)}, f32[2,256]{1,0:T(2,128)}, u32[]{:S(2)}) copy-start(f32[2,256]{1,0:T(2,128)} %get-tuple-element.29) | copy-start | bytes 6148
  222.1 3.8 %collective-permute-start.15 = (f32[8,256]{1,0:T(8,128)S(1)}, f32[8,256]{1,0:T(8,128)S(1)}, u32[]{:S(2)}, u32[]{:S(2)}) collective-permute-start(f32[8,256]{1,0:T(8,128)S(1)} %reduce_sum.78), channel_id=1, source_target_pairs={{96,0},{0,32},{32,64},{64,96},{97,1},{1,33},{33,65},{65,97},{98,2}... | collective-permute-start | bytes 24584 | tf_op jit(solution)/shard_map/ppermute | solution.py:264
  222.5 4.0 %collective-permute-start.14 = (f32[8,256]{1,0:T(8,128)S(1)}, f32[8,256]{1,0:T(8,128)S(1)}, u32[]{:S(2)}, u32[]{:S(2)}) collective-permute-start(f32[8,256]{1,0:T(8,128)S(1)} %reduce_sum.78), channel_id=1, source_target_pairs={{64,0},{96,32},{0,64},{32,96},{65,1},{97,33},{1,65},{33,97},{66,2}... | collective-permute-start | bytes 24584 | tf_op jit(solution)/shard_map/ppermute | solution.py:264
  224.2 2.5 collective-permute-start.13
  226.7 4.0 %collective-permute-start.16 = (f32[8,256]{1,0:T(8,128)S(1)}, f32[8,256]{1,0:T(8,128)S(1)}, u32[]{:S(2)}, u32[]{:S(2)}) collective-permute-start(f32[8,256]{1,0:T(8,128)S(1)} %add_add_fusion), channel_id=1, source_target_pairs={{16,0},{0,16},{17,1},{1,17},{18,2},{2,18},{19,3},{3,19},{20,4},{4,... | collective-permute-start | bytes 24584 | tf_op jit(solution)/shard_map/ppermute | solution.py:264
  231.7 14.1 %copy-start.1 = (bf16[4,2048,128]{2,1,0:T(8,128)(2,1)S(1)}, bf16[4,2048,128]{2,1,0:T(8,128)(2,1)}, u32[]{:S(2)}) copy-start(bf16[4,2048,128]{2,1,0:T(8,128)(2,1)} %param.26) | copy-start | bytes 6291460
Sparse Core Ops, SparseCore 0:
  9.7 44.9 all-gather.4
  59.4 50.8 all-gather.2
  134.5 80.6 reduce-scatter.1

commit v5 on v4

--- a/solution.py
+++ b/solution.py
@@ -20,7 +20,7 @@
 XZ = ("x", "z")
 YC = ("y", "core")
 ALL = ("y", "core", "x", "z")
-GROUPS = ((0, 0), (0, 1), (1, 0), (3, 0), (1, 1), (3, 1), (2, 0), (2, 1))
+GROUPS = ((0, 0), (0, 1), (1, 0), (1, 1), (3, 0), (3, 1), (2, 0), (2, 1))
 CALLS = ((0, 2), (2, 6), (6, 8))
 TILE = 256
 VOCAB_BLOCK = 512
@@ -205,14 +205,19 @@
 def finish_kernel(place_ref, *refs):
     tables, logs_ref, out_ref = refs[: len(CALLS)], refs[-2], refs[-1]
     step = pl.program_id(0)
+    core = lax.rem(place_ref[1], CORE)
     for table_ref, (first, last) in zip(tables, CALLS):
 
-        @pl.when((step >= first) & (step < last))
+        @pl.when((step >= first // CORE) & (step < last // CORE))
         def _(table_ref=table_ref):
-            for head in range(HEADS):
-                values = table_ref[head].astype(F32)
-                shifted = values - logs_ref[:, head : head + 1]
-                out_ref[head] = jnp.where(values > 0.5 * HIDDEN, shifted, 0.0).astype(BF)
+            for position in range(CORE):
+                source = lax.rem(position + core, CORE)
+                for head in range(HEADS):
+                    values = table_ref[source, head].astype(F32)
+                    shifted = values - logs_ref[position, :, head : head + 1]
+                    out_ref[head, position] = jnp.where(
+                        values > 0.5 * HIDDEN, shifted, 0.0
+                    ).astype(BF)
 
 
 def finish(place, tables, logs):
@@ -222,19 +227,24 @@
 
     def table_spec(first, last):
         return spec(
-            (None, HEADS, count, vocab_width),
-            lambda k, p: (jnp.clip(k - first, 0, last - first - 1), 0, 0, 0),
+            (CORE, HEADS, count, vocab_width),
+            lambda k, p: (jnp.clip(k - first // CORE, 0, (last - first) // CORE - 1), 0, 0, 0),
         )
+
+    def pair(k, p):
+        return lax.div(p[1 + CORE * k], CORE)
 
     return pl.pallas_call(
         finish_kernel,
         out_shape=jax.ShapeDtypeStruct((HEADS, groups, count, vocab_width), BF),
         grid_spec=pltpu.PrefetchScalarGridSpec(
             num_scalar_prefetch=1,
-            grid=(groups,),
+            grid=(groups // CORE,),
             in_specs=[table_spec(*call) for call in CALLS]
-            + [spec((None, count, HEADS), lambda k, p: (p[1 + k], 0, 0))],
-            out_specs=spec((HEADS, None, count, vocab_width), lambda k, p: (0, p[1 + k], 0, 0)),
+            + [spec((CORE, count, HEADS), lambda k, p: (pair(k, p), 0, 0))],
+            out_specs=spec(
+                (HEADS, CORE, count, vocab_width), lambda k, p: (0, pair(k, p), 0, 0)
+            ),
         ),
         compiler_params=pltpu.CompilerParams(
             dimension_semantics=("arbitrary",), vmem_limit_bytes=56 << 20
@@ -384,8 +394,8 @@
     draft_copies = copies_of(drafts, units)
     drafts = jnp.transpose(swap(draft_copies, XZ), (1, 2, 0, 3)).reshape(HEADS, rows, -1)
 
-    mlp_partial = unit_terms(after(mlp_rows, drafts), weights)
-    mlp_sum = lax.psum_scatter(mlp_partial, XZ, scatter_dimension=0, tiled=True)
+    mlp_partial = unit_terms(after(mlp_rows, draft_copies), weights)
+    mlp_sum = lax.psum_scatter(after(mlp_partial, drafts), XZ, scatter_dimension=0, tiled=True)
 
     vocab_width = embedding.shape[0]
     start = lax.axis_index(ALL) * vocab_width
@@ -395,24 +405,26 @@
     half = HEADS // 2
     next_up, next_down = ring(drafts, "y", Y, 1), ring(drafts, "y", Y, 3)
     beside = ring(drafts, "core", CORE, 1)
+    table_a, totals_a = some_logits(
+        0, place, [drafts, beside], ((0, 0), (1, 0)), bounds, embedding
+    )
+    next_up, next_down = after([next_up, next_down], totals_a)
     across = [ring(next_up[:half], "y", Y, 1), ring(next_down[half:], "y", Y, 3)]
     beside_up, beside_down = ring(next_up, "core", CORE, 1), ring(next_down, "core", CORE, 1)
-    beside_across = [ring(piece, "core", CORE, 1) for piece in across]
-    table_a, totals_a = some_logits(
-        0, place, [drafts, beside], ((0, 0), (1, 0)), bounds, embedding
-    )
     table_b, totals_b = some_logits(
         1,
         place,
-        after([next_up, next_down, beside_up, beside_down], totals_a, mlp_partial),
+        [next_up, beside_up, next_down, beside_down],
         ((0, 0), (1, 0), (2, 0), (3, 0)),
         bounds,
         embedding,
     )
+    across = after(across, totals_b)
+    beside_across = [ring(piece, "core", CORE, 1) for piece in across]
     table_c, totals_c = some_logits(
         2,
         place,
-        after(across + beside_across, totals_b),
+        across + beside_across,
         ((0, 0), (0, half), (1, 0), (1, half)),
         bounds,
         embedding,

time: 254 us -> 245 us (0.965)
  waiting for transfers between devices: 32.5 us -> 45.8 us
  blocking collectives: 49.4 us -> 37.5 us
  starting transfers between devices: 51 us -> 39.4 us
  local copies, waits for them, and re-layouts: 18.2 us -> 20.9 us
    ppermute x17, starting transfers between devices: 40.2 us -> 24.1 us  [ring(): lax.ppermute(values, axis, [((i + shift) % size, i) for i in range(size)])]
    ppermute x17, waiting for transfers between devices: 10.2 us -> 22.2 us  [ring(): lax.ppermute(values, axis, [((i + shift) % size, i) for i in range(size)])]
    all_to_all x3 -> x2, blocking collectives: 35.6 us -> 23.7 us  [swap(): return lax.all_to_all(copies, axes, split_axis=0, concat_axis=0, tiled=True)]
    all_to_all x3 -> x4, starting transfers between devices: 10.7 us -> 15 us  [swap(): return lax.all_to_all(copies, axes, split_axis=0, concat_axis=0, tiled=True)]
    unnamed x49 -> x51, local copies, waits for them, and re-layouts: 9.64 us -> 11.2 us
    all_to_all x3 -> x4, waiting for transfers between devices: 21.5 us -> 21.6 us  [swap(): return lax.all_to_all(copies, axes, split_axis=0, concat_axis=0, tiled=True)]
  transfers between devices with their start and end apart: 23 -> 24, of which waited for: 9 -> 15; matrix products, arithmetic and copies ran while one was open for 10% -> 17% of each run, Pallas kernels for 22% -> 22%
where the time goes in v5:
time: 245 us; the launch traced here: 243 us
  Pallas kernels  54.4 us (22%)
  waiting for transfers between devices  45.8 us (19%)
  starting transfers between devices  39.4 us (16%)
  blocking collectives  37.5 us (15%)
  matrix products  25 us (10%)
  local copies, waits for them, and re-layouts  20.9 us (9%)
  between operations  14.9 us (6%)
  other arithmetic  5.49 us (2%)
    pallas_call x3, Pallas kernels, some_logits(): pl.pallas_call(functools.partial(logits_kernel, first, parts), out_shape=...  40.1 us
    ppermute x17, starting transfers between devices, ring(): lax.ppermute(values, axis, [((i + shift) % size, i) for i in range(size)])  24.1 us
    all_to_all x2, blocking collectives, swap(): return lax.all_to_all(copies, axes, split_axis=0, concat_axis=0, tiled=True)  23.7 us
    ppermute x17, waiting for transfers between devices, ring(): lax.ppermute(values, axis, [((i + shift) % size, i) for i in range(size)])  22.2 us
    all_to_all x4, waiting for transfers between devices, swap(): return lax.all_to_all(copies, axes, split_axis=0, concat_axis=0, tiled=True)  21.6 us
    all_to_all x4, starting transfers between devices, swap(): return lax.all_to_all(copies, axes, split_axis=0, concat_axis=0, tiled=True)  15 us
    all_gather x1, blocking collectives, out_projection(): group = lax.all_gather(attended, 'z', axis=0, tiled=True)  13.8 us
    dot_general x2, matrix products, unit_terms(): lax.dot_general(active, weights[2], (((1,), (1,)), ((), ())), preferred_e...  12.4 us
  transfers between devices with their start and end apart: 24, of which 15 were waited for; matrix products, arithmetic and copies ran while one was open for 17% of the time, Pallas kernels for 22%

profile of v5, /device:TPU:1, one launch (start us, length us, event | category | flops | bytes accessed | tf_op | source)
XLA Modules:
  0.0 243.3 jit_solution(16932202777641096265)
XLA Ops:
  7.2 0.7 all-gather.5.cloned.1.call-update
  7.9 1.0 constant_dynamic-slice_fusion
  8.9 3.4 %collective-permute-start = (bf16[1024,128]{1,0:T(8,128)(2,1)S(1)}, bf16[1024,128]{1,0:T(8,128)(2,1)S(1)}, u32[]{:S(2)}, u32[]{:S(2)}) collective-permute-start(bf16[1024,128]{1,0:T(8,128)(2,1)S(1)} %constant_dynamic-slice_fusion), channel_id=1, source_target_pairs={{4,0},{8,4},{12,8},{0,12},{5,1},{9,5},{13,9},{1,13},{6,2},{10,6},{... | collective-permute-start | bytes 786440 | tf_op jit(solution)/shard_map/ppermute | solution.py:274
  14.1 0.9 copy.38
  15.0 0.7 copy.31.parents_ref
  15.7 2.2 copy-done.2
  17.9 0.9 copy-done.3
  18.8 3.9 %shard_map.167 = bf16[48,2048]{1,0:T(8,128)(2,1)S(1)} custom-call(s32[1]{0:T(128)S(6)} %copy.42.length_ref, bf16[48,2048]{1,0:T(8,128)(2,1)S(1)} %copy-done.3, bf16[2,48,512]{2,1,0:T(8,128)(2,1)S(1)} %bitcast.94, s32[48,1]{1,0:T(8,128)S(1)} %copy.31.parents_ref, bf16[1,2,2,2048,256]{4,3,2,1,0:T(8,128)(2,1)S(1)} %copy-done.2, ...), custom_call_target="tpu_custom_call" | custom-call | flops 805306368 | bytes 4194304 | tf_op jit(solution)/shard_map/pallas_call | solution.py:78
  22.8 0.7 copy-done.7
  23.5 0.7 copy-done.8
  24.2 3.5 %collective-permute-done.2 = bf16[1024,128]{1,0:T(8,128)(2,1)} collective-permute-done((bf16[1024,128]{1,0:T(8,128)(2,1)S(1)}, bf16[1024,128]{1,0:T(8,128)(2,1)}, u32[]{:S(2)}, u32[]{:S(2)}) %collective-permute-start.2) | collective-permute-done | bytes 262176 | tf_op jit(solution)/shard_map/ppermute | solution.py:274
  27.7 1.0 constant_dynamic-update-slice_fusion.3
  28.7 1.0 constant_dynamic-update-slice_fusion.2
  29.8 1.1 constant_dynamic-update-slice_fusion.1
  30.8 1.0 constant_dynamic-update-slice_fusion
  32.4 13.8 %all_gather.9 = bf16[192,2048]{1,0:T(8,128)(2,1)S(1)} all-gather(bf16[48,2048]{1,0:T(8,128)(2,1)S(1)} %shard_map.167), channel_id=1, replica_groups=mesh['y'=4,'core'=2,'x'=4,'z'=4] {'z'}, dimensions={0}, use_global_device_ids=true | all-gather | bytes 983040 | tf_op jit(solution)/shard_map/all_gather | solution.py:315
  46.2 1.6 fusion.34
  47.8 1.1 fusion.17
  48.9 3.7 %all-to-all-start = ((bf16[4,48,512]{2,1,0:T(8,128)(2,1)}), bf16[4,48,512]{2,1,0:T(8,128)(2,1)S(1)}, u32[]{:S(2)}, u32[]{:S(2)}) async-start(bf16[4,48,512]{2,1,0:T(8,128)(2,1)} %bitcast.2), calls=%async_computation | async-start | bytes 393216 | tf_op jit(solution)/shard_map/all_to_all | solution.py:282
  52.6 5.1 %all-to-all-done = bf16[4,48,512]{2,1,0:T(8,128)(2,1)S(1)} async-done(((bf16[4,48,512]{2,1,0:T(8,128)(2,1)}), bf16[4,48,512]{2,1,0:T(8,128)(2,1)S(1)}, u32[]{:S(2)}, u32[]{:S(2)}) %all-to-all-start) | async-done | bytes 196640 | tf_op jit(solution)/shard_map/all_to_all | solution.py:282
  58.4 0.8 fusion.32
  59.3 1.1 convolution_convert_fusion.2
  60.5 10.2 %all_to_all.30 = bf16[16,4,2048]{2,1,0:T(4,128)(2,1)S(1)} all-to-all(bf16[16,4,2048]{2,1,0:T(4,128)(2,1)S(1)} %broadcast_in_dim.23), channel_id=1, replica_groups=mesh['y'=4,'core'=2,'x'=4,'z'=4] {'x','z'}, dimensions={0} | all-to-all | bytes 524288 | tf_op jit(solution)/shard_map/all_to_all | solution.py:282
  70.8 2.4 fusion.43
  73.2 3.4 %convolution_convert_fusion.1 = bf16[64,2048]{1,0:T(8,128)(2,1)S(1)} fusion(bf16[3,2048,512]{1,2,0:T(8,128)(2,1)} %all-gather.5.cloned.1.call-done, f32[64,512]{1,0:T(8,128)S(1)} %fusion.43, bf16[64,2048]{1,0:T(8,128)(2,1)S(1)} %reshape.102), kind=kOutput, calls=%fused_computation.2 | convolution fusion | flops 268632064 | bytes 4849664 | tf_op jit(solution)/shard_map/dot_general | solution.py:338
  76.6 0.8 reshape.103
  77.4 3.5 %all-to-all-start.2 = ((bf16[16,4,2048]{2,1,0:T(4,128)(2,1)}), bf16[16,4,2048]{2,1,0:T(4,128)(2,1)S(1)}, u32[]{:S(2)}, u32[]{:S(2)}) async-start(bf16[16,4,2048]{2,1,0:T(4,128)(2,1)} %reshape.103), calls=%async_computation.2 | async-start | bytes 524288 | tf_op jit(solution)/shard_map/all_to_all | solution.py:282
  81.0 7.2 %all-to-all-done.2 = bf16[16,4,2048]{2,1,0:T(4,128)(2,1)S(1)} async-done(((bf16[16,4,2048]{2,1,0:T(4,128)(2,1)}), bf16[16,4,2048]{2,1,0:T(4,128)(2,1)S(1)}, u32[]{:S(2)}, u32[]{:S(2)}) %all-to-all-start.2) | async-done | bytes 262176 | tf_op jit(solution)/shard_map/all_to_all | solution.py:282
  89.0 0.8 broadcast_in_dim.24
  89.8 3.5 %all-to-all-start.3 = ((bf16[16,4,2048]{2,1,0:T(4,128)(2,1)}), bf16[16,4,2048]{2,1,0:T(4,128)(2,1)S(1)}, u32[]{:S(2)}, u32[]{:S(2)}) async-start(bf16[16,4,2048]{2,1,0:T(4,128)(2,1)} %broadcast_in_dim.24), calls=%async_computation.3 | async-start | bytes 524288 | tf_op jit(solution)/shard_map/all_to_all | solution.py:282
  93.3 9.2 %all-to-all-done.3 = bf16[16,4,2048]{2,1,0:T(4,128)(2,1)S(1)} async-done(((bf16[16,4,2048]{2,1,0:T(4,128)(2,1)}), bf16[16,4,2048]{2,1,0:T(4,128)(2,1)S(1)}, u32[]{:S(2)}, u32[]{:S(2)}) %all-to-all-start.3) | async-done | bytes 262176 | tf_op jit(solution)/shard_map/all_to_all | solution.py:282
  103.2 1.2 broadcast_in_dim.25
  104.5 4.3 %all-to-all-start.4 = ((bf16[16,4,64,128]{3,2,1,0:T(8,128)(2,1)}), bf16[16,4,64,128]{3,2,1,0:T(8,128)(2,1)S(1)}, u32[]{:S(2)}, u32[]{:S(2)}) async-start(bf16[16,4,64,128]{3,2,1,0:T(8,128)(2,1)} %broadcast_in_dim.25), calls=%async_computation.4 | async-start | bytes 2097152 | tf_op jit(solution)/shard_map/all_to_all | solution.py:282
  109.0 1.3 all-gather.3.cloned.1.call-done
  110.2 5.5 %fusion.4 = f32[768,512]{1,0:T(8,128)} fusion(bf16[768,2048]{1,0:T(8,128)(2,1)} %all-gather.3.cloned.1.call-done, bf16[3,2048,512]{1,2,0:T(8,128)(2,1)} %all-gather.5.cloned.1.call-done), kind=kOutput, calls=%fused_computation.12 | convolution fusion | flops 1610612736 | bytes 6815744 | tf_op jit(solution)/shard_map/dot_general | solution.py:335
  115.8 9.0 %convolution_convert_fusion = bf16[768,2048]{1,0:T(8,128)(2,1)} fusion(bf16[3,2048,512]{1,2,0:T(8,128)(2,1)} %all-gather.5.cloned.1.call-done, f32[768,512]{1,0:T(8,128)} %fusion.4, bf16[768,2048]{1,0:T(8,128)(2,1)} %all-gather.3.cloned.1.call-done), kind=kOutput, calls=%fused_computation | convolution fusion | flops 3226730496 | bytes 12058624 | tf_op jit(solution)/shard_map/dot_general | solution.py:338
  125.0 6.7 %collective-permute-start.4 = (bf16[4,64,2048]{2,1,0:T(8,128)(2,1)S(1)}, bf16[4,64,2048]{2,1,0:T(8,128)(2,1)}, u32[]{:S(2)}, u32[]{:S(2)}) collective-permute-start(bf16[4,64,2048]{2,1,0:T(8,128)(2,1)S(1)} %copy_bitcast_fusion.refs_0_), channel_id=1, source_target_pairs={{16,0},{0,16},{17,1},{1,17},{18,2},{2,18},{19,3},{3,19},{20,4},{4,... | collective-permute-start | bytes 3145736 | tf_op jit(solution)/shard_map/ppermute | solution.py:274
  131.6 2.8 %collective-permute-start.5 = (bf16[4,64,2048]{2,1,0:T(8,128)(2,1)S(1)}, bf16[4,64,2048]{2,1,0:T(8,128)(2,1)S(1)}, u32[]{:S(2)}, u32[]{:S(2)}) collective-permute-start(bf16[4,64,2048]{2,1,0:T(8,128)(2,1)S(1)} %copy_bitcast_fusion.refs_0_), channel_id=1, source_target_pairs={{32,0},{64,32},{96,64},{0,96},{33,1},{65,33},{97,65},{1,97},{34,2}... | collective-permute-start | bytes 3145736 | tf_op jit(solution)/shard_map/ppermute | solution.py:274
  135.2 0.7 broadcast_in_dim.27
  136.0 11.4 %shard_map.168 = (bf16[2,4,64,2048]{3,2,1,0:T(8,128)(2,1)}, f32[2,256]{1,0:T(2,128)}) custom-call(s32[9]{0:T(128)} %stack.42.place_ref, bf16[4,64,2048]{2,1,0:T(8,128)(2,1)} %copy-done.5, bf16[4,64,2048]{2,1,0:T(8,128)(2,1)} %collective-permute-done.4.refs_1_, s32[8,64,2]{2,1,0:T(8,128)} %bitcast.97, bf16[2048,2048]{1,0:T(8,128)(2,1)} %refs_5_.3), custom_call_target="tpu_custom_call" | custom-call | flops 4294967296 | bytes 10485760 | tf_op jit(solution)/shard_map/pallas_call | solution.py:170
  147.3 9.6 %collective-permute-done.5.refs_0_ = bf16[4,64,2048]{2,1,0:T(8,128)(2,1)S(1)} collective-permute-done((bf16[4,64,2048]{2,1,0:T(8,128)(2,1)S(1)}, bf16[4,64,2048]{2,1,0:T(8,128)(2,1)S(1)}, u32[]{:S(2)}, u32[]{:S(2)}) %collective-permute-start.5) | collective-permute-done | bytes 1048608 | tf_op jit(solution)/shard_map/ppermute | solution.py:274
  156.9 3.2 %collective-permute-done.6.refs_2_ = bf16[4,64,2048]{2,1,0:T(8,128)(2,1)} collective-permute-done((bf16[4,64,2048]{2,1,0:T(8,128)(2,1)S(1)}, bf16[4,64,2048]{2,1,0:T(8,128)(2,1)}, u32[]{:S(2)}, u32[]{:S(2)}) %collective-permute-start.6) | collective-permute-done | bytes 1048608 | tf_op jit(solution)/shard_map/ppermute | solution.py:274
  160.1 1.2 collective-permute-start.7
  161.4 1.1 slice.88
  162.5 1.5 collective-permute-start.10
  164.0 1.1 collective-permute-done.7.refs_1_
  165.3 0.7 copy-done.17
  166.1 1.0 copy-done.18
  167.1 17.3 %shard_map.169 = (bf16[4,4,64,2048]{3,2,1,0:T(8,128)(2,1)}, f32[4,256]{1,0:T(4,128)}) custom-call(s32[9]{0:T(128)} %stack.42.place_ref, bf16[4,64,2048]{2,1,0:T(8,128)(2,1)} %copy-done.6, bf16[4,64,2048]{2,1,0:T(8,128)(2,1)} %copy-done.17, bf16[4,64,2048]{2,1,0:T(8,128)(2,1)} %collective-permute-done.6.refs_2_, bf16[4,64,2048]{2,1,0:T(8,128)(2,1)} %copy-done.18, ...), custom_call_target="tpu_custom_call" | custom-call | flops 8589934592 | bytes 12582912 | tf_op jit(solution)/shard_map/pallas_call | solution.py:170
  185.3 1.1 collective-permute-done.11.refs_2_
  186.4 1.0 collective-permute-done.12.refs_3_
  187.4 0.8 copy-done.21
  188.2 11.4 %shard_map.170 = (bf16[2,4,64,2048]{3,2,1,0:T(8,128)(2,1)}, f32[2,256]{1,0:T(2,128)}) custom-call(s32[9]{0:T(128)} %stack.42.place_ref, bf16[2,64,2048]{2,1,0:T(8,128)(2,1)} %copy-done.19, bf16[2,64,2048]{2,1,0:T(8,128)(2,1)} %collective-permute-done.10.refs_1_, bf16[2,64,2048]{2,1,0:T(8,128)(2,1)} %copy-done.20, bf16[2,64,2048]{2,1,0:T(8,128)(2,1)} %copy-done.21, ...), custom_call_target="tpu_custom_call" | custom-call | flops 4294967296 | bytes 10485760 | tf_op jit(solution)/shard_map/pallas_call | solution.py:170
  199.6 0.7 pad_maximum_fusion.5
  200.4 13.5 %all_to_all.31 = f32[16,8,256]{2,1,0:T(8,128)S(1)} all-to-all(f32[16,8,256]{2,1,0:T(8,128)S(1)} %broadcast_in_dim.30), channel_id=1, replica_groups=mesh['y'=4,'core'=2,'x'=4,'z'=4] {'x','z'}, dimensions={0} | all-to-all | bytes 262144 | tf_op jit(solution)/shard_map/all_to_all | solution.py:282
  214.0 1.8 collective-permute-start.14
  215.8 0.9 collective-permute-start.13
  216.7 1.0 collective-permute-done.15
  218.4 3.4 %collective-permute-start.16 = (f32[8,256]{1,0:T(8,128)S(1)}, f32[8,256]{1,0:T(8,128)S(1)}, u32[]{:S(2)}, u32[]{:S(2)}) collective-permute-start(f32[8,256]{1,0:T(8,128)S(1)} %add_add_fusion), channel_id=1, source_target_pairs={{16,0},{0,16},{17,1},{1,17},{18,2},{2,18},{19,3},{3,19},{20,4},{4,... | collective-permute-start | bytes 24584 | tf_op jit(solution)/shard_map/ppermute | solution.py:274
  221.8 0.8 collective-permute-done.16
  222.7 0.9 copy.34
  223.6 10.4 %shard_map.171 = bf16[4,8,64,2048]{3,2,1,0:T(8,128)(2,1)} custom-call(s32[9]{0:T(128)} %stack.42.place_ref, bf16[2,4,64,2048]{3,2,1,0:T(8,128)(2,1)} %get-tuple-element.35.refs_0_, bf16[4,4,64,2048]{3,2,1,0:T(8,128)(2,1)} %get-tuple-element.36.refs_1_, bf16[2,4,64,2048]{3,2,1,0:T(8,128)(2,1)} %get-tuple-element.37.refs_2_, f32[8,64,4]{2,1,0:T(8,128)} %bitcast.96), custom_call_target="tpu_custom_call" | custom-call | flops 12582912 | bytes 16777216 | tf_op jit(solution)/shard_map/pallas_call | solution.py:237
  233.9 1.1 fusion.28
  235.0 1.8 fusion.33
  (103 shorter events, 7.4 us)
Async XLA Ops:
  7.2 95.5 %copy-start = (bf16[4,2048,128]{2,1,0:T(8,128)(2,1)S(1)}, bf16[4,2048,128]{2,1,0:T(8,128)(2,1)}, u32[]{:S(2)}) copy-start(bf16[4,2048,128]{2,1,0:T(8,128)(2,1)} %param.26) | copy-start | bytes 6291460
  7.2 63.6 %all-gather.5.cloned.1.call-start = ((), (), s32[]{:S(2)}) async-start(), calls=%async_computation.8 | async-start | bytes 7077888 | tf_op jit(solution)/shard_map/all_gather | solution.py:366
  8.9 13.9 %copy-start.4 = (bf16[1024,128]{1,0:T(8,128)(2,1)}, bf16[1024,128]{1,0:T(8,128)(2,1)S(1)}, u32[]{:S(2)}) copy-start(bf16[1024,128]{1,0:T(8,128)(2,1)S(1)} %constant_dynamic-slice_fusion) | copy-start | bytes 786436
  8.9 13.9 %collective-permute-start = (bf16[1024,128]{1,0:T(8,128)(2,1)S(1)}, bf16[1024,128]{1,0:T(8,128)(2,1)S(1)}, u32[]{:S(2)}, u32[]{:S(2)}) collective-permute-start(bf16[1024,128]{1,0:T(8,128)(2,1)S(1)} %constant_dynamic-slice_fusion), channel_id=1, source_target_pairs={{4,0},{8,4},{12,8},{0,12},{5,1},{9,5},{13,9},{1,13},{6,2},{10,6},{... | collective-permute-start | bytes 786440 | tf_op jit(solution)/shard_map/ppermute | solution.py:274
  12.3 10.5 %collective-permute-start.1 = (bf16[1024,128]{1,0:T(8,128)(2,1)S(1)}, bf16[1024,128]{1,0:T(8,128)(2,1)S(1)}, u32[]{:S(2)}, u32[]{:S(2)}) collective-permute-start(bf16[1024,128]{1,0:T(8,128)(2,1)S(1)} %constant_dynamic-slice_fusion), channel_id=1, source_target_pairs={{8,0},{12,4},{0,8},{4,12},{9,1},{13,5},{1,9},{5,13},{10,2},{14,6},... | collective-permute-start | bytes 786440 | tf_op jit(solution)/shard_map/ppermute | solution.py:274
  12.8 14.9 %collective-permute-start.2 = (bf16[1024,128]{1,0:T(8,128)(2,1)S(1)}, bf16[1024,128]{1,0:T(8,128)(2,1)}, u32[]{:S(2)}, u32[]{:S(2)}) collective-permute-start(bf16[1024,128]{1,0:T(8,128)(2,1)S(1)} %constant_dynamic-slice_fusion), channel_id=1, source_target_pairs={{12,0},{0,4},{4,8},{8,12},{13,1},{1,5},{5,9},{9,13},{14,2},{2,6},{... | collective-permute-start | bytes 786440 | tf_op jit(solution)/shard_map/ppermute | solution.py:274
  15.7 2.2 copy-start.2
  17.9 0.9 copy-start.3
  22.8 0.7 copy-start.7
  23.5 0.7 copy-start.8
  31.8 14.3 %collective-permute-start.3 = (bf16[1024,512]{1,0:T(8,128)(2,1)S(1)}, bf16[1024,512]{1,0:T(8,128)(2,1)}, u32[]{:S(2)}, u32[]{:S(2)}) collective-permute-start(bf16[1024,512]{1,0:T(8,128)(2,1)S(1)} %constant_dynamic-update-slice_fusion), channel_id=1, source_target_pairs={{16,0},{0,16},{17,1},{1,17},{18,2},{2,18},{19,3},{3,19},{20,4},{4,... | collective-permute-start | bytes 3145736 | tf_op jit(solution)/shard_map/ppermute | solution.py:274
  46.2 6.4 %copy-start.10 = (bf16[2048]{0:T(1024)(128)(2,1)S(1)}, bf16[2048]{0:T(1024)(128)(2,1)}, u32[]{:S(2)}) copy-start(bf16[2048]{0:T(1024)(128)(2,1)} %param.28) | copy-start | bytes 12292
  46.2 6.4 %copy-start.11 = (bf16[2048]{0:T(1024)(128)(2,1)S(1)}, bf16[2048]{0:T(1024)(128)(2,1)}, u32[]{:S(2)}) copy-start(bf16[2048]{0:T(1024)(128)(2,1)} %param.29) | copy-start | bytes 12292
  47.8 10.3 %copy-start.9 = (bf16[48,2048]{1,0:T(8,128)(2,1)S(1)}, bf16[48,2048]{1,0:T(8,128)(2,1)}, u32[]{:S(2)}) copy-start(bf16[48,2048]{1,0:T(8,128)(2,1)} %param.16) | copy-start | bytes 589828
  48.9 10.4 %copy-start.22 = (s32[1,4]{1,0:T(1,128)S(1)}, s32[1,4]{1,0:T(1,128)}, u32[]{:S(2)}) copy-start(s32[1,4]{1,0:T(1,128)} %param.22) | copy-start | bytes 52
  48.9 8.8 %all-to-all-start = ((bf16[4,48,512]{2,1,0:T(8,128)(2,1)}), bf16[4,48,512]{2,1,0:T(8,128)(2,1)S(1)}, u32[]{:S(2)}, u32[]{:S(2)}) async-start(bf16[4,48,512]{2,1,0:T(8,128)(2,1)} %bitcast.2), calls=%async_computation | async-start | bytes 393216 | tf_op jit(solution)/shard_map/all_to_all | solution.py:282
  52.6 57.7 %all-gather.3.cloned.1.call-start = ((), (), s32[]{:S(2)}) async-start(), calls=%async_computation.7 | async-start | bytes 3342336 | tf_op jit(solution)/shard_map/all_gather | solution.py:381
  73.2 7.8 %copy-start.12 = (bf16[2048]{0:T(1024)(128)(2,1)S(1)}, bf16[2048]{0:T(1024)(128)(2,1)}, u32[]{:S(2)}) copy-start(bf16[2048]{0:T(1024)(128)(2,1)} %param.30) | copy-start | bytes 12292
  73.2 7.8 %copy-start.13 = (bf16[2048]{0:T(1024)(128)(2,1)S(1)}, bf16[2048]{0:T(1024)(128)(2,1)}, u32[]{:S(2)}) copy-start(bf16[2048]{0:T(1024)(128)(2,1)} %param.31) | copy-start | bytes 12292
  77.4 10.8 %all-to-all-start.2 = ((bf16[16,4,2048]{2,1,0:T(4,128)(2,1)}), bf16[16,4,2048]{2,1,0:T(4,128)(2,1)S(1)}, u32[]{:S(2)}, u32[]{:S(2)}) async-start(bf16[16,4,2048]{2,1,0:T(4,128)(2,1)} %reshape.103), calls=%async_computation.2 | async-start | bytes 524288 | tf_op jit(solution)/shard_map/all_to_all | solution.py:282
  89.8 12.8 %all-to-all-start.3 = ((bf16[16,4,2048]{2,1,0:T(4,128)(2,1)}), bf16[16,4,2048]{2,1,0:T(4,128)(2,1)S(1)}, u32[]{:S(2)}, u32[]{:S(2)}) async-start(bf16[16,4,2048]{2,1,0:T(4,128)(2,1)} %broadcast_in_dim.24), calls=%async_computation.3 | async-start | bytes 524288 | tf_op jit(solution)/shard_map/all_to_all | solution.py:282
  104.5 20.3 %all-to-all-start.4 = ((bf16[16,4,64,128]{3,2,1,0:T(8,128)(2,1)}), bf16[16,4,64,128]{3,2,1,0:T(8,128)(2,1)S(1)}, u32[]{:S(2)}, u32[]{:S(2)}) async-start(bf16[16,4,64,128]{3,2,1,0:T(8,128)(2,1)} %broadcast_in_dim.25), calls=%async_computation.4 | async-start | bytes 2097152 | tf_op jit(solution)/shard_map/all_to_all | solution.py:282
  108.8 125.2 %reduce-scatter.2.cloned.1.call-start = ((), (), s32[]{:S(2)}) async-start(), calls=%async_computation.9 | async-start | bytes 3342336 | tf_op jit(solution)/shard_map/reduce_scatter | solution.py:398
  124.9 11.0 %copy-start.5 = (bf16[4,64,2048]{2,1,0:T(8,128)(2,1)}, bf16[4,64,2048]{2,1,0:T(8,128)(2,1)S(1)}, u32[]{:S(2)}) copy-start(bf16[4,64,2048]{2,1,0:T(8,128)(2,1)S(1)} %copy_bitcast_fusion.refs_0_) | copy-start | bytes 3145732
  124.9 9.5 %copy-start.16 = (s32[128,2]{0,1:T(2,128)S(1)}, s32[128,2]{0,1:T(2,128)}, u32[]{:S(2)}) copy-start(s32[128,2]{0,1:T(2,128)} %param.23) | copy-start | bytes 3076
  125.0 10.2 %collective-permute-start.4 = (bf16[4,64,2048]{2,1,0:T(8,128)(2,1)S(1)}, bf16[4,64,2048]{2,1,0:T(8,128)(2,1)}, u32[]{:S(2)}, u32[]{:S(2)}) collective-permute-start(bf16[4,64,2048]{2,1,0:T(8,128)(2,1)S(1)} %copy_bitcast_fusion.refs_0_), channel_id=1, source_target_pairs={{16,0},{0,16},{17,1},{1,17},{18,2},{2,18},{19,3},{3,19},{20,4},{4,... | collective-permute-start | bytes 3145736 | tf_op jit(solution)/shard_map/ppermute | solution.py:274
  131.6 25.3 %collective-permute-start.5 = (bf16[4,64,2048]{2,1,0:T(8,128)(2,1)S(1)}, bf16[4,64,2048]{2,1,0:T(8,128)(2,1)S(1)}, u32[]{:S(2)}, u32[]{:S(2)}) collective-permute-start(bf16[4,64,2048]{2,1,0:T(8,128)(2,1)S(1)} %copy_bitcast_fusion.refs_0_), channel_id=1, source_target_pairs={{32,0},{64,32},{96,64},{0,96},{33,1},{65,33},{97,65},{1,97},{34,2}... | collective-permute-start | bytes 3145736 | tf_op jit(solution)/shard_map/ppermute | solution.py:274
  134.4 25.7 %collective-permute-start.6 = (bf16[4,64,2048]{2,1,0:T(8,128)(2,1)S(1)}, bf16[4,64,2048]{2,1,0:T(8,128)(2,1)}, u32[]{:S(2)}, u32[]{:S(2)}) collective-permute-start(bf16[4,64,2048]{2,1,0:T(8,128)(2,1)S(1)} %copy_bitcast_fusion.refs_0_), channel_id=1, source_target_pairs={{96,0},{0,32},{32,64},{64,96},{97,1},{1,33},{33,65},{65,97},{98,2}... | collective-permute-start | bytes 3145736 | tf_op jit(solution)/shard_map/ppermute | solution.py:274
  156.9 8.4 %copy-start.6 = (bf16[4,64,2048]{2,1,0:T(8,128)(2,1)}, bf16[4,64,2048]{2,1,0:T(8,128)(2,1)S(1)}, u32[]{:S(2)}) copy-start(bf16[4,64,2048]{2,1,0:T(8,128)(2,1)S(1)} %collective-permute-done.5.refs_0_) | copy-start | bytes 3145732
  160.1 4.9 %collective-permute-start.7 = (bf16[4,64,2048]{2,1,0:T(8,128)(2,1)S(1)}, bf16[4,64,2048]{2,1,0:T(8,128)(2,1)S(1)}, u32[]{:S(2)}, u32[]{:S(2)}) collective-permute-start(bf16[4,64,2048]{2,1,0:T(8,128)(2,1)S(1)} %collective-permute-done.5.refs_0_), channel_id=1, source_target_pairs={{16,0},{0,16},{17,1},{1,17},{18,2},{2,18},{19,3},{3,19},{20,4},{4,... | collective-permute-start | bytes 3145736 | tf_op jit(solution)/shard_map/ppermute | solution.py:274
  161.3 4.0 %collective-permute-start.8 = (bf16[4,64,2048]{2,1,0:T(8,128)(2,1)}, bf16[4,64,2048]{2,1,0:T(8,128)(2,1)S(1)}, u32[]{:S(2)}, u32[]{:S(2)}) collective-permute-start(bf16[4,64,2048]{2,1,0:T(8,128)(2,1)} %collective-permute-done.6.refs_2_), channel_id=1, source_target_pairs={{16,0},{0,16},{17,1},{1,17},{18,2},{2,18},{19,3},{3,19},{20,4},{4,... | collective-permute-start | bytes 3145736 | tf_op jit(solution)/shard_map/ppermute | solution.py:274
  162.5 21.9 %collective-permute-start.9 = (bf16[2,64,2048]{2,1,0:T(8,128)(2,1)S(1)}, bf16[2,64,2048]{2,1,0:T(8,128)(2,1)S(1)}, u32[]{:S(2)}, u32[]{:S(2)}) collective-permute-start(bf16[2,64,2048]{2,1,0:T(8,128)(2,1)S(1)} %slice.87), channel_id=1, source_target_pairs={{32,0},{64,32},{96,64},{0,96},{33,1},{65,33},{97,65},{1,97},{34,2}... | collective-permute-start | bytes 1572872 | tf_op jit(solution)/shard_map/ppermute | solution.py:274
  162.5 21.9 %collective-permute-start.10 = (bf16[2,64,2048]{2,1,0:T(8,128)(2,1)S(1)}, bf16[2,64,2048]{2,1,0:T(8,128)(2,1)}, u32[]{:S(2)}, u32[]{:S(2)}) collective-permute-start(bf16[2,64,2048]{2,1,0:T(8,128)(2,1)S(1)} %slice.88), channel_id=1, source_target_pairs={{96,0},{0,32},{32,64},{64,96},{97,1},{1,33},{33,65},{65,97},{98,2}... | collective-permute-start | bytes 1572872 | tf_op jit(solution)/shard_map/ppermute | solution.py:274
  165.1 1.0 copy-start.17
  166.1 1.0 copy-start.18
  184.4 3.0 %copy-start.19 = (bf16[2,64,2048]{2,1,0:T(8,128)(2,1)}, bf16[2,64,2048]{2,1,0:T(8,128)(2,1)S(1)}, u32[]{:S(2)}) copy-start(bf16[2,64,2048]{2,1,0:T(8,128)(2,1)S(1)} %collective-permute-done.9.refs_0_) | copy-start | bytes 1572868
  184.4 2.0 collective-permute-start.11
  184.9 2.5 %collective-permute-start.12 = (bf16[2,64,2048]{2,1,0:T(8,128)(2,1)}, bf16[2,64,2048]{2,1,0:T(8,128)(2,1)S(1)}, u32[]{:S(2)}, u32[]{:S(2)}) collective-permute-start(bf16[2,64,2048]{2,1,0:T(8,128)(2,1)} %collective-permute-done.10.refs_1_), channel_id=1, source_target_pairs={{16,0},{0,16},{17,1},{1,17},{18,2},{2,18},{19,3},{3,19},{20,4},{4,... | collective-permute-start | bytes 1572872 | tf_op jit(solution)/shard_map/ppermute | solution.py:274
  185.3 14.3 %copy-start.14 = (f32[4,256]{1,0:T(4,128)S(1)}, f32[4,256]{1,0:T(4,128)}, u32[]{:S(2)}) copy-start(f32[4,256]{1,0:T(4,128)} %get-tuple-element.30) | copy-start | bytes 12292
  185.3 14.3 %copy-start.15 = (f32[2,256]{1,0:T(2,128)S(1)}, f32[2,256]{1,0:T(2,128)}, u32[]{:S(2)}) copy-start(f32[2,256]{1,0:T(2,128)} %get-tuple-element.27) | copy-start | bytes 6148
  186.4 1.0 copy-start.20
  187.4 0.8 copy-start.21
  213.9 3.8 %collective-permute-start.15 = (f32[8,256]{1,0:T(8,128)S(1)}, f32[8,256]{1,0:T(8,128)S(1)}, u32[]{:S(2)}, u32[]{:S(2)}) collective-permute-start(f32[8,256]{1,0:T(8,128)S(1)} %reduce_sum.78), channel_id=1, source_target_pairs={{96,0},{0,32},{32,64},{64,96},{97,1},{1,33},{33,65},{65,97},{98,2}... | collective-permute-start | bytes 24584 | tf_op jit(solution)/shard_map/ppermute | solution.py:274
  214.0 4.1 %collective-permute-start.14 = (f32[8,256]{1,0:T(8,128)S(1)}, f32[8,256]{1,0:T(8,128)S(1)}, u32[]{:S(2)}, u32[]{:S(2)}) collective-permute-start(f32[8,256]{1,0:T(8,128)S(1)} %reduce_sum.78), channel_id=1, source_target_pairs={{64,0},{96,32},{0,64},{32,96},{65,1},{97,33},{1,65},{33,97},{66,2}... | collective-permute-start | bytes 24584 | tf_op jit(solution)/shard_map/ppermute | solution.py:274
  215.8 2.6 %collective-permute-start.13 = (f32[8,256]{1,0:T(8,128)S(1)}, f32[8,256]{1,0:T(8,128)S(1)}, u32[]{:S(2)}, u32[]{:S(2)}) collective-permute-start(f32[8,256]{1,0:T(8,128)S(1)} %reduce_sum.78), channel_id=1, source_target_pairs={{32,0},{64,32},{96,64},{0,96},{33,1},{65,33},{97,65},{1,97},{34,2}... | collective-permute-start | bytes 24584 | tf_op jit(solution)/shard_map/ppermute | solution.py:274
  218.4 4.2 %collective-permute-start.16 = (f32[8,256]{1,0:T(8,128)S(1)}, f32[8,256]{1,0:T(8,128)S(1)}, u32[]{:S(2)}, u32[]{:S(2)}) collective-permute-start(f32[8,256]{1,0:T(8,128)S(1)} %add_add_fusion), channel_id=1, source_target_pairs={{16,0},{0,16},{17,1},{1,17},{18,2},{2,18},{19,3},{3,19},{20,4},{4,... | collective-permute-start | bytes 24584 | tf_op jit(solution)/shard_map/ppermute | solution.py:274
  223.6 13.2 %copy-start.1 = (bf16[4,2048,128]{2,1,0:T(8,128)(2,1)S(1)}, bf16[4,2048,128]{2,1,0:T(8,128)(2,1)}, u32[]{:S(2)}) copy-start(bf16[4,2048,128]{2,1,0:T(8,128)(2,1)} %param.26) | copy-start | bytes 6291460
Sparse Core Ops, SparseCore 0:
  9.7 44.9 all-gather.4
  59.4 50.8 all-gather.2
  125.1 82.0 reduce-scatter.1

commit v6 on v5

--- a/solution.py
+++ b/solution.py
@@ -308,22 +308,27 @@
     return own, ring(own, "core", CORE, 1)
 
 
-def out_projection(attended, own_weight, other_weight):
-    rows, depth = attended.shape
-    half = depth // 2
+def along(values, axis, size):
+    blocks = [values] + [ring(values, axis, size, shift) for shift in range(1, size)]
+    return in_order(blocks, lax.axis_index(axis))
+
+
+def four_columns(group, own_weight, other_weight):
+    half = group.shape[1] // 2
     core = lax.axis_index("core")
-    group = lax.all_gather(attended, "z", axis=0, tiled=True)
     own_part = lax.dynamic_slice_in_dim(group, core * half, half, 1)
     other_part = lax.dynamic_slice_in_dim(group, (1 - core) * half, half, 1)
-    columns = (
+    return (
         jnp.dot(own_part, own_weight, preferred_element_type=F32)
         + jnp.dot(other_part, other_weight, preferred_element_type=F32)
     ).astype(BF)
-    width = columns.shape[1] // X
-    back = swap(columns.reshape(Z, rows, X * width), "z")
+
+
+def all_columns(by_z):
+    width = by_z[0].shape[1] // X
     by_x = in_order(
         [
-            jnp.concatenate([back[z, :, d * width : (d + 1) * width] for z in range(Z)], axis=1)
+            jnp.concatenate([b[:, d * width : (d + 1) * width] for b in by_z], axis=1)
             for d in range(X)
         ],
         lax.axis_index("x"),
@@ -373,17 +378,27 @@
 
     own_half = own_half_of(out_weight)
     pieces = [own_half] + [ring(own_half, "x", X, shift) for shift in range(1, X)]
-    attended = attention(after(tree_q, own_half), tree_kv, kv_cache, cache_lengths, tree_parents)
-    own_weight, other_weight = out_weights(after(pieces, attended))
-    projected = out_projection(attended, own_weight, other_weight)
-    first = (hidden.astype(F32) + rms_scale(projected, attn_post_gain)).astype(BF)
-    normed = rms_scale(first, ff_pre_gain).astype(BF)
-    mlp_rows = lax.all_gather(normed, XZ, axis=0, tiled=True)
-
-    path_rows = spread(pick(normed), XZ, units).reshape(rows, -1)
-    path_terms = swap(unit_terms(path_rows, weights).reshape(units, ACC, -1), XZ)
+    own_weight, other_weight = out_weights(pieces)
+    attended = attention(
+        after(tree_q, own_weight), tree_kv, kv_cache, cache_lengths, tree_parents
+    )
+
+    depth = attended.shape[1]
+    line = jnp.concatenate(
+        along(jnp.concatenate([pick(attended), pick(hidden)], axis=1), "z", Z), axis=0
+    )
+    line_columns = four_columns(line[:, :depth], own_weight, other_weight)
+    line_projected = all_columns(along(line_columns, "z", Z))
+    line_first = (
+        line[:, depth:].astype(F32) + rms_scale(line_projected, attn_post_gain)
+    ).astype(BF)
+    line_normed = rms_scale(line_first, ff_pre_gain).astype(BF)
+    path_rows = jnp.concatenate(along(line_normed, "x", X), axis=0)
+    path_partial = unit_terms(path_rows, weights)
+    path_terms = swap(path_partial.reshape(units, ACC, -1), XZ)
     path_sum = jnp.sum(path_terms.astype(F32), axis=0)
-    path = (pick(first).astype(F32) + rms_scale(path_sum, ff_post_gain)).astype(BF)
+    own_first = lax.dynamic_slice_in_dim(line_first, lax.axis_index("z") * ACC, ACC, 0)
+    path = (own_first.astype(F32) + rms_scale(path_sum, ff_post_gain)).astype(BF)
     path_normed = rms_scale(path, final_gain).astype(BF)
     group_path = spread(path_normed, XZ, units).reshape(rows, -1)
 
@@ -394,8 +409,21 @@
     draft_copies = copies_of(drafts, units)
     drafts = jnp.transpose(swap(draft_copies, XZ), (1, 2, 0, 3)).reshape(HEADS, rows, -1)
 
-    mlp_partial = unit_terms(after(mlp_rows, draft_copies), weights)
-    mlp_sum = lax.psum_scatter(after(mlp_partial, drafts), XZ, scatter_dimension=0, tiled=True)
+    bulk = after(attended, line)
+    group = [bulk] + [ring(bulk, "z", Z, shift) for shift in range(1, Z)]
+    group = jnp.concatenate(after(group, line_normed), axis=0)
+    columns = four_columns(group, own_weight, other_weight)
+    size = attended.shape[0]
+    back = [columns[:size]]
+    for shift in range(1, Z):
+        slot = Z - shift
+        back.append(ring(columns[slot * size : (slot + 1) * size], "z", Z, shift))
+    back = after(back, path_partial)
+    projected = all_columns(in_order(back, lax.axis_index("z")))
+    first = (hidden.astype(F32) + rms_scale(projected, attn_post_gain)).astype(BF)
+    normed = rms_scale(first, ff_pre_gain).astype(BF)
+    mlp_rows = lax.all_gather(normed, XZ, axis=0, tiled=True)
+    mlp_partial = unit_terms(after(mlp_rows, drafts), weights)
 
     vocab_width = embedding.shape[0]
     start = lax.axis_index(ALL) * vocab_width
@@ -408,7 +436,10 @@
     table_a, totals_a = some_logits(
         0, place, [drafts, beside], ((0, 0), (1, 0)), bounds, embedding
     )
-    next_up, next_down = after([next_up, next_down], totals_a)
+    next_up, next_down = after([next_up, next_down], totals_a, mlp_partial)
+    mlp_sum = lax.psum_scatter(
+        after(mlp_partial, next_up, next_down), XZ, scatter_dimension=0, tiled=True
+    )
     across = [ring(next_up[:half], "y", Y, 1), ring(next_down[half:], "y", Y, 3)]
     beside_up, beside_down = ring(next_up, "core", CORE, 1), ring(next_down, "core", CORE, 1)
     table_b, totals_b = some_logits(

time: 245 us -> 249 us (1.016)
  starting transfers between devices: 39.4 us -> 62.2 us
  waiting for transfers between devices: 45.8 us -> 34.8 us
  local copies, waits for them, and re-layouts: 20.9 us -> 15.7 us
  blocking collectives: 37.5 us -> 32.6 us
  other arithmetic: 5.49 us -> 9.09 us
    ppermute x17 -> x32, starting transfers between devices: 24.1 us -> 52.3 us  [ring(): lax.ppermute(values, axis, [((i + shift) % size, i) for i in range(size)])]
    all_gather x1 -> x0, blocking collectives: 13.8 us -> none  [out_projection(): group = lax.all_gather(attended, 'z', axis=0, tiled=True)]
    all_to_all x2, blocking collectives: 23.7 us -> 32.6 us  [swap(): return lax.all_to_all(copies, axes, split_axis=0, concat_axis=0, tiled=True)]
    all_to_all x4 -> x2, waiting for transfers between devices: 21.6 us -> 14.8 us  [swap(): return lax.all_to_all(copies, axes, split_axis=0, concat_axis=0, tiled=True)]
    all_to_all x4 -> x2, starting transfers between devices: 15 us -> 9.81 us  [swap(): return lax.all_to_all(copies, axes, split_axis=0, concat_axis=0, tiled=True)]
    unnamed x51, local copies, waits for them, and re-layouts: 11.2 us -> 8.05 us
    ppermute x17 -> x32, waiting for transfers between devices: 22.2 us -> 19.2 us  [ring(): lax.ppermute(values, axis, [((i + shift) % size, i) for i in range(size)])]
    dot_general x2 -> x1, matrix products: 7.91 us -> 5.51 us  [unit_terms(): gate_part = jnp.dot(mlp_rows, weights[0], preferred_element_type=F32)]
  transfers between devices with their start and end apart: 24 -> 37, of which waited for: 15 -> 11; matrix products, arithmetic and copies ran while one was open for 17% -> 15% of each run, Pallas kernels for 22% -> 22%
where the time goes in v6:
time: 249 us; the launch traced here: 247 us
  starting transfers between devices  62.2 us (25%)
  Pallas kernels  54.5 us (22%)
  waiting for transfers between devices  34.8 us (14%)
  blocking collectives  32.6 us (13%)
  matrix products  23.4 us (9%)
  local copies, waits for them, and re-layouts  15.7 us (6%)
  between operations  15.1 us (6%)
  other arithmetic  9.09 us (4%)
    ppermute x32, starting transfers between devices, ring(): lax.ppermute(values, axis, [((i + shift) % size, i) for i in range(size)])  52.3 us
    pallas_call x3, Pallas kernels, some_logits(): pl.pallas_call(functools.partial(logits_kernel, first, parts), out_shape=...  40.2 us
    all_to_all x2, blocking collectives, swap(): return lax.all_to_all(copies, axes, split_axis=0, concat_axis=0, tiled=True)  32.6 us
    ppermute x32, waiting for transfers between devices, ring(): lax.ppermute(values, axis, [((i + shift) % size, i) for i in range(size)])  19.2 us
    all_to_all x2, waiting for transfers between devices, swap(): return lax.all_to_all(copies, axes, split_axis=0, concat_axis=0, tiled=True)  14.8 us
    dot_general x2, matrix products, unit_terms(): lax.dot_general(active, weights[2], (((1,), (1,)), ((), ())), preferred_e...  12.4 us
    pallas_call x1, Pallas kernels, finish(): pl.pallas_call(finish_kernel, out_shape=jax.ShapeDtypeStruct((HEADS, grou...  10.4 us
    all_to_all x2, starting transfers between devices, swap(): return lax.all_to_all(copies, axes, split_axis=0, concat_axis=0, tiled=True)  9.81 us
  transfers between devices with their start and end apart: 37, of which 11 were waited for; matrix products, arithmetic and copies ran while one was open for 15% of the time, Pallas kernels for 22%

profile of v6, /device:TPU:1, one launch (start us, length us, event | category | flops | bytes accessed | tf_op | source)
XLA Modules:
  0.0 247.5 jit_solution(14880748947174910907)
XLA Ops:
  8.0 1.0 constant_dynamic-slice_fusion
  9.0 2.1 collective-permute-start.2
  11.1 2.5 collective-permute-start.1
  13.5 1.2 collective-permute-start
  15.3 0.9 copy.38
  16.2 0.7 copy.31.parents_ref
  17.0 1.1 convolution_convert_fusion.2
  18.1 6.7 %collective-permute-done.1 = bf16[1024,128]{1,0:T(8,128)(2,1)S(1)} collective-permute-done((bf16[1024,128]{1,0:T(8,128)(2,1)S(1)}, bf16[1024,128]{1,0:T(8,128)(2,1)S(1)}, u32[]{:S(2)}, u32[]{:S(2)}) %collective-permute-start.1) | collective-permute-done | bytes 262176 | tf_op jit(solution)/shard_map/ppermute | solution.py:274
  24.8 1.1 pad_maximum_fusion
  25.9 2.2 copy-done.2
  28.1 3.9 %shard_map.167 = bf16[48,2048]{1,0:T(8,128)(2,1)S(1)} custom-call(s32[1]{0:T(128)S(6)} %copy.42.length_ref, bf16[48,2048]{1,0:T(8,128)(2,1)S(1)} %copy-done.3, bf16[2,48,512]{2,1,0:T(8,128)(2,1)S(1)} %bitcast.61, s32[48,1]{1,0:T(8,128)S(1)} %copy.31.parents_ref, bf16[1,2,2,2048,256]{4,3,2,1,0:T(8,128)(2,1)S(1)} %copy-done.2, ...), custom_call_target="tpu_custom_call" | custom-call | flops 805306368 | bytes 4194304 | tf_op jit(solution)/shard_map/pallas_call | solution.py:78
  32.3 1.7 collective-permute-start.3
  34.0 3.3 %collective-permute-start.4 = (bf16[4,4096]{1,0:T(4,128)(2,1)S(1)}, bf16[4,4096]{1,0:T(4,128)(2,1)S(1)}, u32[]{:S(2)}, u32[]{:S(2)}) collective-permute-start(bf16[4,4096]{1,0:T(4,128)(2,1)S(1)} %pad_maximum_fusion.12), channel_id=1, source_target_pairs={{2,0},{3,1},{0,2},{1,3},{6,4},{7,5},{4,6},{5,7},{10,8},{11,9},{8,1... | collective-permute-start | bytes 98312 | tf_op jit(solution)/shard_map/ppermute | solution.py:274
  38.1 2.4 collective-permute-start.9
  41.1 1.9 collective-permute-done.9
  42.9 1.0 copy-done.5
  44.4 1.0 collective-permute-start.10
  45.4 2.4 collective-permute-start.12
  47.9 0.8 convert_element_type.104
  49.3 0.8 collective-permute-start.6
  50.1 0.8 collective-permute-start.7
  50.9 0.9 collective-permute-start.8
  52.4 1.1 collective-permute-start.16
  53.6 2.3 collective-permute-start.17
  55.8 1.2 collective-permute-start.18
  57.0 4.6 %collective-permute-done.8 = bf16[48,2048]{1,0:T(8,128)(2,1)S(1)} collective-permute-done((bf16[48,2048]{1,0:T(8,128)(2,1)S(1)}, bf16[48,2048]{1,0:T(8,128)(2,1)S(1)}, u32[]{:S(2)}, u32[]{:S(2)}) %collective-permute-start.8) | collective-permute-done | bytes 196640 | tf_op jit(solution)/shard_map/ppermute | solution.py:274
  62.6 1.2 collective-permute-start.14
  63.8 0.8 collective-permute-start.15
  64.7 2.4 fusion.3
  67.0 3.5 %convolution_convert_fusion.1 = bf16[64,2048]{1,0:T(8,128)(2,1)S(1)} fusion(bf16[3,2048,512]{1,2,0:T(8,128)(2,1)} %all-gather.3.cloned.1.call-done, f32[64,512]{1,0:T(8,128)S(1)} %fusion.3, bf16[16,2048]{1,0:T(8,128)(2,1)S(1)} %get-tuple-element.55, bf16[16,2048]{1,0:T(8,128)(2,1)S(1)} %get-tuple-element.56, bf16[16,2048]{1,0:T(8,128)(2,1)S(1)} %get-tuple-element.57, ...), kind=kOutput, calls=%fused_computation.2 | convolution fusion | flops 269942784 | bytes 4849664 | tf_op jit(solution)/shard_map/dot_general | solution.py:343
  71.7 0.8 fusion.27
  72.5 0.8 reshape.110
  73.3 6.2 %all-to-all-start = ((bf16[16,4,2048]{2,1,0:T(4,128)(2,1)}), bf16[16,4,2048]{2,1,0:T(4,128)(2,1)S(1)}, u32[]{:S(2)}, u32[]{:S(2)}) async-start(bf16[16,4,2048]{2,1,0:T(4,128)(2,1)} %reshape.110), calls=%async_computation | async-start | bytes 524288 | tf_op jit(solution)/shard_map/all_to_all | solution.py:282
  79.6 7.4 %all-to-all-done = bf16[16,4,2048]{2,1,0:T(4,128)(2,1)S(1)} async-done(((bf16[16,4,2048]{2,1,0:T(4,128)(2,1)}), bf16[16,4,2048]{2,1,0:T(4,128)(2,1)S(1)}, u32[]{:S(2)}, u32[]{:S(2)}) %all-to-all-start) | async-done | bytes 262176 | tf_op jit(solution)/shard_map/all_to_all | solution.py:282
  87.5 0.8 broadcast_in_dim.21
  88.4 3.6 %all-to-all-start.1 = ((bf16[16,4,2048]{2,1,0:T(4,128)(2,1)}), bf16[16,4,2048]{2,1,0:T(4,128)(2,1)S(1)}, u32[]{:S(2)}, u32[]{:S(2)}) async-start(bf16[16,4,2048]{2,1,0:T(4,128)(2,1)} %broadcast_in_dim.21), calls=%async_computation.1 | async-start | bytes 524288 | tf_op jit(solution)/shard_map/all_to_all | solution.py:282
  92.0 7.5 %all-to-all-done.1 = bf16[16,4,2048]{2,1,0:T(4,128)(2,1)S(1)} async-done(((bf16[16,4,2048]{2,1,0:T(4,128)(2,1)}), bf16[16,4,2048]{2,1,0:T(4,128)(2,1)S(1)}, u32[]{:S(2)}, u32[]{:S(2)}) %all-to-all-start.1) | async-done | bytes 262176 | tf_op jit(solution)/shard_map/all_to_all | solution.py:282
  100.4 21.6 %all_to_all.20 = bf16[16,4,64,128]{3,2,1,0:T(8,128)(2,1)S(1)} all-to-all(bf16[16,4,64,128]{3,2,1,0:T(8,128)(2,1)S(1)} %broadcast_in_dim.22), channel_id=1, replica_groups=mesh['y'=4,'core'=2,'x'=4,'z'=4] {'x','z'}, dimensions={0} | all-to-all | bytes 2097152 | tf_op jit(solution)/shard_map/all_to_all | solution.py:282
  122.1 10.9 %collective-permute-start.21 = (bf16[4,64,2048]{2,1,0:T(8,128)(2,1)S(1)}, bf16[4,64,2048]{2,1,0:T(8,128)(2,1)S(1)}, u32[]{:S(2)}, u32[]{:S(2)}) collective-permute-start(bf16[4,64,2048]{2,1,0:T(8,128)(2,1)S(1)} %copy_bitcast_fusion.refs_0_), channel_id=1, source_target_pairs={{16,0},{0,16},{17,1},{1,17},{18,2},{2,18},{19,3},{3,19},{20,4},{4,... | collective-permute-start | bytes 3145736 | tf_op jit(solution)/shard_map/ppermute | solution.py:274
  133.9 3.3 %collective-permute-start.19 = (bf16[4,64,2048]{2,1,0:T(8,128)(2,1)S(1)}, bf16[4,64,2048]{2,1,0:T(8,128)(2,1)S(1)}, u32[]{:S(2)}, u32[]{:S(2)}) collective-permute-start(bf16[4,64,2048]{2,1,0:T(8,128)(2,1)S(1)} %copy_bitcast_fusion.refs_0_), channel_id=1, source_target_pairs={{32,0},{64,32},{96,64},{0,96},{33,1},{65,33},{97,65},{1,97},{34,2}... | collective-permute-start | bytes 3145736 | tf_op jit(solution)/shard_map/ppermute | solution.py:274
  137.2 0.9 broadcast_in_dim.23
  138.3 11.3 %shard_map.168 = (bf16[2,4,64,2048]{3,2,1,0:T(8,128)(2,1)}, f32[2,256]{1,0:T(2,128)}) custom-call(s32[9]{0:T(128)} %stack.41.place_ref, bf16[4,64,2048]{2,1,0:T(8,128)(2,1)} %copy-done.7, bf16[4,64,2048]{2,1,0:T(8,128)(2,1)} %copy-done.15, s32[8,64,2]{2,1,0:T(8,128)} %bitcast.64, bf16[2048,2048]{1,0:T(8,128)(2,1)} %refs_5_.3), custom_call_target="tpu_custom_call" | custom-call | flops 4294967296 | bytes 10485760 | tf_op jit(solution)/shard_map/pallas_call | solution.py:170
  149.6 5.5 %fusion = f32[768,512]{1,0:T(8,128)} fusion(bf16[768,2048]{1,0:T(8,128)(2,1)} %all-gather.5.cloned.1.call-done, bf16[3,2048,512]{1,2,0:T(8,128)(2,1)} %all-gather.3.cloned.1.call-done), kind=kOutput, calls=%fused_computation.8 | convolution fusion | flops 1610612736 | bytes 6815744 | tf_op jit(solution)/shard_map/dot_general | solution.py:340
  155.1 9.0 %convolution_convert_fusion = bf16[768,2048]{1,0:T(8,128)(2,1)} fusion(bf16[3,2048,512]{1,2,0:T(8,128)(2,1)} %all-gather.3.cloned.1.call-done, f32[768,512]{1,0:T(8,128)} %fusion, bf16[768,2048]{1,0:T(8,128)(2,1)} %all-gather.5.cloned.1.call-done), kind=kOutput, calls=%fused_computation | convolution fusion | flops 3226730496 | bytes 12058624 | tf_op jit(solution)/shard_map/dot_general | solution.py:343
  165.1 1.1 slice.176
  166.2 2.7 %collective-permute-start.24 = (bf16[2,64,2048]{2,1,0:T(8,128)(2,1)S(1)}, bf16[2,64,2048]{2,1,0:T(8,128)(2,1)S(1)}, u32[]{:S(2)}, u32[]{:S(2)}) collective-permute-start(bf16[2,64,2048]{2,1,0:T(8,128)(2,1)S(1)} %slice.175), channel_id=1, source_target_pairs={{32,0},{64,32},{96,64},{0,96},{33,1},{65,33},{97,65},{1,97},{34,2}... | collective-permute-start | bytes 1572872 | tf_op jit(solution)/shard_map/ppermute | solution.py:274
  169.0 1.0 copy-done.16
  170.0 1.0 copy-done.17
  170.9 17.4 %shard_map.169 = (bf16[4,4,64,2048]{3,2,1,0:T(8,128)(2,1)}, f32[4,256]{1,0:T(4,128)}) custom-call(s32[9]{0:T(128)} %stack.41.place_ref, bf16[4,64,2048]{2,1,0:T(8,128)(2,1)} %copy-done.8, bf16[4,64,2048]{2,1,0:T(8,128)(2,1)} %copy-done.16, bf16[4,64,2048]{2,1,0:T(8,128)(2,1)} %collective-permute-done.20.refs_2_, bf16[4,64,2048]{2,1,0:T(8,128)(2,1)} %copy-done.17, ...), custom_call_target="tpu_custom_call" | custom-call | flops 8589934592 | bytes 12582912 | tf_op jit(solution)/shard_map/pallas_call | solution.py:170
  188.4 1.0 collective-permute-start.26
  189.6 1.3 collective-permute-done.26.refs_2_
  190.9 0.7 collective-permute-done.27.refs_3_
  191.7 0.8 copy-done.21
  192.5 11.5 %shard_map.170 = (bf16[2,4,64,2048]{3,2,1,0:T(8,128)(2,1)}, f32[2,256]{1,0:T(2,128)}) custom-call(s32[9]{0:T(128)} %stack.41.place_ref, bf16[2,64,2048]{2,1,0:T(8,128)(2,1)} %copy-done.18, bf16[2,64,2048]{2,1,0:T(8,128)(2,1)} %copy-done.19, bf16[2,64,2048]{2,1,0:T(8,128)(2,1)} %copy-done.20, bf16[2,64,2048]{2,1,0:T(8,128)(2,1)} %copy-done.21, ...), custom_call_target="tpu_custom_call" | custom-call | flops 4294967296 | bytes 10485760 | tf_op jit(solution)/shard_map/pallas_call | solution.py:170
  204.7 11.0 %all_to_all.21 = f32[16,8,256]{2,1,0:T(8,128)S(1)} all-to-all(f32[16,8,256]{2,1,0:T(8,128)S(1)} %broadcast_in_dim.27), channel_id=1, replica_groups=mesh['y'=4,'core'=2,'x'=4,'z'=4] {'x','z'}, dimensions={0} | all-to-all | bytes 262144 | tf_op jit(solution)/shard_map/all_to_all | solution.py:282
  215.9 4.1 %collective-permute-start.29 = (f32[8,256]{1,0:T(8,128)S(1)}, f32[8,256]{1,0:T(8,128)S(1)}, u32[]{:S(2)}, u32[]{:S(2)}) collective-permute-start(f32[8,256]{1,0:T(8,128)S(1)} %reduce_sum.98), channel_id=1, source_target_pairs={{64,0},{96,32},{0,64},{32,96},{65,1},{97,33},{1,65},{33,97},{66,2}... | collective-permute-start | bytes 24584 | tf_op jit(solution)/shard_map/ppermute | solution.py:274
  220.0 1.1 collective-permute-done.29
  221.1 1.7 collective-permute-done.28
  222.8 3.1 %collective-permute-start.31 = (f32[8,256]{1,0:T(8,128)S(1)}, f32[8,256]{1,0:T(8,128)S(1)}, u32[]{:S(2)}, u32[]{:S(2)}) collective-permute-start(f32[8,256]{1,0:T(8,128)S(1)} %add_add_fusion), channel_id=1, source_target_pairs={{16,0},{0,16},{17,1},{1,17},{18,2},{2,18},{19,3},{3,19},{20,4},{4,... | collective-permute-start | bytes 24584 | tf_op jit(solution)/shard_map/ppermute | solution.py:274
  225.9 0.8 collective-permute-done.31
  226.8 0.9 copy.34
  227.7 10.4 %shard_map.171 = bf16[4,8,64,2048]{3,2,1,0:T(8,128)(2,1)} custom-call(s32[9]{0:T(128)} %stack.41.place_ref, bf16[2,4,64,2048]{3,2,1,0:T(8,128)(2,1)} %get-tuple-element.45.refs_0_, bf16[4,4,64,2048]{3,2,1,0:T(8,128)(2,1)} %get-tuple-element.46.refs_1_, bf16[2,4,64,2048]{3,2,1,0:T(8,128)(2,1)} %get-tuple-element.47.refs_2_, f32[8,64,4]{2,1,0:T(8,128)} %bitcast.63), custom_call_target="tpu_custom_call" | custom-call | flops 12582912 | bytes 16777216 | tf_op jit(solution)/shard_map/pallas_call | solution.py:237
  238.1 1.1 fusion.23
  239.2 1.8 fusion.28
  (153 shorter events, 11.2 us)
Async XLA Ops:
  7.2 92.5 %copy-start = (bf16[4,2048,128]{2,1,0:T(8,128)(2,1)S(1)}, bf16[4,2048,128]{2,1,0:T(8,128)(2,1)}, u32[]{:S(2)}) copy-start(bf16[4,2048,128]{2,1,0:T(8,128)(2,1)} %param.26) | copy-start | bytes 6291460
  7.2 18.8 %copy-start.3 = (bf16[48,2048]{1,0:T(8,128)(2,1)S(1)}, bf16[48,2048]{1,0:T(8,128)(2,1)}, u32[]{:S(2)}) copy-start(bf16[48,2048]{1,0:T(8,128)(2,1)} %q_ref) | copy-start | bytes 589828
  7.2 57.5 %all-gather.3.cloned.1.call-start = ((), (), s32[]{:S(2)}) async-start(), calls=%async_computation.5 | async-start | bytes 7077888 | tf_op jit(solution)/shard_map/all_gather | solution.py:371
  7.9 141.7 %all-gather.5.cloned.1.call-start = ((), (), s32[]{:S(2)}) async-start(), calls=%async_computation.6 | async-start | bytes 3342336 | tf_op jit(solution)/shard_map/all_gather | solution.py:425
  9.0 9.2 %collective-permute-start.2 = (bf16[1024,128]{1,0:T(8,128)(2,1)S(1)}, bf16[1024,128]{1,0:T(8,128)(2,1)S(1)}, u32[]{:S(2)}, u32[]{:S(2)}) collective-permute-start(bf16[1024,128]{1,0:T(8,128)(2,1)S(1)} %constant_dynamic-slice_fusion), channel_id=1, source_target_pairs={{12,0},{0,4},{4,8},{8,12},{13,1},{1,5},{5,9},{9,13},{14,2},{2,6},{... | collective-permute-start | bytes 786440 | tf_op jit(solution)/shard_map/ppermute | solution.py:274
  11.1 13.8 %collective-permute-start.1 = (bf16[1024,128]{1,0:T(8,128)(2,1)S(1)}, bf16[1024,128]{1,0:T(8,128)(2,1)S(1)}, u32[]{:S(2)}, u32[]{:S(2)}) collective-permute-start(bf16[1024,128]{1,0:T(8,128)(2,1)S(1)} %constant_dynamic-slice_fusion), channel_id=1, source_target_pairs={{8,0},{12,4},{0,8},{4,12},{9,1},{13,5},{1,9},{5,13},{10,2},{14,6},... | collective-permute-start | bytes 786440 | tf_op jit(solution)/shard_map/ppermute | solution.py:274
  13.5 11.3 %collective-permute-start = (bf16[1024,128]{1,0:T(8,128)(2,1)S(1)}, bf16[1024,128]{1,0:T(8,128)(2,1)S(1)}, u32[]{:S(2)}, u32[]{:S(2)}) collective-permute-start(bf16[1024,128]{1,0:T(8,128)(2,1)S(1)} %constant_dynamic-slice_fusion), channel_id=1, source_target_pairs={{4,0},{8,4},{12,8},{0,12},{5,1},{9,5},{13,9},{1,13},{6,2},{10,6},{... | collective-permute-start | bytes 786440 | tf_op jit(solution)/shard_map/ppermute | solution.py:274
  25.9 2.2 copy-start.2
  28.1 4.0 %copy-start.22 = (s32[1,4]{1,0:T(1,128)S(1)}, s32[1,4]{1,0:T(1,128)}, u32[]{:S(2)}) copy-start(s32[1,4]{1,0:T(1,128)} %param.22) | copy-start | bytes 52
  32.1 12.1 %copy-start.4 = (bf16[1024,512]{1,0:T(8,128)(2,1)S(1)}, bf16[1024,512]{1,0:T(8,128)(2,1)}, u32[]{:S(2)}) copy-start(bf16[1024,512]{1,0:T(8,128)(2,1)} %pad_maximum_fusion) | copy-start | bytes 3145732
  32.3 8.1 %collective-permute-start.3 = (bf16[4,4096]{1,0:T(4,128)(2,1)S(1)}, bf16[4,4096]{1,0:T(4,128)(2,1)S(1)}, u32[]{:S(2)}, u32[]{:S(2)}) collective-permute-start(bf16[4,4096]{1,0:T(4,128)(2,1)S(1)} %pad_maximum_fusion.12), channel_id=1, source_target_pairs={{3,0},{0,1},{1,2},{2,3},{7,4},{4,5},{5,6},{6,7},{11,8},{8,9},{9,10... | collective-permute-start | bytes 98312 | tf_op jit(solution)/shard_map/ppermute | solution.py:274
  34.0 6.4 %collective-permute-start.4 = (bf16[4,4096]{1,0:T(4,128)(2,1)S(1)}, bf16[4,4096]{1,0:T(4,128)(2,1)S(1)}, u32[]{:S(2)}, u32[]{:S(2)}) collective-permute-start(bf16[4,4096]{1,0:T(4,128)(2,1)S(1)} %pad_maximum_fusion.12), channel_id=1, source_target_pairs={{2,0},{3,1},{0,2},{1,3},{6,4},{7,5},{4,6},{5,7},{10,8},{11,9},{8,1... | collective-permute-start | bytes 98312 | tf_op jit(solution)/shard_map/ppermute | solution.py:274
  37.3 3.5 %collective-permute-start.5 = (bf16[4,4096]{1,0:T(4,128)(2,1)S(1)}, bf16[4,4096]{1,0:T(4,128)(2,1)S(1)}, u32[]{:S(2)}, u32[]{:S(2)}) collective-permute-start(bf16[4,4096]{1,0:T(4,128)(2,1)S(1)} %pad_maximum_fusion.12), channel_id=1, source_target_pairs={{1,0},{2,1},{3,2},{0,3},{5,4},{6,5},{7,6},{4,7},{9,8},{10,9},{11,1... | collective-permute-start | bytes 98312 | tf_op jit(solution)/shard_map/ppermute | solution.py:274
  38.1 4.9 %collective-permute-start.9 = (bf16[1024,512]{1,0:T(8,128)(2,1)}, bf16[1024,512]{1,0:T(8,128)(2,1)S(1)}, u32[]{:S(2)}, u32[]{:S(2)}) collective-permute-start(bf16[1024,512]{1,0:T(8,128)(2,1)} %pad_maximum_fusion), channel_id=1, source_target_pairs={{16,0},{0,16},{17,1},{1,17},{18,2},{2,18},{19,3},{3,19},{20,4},{4,... | collective-permute-start | bytes 3145736 | tf_op jit(solution)/shard_map/ppermute | solution.py:274
  42.9 1.0 copy-start.5
  44.4 6.5 %collective-permute-start.10 = (bf16[16,512]{1,0:T(8,128)(2,1)S(1)}, bf16[16,512]{1,0:T(8,128)(2,1)S(1)}, u32[]{:S(2)}, u32[]{:S(2)}) collective-permute-start(bf16[16,512]{1,0:T(8,128)(2,1)S(1)} %fusion.14), channel_id=1, source_target_pairs={{3,0},{0,1},{1,2},{2,3},{7,4},{4,5},{5,6},{6,7},{11,8},{8,9},{9,10... | collective-permute-start | bytes 49160 | tf_op jit(solution)/shard_map/ppermute | solution.py:274
  45.4 6.4 %collective-permute-start.11 = (bf16[16,512]{1,0:T(8,128)(2,1)S(1)}, bf16[16,512]{1,0:T(8,128)(2,1)S(1)}, u32[]{:S(2)}, u32[]{:S(2)}) collective-permute-start(bf16[16,512]{1,0:T(8,128)(2,1)S(1)} %fusion.14), channel_id=1, source_target_pairs={{2,0},{3,1},{0,2},{1,3},{6,4},{7,5},{4,6},{5,7},{10,8},{11,9},{8,1... | collective-permute-start | bytes 49160 | tf_op jit(solution)/shard_map/ppermute | solution.py:274
  45.4 6.4 %collective-permute-start.12 = (bf16[16,512]{1,0:T(8,128)(2,1)S(1)}, bf16[16,512]{1,0:T(8,128)(2,1)S(1)}, u32[]{:S(2)}, u32[]{:S(2)}) collective-permute-start(bf16[16,512]{1,0:T(8,128)(2,1)S(1)} %fusion.14), channel_id=1, source_target_pairs={{1,0},{2,1},{3,2},{0,3},{5,4},{6,5},{7,6},{4,7},{9,8},{10,9},{11,1... | collective-permute-start | bytes 49160 | tf_op jit(solution)/shard_map/ppermute | solution.py:274
  47.9 13.8 %copy-start.6 = (bf16[1024,512]{1,0:T(8,128)(2,1)S(1)}, bf16[1024,512]{1,0:T(8,128)(2,1)}, u32[]{:S(2)}) copy-start(bf16[1024,512]{1,0:T(8,128)(2,1)} %copy-done.5) | copy-start | bytes 3145732
  49.3 6.5 %collective-permute-start.6 = (bf16[48,2048]{1,0:T(8,128)(2,1)S(1)}, bf16[48,2048]{1,0:T(8,128)(2,1)S(1)}, u32[]{:S(2)}, u32[]{:S(2)}) collective-permute-start(bf16[48,2048]{1,0:T(8,128)(2,1)S(1)} %shard_map.167), channel_id=1, source_target_pairs={{1,0},{2,1},{3,2},{0,3},{5,4},{6,5},{7,6},{4,7},{9,8},{10,9},{11,1... | collective-permute-start | bytes 589832 | tf_op jit(solution)/shard_map/ppermute | solution.py:274
  50.1 6.9 %collective-permute-start.7 = (bf16[48,2048]{1,0:T(8,128)(2,1)S(1)}, bf16[48,2048]{1,0:T(8,128)(2,1)S(1)}, u32[]{:S(2)}, u32[]{:S(2)}) collective-permute-start(bf16[48,2048]{1,0:T(8,128)(2,1)S(1)} %shard_map.167), channel_id=1, source_target_pairs={{2,0},{3,1},{0,2},{1,3},{6,4},{7,5},{4,6},{5,7},{10,8},{11,9},{8,1... | collective-permute-start | bytes 589832 | tf_op jit(solution)/shard_map/ppermute | solution.py:274
  50.9 10.7 %collective-permute-start.8 = (bf16[48,2048]{1,0:T(8,128)(2,1)S(1)}, bf16[48,2048]{1,0:T(8,128)(2,1)S(1)}, u32[]{:S(2)}, u32[]{:S(2)}) collective-permute-start(bf16[48,2048]{1,0:T(8,128)(2,1)S(1)} %shard_map.167), channel_id=1, source_target_pairs={{3,0},{0,1},{1,2},{2,3},{7,4},{4,5},{5,6},{6,7},{11,8},{8,9},{9,10... | collective-permute-start | bytes 589832 | tf_op jit(solution)/shard_map/ppermute | solution.py:274
  52.4 11.3 %collective-permute-start.16 = (bf16[16,2048]{1,0:T(8,128)(2,1)S(1)}, bf16[16,2048]{1,0:T(8,128)(2,1)S(1)}, u32[]{:S(2)}, u32[]{:S(2)}) collective-permute-start(bf16[16,2048]{1,0:T(8,128)(2,1)S(1)} %fusion.38), channel_id=1, source_target_pairs={{12,0},{0,4},{4,8},{8,12},{13,1},{1,5},{5,9},{9,13},{14,2},{2,6},{... | collective-permute-start | bytes 196616 | tf_op jit(solution)/shard_map/ppermute | solution.py:274
  53.6 11.0 %collective-permute-start.17 = (bf16[16,2048]{1,0:T(8,128)(2,1)S(1)}, bf16[16,2048]{1,0:T(8,128)(2,1)S(1)}, u32[]{:S(2)}, u32[]{:S(2)}) collective-permute-start(bf16[16,2048]{1,0:T(8,128)(2,1)S(1)} %fusion.38), channel_id=1, source_target_pairs={{8,0},{12,4},{0,8},{4,12},{9,1},{13,5},{1,9},{5,13},{10,2},{14,6},... | collective-permute-start | bytes 196616 | tf_op jit(solution)/shard_map/ppermute | solution.py:274
  55.8 8.7 %collective-permute-start.18 = (bf16[16,2048]{1,0:T(8,128)(2,1)S(1)}, bf16[16,2048]{1,0:T(8,128)(2,1)S(1)}, u32[]{:S(2)}, u32[]{:S(2)}) collective-permute-start(bf16[16,2048]{1,0:T(8,128)(2,1)S(1)} %fusion.38), channel_id=1, source_target_pairs={{4,0},{8,4},{12,8},{0,12},{5,1},{9,5},{13,9},{1,13},{6,2},{10,6},{... | collective-permute-start | bytes 196616 | tf_op jit(solution)/shard_map/ppermute | solution.py:274
  62.5 8.0 %collective-permute-start.13 = (bf16[48,512]{1,0:T(8,128)(2,1)S(1)}, bf16[48,512]{1,0:T(8,128)(2,1)S(1)}, u32[]{:S(2)}, u32[]{:S(2)}) collective-permute-start(bf16[48,512]{1,0:T(8,128)(2,1)S(1)} %get-tuple-element.64), channel_id=1, source_target_pairs={{1,0},{2,1},{3,2},{0,3},{5,4},{6,5},{7,6},{4,7},{9,8},{10,9},{11,1... | collective-permute-start | bytes 147464 | tf_op jit(solution)/shard_map/ppermute | solution.py:274
  62.6 7.9 %collective-permute-start.14 = (bf16[48,512]{1,0:T(8,128)(2,1)S(1)}, bf16[48,512]{1,0:T(8,128)(2,1)S(1)}, u32[]{:S(2)}, u32[]{:S(2)}) collective-permute-start(bf16[48,512]{1,0:T(8,128)(2,1)S(1)} %get-tuple-element.63), channel_id=1, source_target_pairs={{2,0},{3,1},{0,2},{1,3},{6,4},{7,5},{4,6},{5,7},{10,8},{11,9},{8,1... | collective-permute-start | bytes 147464 | tf_op jit(solution)/shard_map/ppermute | solution.py:274
  63.8 6.8 %collective-permute-start.15 = (bf16[48,512]{1,0:T(8,128)(2,1)S(1)}, bf16[48,512]{1,0:T(8,128)(2,1)S(1)}, u32[]{:S(2)}, u32[]{:S(2)}) collective-permute-start(bf16[48,512]{1,0:T(8,128)(2,1)S(1)} %get-tuple-element.62), channel_id=1, source_target_pairs={{3,0},{0,1},{1,2},{2,3},{7,4},{4,5},{5,6},{6,7},{11,8},{8,9},{9,10... | collective-permute-start | bytes 147464 | tf_op jit(solution)/shard_map/ppermute | solution.py:274
  70.5 0.9 copy-start.9
  70.5 9.0 %copy-start.10 = (bf16[2048]{0:T(1024)(128)(2,1)S(1)}, bf16[2048]{0:T(1024)(128)(2,1)}, u32[]{:S(2)}) copy-start(bf16[2048]{0:T(1024)(128)(2,1)} %param.30) | copy-start | bytes 12292
  70.5 9.1 %copy-start.11 = (bf16[2048]{0:T(1024)(128)(2,1)S(1)}, bf16[2048]{0:T(1024)(128)(2,1)}, u32[]{:S(2)}) copy-start(bf16[2048]{0:T(1024)(128)(2,1)} %param.31) | copy-start | bytes 12292
  73.3 13.7 %all-to-all-start = ((bf16[16,4,2048]{2,1,0:T(4,128)(2,1)}), bf16[16,4,2048]{2,1,0:T(4,128)(2,1)S(1)}, u32[]{:S(2)}, u32[]{:S(2)}) async-start(bf16[16,4,2048]{2,1,0:T(4,128)(2,1)} %reshape.110), calls=%async_computation | async-start | bytes 524288 | tf_op jit(solution)/shard_map/all_to_all | solution.py:282
  88.4 11.1 %all-to-all-start.1 = ((bf16[16,4,2048]{2,1,0:T(4,128)(2,1)}), bf16[16,4,2048]{2,1,0:T(4,128)(2,1)S(1)}, u32[]{:S(2)}, u32[]{:S(2)}) async-start(bf16[16,4,2048]{2,1,0:T(4,128)(2,1)} %broadcast_in_dim.21), calls=%async_computation.1 | async-start | bytes 524288 | tf_op jit(solution)/shard_map/all_to_all | solution.py:282
  91.9 146.1 %reduce-scatter.2.cloned.1.call-start = ((), (), s32[]{:S(2)}) async-start(), calls=%async_computation.7 | async-start | bytes 3342336 | tf_op jit(solution)/shard_map/reduce_scatter | solution.py:440
  100.4 32.7 %copy-start.14 = (s32[128,2]{0,1:T(2,128)S(1)}, s32[128,2]{0,1:T(2,128)}, u32[]{:S(2)}) copy-start(s32[128,2]{0,1:T(2,128)} %param.23) | copy-start | bytes 3076
  122.1 15.9 %copy-start.7 = (bf16[4,64,2048]{2,1,0:T(8,128)(2,1)}, bf16[4,64,2048]{2,1,0:T(8,128)(2,1)S(1)}, u32[]{:S(2)}) copy-start(bf16[4,64,2048]{2,1,0:T(8,128)(2,1)S(1)} %copy_bitcast_fusion.refs_0_) | copy-start | bytes 3145732
  122.1 15.0 %collective-permute-start.21 = (bf16[4,64,2048]{2,1,0:T(8,128)(2,1)S(1)}, bf16[4,64,2048]{2,1,0:T(8,128)(2,1)S(1)}, u32[]{:S(2)}, u32[]{:S(2)}) collective-permute-start(bf16[4,64,2048]{2,1,0:T(8,128)(2,1)S(1)} %copy_bitcast_fusion.refs_0_), channel_id=1, source_target_pairs={{16,0},{0,16},{17,1},{1,17},{18,2},{2,18},{19,3},{3,19},{20,4},{4,... | collective-permute-start | bytes 3145736 | tf_op jit(solution)/shard_map/ppermute | solution.py:274
  133.9 30.3 %collective-permute-start.19 = (bf16[4,64,2048]{2,1,0:T(8,128)(2,1)S(1)}, bf16[4,64,2048]{2,1,0:T(8,128)(2,1)S(1)}, u32[]{:S(2)}, u32[]{:S(2)}) collective-permute-start(bf16[4,64,2048]{2,1,0:T(8,128)(2,1)S(1)} %copy_bitcast_fusion.refs_0_), channel_id=1, source_target_pairs={{32,0},{64,32},{96,64},{0,96},{33,1},{65,33},{97,65},{1,97},{34,2}... | collective-permute-start | bytes 3145736 | tf_op jit(solution)/shard_map/ppermute | solution.py:274
  137.2 27.0 %collective-permute-start.20 = (bf16[4,64,2048]{2,1,0:T(8,128)(2,1)S(1)}, bf16[4,64,2048]{2,1,0:T(8,128)(2,1)}, u32[]{:S(2)}, u32[]{:S(2)}) collective-permute-start(bf16[4,64,2048]{2,1,0:T(8,128)(2,1)S(1)} %copy_bitcast_fusion.refs_0_), channel_id=1, source_target_pairs={{96,0},{0,32},{32,64},{64,96},{97,1},{1,33},{33,65},{65,97},{98,2}... | collective-permute-start | bytes 3145736 | tf_op jit(solution)/shard_map/ppermute | solution.py:274
  137.2 1.1 copy-start.15
  164.1 1.0 copy-start.8
  164.2 4.8 %collective-permute-start.22 = (bf16[4,64,2048]{2,1,0:T(8,128)(2,1)S(1)}, bf16[4,64,2048]{2,1,0:T(8,128)(2,1)S(1)}, u32[]{:S(2)}, u32[]{:S(2)}) collective-permute-start(bf16[4,64,2048]{2,1,0:T(8,128)(2,1)S(1)} %collective-permute-done.19.refs_0_), channel_id=1, source_target_pairs={{16,0},{0,16},{17,1},{1,17},{18,2},{2,18},{19,3},{3,19},{20,4},{4,... | collective-permute-start | bytes 3145736 | tf_op jit(solution)/shard_map/ppermute | solution.py:274
  164.6 4.3 %collective-permute-start.23 = (bf16[4,64,2048]{2,1,0:T(8,128)(2,1)}, bf16[4,64,2048]{2,1,0:T(8,128)(2,1)S(1)}, u32[]{:S(2)}, u32[]{:S(2)}) collective-permute-start(bf16[4,64,2048]{2,1,0:T(8,128)(2,1)} %collective-permute-done.20.refs_2_), channel_id=1, source_target_pairs={{16,0},{0,16},{17,1},{1,17},{18,2},{2,18},{19,3},{3,19},{20,4},{4,... | collective-permute-start | bytes 3145736 | tf_op jit(solution)/shard_map/ppermute | solution.py:274
  166.2 22.1 %collective-permute-start.24 = (bf16[2,64,2048]{2,1,0:T(8,128)(2,1)S(1)}, bf16[2,64,2048]{2,1,0:T(8,128)(2,1)S(1)}, u32[]{:S(2)}, u32[]{:S(2)}) collective-permute-start(bf16[2,64,2048]{2,1,0:T(8,128)(2,1)S(1)} %slice.175), channel_id=1, source_target_pairs={{32,0},{64,32},{96,64},{0,96},{33,1},{65,33},{97,65},{1,97},{34,2}... | collective-permute-start | bytes 1572872 | tf_op jit(solution)/shard_map/ppermute | solution.py:274
  169.0 19.4 %collective-permute-start.25 = (bf16[2,64,2048]{2,1,0:T(8,128)(2,1)S(1)}, bf16[2,64,2048]{2,1,0:T(8,128)(2,1)S(1)}, u32[]{:S(2)}, u32[]{:S(2)}) collective-permute-start(bf16[2,64,2048]{2,1,0:T(8,128)(2,1)S(1)} %slice.176), channel_id=1, source_target_pairs={{96,0},{0,32},{32,64},{64,96},{97,1},{1,33},{33,65},{65,97},{98,2}... | collective-permute-start | bytes 1572872 | tf_op jit(solution)/shard_map/ppermute | solution.py:274
  169.0 1.0 copy-start.16
  170.0 1.0 copy-start.17
  188.3 3.3 %copy-start.18 = (bf16[2,64,2048]{2,1,0:T(8,128)(2,1)}, bf16[2,64,2048]{2,1,0:T(8,128)(2,1)S(1)}, u32[]{:S(2)}) copy-start(bf16[2,64,2048]{2,1,0:T(8,128)(2,1)S(1)} %collective-permute-done.24.refs_0_) | copy-start | bytes 1572868
  188.4 3.3 %copy-start.19 = (bf16[2,64,2048]{2,1,0:T(8,128)(2,1)}, bf16[2,64,2048]{2,1,0:T(8,128)(2,1)S(1)}, u32[]{:S(2)}) copy-start(bf16[2,64,2048]{2,1,0:T(8,128)(2,1)S(1)} %collective-permute-done.25.refs_1_) | copy-start | bytes 1572868
  188.4 2.5 %collective-permute-start.26 = (bf16[2,64,2048]{2,1,0:T(8,128)(2,1)S(1)}, bf16[2,64,2048]{2,1,0:T(8,128)(2,1)S(1)}, u32[]{:S(2)}, u32[]{:S(2)}) collective-permute-start(bf16[2,64,2048]{2,1,0:T(8,128)(2,1)S(1)} %collective-permute-done.24.refs_0_), channel_id=1, source_target_pairs={{16,0},{0,16},{17,1},{1,17},{18,2},{2,18},{19,3},{3,19},{20,4},{4,... | collective-permute-start | bytes 1572872 | tf_op jit(solution)/shard_map/ppermute | solution.py:274
  189.3 2.3 collective-permute-start.27
  189.6 14.4 %copy-start.12 = (f32[4,256]{1,0:T(4,128)S(1)}, f32[4,256]{1,0:T(4,128)}, u32[]{:S(2)}) copy-start(f32[4,256]{1,0:T(4,128)} %get-tuple-element.40) | copy-start | bytes 12292
  189.6 14.4 %copy-start.13 = (f32[2,256]{1,0:T(2,128)S(1)}, f32[2,256]{1,0:T(2,128)}, u32[]{:S(2)}) copy-start(f32[2,256]{1,0:T(2,128)} %get-tuple-element.36) | copy-start | bytes 6148
  190.9 0.8 copy-start.20
  191.7 0.8 copy-start.21
  215.8 4.2 %collective-permute-start.30 = (f32[8,256]{1,0:T(8,128)S(1)}, f32[8,256]{1,0:T(8,128)S(1)}, u32[]{:S(2)}, u32[]{:S(2)}) collective-permute-start(f32[8,256]{1,0:T(8,128)S(1)} %reduce_sum.98), channel_id=1, source_target_pairs={{96,0},{0,32},{32,64},{64,96},{97,1},{1,33},{33,65},{65,97},{98,2}... | collective-permute-start | bytes 24584 | tf_op jit(solution)/shard_map/ppermute | solution.py:274
  215.9 5.2 %collective-permute-start.29 = (f32[8,256]{1,0:T(8,128)S(1)}, f32[8,256]{1,0:T(8,128)S(1)}, u32[]{:S(2)}, u32[]{:S(2)}) collective-permute-start(f32[8,256]{1,0:T(8,128)S(1)} %reduce_sum.98), channel_id=1, source_target_pairs={{64,0},{96,32},{0,64},{32,96},{65,1},{97,33},{1,65},{33,97},{66,2}... | collective-permute-start | bytes 24584 | tf_op jit(solution)/shard_map/ppermute | solution.py:274
  220.0 2.8 %collective-permute-start.28 = (f32[8,256]{1,0:T(8,128)S(1)}, f32[8,256]{1,0:T(8,128)S(1)}, u32[]{:S(2)}, u32[]{:S(2)}) collective-permute-start(f32[8,256]{1,0:T(8,128)S(1)} %reduce_sum.98), channel_id=1, source_target_pairs={{32,0},{64,32},{96,64},{0,96},{33,1},{65,33},{97,65},{1,97},{34,2}... | collective-permute-start | bytes 24584 | tf_op jit(solution)/shard_map/ppermute | solution.py:274
  222.8 3.9 %collective-permute-start.31 = (f32[8,256]{1,0:T(8,128)S(1)}, f32[8,256]{1,0:T(8,128)S(1)}, u32[]{:S(2)}, u32[]{:S(2)}) collective-permute-start(f32[8,256]{1,0:T(8,128)S(1)} %add_add_fusion), channel_id=1, source_target_pairs={{16,0},{0,16},{17,1},{1,17},{18,2},{2,18},{19,3},{3,19},{20,4},{4,... | collective-permute-start | bytes 24584 | tf_op jit(solution)/shard_map/ppermute | solution.py:274
  227.7 13.2 %copy-start.1 = (bf16[4,2048,128]{2,1,0:T(8,128)(2,1)S(1)}, bf16[4,2048,128]{2,1,0:T(8,128)(2,1)}, u32[]{:S(2)}) copy-start(bf16[4,2048,128]{2,1,0:T(8,128)(2,1)} %param.26) | copy-start | bytes 6291460
Sparse Core Ops, SparseCore 0:
  9.7 44.5 all-gather.2
  72.6 59.8 all-gather.4
  164.3 73.4 reduce-scatter.1

commit v7 on v4

--- a/solution.py
+++ b/solution.py
@@ -21,7 +21,7 @@
 YC = ("y", "core")
 ALL = ("y", "core", "x", "z")
 GROUPS = ((0, 0), (0, 1), (1, 0), (3, 0), (1, 1), (3, 1), (2, 0), (2, 1))
-CALLS = ((0, 2), (2, 6), (6, 8))
+CALLS = ((0, 2), (2, 4), (4, 8))
 TILE = 256
 VOCAB_BLOCK = 512
 HIDDEN = -1e30
@@ -96,7 +96,7 @@
             ],
         ),
         compiler_params=pltpu.CompilerParams(
-            dimension_semantics=("arbitrary", "arbitrary"), vmem_limit_bytes=24 << 20
+            dimension_semantics=("arbitrary", "arbitrary"), vmem_limit_bytes=60 << 20
         ),
         cost_estimate=pl.CostEstimate(
             flops=4 * rows * QH * HD * slots,
@@ -108,23 +108,15 @@
 
 def logits_kernel(first, parts, place_ref, *refs):
     pieces = refs[: len(parts)]
-    bounds_ref, embedding_ref, out_ref, totals_ref, rows_ref, running, sems = refs[len(parts) :]
+    bounds_ref, embedding_ref, out_ref, totals_ref, rows_ref, running = refs[len(parts) :]
     step, steps = pl.program_id(0), pl.num_programs(0)
     groups, heads, count, depth = rows_ref.shape
     vocab = embedding_ref.shape[0]
 
     @pl.when(step == 0)
     def _():
-        copies = [
-            pltpu.make_async_copy(
-                piece, rows_ref.at[group, low : low + piece.shape[0]], sems.at[number]
-            )
-            for number, (piece, (group, low)) in enumerate(zip(pieces, parts))
-        ]
-        for copy in copies:
-            copy.start()
-        for copy in copies:
-            copy.wait()
+        for piece, (group, low) in zip(pieces, parts):
+            rows_ref[group, low : low + piece.shape[0]] = piece[...]
         running[...] = jnp.zeros_like(running)
 
     every = rows_ref[...].reshape(groups * heads * count, depth)
@@ -176,7 +168,10 @@
         grid_spec=pltpu.PrefetchScalarGridSpec(
             num_scalar_prefetch=1,
             grid=(vocab_width // vocab,),
-            in_specs=[spec(memory_space=pl.ANY)] * len(pieces)
+            in_specs=[
+                spec(piece.shape, lambda j, p: (0, 0, 0), pipeline_mode=pl.Buffered(1))
+                for piece in pieces
+            ]
             + [
                 spec(bounds.shape, lambda j, p: (0, 0, 0)),
                 spec((vocab, depth), lambda j, p: (j, 0)),
@@ -188,7 +183,6 @@
             scratch_shapes=[
                 pltpu.VMEM((groups, HEADS, count, depth), BF),
                 pltpu.VMEM((size, 128), F32),
-                pltpu.SemaphoreType.DMA((len(pieces),)),
             ],
         ),
         compiler_params=pltpu.CompilerParams(
@@ -298,11 +292,11 @@
     return own, ring(own, "core", CORE, 1)
 
 
-def out_projection(attended, own_weight, other_weight):
-    rows, depth = attended.shape
+def out_projection(group, own_weight, other_weight):
+    rows, depth = group[0].shape
     half = depth // 2
     core = lax.axis_index("core")
-    group = lax.all_gather(attended, "z", axis=0, tiled=True)
+    group = jnp.concatenate(group, axis=0)
     own_part = lax.dynamic_slice_in_dim(group, core * half, half, 1)
     other_part = lax.dynamic_slice_in_dim(group, (1 - core) * half, half, 1)
     columns = (
@@ -310,7 +304,9 @@
         + jnp.dot(other_part, other_weight, preferred_element_type=F32)
     ).astype(BF)
     width = columns.shape[1] // X
-    back = swap(columns.reshape(Z, rows, X * width), "z")
+    columns = [columns[z * rows : (z + 1) * rows] for z in range(Z)]
+    columns = jnp.stack(in_order(columns, lax.axis_index("z")))
+    back = swap(columns, "z")
     by_x = in_order(
         [
             jnp.concatenate([back[z, :, d * width : (d + 1) * width] for z in range(Z)], axis=1)
@@ -364,8 +360,11 @@
     own_half = own_half_of(out_weight)
     pieces = [own_half] + [ring(own_half, "x", X, shift) for shift in range(1, X)]
     attended = attention(after(tree_q, own_half), tree_kv, kv_cache, cache_lengths, tree_parents)
-    own_weight, other_weight = out_weights(after(pieces, attended))
-    projected = out_projection(attended, own_weight, other_weight)
+    pieces = after(pieces, attended)
+    sent = after(attended, pieces)
+    group = [sent] + [ring(sent, "z", Z, shift) for shift in range(1, Z)]
+    own_weight, other_weight = out_weights(pieces)
+    projected = out_projection(after(group, other_weight), own_weight, other_weight)
     first = (hidden.astype(F32) + rms_scale(projected, attn_post_gain)).astype(BF)
     normed = rms_scale(first, ff_pre_gain).astype(BF)
     mlp_rows = lax.all_gather(normed, XZ, axis=0, tiled=True)
@@ -384,8 +383,8 @@
     draft_copies = copies_of(drafts, units)
     drafts = jnp.transpose(swap(draft_copies, XZ), (1, 2, 0, 3)).reshape(HEADS, rows, -1)
 
-    mlp_partial = unit_terms(after(mlp_rows, drafts), weights)
-    mlp_sum = lax.psum_scatter(mlp_partial, XZ, scatter_dimension=0, tiled=True)
+    mlp_partial = unit_terms(after(mlp_rows, draft_copies), weights)
+    mlp_sum = lax.psum_scatter(after(mlp_partial, drafts), XZ, scatter_dimension=0, tiled=True)
 
     vocab_width = embedding.shape[0]
     start = lax.axis_index(ALL) * vocab_width
@@ -395,25 +394,22 @@
     half = HEADS // 2
     next_up, next_down = ring(drafts, "y", Y, 1), ring(drafts, "y", Y, 3)
     beside = ring(drafts, "core", CORE, 1)
+    table_a, totals_a = some_logits(
+        0, place, [drafts, beside], ((0, 0), (1, 0)), bounds, embedding
+    )
+    next_up, next_down = after([next_up, next_down], totals_a)
     across = [ring(next_up[:half], "y", Y, 1), ring(next_down[half:], "y", Y, 3)]
     beside_up, beside_down = ring(next_up, "core", CORE, 1), ring(next_down, "core", CORE, 1)
+    table_b, totals_b = some_logits(
+        1, place, [next_up, next_down], ((0, 0), (1, 0)), bounds, embedding
+    )
+    beside_up, beside_down, *across = after([beside_up, beside_down, *across], totals_b)
     beside_across = [ring(piece, "core", CORE, 1) for piece in across]
-    table_a, totals_a = some_logits(
-        0, place, [drafts, beside], ((0, 0), (1, 0)), bounds, embedding
-    )
-    table_b, totals_b = some_logits(
-        1,
-        place,
-        after([next_up, next_down, beside_up, beside_down], totals_a, mlp_partial),
-        ((0, 0), (1, 0), (2, 0), (3, 0)),
-        bounds,
-        embedding,
-    )
     table_c, totals_c = some_logits(
         2,
         place,
-        after(across + beside_across, totals_b),
-        ((0, 0), (0, half), (1, 0), (1, half)),
+        [beside_up, beside_down, *across, *beside_across],
+        ((0, 0), (1, 0), (2, 0), (2, half), (3, 0), (3, half)),
         bounds,
         embedding,
     )
@@ -424,11 +420,11 @@
     whole = sums + ring(sums, "y", Y, 1) + ring(sums, "y", Y, 2) + ring(sums, "y", Y, 3)
     whole = whole + ring(whole, "core", CORE, 1)
     logs = jnp.transpose(jnp.log(whole).reshape(Y * CORE, HEADS, rows), (0, 2, 1))
-    draft_logprobs = finish(place, [table_a, table_b, table_c], logs).reshape(
-        HEADS, Y * CORE * rows, vocab_width
-    )
     mlp_sum = after(mlp_sum, sums)
     tree_out = (first.astype(F32) + rms_scale(mlp_sum, ff_post_gain)).astype(BF)
+    draft_logprobs = finish(place, [table_a, table_b, table_c], after(logs, tree_out)).reshape(
+        HEADS, Y * CORE * rows, vocab_width
+    )
     return (tree_out, draft_logprobs)
 
 

time: 254 us -> 246 us (0.969)
  blocking collectives: 49.4 us -> 23.6 us
  waiting for transfers between devices: 32.5 us -> 56.5 us
  starting transfers between devices: 51 us -> 44.7 us
    ppermute x17 -> x20, waiting for transfers between devices: 10.2 us -> 34.3 us  [ring(): lax.ppermute(values, axis, [((i + shift) % size, i) for i in range(size)])]
    all_gather x1 -> x0, blocking collectives: 13.8 us -> none  [out_projection(): group = lax.all_gather(attended, 'z', axis=0, tiled=True)]
    all_to_all x3 -> x2, blocking collectives: 35.6 us -> 23.6 us  [swap(): return lax.all_to_all(copies, axes, split_axis=0, concat_axis=0, tiled=True)]
    ppermute x17 -> x20, starting transfers between devices: 40.2 us -> 29.5 us  [ring(): lax.ppermute(values, axis, [((i + shift) % size, i) for i in range(size)])]
    all_to_all x3 -> x4, starting transfers between devices: 10.7 us -> 14.9 us  [swap(): return lax.all_to_all(copies, axes, split_axis=0, concat_axis=0, tiled=True)]
    pallas_call x3, Pallas kernels: 40.3 us -> 37.4 us  [some_logits(): pl.pallas_call(functools.partial(logits_kernel, first, parts), out_shape=...]
    unnamed x49 -> x48, local copies, waits for them, and re-layouts: 9.64 us -> 7.2 us
    all_to_all x3 -> x4, waiting for transfers between devices: 21.5 us -> 21.5 us  [swap(): return lax.all_to_all(copies, axes, split_axis=0, concat_axis=0, tiled=True)]
  transfers between devices with their start and end apart: 23 -> 27, of which waited for: 9 -> 16; matrix products, arithmetic and copies ran while one was open for 10% -> 18% of each run, Pallas kernels for 22% -> 18%
where the time goes in v7:
time: 246 us; the launch traced here: 244 us
  waiting for transfers between devices  56.5 us (23%)
  Pallas kernels  55.4 us (23%)
  starting transfers between devices  44.7 us (18%)
  matrix products  24.3 us (10%)
  blocking collectives  23.6 us (10%)
  local copies, waits for them, and re-layouts  18.5 us (8%)
  between operations  15 us (6%)
  other arithmetic  6.25 us (3%)
    pallas_call x3, Pallas kernels, some_logits(): pl.pallas_call(functools.partial(logits_kernel, first, parts), out_shape=...  37.4 us
    ppermute x20, waiting for transfers between devices, ring(): lax.ppermute(values, axis, [((i + shift) % size, i) for i in range(size)])  34.3 us
    ppermute x20, starting transfers between devices, ring(): lax.ppermute(values, axis, [((i + shift) % size, i) for i in range(size)])  29.5 us
    all_to_all x2, blocking collectives, swap(): return lax.all_to_all(copies, axes, split_axis=0, concat_axis=0, tiled=True)  23.6 us
    all_to_all x4, waiting for transfers between devices, swap(): return lax.all_to_all(copies, axes, split_axis=0, concat_axis=0, tiled=True)  21.5 us
    all_to_all x4, starting transfers between devices, swap(): return lax.all_to_all(copies, axes, split_axis=0, concat_axis=0, tiled=True)  14.9 us
    dot_general x2, matrix products, unit_terms(): lax.dot_general(active, weights[2], (((1,), (1,)), ((), ())), preferred_e...  12.4 us
    pallas_call x1, Pallas kernels, finish(): pl.pallas_call(finish_kernel, out_shape=jax.ShapeDtypeStruct((HEADS, grou...  11.5 us
  transfers between devices with their start and end apart: 27, of which 16 were waited for; matrix products, arithmetic and copies ran while one was open for 18% of the time, Pallas kernels for 18%

profile of v7, /device:TPU:1, one launch (start us, length us, event | category | flops | bytes accessed | tf_op | source)
XLA Modules:
  0.0 244.3 jit_solution(4527258878863232281)
XLA Ops:
  7.9 1.0 constant_dynamic-slice_fusion
  8.9 3.4 %collective-permute-start = (bf16[1024,128]{1,0:T(8,128)(2,1)S(1)}, bf16[1024,128]{1,0:T(8,128)(2,1)S(1)}, u32[]{:S(2)}, u32[]{:S(2)}) collective-permute-start(bf16[1024,128]{1,0:T(8,128)(2,1)S(1)} %constant_dynamic-slice_fusion), channel_id=1, source_target_pairs={{4,0},{8,4},{12,8},{0,12},{5,1},{9,5},{13,9},{1,13},{6,2},{10,6},{... | collective-permute-start | bytes 786440 | tf_op jit(solution)/shard_map/ppermute | solution.py:258
  14.1 1.5 copy.38
  15.6 1.3 copy.31.parents_ref
  16.9 6.4 %shard_map.167 = bf16[48,2048]{1,0:T(8,128)(2,1)} custom-call(s32[1]{0:T(128)S(6)} %copy.45.length_ref, bf16[48,2048]{1,0:T(8,128)(2,1)} %q_ref, bf16[2,48,512]{2,1,0:T(8,128)(2,1)} %bitcast.103, s32[48,1]{1,0:T(8,128)} %copy.31.parents_ref, bf16[1,2,2,2048,256]{4,3,2,1,0:T(8,128)(2,1)} %values_ref.1, bf16[1,2,2,2048,256]{4,3,2,1,0:T(8,128)(2,1)} %values_ref.1), custom_call_target="tpu_custom_call" | custom-call | flops 805306368 | bytes 4194304 | tf_op jit(solution)/shard_map/pallas_call | solution.py:78
  23.4 0.7 copy-done.4
  24.1 0.7 copy-done.5
  24.8 2.9 %collective-permute-done.2 = bf16[1024,128]{1,0:T(8,128)(2,1)} collective-permute-done((bf16[1024,128]{1,0:T(8,128)(2,1)S(1)}, bf16[1024,128]{1,0:T(8,128)(2,1)}, u32[]{:S(2)}, u32[]{:S(2)}) %collective-permute-start.2) | collective-permute-done | bytes 262176 | tf_op jit(solution)/shard_map/ppermute | solution.py:258
  27.8 1.0 constant_dynamic-update-slice_fusion.2
  28.8 1.0 constant_dynamic-update-slice_fusion.1
  29.8 1.0 constant_dynamic-update-slice_fusion
  31.5 3.7 %collective-permute-start.3 = (bf16[48,2048]{1,0:T(8,128)(2,1)}, bf16[48,2048]{1,0:T(8,128)(2,1)S(1)}, u32[]{:S(2)}, u32[]{:S(2)}) collective-permute-start(bf16[48,2048]{1,0:T(8,128)(2,1)} %shard_map.167), channel_id=1, source_target_pairs={{1,0},{2,1},{3,2},{0,3},{5,4},{6,5},{7,6},{4,7},{9,8},{10,9},{11,1... | collective-permute-start | bytes 589832 | tf_op jit(solution)/shard_map/ppermute | solution.py:258
  35.2 0.7 collective-permute-start.5
  35.9 8.1 %collective-permute-done.3 = bf16[48,2048]{1,0:T(8,128)(2,1)S(1)} collective-permute-done((bf16[48,2048]{1,0:T(8,128)(2,1)}, bf16[48,2048]{1,0:T(8,128)(2,1)S(1)}, u32[]{:S(2)}, u32[]{:S(2)}) %collective-permute-start.3) | collective-permute-done | bytes 196640 | tf_op jit(solution)/shard_map/ppermute | solution.py:258
  44.0 3.5 %collective-permute-done.5 = bf16[48,2048]{1,0:T(8,128)(2,1)} collective-permute-done((bf16[48,2048]{1,0:T(8,128)(2,1)}, bf16[48,2048]{1,0:T(8,128)(2,1)}, u32[]{:S(2)}, u32[]{:S(2)}) %collective-permute-start.5) | collective-permute-done | bytes 196640 | tf_op jit(solution)/shard_map/ppermute | solution.py:258
  47.5 0.9 constant_dynamic-update-slice_fusion.7
  48.5 0.9 constant_dynamic-update-slice_fusion.4
  49.4 1.6 fusion.34
  51.5 0.7 pad_maximum_fusion
  52.2 3.4 %all-to-all-start = ((bf16[4,48,512]{2,1,0:T(8,128)(2,1)}), bf16[4,48,512]{2,1,0:T(8,128)(2,1)S(1)}, u32[]{:S(2)}, u32[]{:S(2)}) async-start(bf16[4,48,512]{2,1,0:T(8,128)(2,1)} %pad_maximum_fusion), calls=%async_computation | async-start | bytes 393216 | tf_op jit(solution)/shard_map/all_to_all | solution.py:266
  55.8 5.0 %all-to-all-done = bf16[4,48,512]{2,1,0:T(8,128)(2,1)S(1)} async-done(((bf16[4,48,512]{2,1,0:T(8,128)(2,1)}), bf16[4,48,512]{2,1,0:T(8,128)(2,1)S(1)}, u32[]{:S(2)}, u32[]{:S(2)}) %all-to-all-start) | async-done | bytes 196640 | tf_op jit(solution)/shard_map/all_to_all | solution.py:266
  61.4 0.8 fusion.32
  62.3 1.1 convolution_convert_fusion.2
  63.5 10.2 %all_to_all.30 = bf16[16,4,2048]{2,1,0:T(4,128)(2,1)S(1)} all-to-all(bf16[16,4,2048]{2,1,0:T(4,128)(2,1)S(1)} %broadcast_in_dim.23), channel_id=1, replica_groups=mesh['y'=4,'core'=2,'x'=4,'z'=4] {'x','z'}, dimensions={0} | all-to-all | bytes 524288 | tf_op jit(solution)/shard_map/all_to_all | solution.py:266
  73.8 2.4 fusion.43
  76.2 3.5 %convolution_convert_fusion.1 = bf16[64,2048]{1,0:T(8,128)(2,1)S(1)} fusion(bf16[3,2048,512]{1,2,0:T(8,128)(2,1)} %all-gather.5.cloned.1.call-done, f32[64,512]{1,0:T(8,128)S(1)} %fusion.43, bf16[64,2048]{1,0:T(8,128)(2,1)S(1)} %reshape.98), kind=kOutput, calls=%fused_computation.2 | convolution fusion | flops 268632064 | bytes 4849664 | tf_op jit(solution)/shard_map/dot_general | solution.py:324
  79.7 0.8 reshape.99
  80.5 3.7 %all-to-all-start.2 = ((bf16[16,4,2048]{2,1,0:T(4,128)(2,1)}), bf16[16,4,2048]{2,1,0:T(4,128)(2,1)S(1)}, u32[]{:S(2)}, u32[]{:S(2)}) async-start(bf16[16,4,2048]{2,1,0:T(4,128)(2,1)} %reshape.99), calls=%async_computation.2 | async-start | bytes 524288 | tf_op jit(solution)/shard_map/all_to_all | solution.py:266
  84.2 7.3 %all-to-all-done.2 = bf16[16,4,2048]{2,1,0:T(4,128)(2,1)S(1)} async-done(((bf16[16,4,2048]{2,1,0:T(4,128)(2,1)}), bf16[16,4,2048]{2,1,0:T(4,128)(2,1)S(1)}, u32[]{:S(2)}, u32[]{:S(2)}) %all-to-all-start.2) | async-done | bytes 262176 | tf_op jit(solution)/shard_map/all_to_all | solution.py:266
  92.2 0.8 broadcast_in_dim.24
  93.0 3.5 %all-to-all-start.3 = ((bf16[16,4,2048]{2,1,0:T(4,128)(2,1)}), bf16[16,4,2048]{2,1,0:T(4,128)(2,1)S(1)}, u32[]{:S(2)}, u32[]{:S(2)}) async-start(bf16[16,4,2048]{2,1,0:T(4,128)(2,1)} %broadcast_in_dim.24), calls=%async_computation.3 | async-start | bytes 524288 | tf_op jit(solution)/shard_map/all_to_all | solution.py:266
  96.5 9.2 %all-to-all-done.3 = bf16[16,4,2048]{2,1,0:T(4,128)(2,1)S(1)} async-done(((bf16[16,4,2048]{2,1,0:T(4,128)(2,1)}), bf16[16,4,2048]{2,1,0:T(4,128)(2,1)S(1)}, u32[]{:S(2)}, u32[]{:S(2)}) %all-to-all-start.3) | async-done | bytes 262176 | tf_op jit(solution)/shard_map/all_to_all | solution.py:266
  106.4 1.3 broadcast_in_dim.25
  107.7 4.3 %all-to-all-start.4 = ((bf16[16,4,64,128]{3,2,1,0:T(8,128)(2,1)}), bf16[16,4,64,128]{3,2,1,0:T(8,128)(2,1)S(1)}, u32[]{:S(2)}, u32[]{:S(2)}) async-start(bf16[16,4,64,128]{3,2,1,0:T(8,128)(2,1)} %broadcast_in_dim.25), calls=%async_computation.4 | async-start | bytes 2097152 | tf_op jit(solution)/shard_map/all_to_all | solution.py:266
  112.2 5.5 %fusion.4 = f32[768,512]{1,0:T(8,128)} fusion(bf16[768,2048]{1,0:T(8,128)(2,1)} %all-gather.3.cloned.1.call-done, bf16[3,2048,512]{1,2,0:T(8,128)(2,1)} %all-gather.5.cloned.1.call-done), kind=kOutput, calls=%fused_computation.12 | convolution fusion | flops 1610612736 | bytes 6815744 | tf_op jit(solution)/shard_map/dot_general | solution.py:321
  117.8 9.0 %convolution_convert_fusion = bf16[768,2048]{1,0:T(8,128)(2,1)} fusion(bf16[3,2048,512]{1,2,0:T(8,128)(2,1)} %all-gather.5.cloned.1.call-done, f32[768,512]{1,0:T(8,128)} %fusion.4, bf16[768,2048]{1,0:T(8,128)(2,1)} %all-gather.3.cloned.1.call-done), kind=kOutput, calls=%fused_computation | convolution fusion | flops 3226730496 | bytes 12058624 | tf_op jit(solution)/shard_map/dot_general | solution.py:324
  126.9 6.0 %collective-permute-start.7 = (bf16[4,64,2048]{2,1,0:T(8,128)(2,1)S(1)}, bf16[4,64,2048]{2,1,0:T(8,128)(2,1)S(1)}, u32[]{:S(2)}, u32[]{:S(2)}) collective-permute-start(bf16[4,64,2048]{2,1,0:T(8,128)(2,1)S(1)} %copy_bitcast_fusion.refs_0_), channel_id=1, source_target_pairs={{16,0},{0,16},{17,1},{1,17},{18,2},{2,18},{19,3},{3,19},{20,4},{4,... | collective-permute-start | bytes 3145736 | tf_op jit(solution)/shard_map/ppermute | solution.py:258
  133.0 2.7 %collective-permute-start.8 = (bf16[4,64,2048]{2,1,0:T(8,128)(2,1)S(1)}, bf16[4,64,2048]{2,1,0:T(8,128)(2,1)S(1)}, u32[]{:S(2)}, u32[]{:S(2)}) collective-permute-start(bf16[4,64,2048]{2,1,0:T(8,128)(2,1)S(1)} %copy_bitcast_fusion.refs_0_), channel_id=1, source_target_pairs={{32,0},{64,32},{96,64},{0,96},{33,1},{65,33},{97,65},{1,97},{34,2}... | collective-permute-start | bytes 3145736 | tf_op jit(solution)/shard_map/ppermute | solution.py:258
  136.5 0.9 broadcast_in_dim.27
  137.5 10.4 %shard_map.168 = (bf16[2,4,64,2048]{3,2,1,0:T(8,128)(2,1)}, f32[2,256]{1,0:T(2,128)}) custom-call(s32[9]{0:T(128)} %stack.62.place_ref, bf16[4,64,2048]{2,1,0:T(8,128)(2,1)} %copy-done.2, bf16[4,64,2048]{2,1,0:T(8,128)(2,1)} %copy-done.14, s32[8,64,2]{2,1,0:T(8,128)} %bitcast.104, bf16[2048,2048]{1,0:T(8,128)(2,1)} %refs_7_.1), custom_call_target="tpu_custom_call" | custom-call | flops 4294967296 | bytes 10485760 | tf_op jit(solution)/shard_map/pallas_call | solution.py:162
  148.0 10.2 %collective-permute-done.8.refs_0_ = bf16[4,64,2048]{2,1,0:T(8,128)(2,1)S(1)} collective-permute-done((bf16[4,64,2048]{2,1,0:T(8,128)(2,1)S(1)}, bf16[4,64,2048]{2,1,0:T(8,128)(2,1)S(1)}, u32[]{:S(2)}, u32[]{:S(2)}) %collective-permute-start.8) | collective-permute-done | bytes 1048608 | tf_op jit(solution)/shard_map/ppermute | solution.py:258
  158.2 3.2 %collective-permute-done.9.refs_1_ = bf16[4,64,2048]{2,1,0:T(8,128)(2,1)} collective-permute-done((bf16[4,64,2048]{2,1,0:T(8,128)(2,1)S(1)}, bf16[4,64,2048]{2,1,0:T(8,128)(2,1)}, u32[]{:S(2)}, u32[]{:S(2)}) %collective-permute-start.9) | collective-permute-done | bytes 1048608 | tf_op jit(solution)/shard_map/ppermute | solution.py:258
  161.4 1.2 collective-permute-start.10
  162.6 1.1 slice.104
  163.8 1.5 collective-permute-start.13
  165.3 10.6 %shard_map.169 = (bf16[2,4,64,2048]{3,2,1,0:T(8,128)(2,1)}, f32[2,256]{1,0:T(2,128)}) custom-call(s32[9]{0:T(128)} %stack.62.place_ref, bf16[4,64,2048]{2,1,0:T(8,128)(2,1)} %copy-done.3, bf16[4,64,2048]{2,1,0:T(8,128)(2,1)} %collective-permute-done.9.refs_1_, s32[8,64,2]{2,1,0:T(8,128)} %bitcast.105, bf16[2048,2048]{1,0:T(8,128)(2,1)} %refs_7_.1), custom_call_target="tpu_custom_call" | custom-call | flops 4294967296 | bytes 10485760 | tf_op jit(solution)/shard_map/pallas_call | solution.py:162
  175.8 1.0 collective-permute-done.12.refs_2_
  176.9 1.2 collective-permute-done.13.refs_3_
  178.1 1.5 collective-permute-start.14
  179.6 0.9 collective-permute-start.15
  181.4 0.9 collective-permute-done.15.refs_5_
  182.3 0.8 copy-done.18
  183.1 16.4 %shard_map.170 = (bf16[4,4,64,2048]{3,2,1,0:T(8,128)(2,1)}, f32[4,256]{1,0:T(4,128)}) custom-call(s32[9]{0:T(128)} %stack.62.place_ref, bf16[4,64,2048]{2,1,0:T(8,128)(2,1)} %copy-done.15, bf16[4,64,2048]{2,1,0:T(8,128)(2,1)} %copy-done.16, bf16[2,64,2048]{2,1,0:T(8,128)(2,1)} %collective-permute-done.12.refs_2_, ...), custom_call_target="tpu_custom_call" | custom-call | flops 8589934592 | bytes 12582912 | tf_op jit(solution)/shard_map/pallas_call | solution.py:162
  199.6 0.7 pad_maximum_fusion.6
  200.4 13.4 %all_to_all.31 = f32[16,8,256]{2,1,0:T(8,128)S(1)} all-to-all(f32[16,8,256]{2,1,0:T(8,128)S(1)} %broadcast_in_dim.30), channel_id=1, replica_groups=mesh['y'=4,'core'=2,'x'=4,'z'=4] {'x','z'}, dimensions={0} | all-to-all | bytes 262144 | tf_op jit(solution)/shard_map/all_to_all | solution.py:266
  214.1 1.1 collective-permute-start.17
  215.1 1.4 collective-permute-start.16
  216.6 1.0 collective-permute-done.18
  218.3 3.3 %collective-permute-start.19 = (f32[8,256]{1,0:T(8,128)S(1)}, f32[8,256]{1,0:T(8,128)S(1)}, u32[]{:S(2)}, u32[]{:S(2)}) collective-permute-start(f32[8,256]{1,0:T(8,128)S(1)} %add_add_fusion), channel_id=1, source_target_pairs={{16,0},{0,16},{17,1},{1,17},{18,2},{2,18},{19,3},{3,19},{20,4},{4,... | collective-permute-start | bytes 24584 | tf_op jit(solution)/shard_map/ppermute | solution.py:258
  221.6 0.8 collective-permute-done.19
  222.5 0.9 copy.34
  223.4 1.1 fusion.28
  224.5 1.8 fusion.33
  226.2 11.5 %shard_map.171 = bf16[4,8,64,2048]{3,2,1,0:T(8,128)(2,1)} custom-call(s32[9]{0:T(128)} %stack.62.place_ref, bf16[2,4,64,2048]{3,2,1,0:T(8,128)(2,1)} %get-tuple-element.50.refs_0_, bf16[2,4,64,2048]{3,2,1,0:T(8,128)(2,1)} %get-tuple-element.51.refs_1_, bf16[4,4,64,2048]{3,2,1,0:T(8,128)(2,1)} %get-tuple-element.52.refs_2_, f32[8,64,4]{2,1,0:T(8,128)} %bitcast.102), custom_call_target="tpu_custom_call" | custom-call | flops 12582912 | bytes 16777216 | tf_op jit(solution)/shard_map/pallas_call | solution.py:223
  (109 shorter events, 8.7 us)
Async XLA Ops:
  7.2 98.7 %copy-start = (bf16[4,2048,128]{2,1,0:T(8,128)(2,1)S(1)}, bf16[4,2048,128]{2,1,0:T(8,128)(2,1)}, u32[]{:S(2)}) copy-start(bf16[4,2048,128]{2,1,0:T(8,128)(2,1)} %param.26) | copy-start | bytes 6291460
  7.2 66.6 %all-gather.5.cloned.1.call-start = ((), (), s32[]{:S(2)}) async-start(), calls=%async_computation.8 | async-start | bytes 7077888 | tf_op jit(solution)/shard_map/all_gather | solution.py:352
  8.9 14.5 %collective-permute-start = (bf16[1024,128]{1,0:T(8,128)(2,1)S(1)}, bf16[1024,128]{1,0:T(8,128)(2,1)S(1)}, u32[]{:S(2)}, u32[]{:S(2)}) collective-permute-start(bf16[1024,128]{1,0:T(8,128)(2,1)S(1)} %constant_dynamic-slice_fusion), channel_id=1, source_target_pairs={{4,0},{8,4},{12,8},{0,12},{5,1},{9,5},{13,9},{1,13},{6,2},{10,6},{... | collective-permute-start | bytes 786440 | tf_op jit(solution)/shard_map/ppermute | solution.py:258
  12.3 11.1 %collective-permute-start.1 = (bf16[1024,128]{1,0:T(8,128)(2,1)S(1)}, bf16[1024,128]{1,0:T(8,128)(2,1)S(1)}, u32[]{:S(2)}, u32[]{:S(2)}) collective-permute-start(bf16[1024,128]{1,0:T(8,128)(2,1)S(1)} %constant_dynamic-slice_fusion), channel_id=1, source_target_pairs={{8,0},{12,4},{0,8},{4,12},{9,1},{13,5},{1,9},{5,13},{10,2},{14,6},... | collective-permute-start | bytes 786440 | tf_op jit(solution)/shard_map/ppermute | solution.py:258
  12.8 14.9 %collective-permute-start.2 = (bf16[1024,128]{1,0:T(8,128)(2,1)S(1)}, bf16[1024,128]{1,0:T(8,128)(2,1)}, u32[]{:S(2)}, u32[]{:S(2)}) collective-permute-start(bf16[1024,128]{1,0:T(8,128)(2,1)S(1)} %constant_dynamic-slice_fusion), channel_id=1, source_target_pairs={{12,0},{0,4},{4,8},{8,12},{13,1},{1,5},{5,9},{9,13},{14,2},{2,6},{... | collective-permute-start | bytes 786440 | tf_op jit(solution)/shard_map/ppermute | solution.py:258
  23.4 0.7 copy-start.4
  24.1 0.7 copy-start.5
  30.8 16.7 %collective-permute-start.6 = (bf16[1024,512]{1,0:T(8,128)(2,1)S(1)}, bf16[1024,512]{1,0:T(8,128)(2,1)}, u32[]{:S(2)}, u32[]{:S(2)}) collective-permute-start(bf16[1024,512]{1,0:T(8,128)(2,1)S(1)} %constant_dynamic-update-slice_fusion), channel_id=1, source_target_pairs={{16,0},{0,16},{17,1},{1,17},{18,2},{2,18},{19,3},{3,19},{20,4},{4,... | collective-permute-start | bytes 3145736 | tf_op jit(solution)/shard_map/ppermute | solution.py:258
  31.5 12.5 %collective-permute-start.3 = (bf16[48,2048]{1,0:T(8,128)(2,1)}, bf16[48,2048]{1,0:T(8,128)(2,1)S(1)}, u32[]{:S(2)}, u32[]{:S(2)}) collective-permute-start(bf16[48,2048]{1,0:T(8,128)(2,1)} %shard_map.167), channel_id=1, source_target_pairs={{1,0},{2,1},{3,2},{0,3},{5,4},{6,5},{7,6},{4,7},{9,8},{10,9},{11,1... | collective-permute-start | bytes 589832 | tf_op jit(solution)/shard_map/ppermute | solution.py:258
  35.2 8.8 %collective-permute-start.4 = (bf16[48,2048]{1,0:T(8,128)(2,1)}, bf16[48,2048]{1,0:T(8,128)(2,1)S(1)}, u32[]{:S(2)}, u32[]{:S(2)}) collective-permute-start(bf16[48,2048]{1,0:T(8,128)(2,1)} %shard_map.167), channel_id=1, source_target_pairs={{2,0},{3,1},{0,2},{1,3},{6,4},{7,5},{4,6},{5,7},{10,8},{11,9},{8,1... | collective-permute-start | bytes 589832 | tf_op jit(solution)/shard_map/ppermute | solution.py:258
  35.2 12.3 %collective-permute-start.5 = (bf16[48,2048]{1,0:T(8,128)(2,1)}, bf16[48,2048]{1,0:T(8,128)(2,1)}, u32[]{:S(2)}, u32[]{:S(2)}) collective-permute-start(bf16[48,2048]{1,0:T(8,128)(2,1)} %shard_map.167), channel_id=1, source_target_pairs={{3,0},{0,1},{1,2},{2,3},{7,4},{4,5},{5,6},{6,7},{11,8},{8,9},{9,10... | collective-permute-start | bytes 589832 | tf_op jit(solution)/shard_map/ppermute | solution.py:258
  51.0 4.7 %copy-start.7 = (bf16[2048]{0:T(1024)(128)(2,1)S(1)}, bf16[2048]{0:T(1024)(128)(2,1)}, u32[]{:S(2)}) copy-start(bf16[2048]{0:T(1024)(128)(2,1)} %param.28) | copy-start | bytes 12292
  51.0 4.7 %copy-start.8 = (bf16[2048]{0:T(1024)(128)(2,1)S(1)}, bf16[2048]{0:T(1024)(128)(2,1)}, u32[]{:S(2)}) copy-start(bf16[2048]{0:T(1024)(128)(2,1)} %param.29) | copy-start | bytes 12292
  51.1 10.1 %copy-start.6 = (bf16[48,2048]{1,0:T(8,128)(2,1)S(1)}, bf16[48,2048]{1,0:T(8,128)(2,1)}, u32[]{:S(2)}) copy-start(bf16[48,2048]{1,0:T(8,128)(2,1)} %param.16) | copy-start | bytes 589828
  51.5 10.8 %copy-start.19 = (s32[1,4]{1,0:T(1,128)S(1)}, s32[1,4]{1,0:T(1,128)}, u32[]{:S(2)}) copy-start(s32[1,4]{1,0:T(1,128)} %param.22) | copy-start | bytes 52
  52.2 8.5 %all-to-all-start = ((bf16[4,48,512]{2,1,0:T(8,128)(2,1)}), bf16[4,48,512]{2,1,0:T(8,128)(2,1)S(1)}, u32[]{:S(2)}, u32[]{:S(2)}) async-start(bf16[4,48,512]{2,1,0:T(8,128)(2,1)} %pad_maximum_fusion), calls=%async_computation | async-start | bytes 393216 | tf_op jit(solution)/shard_map/all_to_all | solution.py:266
  55.6 56.6 %all-gather.3.cloned.1.call-start = ((), (), s32[]{:S(2)}) async-start(), calls=%async_computation.7 | async-start | bytes 3342336 | tf_op jit(solution)/shard_map/all_gather | solution.py:370
  76.2 8.0 %copy-start.9 = (bf16[2048]{0:T(1024)(128)(2,1)S(1)}, bf16[2048]{0:T(1024)(128)(2,1)}, u32[]{:S(2)}) copy-start(bf16[2048]{0:T(1024)(128)(2,1)} %param.30) | copy-start | bytes 12292
  76.2 8.0 %copy-start.10 = (bf16[2048]{0:T(1024)(128)(2,1)S(1)}, bf16[2048]{0:T(1024)(128)(2,1)}, u32[]{:S(2)}) copy-start(bf16[2048]{0:T(1024)(128)(2,1)} %param.31) | copy-start | bytes 12292
  80.5 11.0 %all-to-all-start.2 = ((bf16[16,4,2048]{2,1,0:T(4,128)(2,1)}), bf16[16,4,2048]{2,1,0:T(4,128)(2,1)S(1)}, u32[]{:S(2)}, u32[]{:S(2)}) async-start(bf16[16,4,2048]{2,1,0:T(4,128)(2,1)} %reshape.99), calls=%async_computation.2 | async-start | bytes 524288 | tf_op jit(solution)/shard_map/all_to_all | solution.py:266
  93.0 12.8 %all-to-all-start.3 = ((bf16[16,4,2048]{2,1,0:T(4,128)(2,1)}), bf16[16,4,2048]{2,1,0:T(4,128)(2,1)S(1)}, u32[]{:S(2)}, u32[]{:S(2)}) async-start(bf16[16,4,2048]{2,1,0:T(4,128)(2,1)} %broadcast_in_dim.24), calls=%async_computation.3 | async-start | bytes 524288 | tf_op jit(solution)/shard_map/all_to_all | solution.py:266
  107.7 19.0 %all-to-all-start.4 = ((bf16[16,4,64,128]{3,2,1,0:T(8,128)(2,1)}), bf16[16,4,64,128]{3,2,1,0:T(8,128)(2,1)S(1)}, u32[]{:S(2)}, u32[]{:S(2)}) async-start(bf16[16,4,64,128]{3,2,1,0:T(8,128)(2,1)} %broadcast_in_dim.25), calls=%async_computation.4 | async-start | bytes 2097152 | tf_op jit(solution)/shard_map/all_to_all | solution.py:266
  112.0 111.4 %reduce-scatter.2.cloned.1.call-start = ((), (), s32[]{:S(2)}) async-start(), calls=%async_computation.9 | async-start | bytes 3342336 | tf_op jit(solution)/shard_map/reduce_scatter | solution.py:387
  126.9 10.5 %copy-start.2 = (bf16[4,64,2048]{2,1,0:T(8,128)(2,1)}, bf16[4,64,2048]{2,1,0:T(8,128)(2,1)S(1)}, u32[]{:S(2)}) copy-start(bf16[4,64,2048]{2,1,0:T(8,128)(2,1)S(1)} %copy_bitcast_fusion.refs_0_) | copy-start | bytes 3145732
  126.9 8.8 %copy-start.13 = (s32[128,2]{0,1:T(2,128)S(1)}, s32[128,2]{0,1:T(2,128)}, u32[]{:S(2)}) copy-start(s32[128,2]{0,1:T(2,128)} %param.23) | copy-start | bytes 3076
  126.9 9.5 %collective-permute-start.7 = (bf16[4,64,2048]{2,1,0:T(8,128)(2,1)S(1)}, bf16[4,64,2048]{2,1,0:T(8,128)(2,1)S(1)}, u32[]{:S(2)}, u32[]{:S(2)}) collective-permute-start(bf16[4,64,2048]{2,1,0:T(8,128)(2,1)S(1)} %copy_bitcast_fusion.refs_0_), channel_id=1, source_target_pairs={{16,0},{0,16},{17,1},{1,17},{18,2},{2,18},{19,3},{3,19},{20,4},{4,... | collective-permute-start | bytes 3145736 | tf_op jit(solution)/shard_map/ppermute | solution.py:258
  133.0 25.2 %collective-permute-start.8 = (bf16[4,64,2048]{2,1,0:T(8,128)(2,1)S(1)}, bf16[4,64,2048]{2,1,0:T(8,128)(2,1)S(1)}, u32[]{:S(2)}, u32[]{:S(2)}) collective-permute-start(bf16[4,64,2048]{2,1,0:T(8,128)(2,1)S(1)} %copy_bitcast_fusion.refs_0_), channel_id=1, source_target_pairs={{32,0},{64,32},{96,64},{0,96},{33,1},{65,33},{97,65},{1,97},{34,2}... | collective-permute-start | bytes 3145736 | tf_op jit(solution)/shard_map/ppermute | solution.py:258
  135.7 25.7 %collective-permute-start.9 = (bf16[4,64,2048]{2,1,0:T(8,128)(2,1)S(1)}, bf16[4,64,2048]{2,1,0:T(8,128)(2,1)}, u32[]{:S(2)}, u32[]{:S(2)}) collective-permute-start(bf16[4,64,2048]{2,1,0:T(8,128)(2,1)S(1)} %copy_bitcast_fusion.refs_0_), channel_id=1, source_target_pairs={{96,0},{0,32},{32,64},{64,96},{97,1},{1,33},{33,65},{65,97},{98,2}... | collective-permute-start | bytes 3145736 | tf_op jit(solution)/shard_map/ppermute | solution.py:258
  136.5 1.1 copy-start.14
  158.2 7.1 %copy-start.3 = (bf16[4,64,2048]{2,1,0:T(8,128)(2,1)}, bf16[4,64,2048]{2,1,0:T(8,128)(2,1)S(1)}, u32[]{:S(2)}) copy-start(bf16[4,64,2048]{2,1,0:T(8,128)(2,1)S(1)} %collective-permute-done.8.refs_0_) | copy-start | bytes 3145732
  161.4 16.7 %collective-permute-start.10 = (bf16[4,64,2048]{2,1,0:T(8,128)(2,1)S(1)}, bf16[4,64,2048]{2,1,0:T(8,128)(2,1)S(1)}, u32[]{:S(2)}, u32[]{:S(2)}) collective-permute-start(bf16[4,64,2048]{2,1,0:T(8,128)(2,1)S(1)} %collective-permute-done.8.refs_0_), channel_id=1, source_target_pairs={{16,0},{0,16},{17,1},{1,17},{18,2},{2,18},{19,3},{3,19},{20,4},{4,... | collective-permute-start | bytes 3145736 | tf_op jit(solution)/shard_map/ppermute | solution.py:258
  162.6 15.5 %collective-permute-start.11 = (bf16[4,64,2048]{2,1,0:T(8,128)(2,1)}, bf16[4,64,2048]{2,1,0:T(8,128)(2,1)S(1)}, u32[]{:S(2)}, u32[]{:S(2)}) collective-permute-start(bf16[4,64,2048]{2,1,0:T(8,128)(2,1)} %collective-permute-done.9.refs_1_), channel_id=1, source_target_pairs={{16,0},{0,16},{17,1},{1,17},{18,2},{2,18},{19,3},{3,19},{20,4},{4,... | collective-permute-start | bytes 3145736 | tf_op jit(solution)/shard_map/ppermute | solution.py:258
  163.7 13.1 %collective-permute-start.12 = (bf16[2,64,2048]{2,1,0:T(8,128)(2,1)S(1)}, bf16[2,64,2048]{2,1,0:T(8,128)(2,1)}, u32[]{:S(2)}, u32[]{:S(2)}) collective-permute-start(bf16[2,64,2048]{2,1,0:T(8,128)(2,1)S(1)} %slice.103), channel_id=1, source_target_pairs={{32,0},{64,32},{96,64},{0,96},{33,1},{65,33},{97,65},{1,97},{34,2}... | collective-permute-start | bytes 1572872 | tf_op jit(solution)/shard_map/ppermute | solution.py:258
  163.8 14.3 %collective-permute-start.13 = (bf16[2,64,2048]{2,1,0:T(8,128)(2,1)S(1)}, bf16[2,64,2048]{2,1,0:T(8,128)(2,1)}, u32[]{:S(2)}, u32[]{:S(2)}) collective-permute-start(bf16[2,64,2048]{2,1,0:T(8,128)(2,1)S(1)} %slice.104), channel_id=1, source_target_pairs={{96,0},{0,32},{32,64},{64,96},{97,1},{1,33},{33,65},{65,97},{98,2}... | collective-permute-start | bytes 1572872 | tf_op jit(solution)/shard_map/ppermute | solution.py:258
  178.1 4.2 %copy-start.15 = (bf16[4,64,2048]{2,1,0:T(8,128)(2,1)}, bf16[4,64,2048]{2,1,0:T(8,128)(2,1)S(1)}, u32[]{:S(2)}) copy-start(bf16[4,64,2048]{2,1,0:T(8,128)(2,1)S(1)} %collective-permute-done.10.refs_0_) | copy-start | bytes 3145732
  178.1 1.6 copy-start.16
  178.1 3.3 %collective-permute-start.14 = (bf16[2,64,2048]{2,1,0:T(8,128)(2,1)}, bf16[2,64,2048]{2,1,0:T(8,128)(2,1)S(1)}, u32[]{:S(2)}, u32[]{:S(2)}) collective-permute-start(bf16[2,64,2048]{2,1,0:T(8,128)(2,1)} %collective-permute-done.12.refs_2_), channel_id=1, source_target_pairs={{16,0},{0,16},{17,1},{1,17},{18,2},{2,18},{19,3},{3,19},{20,4},{4,... | collective-permute-start | bytes 1572872 | tf_op jit(solution)/shard_map/ppermute | solution.py:258
  179.6 2.7 %collective-permute-start.15 = (bf16[2,64,2048]{2,1,0:T(8,128)(2,1)}, bf16[2,64,2048]{2,1,0:T(8,128)(2,1)S(1)}, u32[]{:S(2)}, u32[]{:S(2)}) collective-permute-start(bf16[2,64,2048]{2,1,0:T(8,128)(2,1)} %collective-permute-done.13.refs_3_), channel_id=1, source_target_pairs={{16,0},{0,16},{17,1},{1,17},{18,2},{2,18},{19,3},{3,19},{20,4},{4,... | collective-permute-start | bytes 1572872 | tf_op jit(solution)/shard_map/ppermute | solution.py:258
  180.7 18.8 %copy-start.11 = (f32[2,256]{1,0:T(2,128)S(1)}, f32[2,256]{1,0:T(2,128)}, u32[]{:S(2)}) copy-start(f32[2,256]{1,0:T(2,128)} %get-tuple-element.40) | copy-start | bytes 6148
  180.7 18.8 %copy-start.12 = (f32[2,256]{1,0:T(2,128)S(1)}, f32[2,256]{1,0:T(2,128)}, u32[]{:S(2)}) copy-start(f32[2,256]{1,0:T(2,128)} %get-tuple-element.43) | copy-start | bytes 6148
  181.4 0.9 copy-start.17
  182.3 0.8 copy-start.18
  213.8 3.8 %collective-permute-start.18 = (f32[8,256]{1,0:T(8,128)S(1)}, f32[8,256]{1,0:T(8,128)S(1)}, u32[]{:S(2)}, u32[]{:S(2)}) collective-permute-start(f32[8,256]{1,0:T(8,128)S(1)} %reduce_sum.78), channel_id=1, source_target_pairs={{96,0},{0,32},{32,64},{64,96},{97,1},{1,33},{33,65},{65,97},{98,2}... | collective-permute-start | bytes 24584 | tf_op jit(solution)/shard_map/ppermute | solution.py:258
  214.1 4.0 %collective-permute-start.17 = (f32[8,256]{1,0:T(8,128)S(1)}, f32[8,256]{1,0:T(8,128)S(1)}, u32[]{:S(2)}, u32[]{:S(2)}) collective-permute-start(f32[8,256]{1,0:T(8,128)S(1)} %reduce_sum.78), channel_id=1, source_target_pairs={{64,0},{96,32},{0,64},{32,96},{65,1},{97,33},{1,65},{33,97},{66,2}... | collective-permute-start | bytes 24584 | tf_op jit(solution)/shard_map/ppermute | solution.py:258
  215.1 3.1 %collective-permute-start.16 = (f32[8,256]{1,0:T(8,128)S(1)}, f32[8,256]{1,0:T(8,128)S(1)}, u32[]{:S(2)}, u32[]{:S(2)}) collective-permute-start(f32[8,256]{1,0:T(8,128)S(1)} %reduce_sum.78), channel_id=1, source_target_pairs={{32,0},{64,32},{96,64},{0,96},{33,1},{65,33},{97,65},{1,97},{34,2}... | collective-permute-start | bytes 24584 | tf_op jit(solution)/shard_map/ppermute | solution.py:258
  218.3 4.1 %collective-permute-start.19 = (f32[8,256]{1,0:T(8,128)S(1)}, f32[8,256]{1,0:T(8,128)S(1)}, u32[]{:S(2)}, u32[]{:S(2)}) collective-permute-start(f32[8,256]{1,0:T(8,128)S(1)} %add_add_fusion), channel_id=1, source_target_pairs={{16,0},{0,16},{17,1},{1,17},{18,2},{2,18},{19,3},{3,19},{20,4},{4,... | collective-permute-start | bytes 24584 | tf_op jit(solution)/shard_map/ppermute | solution.py:258
  226.2 11.6 %copy-start.1 = (bf16[4,2048,128]{2,1,0:T(8,128)(2,1)S(1)}, bf16[4,2048,128]{2,1,0:T(8,128)(2,1)}, u32[]{:S(2)}) copy-start(bf16[4,2048,128]{2,1,0:T(8,128)(2,1)} %param.26) | copy-start | bytes 6291460
Sparse Core Ops, SparseCore 0:
  9.7 44.5 all-gather.4
  62.4 49.2 all-gather.2
  127.0 81.3 reduce-scatter.1

commit v8 on v5

--- a/solution.py
+++ b/solution.py
@@ -108,23 +108,15 @@
 
 def logits_kernel(first, parts, place_ref, *refs):
     pieces = refs[: len(parts)]
-    bounds_ref, embedding_ref, out_ref, totals_ref, rows_ref, running, sems = refs[len(parts) :]
+    bounds_ref, embedding_ref, out_ref, totals_ref, rows_ref, running = refs[len(parts) :]
     step, steps = pl.program_id(0), pl.num_programs(0)
     groups, heads, count, depth = rows_ref.shape
     vocab = embedding_ref.shape[0]
 
     @pl.when(step == 0)
     def _():
-        copies = [
-            pltpu.make_async_copy(
-                piece, rows_ref.at[group, low : low + piece.shape[0]], sems.at[number]
-            )
-            for number, (piece, (group, low)) in enumerate(zip(pieces, parts))
-        ]
-        for copy in copies:
-            copy.start()
-        for copy in copies:
-            copy.wait()
+        for piece, (group, low) in zip(pieces, parts):
+            rows_ref[group, low : low + piece.shape[0]] = piece[...]
         running[...] = jnp.zeros_like(running)
 
     every = rows_ref[...].reshape(groups * heads * count, depth)
@@ -159,36 +151,37 @@
             )
 
 
-def some_logits(call, place, pieces, parts, bounds, embedding):
-    first, last = CALLS[call]
-    groups = last - first
+def some_logits(first, shape, place, pieces, parts, bounds, embedding):
+    groups, heads = shape
     count, depth = pieces[0].shape[1:]
     vocab_width = embedding.shape[0]
     vocab = min(VOCAB_BLOCK, vocab_width)
-    size = groups * HEADS * count
+    size = groups * heads * count
     spec = pl.BlockSpec
     return pl.pallas_call(
         functools.partial(logits_kernel, first, parts),
         out_shape=(
-            jax.ShapeDtypeStruct((groups, HEADS, count, vocab_width), BF),
-            jax.ShapeDtypeStruct((groups, HEADS * count), F32),
+            jax.ShapeDtypeStruct((groups, heads, count, vocab_width), BF),
+            jax.ShapeDtypeStruct((groups, heads * count), F32),
         ),
         grid_spec=pltpu.PrefetchScalarGridSpec(
             num_scalar_prefetch=1,
             grid=(vocab_width // vocab,),
-            in_specs=[spec(memory_space=pl.ANY)] * len(pieces)
+            in_specs=[
+                spec(piece.shape, lambda j, p: (0, 0, 0), pipeline_mode=pl.Buffered(1))
+                for piece in pieces
+            ]
             + [
                 spec(bounds.shape, lambda j, p: (0, 0, 0)),
                 spec((vocab, depth), lambda j, p: (j, 0)),
             ],
             out_specs=(
-                spec((groups, HEADS, count, vocab), lambda j, p: (0, 0, 0, j)),
-                spec((groups, HEADS * count), lambda j, p: (0, 0)),
+                spec((groups, heads, count, vocab), lambda j, p: (0, 0, 0, j)),
+                spec((groups, heads * count), lambda j, p: (0, 0)),
             ),
             scratch_shapes=[
-                pltpu.VMEM((groups, HEADS, count, depth), BF),
+                pltpu.VMEM((groups, heads, count, depth), BF),
                 pltpu.VMEM((size, 128), F32),
-                pltpu.SemaphoreType.DMA((len(pieces),)),
             ],
         ),
         compiler_params=pltpu.CompilerParams(
@@ -203,17 +196,19 @@
 
 
 def finish_kernel(place_ref, *refs):
-    tables, logs_ref, out_ref = refs[: len(CALLS)], refs[-2], refs[-1]
+    logs_ref, out_ref = refs[-2:]
+    tables = ((refs[0],), refs[1:3], (refs[3],))
     step = pl.program_id(0)
     core = lax.rem(place_ref[1], CORE)
-    for table_ref, (first, last) in zip(tables, CALLS):
+    for shared, (first, last) in zip(tables, CALLS):
 
         @pl.when((step >= first // CORE) & (step < last // CORE))
-        def _(table_ref=table_ref):
+        def _(shared=shared):
+            heads = HEADS // len(shared)
             for position in range(CORE):
                 source = lax.rem(position + core, CORE)
                 for head in range(HEADS):
-                    values = table_ref[source, head].astype(F32)
+                    values = shared[head // heads][source, head % heads].astype(F32)
                     shifted = values - logs_ref[position, :, head : head + 1]
                     out_ref[head, position] = jnp.where(
                         values > 0.5 * HIDDEN, shifted, 0.0
@@ -225,22 +220,23 @@
     groups = len(GROUPS)
     spec = pl.BlockSpec
 
-    def table_spec(first, last):
+    def table_spec(table, first, last):
         return spec(
-            (CORE, HEADS, count, vocab_width),
+            (CORE, table.shape[1], count, vocab_width),
             lambda k, p: (jnp.clip(k - first // CORE, 0, (last - first) // CORE - 1), 0, 0, 0),
         )
 
     def pair(k, p):
         return lax.div(p[1 + CORE * k], CORE)
 
+    calls = (CALLS[0], CALLS[1], CALLS[1], CALLS[2])
     return pl.pallas_call(
         finish_kernel,
         out_shape=jax.ShapeDtypeStruct((HEADS, groups, count, vocab_width), BF),
         grid_spec=pltpu.PrefetchScalarGridSpec(
             num_scalar_prefetch=1,
             grid=(groups // CORE,),
-            in_specs=[table_spec(*call) for call in CALLS]
+            in_specs=[table_spec(table, *call) for table, call in zip(tables, calls)]
             + [spec((CORE, count, HEADS), lambda k, p: (pair(k, p), 0, 0))],
             out_specs=spec(
                 (HEADS, CORE, count, vocab_width), lambda k, p: (0, pair(k, p), 0, 0)
@@ -403,44 +399,66 @@
     place = jnp.stack([start] + order).astype(jnp.int32)
     bounds = jnp.repeat(tenant_ranges, ACC, axis=0).reshape(Y * CORE, rows, 2)
     half = HEADS // 2
-    next_up, next_down = ring(drafts, "y", Y, 1), ring(drafts, "y", Y, 3)
+    pair = ((0, 0), (1, 0))
+    four = pair + ((2, 0), (3, 0))
+    low = drafts[:half]
+    up_low, down_low = ring(low, "y", Y, 1), ring(low, "y", Y, 3)
     beside = ring(drafts, "core", CORE, 1)
+    high = after(drafts[half:], beside)
+    up_high, down_high = ring(high, "y", Y, 1), ring(high, "y", Y, 3)
     table_a, totals_a = some_logits(
-        0, place, [drafts, beside], ((0, 0), (1, 0)), bounds, embedding
-    )
-    next_up, next_down = after([next_up, next_down], totals_a)
-    across = [ring(next_up[:half], "y", Y, 1), ring(next_down[half:], "y", Y, 3)]
-    beside_up, beside_down = ring(next_up, "core", CORE, 1), ring(next_down, "core", CORE, 1)
+        0, (2, HEADS), place, [drafts, beside], pair, bounds, embedding
+    )
+    up_low, down_low = after([up_low, down_low], totals_a)
+    across_low = ring(up_low, "y", Y, 1)
+    beside_low = [ring(piece, "core", CORE, 1) for piece in (up_low, down_low)]
     table_b, totals_b = some_logits(
-        1,
+        2,
+        (4, half),
         place,
-        [next_up, beside_up, next_down, beside_down],
-        ((0, 0), (1, 0), (2, 0), (3, 0)),
+        [up_low, beside_low[0], down_low, beside_low[1]],
+        four,
         bounds,
         embedding,
     )
-    across = after(across, totals_b)
-    beside_across = [ring(piece, "core", CORE, 1) for piece in across]
+    up_high, down_high = after([up_high, down_high], totals_b)
+    across_high = ring(down_high, "y", Y, 3)
+    beside_high = [ring(piece, "core", CORE, 1) for piece in (up_high, down_high)]
     table_c, totals_c = some_logits(
         2,
+        (4, half),
+        place,
+        [up_high, beside_high[0], down_high, beside_high[1]],
+        four,
+        bounds,
+        embedding,
+    )
+    across = after([across_low, across_high], totals_c)
+    beside_across = [ring(piece, "core", CORE, 1) for piece in across]
+    table_d, totals_d = some_logits(
+        6,
+        (2, HEADS),
         place,
         across + beside_across,
         ((0, 0), (0, half), (1, 0), (1, half)),
         bounds,
         embedding,
     )
-    sums = jnp.concatenate([totals_a, totals_b, totals_c], axis=0)
+    totals_b = jnp.concatenate([totals_b, totals_c], axis=1)
+    sums = jnp.concatenate([totals_a, totals_b, totals_d], axis=0)
     here = place[1:, None] == jnp.arange(Y * CORE, dtype=jnp.int32)[None, :]
     sums = jnp.sum(jnp.where(here[:, :, None], sums[:, None, :], 0.0), axis=0)
     sums = jnp.sum(spread(sums, XZ, units), axis=0)
-    whole = sums + ring(sums, "y", Y, 1) + ring(sums, "y", Y, 2) + ring(sums, "y", Y, 3)
+    around = [ring(sums, "y", Y, shift) for shift in range(1, Y)]
+    mlp_sum = after(mlp_sum, sums)
+    tree_out = (first.astype(F32) + rms_scale(mlp_sum, ff_post_gain)).astype(BF)
+    around = after(around, tree_out)
+    whole = sums + around[0] + around[1] + around[2]
     whole = whole + ring(whole, "core", CORE, 1)
     logs = jnp.transpose(jnp.log(whole).reshape(Y * CORE, HEADS, rows), (0, 2, 1))
-    draft_logprobs = finish(place, [table_a, table_b, table_c], logs).reshape(
+    draft_logprobs = finish(place, [table_a, table_b, table_c, table_d], logs).reshape(
         HEADS, Y * CORE * rows, vocab_width
     )
-    mlp_sum = after(mlp_sum, sums)
-    tree_out = (first.astype(F32) + rms_scale(mlp_sum, ff_post_gain)).astype(BF)
     return (tree_out, draft_logprobs)
 
 

time: 245 us -> 238 us (0.971)
  waiting for transfers between devices: 45.8 us -> 35.5 us
  starting transfers between devices: 39.4 us -> 43.1 us
    ppermute x17 -> x21, waiting for transfers between devices: 22.2 us -> 11.9 us  [ring(): lax.ppermute(values, axis, [((i + shift) % size, i) for i in range(size)])]
    ppermute x17 -> x21, starting transfers between devices: 24.1 us -> 27.9 us  [ring(): lax.ppermute(values, axis, [((i + shift) % size, i) for i in range(size)])]
    pallas_call x3 -> x4, Pallas kernels: 40.1 us -> 42 us  [some_logits(): pl.pallas_call(functools.partial(logits_kernel, first, parts), out_shape=...]
    unnamed x51 -> x64, local copies, waits for them, and re-layouts: 11.2 us -> 11.9 us
  transfers between devices with their start and end apart: 24 -> 28, of which waited for: 15 -> 16; matrix products, arithmetic and copies ran while one was open for 17% -> 17% of each run, Pallas kernels for 22% -> 19%
where the time goes in v8:
time: 238 us; the launch traced here: 236 us
  Pallas kernels  56.3 us (24%)
  starting transfers between devices  43.1 us (18%)
  blocking collectives  37.1 us (16%)
  waiting for transfers between devices  35.5 us (15%)
  matrix products  23.3 us (10%)
  local copies, waits for them, and re-layouts  20.7 us (9%)
  between operations  14.9 us (6%)
  other arithmetic  5.5 us (2%)
    pallas_call x4, Pallas kernels, some_logits(): pl.pallas_call(functools.partial(logits_kernel, first, parts), out_shape=...  42 us
    ppermute x21, starting transfers between devices, ring(): lax.ppermute(values, axis, [((i + shift) % size, i) for i in range(size)])  27.9 us
    all_to_all x2, blocking collectives, swap(): return lax.all_to_all(copies, axes, split_axis=0, concat_axis=0, tiled=True)  23.3 us
    all_to_all x4, waiting for transfers between devices, swap(): return lax.all_to_all(copies, axes, split_axis=0, concat_axis=0, tiled=True)  21.6 us
    all_to_all x4, starting transfers between devices, swap(): return lax.all_to_all(copies, axes, split_axis=0, concat_axis=0, tiled=True)  15 us
    all_gather x1, blocking collectives, out_projection(): group = lax.all_gather(attended, 'z', axis=0, tiled=True)  13.8 us
    unnamed x64, local copies, waits for them, and re-layouts  11.9 us
    dot_general x2, matrix products, unit_terms(): lax.dot_general(active, weights[2], (((1,), (1,)), ((), ())), preferred_e...  11.9 us
  transfers between devices with their start and end apart: 28, of which 16 were waited for; matrix products, arithmetic and copies ran while one was open for 17% of the time, Pallas kernels for 19%

profile of v8, /device:TPU:1, one launch (start us, length us, event | category | flops | bytes accessed | tf_op | source)
XLA Modules:
  0.0 236.5 jit_solution(11583395104553642002)
XLA Ops:
  7.9 1.0 constant_dynamic-slice_fusion
  8.9 3.4 %collective-permute-start = (bf16[1024,128]{1,0:T(8,128)(2,1)S(1)}, bf16[1024,128]{1,0:T(8,128)(2,1)S(1)}, u32[]{:S(2)}, u32[]{:S(2)}) collective-permute-start(bf16[1024,128]{1,0:T(8,128)(2,1)S(1)} %constant_dynamic-slice_fusion), channel_id=1, source_target_pairs={{4,0},{8,4},{12,8},{0,12},{5,1},{9,5},{13,9},{1,13},{6,2},{10,6},{... | collective-permute-start | bytes 786440 | tf_op jit(solution)/shard_map/ppermute | solution.py:270
  14.1 0.9 copy.48
  15.0 0.7 copy.33.parents_ref
  15.7 2.2 copy-done.2
  17.9 0.9 copy-done.3
  18.8 3.9 %shard_map.167 = bf16[48,2048]{1,0:T(8,128)(2,1)S(1)} custom-call(s32[1]{0:T(128)S(6)} %copy.52.length_ref, bf16[48,2048]{1,0:T(8,128)(2,1)S(1)} %copy-done.3, bf16[2,48,512]{2,1,0:T(8,128)(2,1)S(1)} %bitcast.104, s32[48,1]{1,0:T(8,128)S(1)} %copy.33.parents_ref, bf16[1,2,2,2048,256]{4,3,2,1,0:T(8,128)(2,1)S(1)} %copy-done.2, ...), custom_call_target="tpu_custom_call" | custom-call | flops 805306368 | bytes 4194304 | tf_op jit(solution)/shard_map/pallas_call | solution.py:78
  23.5 0.7 copy-done.7
  24.2 3.5 %collective-permute-done.2 = bf16[1024,128]{1,0:T(8,128)(2,1)} collective-permute-done((bf16[1024,128]{1,0:T(8,128)(2,1)S(1)}, bf16[1024,128]{1,0:T(8,128)(2,1)}, u32[]{:S(2)}, u32[]{:S(2)}) %collective-permute-start.2) | collective-permute-done | bytes 262176 | tf_op jit(solution)/shard_map/ppermute | solution.py:270
  27.7 1.0 constant_dynamic-update-slice_fusion.3
  28.7 1.0 constant_dynamic-update-slice_fusion.2
  29.8 1.1 constant_dynamic-update-slice_fusion.1
  30.8 1.0 constant_dynamic-update-slice_fusion
  32.4 13.8 %all_gather.9 = bf16[192,2048]{1,0:T(8,128)(2,1)S(1)} all-gather(bf16[48,2048]{1,0:T(8,128)(2,1)S(1)} %shard_map.167), channel_id=1, replica_groups=mesh['y'=4,'core'=2,'x'=4,'z'=4] {'z'}, dimensions={0}, use_global_device_ids=true | all-gather | bytes 983040 | tf_op jit(solution)/shard_map/all_gather | solution.py:311
  46.2 1.6 fusion.34
  47.8 1.1 fusion.17
  48.9 3.7 %all-to-all-start = ((bf16[4,48,512]{2,1,0:T(8,128)(2,1)}), bf16[4,48,512]{2,1,0:T(8,128)(2,1)S(1)}, u32[]{:S(2)}, u32[]{:S(2)}) async-start(bf16[4,48,512]{2,1,0:T(8,128)(2,1)} %bitcast.2), calls=%async_computation | async-start | bytes 393216 | tf_op jit(solution)/shard_map/all_to_all | solution.py:278
  52.6 5.1 %all-to-all-done = bf16[4,48,512]{2,1,0:T(8,128)(2,1)S(1)} async-done(((bf16[4,48,512]{2,1,0:T(8,128)(2,1)}), bf16[4,48,512]{2,1,0:T(8,128)(2,1)S(1)}, u32[]{:S(2)}, u32[]{:S(2)}) %all-to-all-start) | async-done | bytes 196640 | tf_op jit(solution)/shard_map/all_to_all | solution.py:278
  58.4 0.8 fusion.32
  59.3 1.1 convolution_convert_fusion.2
  60.5 10.1 %all_to_all.30 = bf16[16,4,2048]{2,1,0:T(4,128)(2,1)S(1)} all-to-all(bf16[16,4,2048]{2,1,0:T(4,128)(2,1)S(1)} %broadcast_in_dim.23), channel_id=1, replica_groups=mesh['y'=4,'core'=2,'x'=4,'z'=4] {'x','z'}, dimensions={0} | all-to-all | bytes 524288 | tf_op jit(solution)/shard_map/all_to_all | solution.py:278
  70.7 2.4 %fusion.43 = f32[64,512]{1,0:T(8,128)S(1)} fusion(bf16[64,2048]{1,0:T(8,128)(2,1)S(1)} %reshape.104, bf16[3,2048,512]{1,2,0:T(8,128)(2,1)} %all-gather.5.cloned.1.call-done), kind=kOutput, calls=%fused_computation.68 | convolution fusion | flops 134479872 | bytes 2490368 | tf_op jit(solution)/shard_map/dot_general | solution.py:331
  73.1 3.4 %convolution_convert_fusion.1 = bf16[64,2048]{1,0:T(8,128)(2,1)S(1)} fusion(bf16[3,2048,512]{1,2,0:T(8,128)(2,1)} %all-gather.5.cloned.1.call-done, f32[64,512]{1,0:T(8,128)S(1)} %fusion.43, bf16[64,2048]{1,0:T(8,128)(2,1)S(1)} %reshape.104), kind=kOutput, calls=%fused_computation.2 | convolution fusion | flops 268632064 | bytes 4849664 | tf_op jit(solution)/shard_map/dot_general | solution.py:334
  76.6 0.8 reshape.105
  77.4 3.5 %all-to-all-start.2 = ((bf16[16,4,2048]{2,1,0:T(4,128)(2,1)}), bf16[16,4,2048]{2,1,0:T(4,128)(2,1)S(1)}, u32[]{:S(2)}, u32[]{:S(2)}) async-start(bf16[16,4,2048]{2,1,0:T(4,128)(2,1)} %reshape.105), calls=%async_computation.2 | async-start | bytes 524288 | tf_op jit(solution)/shard_map/all_to_all | solution.py:278
  81.0 7.2 %all-to-all-done.2 = bf16[16,4,2048]{2,1,0:T(4,128)(2,1)S(1)} async-done(((bf16[16,4,2048]{2,1,0:T(4,128)(2,1)}), bf16[16,4,2048]{2,1,0:T(4,128)(2,1)S(1)}, u32[]{:S(2)}, u32[]{:S(2)}) %all-to-all-start.2) | async-done | bytes 262176 | tf_op jit(solution)/shard_map/all_to_all | solution.py:278
  88.9 0.8 broadcast_in_dim.24
  89.7 3.5 %all-to-all-start.3 = ((bf16[16,4,2048]{2,1,0:T(4,128)(2,1)}), bf16[16,4,2048]{2,1,0:T(4,128)(2,1)S(1)}, u32[]{:S(2)}, u32[]{:S(2)}) async-start(bf16[16,4,2048]{2,1,0:T(4,128)(2,1)} %broadcast_in_dim.24), calls=%async_computation.3 | async-start | bytes 524288 | tf_op jit(solution)/shard_map/all_to_all | solution.py:278
  93.2 9.2 %all-to-all-done.3 = bf16[16,4,2048]{2,1,0:T(4,128)(2,1)S(1)} async-done(((bf16[16,4,2048]{2,1,0:T(4,128)(2,1)}), bf16[16,4,2048]{2,1,0:T(4,128)(2,1)S(1)}, u32[]{:S(2)}, u32[]{:S(2)}) %all-to-all-start.3) | async-done | bytes 262176 | tf_op jit(solution)/shard_map/all_to_all | solution.py:278
  103.1 1.2 broadcast_in_dim.25
  104.4 4.3 %all-to-all-start.4 = ((bf16[16,4,64,128]{3,2,1,0:T(8,128)(2,1)}), bf16[16,4,64,128]{3,2,1,0:T(8,128)(2,1)S(1)}, u32[]{:S(2)}, u32[]{:S(2)}) async-start(bf16[16,4,64,128]{3,2,1,0:T(8,128)(2,1)} %broadcast_in_dim.25), calls=%async_computation.4 | async-start | bytes 2097152 | tf_op jit(solution)/shard_map/all_to_all | solution.py:278
  108.9 1.3 all-gather.3.cloned.1.call-done
  110.2 4.4 %fusion.4 = f32[768,512]{1,0:T(8,128)S(1)} fusion(bf16[768,2048]{1,0:T(8,128)(2,1)} %all-gather.3.cloned.1.call-done, bf16[3,2048,512]{1,2,0:T(8,128)(2,1)} %all-gather.5.cloned.1.call-done), kind=kOutput, calls=%fused_computation.12 | convolution fusion | flops 1610612736 | bytes 6815744 | tf_op jit(solution)/shard_map/dot_general | solution.py:331
  114.6 8.5 %convolution_convert_fusion = bf16[768,2048]{1,0:T(8,128)(2,1)} fusion(bf16[3,2048,512]{1,2,0:T(8,128)(2,1)} %all-gather.5.cloned.1.call-done, f32[768,512]{1,0:T(8,128)S(1)} %fusion.4, bf16[768,2048]{1,0:T(8,128)(2,1)} %all-gather.3.cloned.1.call-done), kind=kOutput, calls=%fused_computation | convolution fusion | flops 3226730496 | bytes 12058624 | tf_op jit(solution)/shard_map/dot_general | solution.py:334
  123.3 6.6 %collective-permute-start.4 = (bf16[4,64,2048]{2,1,0:T(8,128)(2,1)S(1)}, bf16[4,64,2048]{2,1,0:T(8,128)(2,1)}, u32[]{:S(2)}, u32[]{:S(2)}) collective-permute-start(bf16[4,64,2048]{2,1,0:T(8,128)(2,1)S(1)} %copy_bitcast_fusion.refs_0_), channel_id=1, source_target_pairs={{16,0},{0,16},{17,1},{1,17},{18,2},{2,18},{19,3},{3,19},{20,4},{4,... | collective-permute-start | bytes 3145736 | tf_op jit(solution)/shard_map/ppermute | solution.py:270
  130.1 2.8 %collective-permute-start.5 = (bf16[2,64,2048]{2,1,0:T(8,128)(2,1)S(1)}, bf16[2,64,2048]{2,1,0:T(8,128)(2,1)S(1)}, u32[]{:S(2)}, u32[]{:S(2)}) collective-permute-start(bf16[2,64,2048]{2,1,0:T(8,128)(2,1)S(1)} %bitcast.108), channel_id=1, source_target_pairs={{32,0},{64,32},{96,64},{0,96},{33,1},{65,33},{97,65},{1,97},{34,2}... | collective-permute-start | bytes 1572872 | tf_op jit(solution)/shard_map/ppermute | solution.py:270
  133.8 0.7 broadcast_in_dim.27
  134.5 10.4 %shard_map.168 = (bf16[2,4,64,2048]{3,2,1,0:T(8,128)(2,1)}, f32[2,256]{1,0:T(2,128)}) custom-call(s32[9]{0:T(128)} %stack.42.place_ref, bf16[4,64,2048]{2,1,0:T(8,128)(2,1)} %copy-done.5, bf16[4,64,2048]{2,1,0:T(8,128)(2,1)} %collective-permute-done.4.refs_1_, s32[8,64,2]{2,1,0:T(8,128)} %bitcast.112, bf16[2048,2048]{1,0:T(8,128)(2,1)} %refs_5_.5), custom_call_target="tpu_custom_call" | custom-call | flops 4294967296 | bytes 10485760 | tf_op jit(solution)/shard_map/pallas_call | solution.py:161
  144.9 1.7 collective-permute-done.6.refs_2_
  146.7 1.9 collective-permute-start.7
  149.3 1.0 collective-permute-start.10
  151.7 0.8 copy-done.25
  152.5 10.5 %shard_map.169 = (bf16[4,2,64,2048]{3,2,1,0:T(8,128)(2,1)}, f32[4,128]{1,0:T(4,128)}) custom-call(s32[9]{0:T(128)} %stack.42.place_ref, bf16[2,64,2048]{2,1,0:T(8,128)(2,1)} %copy-done.17, bf16[2,64,2048]{2,1,0:T(8,128)(2,1)} %copy-done.23, bf16[2,64,2048]{2,1,0:T(8,128)(2,1)} %collective-permute-done.6.refs_2_, bf16[2,64,2048]{2,1,0:T(8,128)(2,1)} %copy-done.25, ...), custom_call_target="tpu_custom_call" | custom-call | flops 4294967296 | bytes 10485760 | tf_op jit(solution)/shard_map/pallas_call | solution.py:161
  163.4 1.5 collective-permute-start.11
  165.5 0.8 collective-permute-start.14
  166.4 0.7 collective-permute-done.12.refs_3_
  167.2 0.8 copy-done.27
  168.0 10.6 %shard_map.170 = (bf16[4,2,64,2048]{3,2,1,0:T(8,128)(2,1)}, f32[4,128]{1,0:T(4,128)}) custom-call(s32[9]{0:T(128)} %stack.42.place_ref, bf16[2,64,2048]{2,1,0:T(8,128)(2,1)} %copy-done.21, bf16[2,64,2048]{2,1,0:T(8,128)(2,1)} %copy-done.26, bf16[2,64,2048]{2,1,0:T(8,128)(2,1)} %copy-done.19, bf16[2,64,2048]{2,1,0:T(8,128)(2,1)} %copy-done.27, ...), custom_call_target="tpu_custom_call" | custom-call | flops 4294967296 | bytes 10485760 | tf_op jit(solution)/shard_map/pallas_call | solution.py:161
  178.7 0.8 collective-permute-done.14.refs_1_
  179.5 1.6 collective-permute-start.15
  181.2 1.4 collective-permute-done.15.refs_2_
  182.6 0.7 collective-permute-done.16.refs_3_
  183.4 0.8 copy-done.24
  184.2 10.5 %shard_map.171 = (bf16[2,4,64,2048]{3,2,1,0:T(8,128)(2,1)}, f32[2,256]{1,0:T(2,128)}) custom-call(s32[9]{0:T(128)} %stack.42.place_ref, bf16[2,64,2048]{2,1,0:T(8,128)(2,1)} %copy-done.18, bf16[2,64,2048]{2,1,0:T(8,128)(2,1)} %copy-done.20, bf16[2,64,2048]{2,1,0:T(8,128)(2,1)} %copy-done.22, bf16[2,64,2048]{2,1,0:T(8,128)(2,1)} %copy-done.24, ...), custom_call_target="tpu_custom_call" | custom-call | flops 4294967296 | bytes 10485760 | tf_op jit(solution)/shard_map/pallas_call | solution.py:161
  194.7 0.7 pad_maximum_fusion.5
  195.5 13.2 %all_to_all.31 = f32[16,8,256]{2,1,0:T(8,128)S(1)} all-to-all(f32[16,8,256]{2,1,0:T(8,128)S(1)} %broadcast_in_dim.30), channel_id=1, replica_groups=mesh['y'=4,'core'=2,'x'=4,'z'=4] {'x','z'}, dimensions={0} | all-to-all | bytes 262144 | tf_op jit(solution)/shard_map/all_to_all | solution.py:278
  209.3 1.3 collective-permute-start.18
  210.6 1.1 fusion.28
  211.7 1.8 fusion.33
  213.4 0.9 collective-permute-done.19
  214.3 3.5 %collective-permute-start.20 = (f32[8,256]{1,0:T(8,128)S(1)}, f32[8,256]{1,0:T(8,128)S(1)}, u32[]{:S(2)}, u32[]{:S(2)}) collective-permute-start(f32[8,256]{1,0:T(8,128)S(1)} %add_add_fusion), channel_id=1, source_target_pairs={{16,0},{0,16},{17,1},{1,17},{18,2},{2,18},{19,3},{3,19},{20,4},{4,... | collective-permute-start | bytes 24584 | tf_op jit(solution)/shard_map/ppermute | solution.py:270
  217.8 0.8 collective-permute-done.20
  218.7 0.9 copy.38
  219.6 10.3 %shard_map.172 = bf16[4,8,64,2048]{3,2,1,0:T(8,128)(2,1)} custom-call(s32[9]{0:T(128)} %stack.42.place_ref, bf16[2,4,64,2048]{3,2,1,0:T(8,128)(2,1)} %get-tuple-element.47.refs_0_, bf16[4,2,64,2048]{3,2,1,0:T(8,128)(2,1)} %get-tuple-element.48.refs_1_, bf16[4,2,64,2048]{3,2,1,0:T(8,128)(2,1)} %get-tuple-element.49.refs_2_, ...), custom_call_target="tpu_custom_call" | custom-call | flops 12582912 | bytes 16777216 | tf_op jit(solution)/shard_map/pallas_call | solution.py:233
  (125 shorter events, 11.0 us)
Async XLA Ops:
  7.2 95.5 %copy-start = (bf16[4,2048,128]{2,1,0:T(8,128)(2,1)S(1)}, bf16[4,2048,128]{2,1,0:T(8,128)(2,1)}, u32[]{:S(2)}) copy-start(bf16[4,2048,128]{2,1,0:T(8,128)(2,1)} %param.26) | copy-start | bytes 6291460
  7.2 63.5 %all-gather.5.cloned.1.call-start = ((), (), s32[]{:S(2)}) async-start(), calls=%async_computation.8 | async-start | bytes 7077888 | tf_op jit(solution)/shard_map/all_gather | solution.py:362
  8.9 13.9 %copy-start.4 = (bf16[1024,128]{1,0:T(8,128)(2,1)}, bf16[1024,128]{1,0:T(8,128)(2,1)S(1)}, u32[]{:S(2)}) copy-start(bf16[1024,128]{1,0:T(8,128)(2,1)S(1)} %constant_dynamic-slice_fusion) | copy-start | bytes 786436
  8.9 13.9 %collective-permute-start = (bf16[1024,128]{1,0:T(8,128)(2,1)S(1)}, bf16[1024,128]{1,0:T(8,128)(2,1)S(1)}, u32[]{:S(2)}, u32[]{:S(2)}) collective-permute-start(bf16[1024,128]{1,0:T(8,128)(2,1)S(1)} %constant_dynamic-slice_fusion), channel_id=1, source_target_pairs={{4,0},{8,4},{12,8},{0,12},{5,1},{9,5},{13,9},{1,13},{6,2},{10,6},{... | collective-permute-start | bytes 786440 | tf_op jit(solution)/shard_map/ppermute | solution.py:270
  12.3 10.5 %collective-permute-start.1 = (bf16[1024,128]{1,0:T(8,128)(2,1)S(1)}, bf16[1024,128]{1,0:T(8,128)(2,1)S(1)}, u32[]{:S(2)}, u32[]{:S(2)}) collective-permute-start(bf16[1024,128]{1,0:T(8,128)(2,1)S(1)} %constant_dynamic-slice_fusion), channel_id=1, source_target_pairs={{8,0},{12,4},{0,8},{4,12},{9,1},{13,5},{1,9},{5,13},{10,2},{14,6},... | collective-permute-start | bytes 786440 | tf_op jit(solution)/shard_map/ppermute | solution.py:270
  12.8 14.9 %collective-permute-start.2 = (bf16[1024,128]{1,0:T(8,128)(2,1)S(1)}, bf16[1024,128]{1,0:T(8,128)(2,1)}, u32[]{:S(2)}, u32[]{:S(2)}) collective-permute-start(bf16[1024,128]{1,0:T(8,128)(2,1)S(1)} %constant_dynamic-slice_fusion), channel_id=1, source_target_pairs={{12,0},{0,4},{4,8},{8,12},{13,1},{1,5},{5,9},{9,13},{14,2},{2,6},{... | collective-permute-start | bytes 786440 | tf_op jit(solution)/shard_map/ppermute | solution.py:270
  15.7 2.2 copy-start.2
  17.9 0.9 copy-start.3
  22.8 0.7 copy-start.6
  23.5 0.7 copy-start.7
  31.8 14.3 %collective-permute-start.3 = (bf16[1024,512]{1,0:T(8,128)(2,1)S(1)}, bf16[1024,512]{1,0:T(8,128)(2,1)}, u32[]{:S(2)}, u32[]{:S(2)}) collective-permute-start(bf16[1024,512]{1,0:T(8,128)(2,1)S(1)} %constant_dynamic-update-slice_fusion), channel_id=1, source_target_pairs={{16,0},{0,16},{17,1},{1,17},{18,2},{2,18},{19,3},{3,19},{20,4},{4,... | collective-permute-start | bytes 3145736 | tf_op jit(solution)/shard_map/ppermute | solution.py:270
  46.2 6.4 %copy-start.9 = (bf16[2048]{0:T(1024)(128)(2,1)S(1)}, bf16[2048]{0:T(1024)(128)(2,1)}, u32[]{:S(2)}) copy-start(bf16[2048]{0:T(1024)(128)(2,1)} %param.28) | copy-start | bytes 12292
  46.2 6.4 %copy-start.10 = (bf16[2048]{0:T(1024)(128)(2,1)S(1)}, bf16[2048]{0:T(1024)(128)(2,1)}, u32[]{:S(2)}) copy-start(bf16[2048]{0:T(1024)(128)(2,1)} %param.29) | copy-start | bytes 12292
  47.8 10.3 %copy-start.8 = (bf16[48,2048]{1,0:T(8,128)(2,1)S(1)}, bf16[48,2048]{1,0:T(8,128)(2,1)}, u32[]{:S(2)}) copy-start(bf16[48,2048]{1,0:T(8,128)(2,1)} %param.16) | copy-start | bytes 589828
  48.9 10.4 %copy-start.28 = (s32[1,4]{1,0:T(1,128)S(1)}, s32[1,4]{1,0:T(1,128)}, u32[]{:S(2)}) copy-start(s32[1,4]{1,0:T(1,128)} %param.22) | copy-start | bytes 52
  48.9 8.8 %all-to-all-start = ((bf16[4,48,512]{2,1,0:T(8,128)(2,1)}), bf16[4,48,512]{2,1,0:T(8,128)(2,1)S(1)}, u32[]{:S(2)}, u32[]{:S(2)}) async-start(bf16[4,48,512]{2,1,0:T(8,128)(2,1)} %bitcast.2), calls=%async_computation | async-start | bytes 393216 | tf_op jit(solution)/shard_map/all_to_all | solution.py:278
  52.6 57.6 %all-gather.3.cloned.1.call-start = ((), (), s32[]{:S(2)}) async-start(), calls=%async_computation.7 | async-start | bytes 3342336 | tf_op jit(solution)/shard_map/all_gather | solution.py:377
  73.1 7.8 %copy-start.11 = (bf16[2048]{0:T(1024)(128)(2,1)S(1)}, bf16[2048]{0:T(1024)(128)(2,1)}, u32[]{:S(2)}) copy-start(bf16[2048]{0:T(1024)(128)(2,1)} %param.30) | copy-start | bytes 12292
  73.1 7.8 %copy-start.12 = (bf16[2048]{0:T(1024)(128)(2,1)S(1)}, bf16[2048]{0:T(1024)(128)(2,1)}, u32[]{:S(2)}) copy-start(bf16[2048]{0:T(1024)(128)(2,1)} %param.31) | copy-start | bytes 12292
  77.4 10.8 %all-to-all-start.2 = ((bf16[16,4,2048]{2,1,0:T(4,128)(2,1)}), bf16[16,4,2048]{2,1,0:T(4,128)(2,1)S(1)}, u32[]{:S(2)}, u32[]{:S(2)}) async-start(bf16[16,4,2048]{2,1,0:T(4,128)(2,1)} %reshape.105), calls=%async_computation.2 | async-start | bytes 524288 | tf_op jit(solution)/shard_map/all_to_all | solution.py:278
  89.7 12.8 %all-to-all-start.3 = ((bf16[16,4,2048]{2,1,0:T(4,128)(2,1)}), bf16[16,4,2048]{2,1,0:T(4,128)(2,1)S(1)}, u32[]{:S(2)}, u32[]{:S(2)}) async-start(bf16[16,4,2048]{2,1,0:T(4,128)(2,1)} %broadcast_in_dim.24), calls=%async_computation.3 | async-start | bytes 524288 | tf_op jit(solution)/shard_map/all_to_all | solution.py:278
  104.4 18.7 %all-to-all-start.4 = ((bf16[16,4,64,128]{3,2,1,0:T(8,128)(2,1)}), bf16[16,4,64,128]{3,2,1,0:T(8,128)(2,1)S(1)}, u32[]{:S(2)}, u32[]{:S(2)}) async-start(bf16[16,4,64,128]{3,2,1,0:T(8,128)(2,1)} %broadcast_in_dim.25), calls=%async_computation.4 | async-start | bytes 2097152 | tf_op jit(solution)/shard_map/all_to_all | solution.py:278
  108.7 101.9 %reduce-scatter.2.cloned.1.call-start = ((), (), s32[]{:S(2)}) async-start(), calls=%async_computation.9 | async-start | bytes 3342336 | tf_op jit(solution)/shard_map/reduce_scatter | solution.py:394
  123.2 6.8 %copy-start.5 = (bf16[4,64,2048]{2,1,0:T(8,128)(2,1)}, bf16[4,64,2048]{2,1,0:T(8,128)(2,1)S(1)}, u32[]{:S(2)}) copy-start(bf16[4,64,2048]{2,1,0:T(8,128)(2,1)S(1)} %copy_bitcast_fusion.refs_0_) | copy-start | bytes 3145732
  123.3 9.7 %copy-start.16 = (s32[128,2]{0,1:T(2,128)S(1)}, s32[128,2]{0,1:T(2,128)}, u32[]{:S(2)}) copy-start(s32[128,2]{0,1:T(2,128)} %param.23) | copy-start | bytes 3076
  123.3 10.5 %collective-permute-start.4 = (bf16[4,64,2048]{2,1,0:T(8,128)(2,1)S(1)}, bf16[4,64,2048]{2,1,0:T(8,128)(2,1)}, u32[]{:S(2)}, u32[]{:S(2)}) collective-permute-start(bf16[4,64,2048]{2,1,0:T(8,128)(2,1)S(1)} %copy_bitcast_fusion.refs_0_), channel_id=1, source_target_pairs={{16,0},{0,16},{17,1},{1,17},{18,2},{2,18},{19,3},{3,19},{20,4},{4,... | collective-permute-start | bytes 3145736 | tf_op jit(solution)/shard_map/ppermute | solution.py:270
  130.1 14.8 %collective-permute-start.5 = (bf16[2,64,2048]{2,1,0:T(8,128)(2,1)S(1)}, bf16[2,64,2048]{2,1,0:T(8,128)(2,1)S(1)}, u32[]{:S(2)}, u32[]{:S(2)}) collective-permute-start(bf16[2,64,2048]{2,1,0:T(8,128)(2,1)S(1)} %bitcast.108), channel_id=1, source_target_pairs={{32,0},{64,32},{96,64},{0,96},{33,1},{65,33},{97,65},{1,97},{34,2}... | collective-permute-start | bytes 1572872 | tf_op jit(solution)/shard_map/ppermute | solution.py:270
  133.0 13.7 %collective-permute-start.6 = (bf16[2,64,2048]{2,1,0:T(8,128)(2,1)S(1)}, bf16[2,64,2048]{2,1,0:T(8,128)(2,1)}, u32[]{:S(2)}, u32[]{:S(2)}) collective-permute-start(bf16[2,64,2048]{2,1,0:T(8,128)(2,1)S(1)} %bitcast.109), channel_id=1, source_target_pairs={{96,0},{0,32},{32,64},{64,96},{97,1},{1,33},{33,65},{65,97},{98,2}... | collective-permute-start | bytes 1572872 | tf_op jit(solution)/shard_map/ppermute | solution.py:270
  144.9 6.2 %copy-start.17 = (bf16[2,64,2048]{2,1,0:T(8,128)(2,1)}, bf16[2,64,2048]{2,1,0:T(8,128)(2,1)S(1)}, u32[]{:S(2)}) copy-start(bf16[2,64,2048]{2,1,0:T(8,128)(2,1)S(1)} %collective-permute-done.5.refs_0_) | copy-start | bytes 1572868
  146.7 4.2 %collective-permute-start.7 = (bf16[2,64,2048]{2,1,0:T(8,128)(2,1)S(1)}, bf16[2,64,2048]{2,1,0:T(8,128)(2,1)S(1)}, u32[]{:S(2)}, u32[]{:S(2)}) collective-permute-start(bf16[2,64,2048]{2,1,0:T(8,128)(2,1)S(1)} %collective-permute-done.5.refs_0_), channel_id=1, source_target_pairs={{16,0},{0,16},{17,1},{1,17},{18,2},{2,18},{19,3},{3,19},{20,4},{4,... | collective-permute-start | bytes 1572872 | tf_op jit(solution)/shard_map/ppermute | solution.py:270
  148.6 2.5 %collective-permute-start.8 = (bf16[2,64,2048]{2,1,0:T(8,128)(2,1)}, bf16[2,64,2048]{2,1,0:T(8,128)(2,1)S(1)}, u32[]{:S(2)}, u32[]{:S(2)}) collective-permute-start(bf16[2,64,2048]{2,1,0:T(8,128)(2,1)} %collective-permute-done.6.refs_2_), channel_id=1, source_target_pairs={{16,0},{0,16},{17,1},{1,17},{18,2},{2,18},{19,3},{3,19},{20,4},{4,... | collective-permute-start | bytes 1572872 | tf_op jit(solution)/shard_map/ppermute | solution.py:270
  148.8 14.3 %collective-permute-start.9 = (bf16[2,64,2048]{2,1,0:T(8,128)(2,1)S(1)}, bf16[2,64,2048]{2,1,0:T(8,128)(2,1)S(1)}, u32[]{:S(2)}, u32[]{:S(2)}) collective-permute-start(bf16[2,64,2048]{2,1,0:T(8,128)(2,1)S(1)} %bitcast.110), channel_id=1, source_target_pairs={{32,0},{64,32},{96,64},{0,96},{33,1},{65,33},{97,65},{1,97},{34,2}... | collective-permute-start | bytes 1572872 | tf_op jit(solution)/shard_map/ppermute | solution.py:270
  149.3 14.1 %collective-permute-start.10 = (bf16[2,64,2048]{2,1,0:T(8,128)(2,1)S(1)}, bf16[2,64,2048]{2,1,0:T(8,128)(2,1)S(1)}, u32[]{:S(2)}, u32[]{:S(2)}) collective-permute-start(bf16[2,64,2048]{2,1,0:T(8,128)(2,1)S(1)} %bitcast.111), channel_id=1, source_target_pairs={{96,0},{0,32},{32,64},{64,96},{97,1},{1,33},{33,65},{65,97},{98,2}... | collective-permute-start | bytes 1572872 | tf_op jit(solution)/shard_map/ppermute | solution.py:270
  150.9 0.8 copy-start.23
  151.7 0.8 copy-start.25
  163.0 4.1 %copy-start.21 = (bf16[2,64,2048]{2,1,0:T(8,128)(2,1)}, bf16[2,64,2048]{2,1,0:T(8,128)(2,1)S(1)}, u32[]{:S(2)}) copy-start(bf16[2,64,2048]{2,1,0:T(8,128)(2,1)S(1)} %collective-permute-done.9.refs_0_) | copy-start | bytes 1572868
  163.4 3.8 %copy-start.19 = (bf16[2,64,2048]{2,1,0:T(8,128)(2,1)}, bf16[2,64,2048]{2,1,0:T(8,128)(2,1)S(1)}, u32[]{:S(2)}) copy-start(bf16[2,64,2048]{2,1,0:T(8,128)(2,1)S(1)} %collective-permute-done.10.refs_2_) | copy-start | bytes 1572868
  163.4 3.0 %collective-permute-start.11 = (bf16[2,64,2048]{2,1,0:T(8,128)(2,1)S(1)}, bf16[2,64,2048]{2,1,0:T(8,128)(2,1)S(1)}, u32[]{:S(2)}, u32[]{:S(2)}) collective-permute-start(bf16[2,64,2048]{2,1,0:T(8,128)(2,1)S(1)} %collective-permute-done.9.refs_0_), channel_id=1, source_target_pairs={{16,0},{0,16},{17,1},{1,17},{18,2},{2,18},{19,3},{3,19},{20,4},{4,... | collective-permute-start | bytes 1572872 | tf_op jit(solution)/shard_map/ppermute | solution.py:270
  164.8 2.3 collective-permute-start.12
  164.8 13.8 %collective-permute-start.13 = (bf16[2,64,2048]{2,1,0:T(8,128)(2,1)}, bf16[2,64,2048]{2,1,0:T(8,128)(2,1)S(1)}, u32[]{:S(2)}, u32[]{:S(2)}) collective-permute-start(bf16[2,64,2048]{2,1,0:T(8,128)(2,1)} %copy-done.17), channel_id=1, source_target_pairs={{32,0},{64,32},{96,64},{0,96},{33,1},{65,33},{97,65},{1,97},{34,2}... | collective-permute-start | bytes 1572872 | tf_op jit(solution)/shard_map/ppermute | solution.py:270
  165.5 14.0 %collective-permute-start.14 = (bf16[2,64,2048]{2,1,0:T(8,128)(2,1)S(1)}, bf16[2,64,2048]{2,1,0:T(8,128)(2,1)S(1)}, u32[]{:S(2)}, u32[]{:S(2)}) collective-permute-start(bf16[2,64,2048]{2,1,0:T(8,128)(2,1)S(1)} %collective-permute-done.10.refs_2_), channel_id=1, source_target_pairs={{96,0},{0,32},{32,64},{64,96},{97,1},{1,33},{33,65},{65,97},{98,2}... | collective-permute-start | bytes 1572872 | tf_op jit(solution)/shard_map/ppermute | solution.py:270
  166.4 0.9 copy-start.26
  167.2 0.8 copy-start.27
  178.7 4.7 %copy-start.18 = (bf16[2,64,2048]{2,1,0:T(8,128)(2,1)}, bf16[2,64,2048]{2,1,0:T(8,128)(2,1)S(1)}, u32[]{:S(2)}) copy-start(bf16[2,64,2048]{2,1,0:T(8,128)(2,1)S(1)} %collective-permute-done.13.refs_0_) | copy-start | bytes 1572868
  179.5 3.9 %copy-start.20 = (bf16[2,64,2048]{2,1,0:T(8,128)(2,1)}, bf16[2,64,2048]{2,1,0:T(8,128)(2,1)S(1)}, u32[]{:S(2)}) copy-start(bf16[2,64,2048]{2,1,0:T(8,128)(2,1)S(1)} %collective-permute-done.14.refs_1_) | copy-start | bytes 1572868
  179.5 3.1 %collective-permute-start.15 = (bf16[2,64,2048]{2,1,0:T(8,128)(2,1)S(1)}, bf16[2,64,2048]{2,1,0:T(8,128)(2,1)S(1)}, u32[]{:S(2)}, u32[]{:S(2)}) collective-permute-start(bf16[2,64,2048]{2,1,0:T(8,128)(2,1)S(1)} %collective-permute-done.13.refs_0_), channel_id=1, source_target_pairs={{16,0},{0,16},{17,1},{1,17},{18,2},{2,18},{19,3},{3,19},{20,4},{4,... | collective-permute-start | bytes 1572872 | tf_op jit(solution)/shard_map/ppermute | solution.py:270
  181.0 2.3 collective-permute-start.16
  181.2 13.5 %copy-start.13 = (f32[2,256]{1,0:T(2,128)S(1)}, f32[2,256]{1,0:T(2,128)}, u32[]{:S(2)}) copy-start(f32[2,256]{1,0:T(2,128)} %get-tuple-element.35) | copy-start | bytes 6148
  181.2 13.5 %copy-start.14 = (f32[4,128]{1,0:T(4,128)S(1)}, f32[4,128]{1,0:T(4,128)}, u32[]{:S(2)}) copy-start(f32[4,128]{1,0:T(4,128)} %get-tuple-element.38) | copy-start | bytes 6148
  181.2 13.5 %copy-start.15 = (f32[4,128]{1,0:T(4,128)S(1)}, f32[4,128]{1,0:T(4,128)}, u32[]{:S(2)}) copy-start(f32[4,128]{1,0:T(4,128)} %get-tuple-element.42) | copy-start | bytes 6148
  182.6 0.8 copy-start.22
  183.4 0.8 copy-start.24
  208.7 4.7 %collective-permute-start.17 = (f32[8,256]{1,0:T(8,128)S(1)}, f32[8,256]{1,0:T(8,128)S(1)}, u32[]{:S(2)}, u32[]{:S(2)}) collective-permute-start(f32[8,256]{1,0:T(8,128)S(1)} %reduce_sum.78), channel_id=1, source_target_pairs={{32,0},{64,32},{96,64},{0,96},{33,1},{65,33},{97,65},{1,97},{34,2}... | collective-permute-start | bytes 24584 | tf_op jit(solution)/shard_map/ppermute | solution.py:270
  209.3 4.1 %collective-permute-start.18 = (f32[8,256]{1,0:T(8,128)S(1)}, f32[8,256]{1,0:T(8,128)S(1)}, u32[]{:S(2)}, u32[]{:S(2)}) collective-permute-start(f32[8,256]{1,0:T(8,128)S(1)} %reduce_sum.78), channel_id=1, source_target_pairs={{64,0},{96,32},{0,64},{32,96},{65,1},{97,33},{1,65},{33,97},{66,2}... | collective-permute-start | bytes 24584 | tf_op jit(solution)/shard_map/ppermute | solution.py:270
  210.6 3.7 %collective-permute-start.19 = (f32[8,256]{1,0:T(8,128)S(1)}, f32[8,256]{1,0:T(8,128)S(1)}, u32[]{:S(2)}, u32[]{:S(2)}) collective-permute-start(f32[8,256]{1,0:T(8,128)S(1)} %reduce_sum.78), channel_id=1, source_target_pairs={{96,0},{0,32},{32,64},{64,96},{97,1},{1,33},{33,65},{65,97},{98,2}... | collective-permute-start | bytes 24584 | tf_op jit(solution)/shard_map/ppermute | solution.py:270
  214.3 4.3 %collective-permute-start.20 = (f32[8,256]{1,0:T(8,128)S(1)}, f32[8,256]{1,0:T(8,128)S(1)}, u32[]{:S(2)}, u32[]{:S(2)}) collective-permute-start(f32[8,256]{1,0:T(8,128)S(1)} %add_add_fusion), channel_id=1, source_target_pairs={{16,0},{0,16},{17,1},{1,17},{18,2},{2,18},{19,3},{3,19},{20,4},{4,... | collective-permute-start | bytes 24584 | tf_op jit(solution)/shard_map/ppermute | solution.py:270
  219.6 10.3 %copy-start.1 = (bf16[4,2048,128]{2,1,0:T(8,128)(2,1)S(1)}, bf16[4,2048,128]{2,1,0:T(8,128)(2,1)}, u32[]{:S(2)}) copy-start(bf16[4,2048,128]{2,1,0:T(8,128)(2,1)} %param.26) | copy-start | bytes 6291460
Sparse Core Ops, SparseCore 0:
  9.7 44.9 all-gather.4
  59.4 50.8 all-gather.2
  123.4 81.8 reduce-scatter.1

commit v9 on v8

--- a/solution.py
+++ b/solution.py
@@ -185,7 +185,7 @@
             ],
         ),
         compiler_params=pltpu.CompilerParams(
-            dimension_semantics=("arbitrary",), vmem_limit_bytes=56 << 20
+            dimension_semantics=("arbitrary",), vmem_limit_bytes=50 << 20
         ),
         cost_estimate=pl.CostEstimate(
             flops=2 * size * vocab_width * depth,

time: 238 us -> 238 us (level)
  waiting for transfers between devices: 35.5 us -> 42.7 us
  local copies, waits for them, and re-layouts: 20.7 us -> 16.5 us
  Pallas kernels: 56.3 us -> 53.2 us
    ppermute x21, waiting for transfers between devices: 11.9 us -> 19.1 us  [ring(): lax.ppermute(values, axis, [((i + shift) % size, i) for i in range(size)])]
    unnamed x64 -> x34, local copies, waits for them, and re-layouts: 11.9 us -> 8.17 us
    pallas_call x4, Pallas kernels: 42 us -> 38.9 us  [some_logits(): pl.pallas_call(functools.partial(logits_kernel, first, parts), out_shape=...]
  transfers between devices with their start and end apart: 28 -> 28, of which waited for: 16 -> 19; matrix products, arithmetic and copies ran while one was open for 17% -> 18% of each run, Pallas kernels for 19% -> 18%
where the time goes in v9:
time: 238 us; the launch traced here: 237 us
  Pallas kernels  53.2 us (22%)
  waiting for transfers between devices  42.7 us (18%)
  starting transfers between devices  42.4 us (18%)
  blocking collectives  37.4 us (16%)
  matrix products  24.9 us (10%)
  local copies, waits for them, and re-layouts  16.5 us (7%)
  between operations  14.8 us (6%)
  other arithmetic  4.82 us (2%)
    pallas_call x4, Pallas kernels, some_logits(): pl.pallas_call(functools.partial(logits_kernel, first, parts), out_shape=...  38.9 us
    ppermute x21, starting transfers between devices, ring(): lax.ppermute(values, axis, [((i + shift) % size, i) for i in range(size)])  27.1 us
    all_to_all x2, blocking collectives, swap(): return lax.all_to_all(copies, axes, split_axis=0, concat_axis=0, tiled=True)  23.6 us
    all_to_all x4, waiting for transfers between devices, swap(): return lax.all_to_all(copies, axes, split_axis=0, concat_axis=0, tiled=True)  21.6 us
    ppermute x21, waiting for transfers between devices, ring(): lax.ppermute(values, axis, [((i + shift) % size, i) for i in range(size)])  19.1 us
    all_to_all x4, starting transfers between devices, swap(): return lax.all_to_all(copies, axes, split_axis=0, concat_axis=0, tiled=True)  15 us
    all_gather x1, blocking collectives, out_projection(): group = lax.all_gather(attended, 'z', axis=0, tiled=True)  13.8 us
    dot_general x2, matrix products, unit_terms(): lax.dot_general(active, weights[2], (((1,), (1,)), ((), ())), preferred_e...  12.4 us
  transfers between devices with their start and end apart: 28, of which 19 were waited for; matrix products, arithmetic and copies ran while one was open for 18% of the time, Pallas kernels for 18%

profile of v9, /device:TPU:1, one launch (start us, length us, event | category | flops | bytes accessed | tf_op | source)
XLA Modules:
  0.0 236.7 jit_solution(12048715273878235037)
XLA Ops:
  7.9 1.0 constant_dynamic-slice_fusion
  8.9 3.4 %collective-permute-start = (bf16[1024,128]{1,0:T(8,128)(2,1)S(1)}, bf16[1024,128]{1,0:T(8,128)(2,1)}, u32[]{:S(2)}, u32[]{:S(2)}) collective-permute-start(bf16[1024,128]{1,0:T(8,128)(2,1)S(1)} %constant_dynamic-slice_fusion), channel_id=1, source_target_pairs={{4,0},{8,4},{12,8},{0,12},{5,1},{9,5},{13,9},{1,13},{6,2},{10,6},{... | collective-permute-start | bytes 786440 | tf_op jit(solution)/shard_map/ppermute | solution.py:270
  14.1 0.9 copy.48
  15.0 0.7 copy.33.parents_ref
  15.7 2.2 copy-done.2
  17.9 0.9 copy-done.3
  18.8 4.0 %shard_map.167 = bf16[48,2048]{1,0:T(8,128)(2,1)S(1)} custom-call(s32[1]{0:T(128)S(6)} %copy.52.length_ref, bf16[48,2048]{1,0:T(8,128)(2,1)S(1)} %copy-done.3, bf16[2,48,512]{2,1,0:T(8,128)(2,1)S(1)} %bitcast.104, s32[48,1]{1,0:T(8,128)S(1)} %copy.33.parents_ref, bf16[1,2,2,2048,256]{4,3,2,1,0:T(8,128)(2,1)S(1)} %copy-done.2, ...), custom_call_target="tpu_custom_call" | custom-call | flops 805306368 | bytes 4194304 | tf_op jit(solution)/shard_map/pallas_call | solution.py:78
  22.9 4.9 %collective-permute-done.2 = bf16[1024,128]{1,0:T(8,128)(2,1)} collective-permute-done((bf16[1024,128]{1,0:T(8,128)(2,1)S(1)}, bf16[1024,128]{1,0:T(8,128)(2,1)}, u32[]{:S(2)}, u32[]{:S(2)}) %collective-permute-start.2) | collective-permute-done | bytes 262176 | tf_op jit(solution)/shard_map/ppermute | solution.py:270
  27.7 1.0 constant_dynamic-update-slice_fusion.3
  28.7 1.0 constant_dynamic-update-slice_fusion.2
  29.8 1.1 constant_dynamic-update-slice_fusion.1
  30.8 1.0 constant_dynamic-update-slice_fusion
  32.4 13.8 %all_gather.9 = bf16[192,2048]{1,0:T(8,128)(2,1)S(1)} all-gather(bf16[48,2048]{1,0:T(8,128)(2,1)S(1)} %shard_map.167), channel_id=1, replica_groups=mesh['y'=4,'core'=2,'x'=4,'z'=4] {'z'}, dimensions={0}, use_global_device_ids=true | all-gather | bytes 983040 | tf_op jit(solution)/shard_map/all_gather | solution.py:311
  46.2 1.6 fusion.34
  47.8 1.1 fusion.17
  48.9 3.7 %all-to-all-start = ((bf16[4,48,512]{2,1,0:T(8,128)(2,1)}), bf16[4,48,512]{2,1,0:T(8,128)(2,1)S(1)}, u32[]{:S(2)}, u32[]{:S(2)}) async-start(bf16[4,48,512]{2,1,0:T(8,128)(2,1)} %bitcast.2), calls=%async_computation | async-start | bytes 393216 | tf_op jit(solution)/shard_map/all_to_all | solution.py:278
  52.6 5.1 %all-to-all-done = bf16[4,48,512]{2,1,0:T(8,128)(2,1)S(1)} async-done(((bf16[4,48,512]{2,1,0:T(8,128)(2,1)}), bf16[4,48,512]{2,1,0:T(8,128)(2,1)S(1)}, u32[]{:S(2)}, u32[]{:S(2)}) %all-to-all-start) | async-done | bytes 196640 | tf_op jit(solution)/shard_map/all_to_all | solution.py:278
  58.4 0.8 fusion.32
  59.2 1.1 convolution_convert_fusion.2
  60.5 9.9 %all_to_all.30 = bf16[16,4,2048]{2,1,0:T(4,128)(2,1)S(1)} all-to-all(bf16[16,4,2048]{2,1,0:T(4,128)(2,1)S(1)} %broadcast_in_dim.23), channel_id=1, replica_groups=mesh['y'=4,'core'=2,'x'=4,'z'=4] {'x','z'}, dimensions={0} | all-to-all | bytes 524288 | tf_op jit(solution)/shard_map/all_to_all | solution.py:278
  70.5 2.4 %fusion.43 = f32[64,512]{1,0:T(8,128)S(1)} fusion(bf16[64,2048]{1,0:T(8,128)(2,1)S(1)} %reshape.104, bf16[3,2048,512]{1,2,0:T(8,128)(2,1)} %all-gather.5.cloned.1.call-done), kind=kOutput, calls=%fused_computation.68 | convolution fusion | flops 134479872 | bytes 2490368 | tf_op jit(solution)/shard_map/dot_general | solution.py:331
  72.9 3.4 %convolution_convert_fusion.1 = bf16[64,2048]{1,0:T(8,128)(2,1)S(1)} fusion(bf16[3,2048,512]{1,2,0:T(8,128)(2,1)} %all-gather.5.cloned.1.call-done, f32[64,512]{1,0:T(8,128)S(1)} %fusion.43, bf16[64,2048]{1,0:T(8,128)(2,1)S(1)} %reshape.104), kind=kOutput, calls=%fused_computation.2 | convolution fusion | flops 268632064 | bytes 4849664 | tf_op jit(solution)/shard_map/dot_general | solution.py:334
  76.4 0.8 reshape.105
  77.2 3.5 %all-to-all-start.2 = ((bf16[16,4,2048]{2,1,0:T(4,128)(2,1)}), bf16[16,4,2048]{2,1,0:T(4,128)(2,1)S(1)}, u32[]{:S(2)}, u32[]{:S(2)}) async-start(bf16[16,4,2048]{2,1,0:T(4,128)(2,1)} %reshape.105), calls=%async_computation.2 | async-start | bytes 524288 | tf_op jit(solution)/shard_map/all_to_all | solution.py:278
  80.7 7.2 %all-to-all-done.2 = bf16[16,4,2048]{2,1,0:T(4,128)(2,1)S(1)} async-done(((bf16[16,4,2048]{2,1,0:T(4,128)(2,1)}), bf16[16,4,2048]{2,1,0:T(4,128)(2,1)S(1)}, u32[]{:S(2)}, u32[]{:S(2)}) %all-to-all-start.2) | async-done | bytes 262176 | tf_op jit(solution)/shard_map/all_to_all | solution.py:278
  88.7 0.8 broadcast_in_dim.24
  89.5 3.5 %all-to-all-start.3 = ((bf16[16,4,2048]{2,1,0:T(4,128)(2,1)}), bf16[16,4,2048]{2,1,0:T(4,128)(2,1)S(1)}, u32[]{:S(2)}, u32[]{:S(2)}) async-start(bf16[16,4,2048]{2,1,0:T(4,128)(2,1)} %broadcast_in_dim.24), calls=%async_computation.3 | async-start | bytes 524288 | tf_op jit(solution)/shard_map/all_to_all | solution.py:278
  93.0 9.2 %all-to-all-done.3 = bf16[16,4,2048]{2,1,0:T(4,128)(2,1)S(1)} async-done(((bf16[16,4,2048]{2,1,0:T(4,128)(2,1)}), bf16[16,4,2048]{2,1,0:T(4,128)(2,1)S(1)}, u32[]{:S(2)}, u32[]{:S(2)}) %all-to-all-start.3) | async-done | bytes 262176 | tf_op jit(solution)/shard_map/all_to_all | solution.py:278
  102.9 1.2 broadcast_in_dim.25
  104.2 4.3 %all-to-all-start.4 = ((bf16[16,4,64,128]{3,2,1,0:T(8,128)(2,1)}), bf16[16,4,64,128]{3,2,1,0:T(8,128)(2,1)S(1)}, u32[]{:S(2)}, u32[]{:S(2)}) async-start(bf16[16,4,64,128]{3,2,1,0:T(8,128)(2,1)} %broadcast_in_dim.25), calls=%async_computation.4 | async-start | bytes 2097152 | tf_op jit(solution)/shard_map/all_to_all | solution.py:278
  108.7 1.2 all-gather.3.cloned.1.call-done
  109.8 5.5 %fusion.4 = f32[768,512]{1,0:T(8,128)} fusion(bf16[768,2048]{1,0:T(8,128)(2,1)} %all-gather.3.cloned.1.call-done, bf16[3,2048,512]{1,2,0:T(8,128)(2,1)} %all-gather.5.cloned.1.call-done), kind=kOutput, calls=%fused_computation.12 | convolution fusion | flops 1610612736 | bytes 6815744 | tf_op jit(solution)/shard_map/dot_general | solution.py:331
  115.4 8.9 %convolution_convert_fusion = bf16[768,2048]{1,0:T(8,128)(2,1)} fusion(bf16[3,2048,512]{1,2,0:T(8,128)(2,1)} %all-gather.5.cloned.1.call-done, f32[768,512]{1,0:T(8,128)} %fusion.4, bf16[768,2048]{1,0:T(8,128)(2,1)} %all-gather.3.cloned.1.call-done), kind=kOutput, calls=%fused_computation | convolution fusion | flops 3226730496 | bytes 12058624 | tf_op jit(solution)/shard_map/dot_general | solution.py:334
  124.5 6.6 %collective-permute-start.4 = (bf16[4,64,2048]{2,1,0:T(8,128)(2,1)S(1)}, bf16[4,64,2048]{2,1,0:T(8,128)(2,1)S(1)}, u32[]{:S(2)}, u32[]{:S(2)}) collective-permute-start(bf16[4,64,2048]{2,1,0:T(8,128)(2,1)S(1)} %copy_bitcast_fusion.refs_0_), channel_id=1, source_target_pairs={{16,0},{0,16},{17,1},{1,17},{18,2},{2,18},{19,3},{3,19},{20,4},{4,... | collective-permute-start | bytes 3145736 | tf_op jit(solution)/shard_map/ppermute | solution.py:270
  131.2 0.9 slice_bitcast_fusion.19
  132.1 0.9 copy.47
  133.0 2.6 %collective-permute-start.5 = (bf16[2,64,2048]{2,1,0:T(8,128)(2,1)}, bf16[2,64,2048]{2,1,0:T(8,128)(2,1)S(1)}, u32[]{:S(2)}, u32[]{:S(2)}) collective-permute-start(bf16[2,64,2048]{2,1,0:T(8,128)(2,1)} %bitcast.102), channel_id=1, source_target_pairs={{32,0},{64,32},{96,64},{0,96},{33,1},{65,33},{97,65},{1,97},{34,2}... | collective-permute-start | bytes 1572872 | tf_op jit(solution)/shard_map/ppermute | solution.py:270
  135.9 9.7 %shard_map.168 = (bf16[2,4,64,2048]{3,2,1,0:T(8,128)(2,1)}, f32[2,256]{1,0:T(2,128)S(1)}) custom-call(s32[9]{0:T(128)S(1)} %stack.42.place_ref, bf16[4,64,2048]{2,1,0:T(8,128)(2,1)S(1)} %copy_bitcast_fusion.refs_0_, bf16[4,64,2048]{2,1,0:T(8,128)(2,1)S(1)} %collective-permute-done.4.refs_1_, s32[8,64,2]{2,1,0:T(8,128)S(1)} %bitcast.105, ...), custom_call_target="tpu_custom_call" | custom-call | flops 4294967296 | bytes 10485760 | tf_op jit(solution)/shard_map/pallas_call | solution.py:161
  145.6 1.7 collective-permute-done.5.refs_0_
  147.3 3.1 %collective-permute-done.6.refs_2_ = bf16[2,64,2048]{2,1,0:T(8,128)(2,1)} collective-permute-done((bf16[2,64,2048]{2,1,0:T(8,128)(2,1)}, bf16[2,64,2048]{2,1,0:T(8,128)(2,1)}, u32[]{:S(2)}, u32[]{:S(2)}) %collective-permute-start.6) | collective-permute-done | bytes 524320 | tf_op jit(solution)/shard_map/ppermute | solution.py:270
  150.4 1.1 collective-permute-start.7
  151.7 1.5 collective-permute-start.10
  154.0 9.8 %shard_map.169 = (bf16[4,2,64,2048]{3,2,1,0:T(8,128)(2,1)}, f32[4,128]{1,0:T(4,128)S(1)}) custom-call(s32[9]{0:T(128)S(1)} %stack.42.place_ref, bf16[2,64,2048]{2,1,0:T(8,128)(2,1)S(1)} %collective-permute-done.5.refs_0_, bf16[2,64,2048]{2,1,0:T(8,128)(2,1)S(1)} %collective-permute-done.7.refs_1_, bf16[2,64,2048]{2,1,0:T(8,128)(2,1)} %collective-permute-done.6.refs_2_, ...), custom_call_target="tpu_custom_call" | custom-call | flops 4294967296 | bytes 10485760 | tf_op jit(solution)/shard_map/pallas_call | solution.py:161
  163.8 1.0 collective-permute-done.9.refs_0_
  164.8 1.1 collective-permute-done.10.refs_2_
  165.9 1.5 collective-permute-start.11
  167.3 1.5 collective-permute-start.14
  168.9 0.7 collective-permute-done.12.refs_3_
  169.6 9.8 %shard_map.170 = (bf16[4,2,64,2048]{3,2,1,0:T(8,128)(2,1)}, f32[4,128]{1,0:T(4,128)S(1)}) custom-call(s32[9]{0:T(128)S(1)} %stack.42.place_ref, bf16[2,64,2048]{2,1,0:T(8,128)(2,1)S(1)} %collective-permute-done.9.refs_0_, bf16[2,64,2048]{2,1,0:T(8,128)(2,1)S(1)} %collective-permute-done.11.refs_1_, bf16[2,64,2048]{2,1,0:T(8,128)(2,1)S(1)} %collective-permute-done.10.refs_2_, ...), custom_call_target="tpu_custom_call" | custom-call | flops 4294967296 | bytes 10485760 | tf_op jit(solution)/shard_map/pallas_call | solution.py:161
  179.4 1.0 collective-permute-done.13.refs_0_
  180.4 0.9 collective-permute-done.14.refs_1_
  181.3 1.6 collective-permute-start.15
  183.1 1.4 collective-permute-done.15.refs_2_
  184.4 0.7 collective-permute-done.16.refs_3_
  185.2 9.6 %shard_map.171 = (bf16[2,4,64,2048]{3,2,1,0:T(8,128)(2,1)}, f32[2,256]{1,0:T(2,128)S(1)}) custom-call(s32[9]{0:T(128)S(1)} %stack.42.place_ref, bf16[2,64,2048]{2,1,0:T(8,128)(2,1)S(1)} %collective-permute-done.13.refs_0_, bf16[2,64,2048]{2,1,0:T(8,128)(2,1)S(1)} %collective-permute-done.14.refs_1_, ...), custom_call_target="tpu_custom_call" | custom-call | flops 4294967296 | bytes 10485760 | tf_op jit(solution)/shard_map/pallas_call | solution.py:161
  194.9 13.7 %all_to_all.31 = f32[16,8,256]{2,1,0:T(8,128)S(1)} all-to-all(f32[16,8,256]{2,1,0:T(8,128)S(1)} %broadcast_in_dim.30), channel_id=1, replica_groups=mesh['y'=4,'core'=2,'x'=4,'z'=4] {'x','z'}, dimensions={0} | all-to-all | bytes 262144 | tf_op jit(solution)/shard_map/all_to_all | solution.py:278
  208.7 2.0 collective-permute-start.18
  210.7 1.1 fusion.28
  211.8 1.8 fusion.33
  213.5 0.9 collective-permute-done.19
  214.4 3.6 %collective-permute-start.20 = (f32[8,256]{1,0:T(8,128)S(1)}, f32[8,256]{1,0:T(8,128)S(1)}, u32[]{:S(2)}, u32[]{:S(2)}) collective-permute-start(f32[8,256]{1,0:T(8,128)S(1)} %add_add_fusion), channel_id=1, source_target_pairs={{16,0},{0,16},{17,1},{1,17},{18,2},{2,18},{19,3},{3,19},{20,4},{4,... | collective-permute-start | bytes 24584 | tf_op jit(solution)/shard_map/ppermute | solution.py:270
  218.0 0.8 collective-permute-done.20
  218.9 0.9 copy.38
  219.8 10.3 %shard_map.172 = bf16[4,8,64,2048]{3,2,1,0:T(8,128)(2,1)} custom-call(s32[9]{0:T(128)} %copy-done.4, bf16[2,4,64,2048]{3,2,1,0:T(8,128)(2,1)} %get-tuple-element.47.refs_0_, bf16[4,2,64,2048]{3,2,1,0:T(8,128)(2,1)} %get-tuple-element.48.refs_1_, bf16[4,2,64,2048]{3,2,1,0:T(8,128)(2,1)} %get-tuple-element.49.refs_2_, ...), custom_call_target="tpu_custom_call" | custom-call | flops 12582912 | bytes 16777216 | tf_op jit(solution)/shard_map/pallas_call | solution.py:233
  (95 shorter events, 6.8 us)
Async XLA Ops:
  7.2 95.2 %copy-start = (bf16[4,2048,128]{2,1,0:T(8,128)(2,1)S(1)}, bf16[4,2048,128]{2,1,0:T(8,128)(2,1)}, u32[]{:S(2)}) copy-start(bf16[4,2048,128]{2,1,0:T(8,128)(2,1)} %param.26) | copy-start | bytes 6291460
  7.2 63.3 %all-gather.5.cloned.1.call-start = ((), (), s32[]{:S(2)}) async-start(), calls=%async_computation.8 | async-start | bytes 7077888 | tf_op jit(solution)/shard_map/all_gather | solution.py:362
  8.9 14.0 %copy-start.6 = (bf16[1024,128]{1,0:T(8,128)(2,1)}, bf16[1024,128]{1,0:T(8,128)(2,1)S(1)}, u32[]{:S(2)}) copy-start(bf16[1024,128]{1,0:T(8,128)(2,1)S(1)} %constant_dynamic-slice_fusion) | copy-start | bytes 786436
  8.9 13.9 %collective-permute-start = (bf16[1024,128]{1,0:T(8,128)(2,1)S(1)}, bf16[1024,128]{1,0:T(8,128)(2,1)}, u32[]{:S(2)}, u32[]{:S(2)}) collective-permute-start(bf16[1024,128]{1,0:T(8,128)(2,1)S(1)} %constant_dynamic-slice_fusion), channel_id=1, source_target_pairs={{4,0},{8,4},{12,8},{0,12},{5,1},{9,5},{13,9},{1,13},{6,2},{10,6},{... | collective-permute-start | bytes 786440 | tf_op jit(solution)/shard_map/ppermute | solution.py:270
  12.3 10.6 %collective-permute-start.1 = (bf16[1024,128]{1,0:T(8,128)(2,1)S(1)}, bf16[1024,128]{1,0:T(8,128)(2,1)}, u32[]{:S(2)}, u32[]{:S(2)}) collective-permute-start(bf16[1024,128]{1,0:T(8,128)(2,1)S(1)} %constant_dynamic-slice_fusion), channel_id=1, source_target_pairs={{8,0},{12,4},{0,8},{4,12},{9,1},{13,5},{1,9},{5,13},{10,2},{14,6},... | collective-permute-start | bytes 786440 | tf_op jit(solution)/shard_map/ppermute | solution.py:270
  12.8 14.9 %collective-permute-start.2 = (bf16[1024,128]{1,0:T(8,128)(2,1)S(1)}, bf16[1024,128]{1,0:T(8,128)(2,1)}, u32[]{:S(2)}, u32[]{:S(2)}) collective-permute-start(bf16[1024,128]{1,0:T(8,128)(2,1)S(1)} %constant_dynamic-slice_fusion), channel_id=1, source_target_pairs={{12,0},{0,4},{4,8},{8,12},{13,1},{1,5},{5,9},{9,13},{14,2},{2,6},{... | collective-permute-start | bytes 786440 | tf_op jit(solution)/shard_map/ppermute | solution.py:270
  15.7 2.2 copy-start.2
  17.9 0.9 copy-start.3
  31.8 14.3 %collective-permute-start.3 = (bf16[1024,512]{1,0:T(8,128)(2,1)S(1)}, bf16[1024,512]{1,0:T(8,128)(2,1)}, u32[]{:S(2)}, u32[]{:S(2)}) collective-permute-start(bf16[1024,512]{1,0:T(8,128)(2,1)S(1)} %constant_dynamic-update-slice_fusion), channel_id=1, source_target_pairs={{16,0},{0,16},{17,1},{1,17},{18,2},{2,18},{19,3},{3,19},{20,4},{4,... | collective-permute-start | bytes 3145736 | tf_op jit(solution)/shard_map/ppermute | solution.py:270
  46.2 6.4 %copy-start.8 = (bf16[2048]{0:T(1024)(128)(2,1)S(1)}, bf16[2048]{0:T(1024)(128)(2,1)}, u32[]{:S(2)}) copy-start(bf16[2048]{0:T(1024)(128)(2,1)} %param.28) | copy-start | bytes 12292
  46.2 6.4 %copy-start.9 = (bf16[2048]{0:T(1024)(128)(2,1)S(1)}, bf16[2048]{0:T(1024)(128)(2,1)}, u32[]{:S(2)}) copy-start(bf16[2048]{0:T(1024)(128)(2,1)} %param.29) | copy-start | bytes 12292
  47.8 10.3 %copy-start.7 = (bf16[48,2048]{1,0:T(8,128)(2,1)S(1)}, bf16[48,2048]{1,0:T(8,128)(2,1)}, u32[]{:S(2)}) copy-start(bf16[48,2048]{1,0:T(8,128)(2,1)} %param.16) | copy-start | bytes 589828
  48.9 10.3 %copy-start.13 = (s32[1,4]{1,0:T(1,128)S(1)}, s32[1,4]{1,0:T(1,128)}, u32[]{:S(2)}) copy-start(s32[1,4]{1,0:T(1,128)} %param.22) | copy-start | bytes 52
  48.9 8.8 %all-to-all-start = ((bf16[4,48,512]{2,1,0:T(8,128)(2,1)}), bf16[4,48,512]{2,1,0:T(8,128)(2,1)S(1)}, u32[]{:S(2)}, u32[]{:S(2)}) async-start(bf16[4,48,512]{2,1,0:T(8,128)(2,1)} %bitcast.2), calls=%async_computation | async-start | bytes 393216 | tf_op jit(solution)/shard_map/all_to_all | solution.py:278
  52.6 57.3 %all-gather.3.cloned.1.call-start = ((), (), s32[]{:S(2)}) async-start(), calls=%async_computation.7 | async-start | bytes 3342336 | tf_op jit(solution)/shard_map/all_gather | solution.py:377
  72.9 7.8 %copy-start.10 = (bf16[2048]{0:T(1024)(128)(2,1)S(1)}, bf16[2048]{0:T(1024)(128)(2,1)}, u32[]{:S(2)}) copy-start(bf16[2048]{0:T(1024)(128)(2,1)} %param.30) | copy-start | bytes 12292
  72.9 7.8 %copy-start.11 = (bf16[2048]{0:T(1024)(128)(2,1)S(1)}, bf16[2048]{0:T(1024)(128)(2,1)}, u32[]{:S(2)}) copy-start(bf16[2048]{0:T(1024)(128)(2,1)} %param.31) | copy-start | bytes 12292
  77.2 10.8 %all-to-all-start.2 = ((bf16[16,4,2048]{2,1,0:T(4,128)(2,1)}), bf16[16,4,2048]{2,1,0:T(4,128)(2,1)S(1)}, u32[]{:S(2)}, u32[]{:S(2)}) async-start(bf16[16,4,2048]{2,1,0:T(4,128)(2,1)} %reshape.105), calls=%async_computation.2 | async-start | bytes 524288 | tf_op jit(solution)/shard_map/all_to_all | solution.py:278
  89.5 12.8 %all-to-all-start.3 = ((bf16[16,4,2048]{2,1,0:T(4,128)(2,1)}), bf16[16,4,2048]{2,1,0:T(4,128)(2,1)S(1)}, u32[]{:S(2)}, u32[]{:S(2)}) async-start(bf16[16,4,2048]{2,1,0:T(4,128)(2,1)} %broadcast_in_dim.24), calls=%async_computation.3 | async-start | bytes 524288 | tf_op jit(solution)/shard_map/all_to_all | solution.py:278
  104.2 20.2 %all-to-all-start.4 = ((bf16[16,4,64,128]{3,2,1,0:T(8,128)(2,1)}), bf16[16,4,64,128]{3,2,1,0:T(8,128)(2,1)S(1)}, u32[]{:S(2)}, u32[]{:S(2)}) async-start(bf16[16,4,64,128]{3,2,1,0:T(8,128)(2,1)} %broadcast_in_dim.25), calls=%async_computation.4 | async-start | bytes 2097152 | tf_op jit(solution)/shard_map/all_to_all | solution.py:278
  108.4 102.3 %reduce-scatter.2.cloned.1.call-start = ((), (), s32[]{:S(2)}) async-start(), calls=%async_computation.9 | async-start | bytes 3342336 | tf_op jit(solution)/shard_map/reduce_scatter | solution.py:394
  124.5 11.1 %copy-start.12 = (s32[128,2]{0,1:T(2,128)S(1)}, s32[128,2]{0,1:T(2,128)}, u32[]{:S(2)}) copy-start(s32[128,2]{0,1:T(2,128)} %param.23) | copy-start | bytes 3076
  124.5 11.3 %collective-permute-start.4 = (bf16[4,64,2048]{2,1,0:T(8,128)(2,1)S(1)}, bf16[4,64,2048]{2,1,0:T(8,128)(2,1)S(1)}, u32[]{:S(2)}, u32[]{:S(2)}) collective-permute-start(bf16[4,64,2048]{2,1,0:T(8,128)(2,1)S(1)} %copy_bitcast_fusion.refs_0_), channel_id=1, source_target_pairs={{16,0},{0,16},{17,1},{1,17},{18,2},{2,18},{19,3},{3,19},{20,4},{4,... | collective-permute-start | bytes 3145736 | tf_op jit(solution)/shard_map/ppermute | solution.py:270
  133.0 14.3 %collective-permute-start.5 = (bf16[2,64,2048]{2,1,0:T(8,128)(2,1)}, bf16[2,64,2048]{2,1,0:T(8,128)(2,1)S(1)}, u32[]{:S(2)}, u32[]{:S(2)}) collective-permute-start(bf16[2,64,2048]{2,1,0:T(8,128)(2,1)} %bitcast.102), channel_id=1, source_target_pairs={{32,0},{64,32},{96,64},{0,96},{33,1},{65,33},{97,65},{1,97},{34,2}... | collective-permute-start | bytes 1572872 | tf_op jit(solution)/shard_map/ppermute | solution.py:270
  135.6 14.8 %collective-permute-start.6 = (bf16[2,64,2048]{2,1,0:T(8,128)(2,1)}, bf16[2,64,2048]{2,1,0:T(8,128)(2,1)}, u32[]{:S(2)}, u32[]{:S(2)}) collective-permute-start(bf16[2,64,2048]{2,1,0:T(8,128)(2,1)} %bitcast.102), channel_id=1, source_target_pairs={{96,0},{0,32},{32,64},{64,96},{97,1},{1,33},{33,65},{65,97},{98,2}... | collective-permute-start | bytes 1572872 | tf_op jit(solution)/shard_map/ppermute | solution.py:270
  135.8 49.3 %copy-start.4 = (s32[9]{0:T(128)}, s32[9]{0:T(128)S(1)}, u32[]{:S(2)}) copy-start(s32[9]{0:T(128)S(1)} %stack.42.place_ref) | copy-start | bytes 112
  135.9 15.6 %copy-start.5 = (bf16[16,2,8,8,128]{4,3,2,1,0:T(8,128)(2,1)S(1)}, bf16[16,2,8,8,128]{4,3,2,1,0:T(8,128)(2,1)}, u32[]{:S(2)}) copy-start(bf16[16,2,8,8,128]{4,3,2,1,0:T(8,128)(2,1)} %get-tuple-element.56) | copy-start | bytes 1572868
  150.4 3.4 %collective-permute-start.7 = (bf16[2,64,2048]{2,1,0:T(8,128)(2,1)S(1)}, bf16[2,64,2048]{2,1,0:T(8,128)(2,1)S(1)}, u32[]{:S(2)}, u32[]{:S(2)}) collective-permute-start(bf16[2,64,2048]{2,1,0:T(8,128)(2,1)S(1)} %collective-permute-done.5.refs_0_), channel_id=1, source_target_pairs={{16,0},{0,16},{17,1},{1,17},{18,2},{2,18},{19,3},{3,19},{20,4},{4,... | collective-permute-start | bytes 1572872 | tf_op jit(solution)/shard_map/ppermute | solution.py:270
  151.5 2.5 %collective-permute-start.8 = (bf16[2,64,2048]{2,1,0:T(8,128)(2,1)}, bf16[2,64,2048]{2,1,0:T(8,128)(2,1)S(1)}, u32[]{:S(2)}, u32[]{:S(2)}) collective-permute-start(bf16[2,64,2048]{2,1,0:T(8,128)(2,1)} %collective-permute-done.6.refs_2_), channel_id=1, source_target_pairs={{16,0},{0,16},{17,1},{1,17},{18,2},{2,18},{19,3},{3,19},{20,4},{4,... | collective-permute-start | bytes 1572872 | tf_op jit(solution)/shard_map/ppermute | solution.py:270
  151.6 13.2 %collective-permute-start.9 = (bf16[2,64,2048]{2,1,0:T(8,128)(2,1)S(1)}, bf16[2,64,2048]{2,1,0:T(8,128)(2,1)S(1)}, u32[]{:S(2)}, u32[]{:S(2)}) collective-permute-start(bf16[2,64,2048]{2,1,0:T(8,128)(2,1)S(1)} %bitcast.112), channel_id=1, source_target_pairs={{32,0},{64,32},{96,64},{0,96},{33,1},{65,33},{97,65},{1,97},{34,2}... | collective-permute-start | bytes 1572872 | tf_op jit(solution)/shard_map/ppermute | solution.py:270
  151.7 14.2 %collective-permute-start.10 = (bf16[2,64,2048]{2,1,0:T(8,128)(2,1)S(1)}, bf16[2,64,2048]{2,1,0:T(8,128)(2,1)S(1)}, u32[]{:S(2)}, u32[]{:S(2)}) collective-permute-start(bf16[2,64,2048]{2,1,0:T(8,128)(2,1)S(1)} %bitcast.113), channel_id=1, source_target_pairs={{96,0},{0,32},{32,64},{64,96},{97,1},{1,33},{33,65},{65,97},{98,2}... | collective-permute-start | bytes 1572872 | tf_op jit(solution)/shard_map/ppermute | solution.py:270
  165.9 3.0 %collective-permute-start.11 = (bf16[2,64,2048]{2,1,0:T(8,128)(2,1)S(1)}, bf16[2,64,2048]{2,1,0:T(8,128)(2,1)S(1)}, u32[]{:S(2)}, u32[]{:S(2)}) collective-permute-start(bf16[2,64,2048]{2,1,0:T(8,128)(2,1)S(1)} %collective-permute-done.9.refs_0_), channel_id=1, source_target_pairs={{16,0},{0,16},{17,1},{1,17},{18,2},{2,18},{19,3},{3,19},{20,4},{4,... | collective-permute-start | bytes 1572872 | tf_op jit(solution)/shard_map/ppermute | solution.py:270
  167.3 2.3 collective-permute-start.12
  167.3 13.1 %collective-permute-start.13 = (bf16[2,64,2048]{2,1,0:T(8,128)(2,1)S(1)}, bf16[2,64,2048]{2,1,0:T(8,128)(2,1)S(1)}, u32[]{:S(2)}, u32[]{:S(2)}) collective-permute-start(bf16[2,64,2048]{2,1,0:T(8,128)(2,1)S(1)} %collective-permute-done.5.refs_0_), channel_id=1, source_target_pairs={{32,0},{64,32},{96,64},{0,96},{33,1},{65,33},{97,65},{1,97},{34,2}... | collective-permute-start | bytes 1572872 | tf_op jit(solution)/shard_map/ppermute | solution.py:270
  167.3 14.0 %collective-permute-start.14 = (bf16[2,64,2048]{2,1,0:T(8,128)(2,1)S(1)}, bf16[2,64,2048]{2,1,0:T(8,128)(2,1)S(1)}, u32[]{:S(2)}, u32[]{:S(2)}) collective-permute-start(bf16[2,64,2048]{2,1,0:T(8,128)(2,1)S(1)} %collective-permute-done.10.refs_2_), channel_id=1, source_target_pairs={{96,0},{0,32},{32,64},{64,96},{97,1},{1,33},{33,65},{65,97},{98,2}... | collective-permute-start | bytes 1572872 | tf_op jit(solution)/shard_map/ppermute | solution.py:270
  181.3 3.1 %collective-permute-start.15 = (bf16[2,64,2048]{2,1,0:T(8,128)(2,1)S(1)}, bf16[2,64,2048]{2,1,0:T(8,128)(2,1)S(1)}, u32[]{:S(2)}, u32[]{:S(2)}) collective-permute-start(bf16[2,64,2048]{2,1,0:T(8,128)(2,1)S(1)} %collective-permute-done.13.refs_0_), channel_id=1, source_target_pairs={{16,0},{0,16},{17,1},{1,17},{18,2},{2,18},{19,3},{3,19},{20,4},{4,... | collective-permute-start | bytes 1572872 | tf_op jit(solution)/shard_map/ppermute | solution.py:270
  182.9 2.3 collective-permute-start.16
  208.6 4.9 %collective-permute-start.17 = (f32[8,256]{1,0:T(8,128)S(1)}, f32[8,256]{1,0:T(8,128)S(1)}, u32[]{:S(2)}, u32[]{:S(2)}) collective-permute-start(f32[8,256]{1,0:T(8,128)S(1)} %reduce_sum.78), channel_id=1, source_target_pairs={{32,0},{64,32},{96,64},{0,96},{33,1},{65,33},{97,65},{1,97},{34,2}... | collective-permute-start | bytes 24584 | tf_op jit(solution)/shard_map/ppermute | solution.py:270
  208.7 4.9 %collective-permute-start.18 = (f32[8,256]{1,0:T(8,128)S(1)}, f32[8,256]{1,0:T(8,128)S(1)}, u32[]{:S(2)}, u32[]{:S(2)}) collective-permute-start(f32[8,256]{1,0:T(8,128)S(1)} %reduce_sum.78), channel_id=1, source_target_pairs={{64,0},{96,32},{0,64},{32,96},{65,1},{97,33},{1,65},{33,97},{66,2}... | collective-permute-start | bytes 24584 | tf_op jit(solution)/shard_map/ppermute | solution.py:270
  210.7 3.7 %collective-permute-start.19 = (f32[8,256]{1,0:T(8,128)S(1)}, f32[8,256]{1,0:T(8,128)S(1)}, u32[]{:S(2)}, u32[]{:S(2)}) collective-permute-start(f32[8,256]{1,0:T(8,128)S(1)} %reduce_sum.78), channel_id=1, source_target_pairs={{96,0},{0,32},{32,64},{64,96},{97,1},{1,33},{33,65},{65,97},{98,2}... | collective-permute-start | bytes 24584 | tf_op jit(solution)/shard_map/ppermute | solution.py:270
  214.4 4.4 %collective-permute-start.20 = (f32[8,256]{1,0:T(8,128)S(1)}, f32[8,256]{1,0:T(8,128)S(1)}, u32[]{:S(2)}, u32[]{:S(2)}) collective-permute-start(f32[8,256]{1,0:T(8,128)S(1)} %add_add_fusion), channel_id=1, source_target_pairs={{16,0},{0,16},{17,1},{1,17},{18,2},{2,18},{19,3},{3,19},{20,4},{4,... | collective-permute-start | bytes 24584 | tf_op jit(solution)/shard_map/ppermute | solution.py:270
  219.8 10.3 %copy-start.1 = (bf16[4,2048,128]{2,1,0:T(8,128)(2,1)S(1)}, bf16[4,2048,128]{2,1,0:T(8,128)(2,1)}, u32[]{:S(2)}) copy-start(bf16[4,2048,128]{2,1,0:T(8,128)(2,1)} %param.26) | copy-start | bytes 6291460
Sparse Core Ops, SparseCore 0:
  9.7 44.9 all-gather.4
  59.4 50.4 all-gather.2
  124.6 81.9 reduce-scatter.1

commit v10 on v9

--- a/solution.py
+++ b/solution.py
@@ -294,27 +294,11 @@
     return ordered
 
 
-def own_half_of(out_weight):
-    half = out_weight.shape[0] // 2
-    return lax.dynamic_slice_in_dim(out_weight, lax.axis_index("core") * half, half, 0)
-
-
-def out_weights(pieces):
-    own = jnp.concatenate(pieces, axis=1)
-    return own, ring(own, "core", CORE, 1)
-
-
-def out_projection(attended, own_weight, other_weight):
-    rows, depth = attended.shape
-    half = depth // 2
-    core = lax.axis_index("core")
-    group = lax.all_gather(attended, "z", axis=0, tiled=True)
-    own_part = lax.dynamic_slice_in_dim(group, core * half, half, 1)
-    other_part = lax.dynamic_slice_in_dim(group, (1 - core) * half, half, 1)
-    columns = (
-        jnp.dot(own_part, own_weight, preferred_element_type=F32)
-        + jnp.dot(other_part, other_weight, preferred_element_type=F32)
-    ).astype(BF)
+def out_projection(group, weights):
+    rows = group.shape[0] // Z
+    columns = jnp.concatenate(
+        [jnp.dot(group, w, preferred_element_type=F32).astype(BF) for w in weights], axis=1
+    )
     width = columns.shape[1] // X
     back = swap(columns.reshape(Z, rows, X * width), "z")
     by_x = in_order(
@@ -367,11 +351,10 @@
     def pick(values):
         return jnp.dot(chosen, values, preferred_element_type=F32).astype(BF)
 
-    own_half = own_half_of(out_weight)
-    pieces = [own_half] + [ring(own_half, "x", X, shift) for shift in range(1, X)]
-    attended = attention(after(tree_q, own_half), tree_kv, kv_cache, cache_lengths, tree_parents)
-    own_weight, other_weight = out_weights(after(pieces, attended))
-    projected = out_projection(attended, own_weight, other_weight)
+    pieces = [ring(out_weight, "x", X, shift) for shift in range(1, X)]
+    attended = attention(tree_q, tree_kv, kv_cache, cache_lengths, tree_parents)
+    group = lax.all_gather(attended, "z", axis=0, tiled=True)
+    projected = out_projection(group, [out_weight] + after(pieces, group))
     first = (hidden.astype(F32) + rms_scale(projected, attn_post_gain)).astype(BF)
     normed = rms_scale(first, ff_pre_gain).astype(BF)
     mlp_rows = lax.all_gather(normed, XZ, axis=0, tiled=True)

time: 238 us -> 231 us (0.971)
  local copies, waits for them, and re-layouts: 16.5 us -> 11.4 us
  starting transfers between devices: 42.4 us -> 37.5 us
  waiting for transfers between devices: 42.7 us -> 45.1 us
    ppermute x21 -> x20, starting transfers between devices: 27.1 us -> 20.8 us  [ring(): lax.ppermute(values, axis, [((i + shift) % size, i) for i in range(size)])]
    all_gather x1, waiting for transfers between devices: 1.17 us -> 5.51 us  [per_device(): mlp_rows = lax.all_gather(normed, XZ, axis=0, tiled=True)]
    unnamed x34 -> x31, local copies, waits for them, and re-layouts: 8.17 us -> 5.1 us
    ppermute x21 -> x20, waiting for transfers between devices: 19.1 us -> 16.5 us  [ring(): lax.ppermute(values, axis, [((i + shift) % size, i) for i in range(size)])]
  transfers between devices with their start and end apart: 28 -> 27, of which waited for: 19 -> 19; matrix products, arithmetic and copies ran while one was open for 18% -> 16% of each run, Pallas kernels for 18% -> 19%
where the time goes in v10:
time: 231 us; the launch traced here: 230 us
  Pallas kernels  53.3 us (23%)
  waiting for transfers between devices  45.1 us (20%)
  starting transfers between devices  37.5 us (16%)
  blocking collectives  37.2 us (16%)
  matrix products  24.8 us (11%)
  between operations  14.8 us (6%)
  local copies, waits for them, and re-layouts  11.4 us (5%)
  other arithmetic  5.52 us (2%)
    pallas_call x4, Pallas kernels, some_logits(): pl.pallas_call(functools.partial(logits_kernel, first, parts), out_shape=...  38.9 us
    all_to_all x2, blocking collectives, swap(): return lax.all_to_all(copies, axes, split_axis=0, concat_axis=0, tiled=True)  23.4 us
    all_to_all x4, waiting for transfers between devices, swap(): return lax.all_to_all(copies, axes, split_axis=0, concat_axis=0, tiled=True)  22.3 us
    ppermute x20, starting transfers between devices, ring(): lax.ppermute(values, axis, [((i + shift) % size, i) for i in range(size)])  20.8 us
    ppermute x20, waiting for transfers between devices, ring(): lax.ppermute(values, axis, [((i + shift) % size, i) for i in range(size)])  16.5 us
    all_to_all x4, starting transfers between devices, swap(): return lax.all_to_all(copies, axes, split_axis=0, concat_axis=0, tiled=True)  16.4 us
    all_gather x1, blocking collectives, per_device(): group = lax.all_gather(attended, 'z', axis=0, tiled=True)  13.8 us
    dot_general x2, matrix products, unit_terms(): lax.dot_general(active, weights[2], (((1,), (1,)), ((), ())), preferred_e...  12.5 us
  transfers between devices with their start and end apart: 27, of which 19 were waited for; matrix products, arithmetic and copies ran while one was open for 16% of the time, Pallas kernels for 19%

profile of v10, /device:TPU:1, one launch (start us, length us, event | category | flops | bytes accessed | tf_op | source)
XLA Modules:
  0.0 229.5 jit_solution(5150458612421190937)
XLA Ops:
  7.2 0.7 all-gather.5.cloned.1.call-update
  7.9 3.4 %collective-permute-start = (bf16[2048,128]{1,0:T(8,128)(2,1)}, bf16[2048,128]{1,0:T(8,128)(2,1)S(1)}, u32[]{:S(2)}, u32[]{:S(2)}) collective-permute-start(bf16[2048,128]{1,0:T(8,128)(2,1)} %param.24), channel_id=1, source_target_pairs={{4,0},{8,4},{12,8},{0,12},{5,1},{9,5},{13,9},{1,13},{6,2},{10,6},{... | collective-permute-start | bytes 1572872 | tf_op jit(solution)/shard_map/ppermute | solution.py:270
  11.3 0.5 collective-permute-start.1
  11.8 0.6 collective-permute-start.2
  13.1 0.9 copy.48
  14.0 0.7 copy.33.parents_ref
  14.7 2.2 copy-done.2
  16.9 0.9 copy-done.3
  17.8 4.0 %shard_map.167 = bf16[48,2048]{1,0:T(8,128)(2,1)S(1)} custom-call(s32[1]{0:T(128)S(6)} %copy.49.length_ref, bf16[48,2048]{1,0:T(8,128)(2,1)S(1)} %copy-done.3, bf16[2,48,512]{2,1,0:T(8,128)(2,1)S(1)} %bitcast.110, s32[48,1]{1,0:T(8,128)S(1)} %copy.33.parents_ref, bf16[1,2,2,2048,256]{4,3,2,1,0:T(8,128)(2,1)S(1)} %copy-done.2, ...), custom_call_target="tpu_custom_call" | custom-call | flops 805306368 | bytes 4194304 | tf_op jit(solution)/shard_map/pallas_call | solution.py:78
  21.8 13.8 %all_gather.9 = bf16[192,2048]{1,0:T(8,128)(2,1)S(1)} all-gather(bf16[48,2048]{1,0:T(8,128)(2,1)S(1)} %shard_map.167), channel_id=1, replica_groups=mesh['y'=4,'core'=2,'x'=4,'z'=4] {'z'}, dimensions={0}, use_global_device_ids=true | all-gather | bytes 983040 | tf_op jit(solution)/shard_map/all_gather | solution.py:356
  36.0 2.2 collective-permute-done.2
  38.2 1.4 convolution_convert_fusion.4
  40.4 0.7 pad_maximum_fusion
  41.1 5.0 %all-to-all-start = ((bf16[4,48,512]{2,1,0:T(8,128)(2,1)}), bf16[4,48,512]{2,1,0:T(8,128)(2,1)S(1)}, u32[]{:S(2)}, u32[]{:S(2)}) async-start(bf16[4,48,512]{2,1,0:T(8,128)(2,1)} %bitcast.2), calls=%async_computation | async-start | bytes 393216 | tf_op jit(solution)/shard_map/all_to_all | solution.py:278
  46.1 5.2 %all-to-all-done = bf16[4,48,512]{2,1,0:T(8,128)(2,1)S(1)} async-done(((bf16[4,48,512]{2,1,0:T(8,128)(2,1)}), bf16[4,48,512]{2,1,0:T(8,128)(2,1)S(1)}, u32[]{:S(2)}, u32[]{:S(2)}) %all-to-all-start) | async-done | bytes 196640 | tf_op jit(solution)/shard_map/all_to_all | solution.py:278
  52.0 0.8 fusion.31
  52.8 1.1 convolution_convert_fusion.2
  54.1 9.9 %all_to_all.30 = bf16[16,4,2048]{2,1,0:T(4,128)(2,1)S(1)} all-to-all(bf16[16,4,2048]{2,1,0:T(4,128)(2,1)S(1)} %broadcast_in_dim.23), channel_id=1, replica_groups=mesh['y'=4,'core'=2,'x'=4,'z'=4] {'x','z'}, dimensions={0} | all-to-all | bytes 524288 | tf_op jit(solution)/shard_map/all_to_all | solution.py:278
  64.1 2.4 %fusion.39 = f32[64,512]{1,0:T(8,128)S(1)} fusion(bf16[64,2048]{1,0:T(8,128)(2,1)S(1)} %reshape.104, bf16[3,2048,512]{1,2,0:T(8,128)(2,1)} %all-gather.5.cloned.1.call-done), kind=kOutput, calls=%fused_computation.68 | convolution fusion | flops 134479872 | bytes 2490368 | tf_op jit(solution)/shard_map/dot_general | solution.py:315
  66.5 3.5 %convolution_convert_fusion.1 = bf16[64,2048]{1,0:T(8,128)(2,1)S(1)} fusion(bf16[3,2048,512]{1,2,0:T(8,128)(2,1)} %all-gather.5.cloned.1.call-done, f32[64,512]{1,0:T(8,128)S(1)} %fusion.39, bf16[64,2048]{1,0:T(8,128)(2,1)S(1)} %reshape.104), kind=kOutput, calls=%fused_computation.2 | convolution fusion | flops 268632064 | bytes 4849664 | tf_op jit(solution)/shard_map/dot_general | solution.py:318
  70.1 0.8 reshape.105
  70.9 3.6 %all-to-all-start.2 = ((bf16[16,4,2048]{2,1,0:T(4,128)(2,1)}), bf16[16,4,2048]{2,1,0:T(4,128)(2,1)S(1)}, u32[]{:S(2)}, u32[]{:S(2)}) async-start(bf16[16,4,2048]{2,1,0:T(4,128)(2,1)} %reshape.105), calls=%async_computation.2 | async-start | bytes 524288 | tf_op jit(solution)/shard_map/all_to_all | solution.py:278
  74.5 7.9 %all-to-all-done.2 = bf16[16,4,2048]{2,1,0:T(4,128)(2,1)S(1)} async-done(((bf16[16,4,2048]{2,1,0:T(4,128)(2,1)}), bf16[16,4,2048]{2,1,0:T(4,128)(2,1)S(1)}, u32[]{:S(2)}, u32[]{:S(2)}) %all-to-all-start.2) | async-done | bytes 262176 | tf_op jit(solution)/shard_map/all_to_all | solution.py:278
  83.1 0.8 broadcast_in_dim.24
  83.9 3.5 %all-to-all-start.3 = ((bf16[16,4,2048]{2,1,0:T(4,128)(2,1)}), bf16[16,4,2048]{2,1,0:T(4,128)(2,1)S(1)}, u32[]{:S(2)}, u32[]{:S(2)}) async-start(bf16[16,4,2048]{2,1,0:T(4,128)(2,1)} %broadcast_in_dim.24), calls=%async_computation.3 | async-start | bytes 524288 | tf_op jit(solution)/shard_map/all_to_all | solution.py:278
  87.4 9.2 %all-to-all-done.3 = bf16[16,4,2048]{2,1,0:T(4,128)(2,1)S(1)} async-done(((bf16[16,4,2048]{2,1,0:T(4,128)(2,1)}), bf16[16,4,2048]{2,1,0:T(4,128)(2,1)S(1)}, u32[]{:S(2)}, u32[]{:S(2)}) %all-to-all-start.3) | async-done | bytes 262176 | tf_op jit(solution)/shard_map/all_to_all | solution.py:278
  96.8 0.5 add_convert_fusion
  97.3 1.2 broadcast_in_dim.25
  98.5 4.3 %all-to-all-start.4 = ((bf16[16,4,64,128]{3,2,1,0:T(8,128)(2,1)}), bf16[16,4,64,128]{3,2,1,0:T(8,128)(2,1)S(1)}, u32[]{:S(2)}, u32[]{:S(2)}) async-start(bf16[16,4,64,128]{3,2,1,0:T(8,128)(2,1)} %broadcast_in_dim.25), calls=%async_computation.4 | async-start | bytes 2097152 | tf_op jit(solution)/shard_map/all_to_all | solution.py:278
  103.0 5.5 %all-gather.3.cloned.1.call-done = bf16[768,2048]{1,0:T(8,128)(2,1)} async-done(((bf16[48,2048]{1,0:T(8,128)(2,1)}), bf16[768,2048]{1,0:T(8,128)(2,1)}) %all-gather.3.cloned.1.call-update) | async-done | bytes 3145744 | tf_op jit(solution)/shard_map/all_gather | solution.py:360
  108.6 5.5 %fusion.4 = f32[768,512]{1,0:T(8,128)} fusion(bf16[768,2048]{1,0:T(8,128)(2,1)} %all-gather.3.cloned.1.call-done, bf16[3,2048,512]{1,2,0:T(8,128)(2,1)} %all-gather.5.cloned.1.call-done), kind=kOutput, calls=%fused_computation.12 | convolution fusion | flops 1610612736 | bytes 6815744 | tf_op jit(solution)/shard_map/dot_general | solution.py:315
  114.1 8.9 %convolution_convert_fusion = bf16[768,2048]{1,0:T(8,128)(2,1)} fusion(bf16[3,2048,512]{1,2,0:T(8,128)(2,1)} %all-gather.5.cloned.1.call-done, f32[768,512]{1,0:T(8,128)} %fusion.4, bf16[768,2048]{1,0:T(8,128)(2,1)} %all-gather.3.cloned.1.call-done), kind=kOutput, calls=%fused_computation | convolution fusion | flops 3226730496 | bytes 12058624 | tf_op jit(solution)/shard_map/dot_general | solution.py:318
  123.2 0.8 collective-permute-start.3
  124.0 0.9 slice_bitcast_fusion.19
  124.9 0.9 copy.47
  125.8 2.8 %collective-permute-start.4 = (bf16[2,64,2048]{2,1,0:T(8,128)(2,1)}, bf16[2,64,2048]{2,1,0:T(8,128)(2,1)S(1)}, u32[]{:S(2)}, u32[]{:S(2)}) collective-permute-start(bf16[2,64,2048]{2,1,0:T(8,128)(2,1)} %bitcast.108), channel_id=1, source_target_pairs={{32,0},{64,32},{96,64},{0,96},{33,1},{65,33},{97,65},{1,97},{34,2}... | collective-permute-start | bytes 1572872 | tf_op jit(solution)/shard_map/ppermute | solution.py:270
  128.9 9.7 %shard_map.168 = (bf16[2,4,64,2048]{3,2,1,0:T(8,128)(2,1)}, f32[2,256]{1,0:T(2,128)S(1)}) custom-call(s32[9]{0:T(128)S(1)} %stack.42.place_ref, bf16[4,64,2048]{2,1,0:T(8,128)(2,1)S(1)} %copy_bitcast_fusion.refs_0_, bf16[4,64,2048]{2,1,0:T(8,128)(2,1)S(1)} %collective-permute-done.3.refs_1_, s32[8,64,2]{2,1,0:T(8,128)S(1)} %bitcast.111, ...), custom_call_target="tpu_custom_call" | custom-call | flops 4294967296 | bytes 10485760 | tf_op jit(solution)/shard_map/pallas_call | solution.py:161
  138.5 1.7 collective-permute-done.4.refs_0_
  140.3 3.1 %collective-permute-done.5.refs_2_ = bf16[2,64,2048]{2,1,0:T(8,128)(2,1)} collective-permute-done((bf16[2,64,2048]{2,1,0:T(8,128)(2,1)}, bf16[2,64,2048]{2,1,0:T(8,128)(2,1)}, u32[]{:S(2)}, u32[]{:S(2)}) %collective-permute-start.5) | collective-permute-done | bytes 524320 | tf_op jit(solution)/shard_map/ppermute | solution.py:270
  143.3 1.1 collective-permute-start.6
  144.7 1.5 collective-permute-start.9
  146.1 0.6 collective-permute-done.6.refs_1_
  147.0 9.8 %shard_map.169 = (bf16[4,2,64,2048]{3,2,1,0:T(8,128)(2,1)}, f32[4,128]{1,0:T(4,128)S(1)}) custom-call(s32[9]{0:T(128)S(1)} %stack.42.place_ref, bf16[2,64,2048]{2,1,0:T(8,128)(2,1)S(1)} %collective-permute-done.4.refs_0_, bf16[2,64,2048]{2,1,0:T(8,128)(2,1)S(1)} %collective-permute-done.6.refs_1_, bf16[2,64,2048]{2,1,0:T(8,128)(2,1)} %collective-permute-done.5.refs_2_, ...), custom_call_target="tpu_custom_call" | custom-call | flops 4294967296 | bytes 10485760 | tf_op jit(solution)/shard_map/pallas_call | solution.py:161
  156.7 1.0 collective-permute-done.8.refs_0_
  157.7 1.1 collective-permute-done.9.refs_2_
  158.8 1.5 collective-permute-start.10
  160.3 1.5 collective-permute-start.13
  161.8 0.7 collective-permute-done.11.refs_3_
  162.6 9.8 %shard_map.170 = (bf16[4,2,64,2048]{3,2,1,0:T(8,128)(2,1)}, f32[4,128]{1,0:T(4,128)S(1)}) custom-call(s32[9]{0:T(128)S(1)} %stack.42.place_ref, bf16[2,64,2048]{2,1,0:T(8,128)(2,1)S(1)} %collective-permute-done.8.refs_0_, bf16[2,64,2048]{2,1,0:T(8,128)(2,1)S(1)} %collective-permute-done.10.refs_1_, bf16[2,64,2048]{2,1,0:T(8,128)(2,1)S(1)} %collective-permute-done.9.refs_2_, ...), custom_call_target="tpu_custom_call" | custom-call | flops 4294967296 | bytes 10485760 | tf_op jit(solution)/shard_map/pallas_call | solution.py:161
  172.4 1.0 collective-permute-done.12.refs_0_
  173.3 1.0 collective-permute-done.13.refs_1_
  174.4 1.5 collective-permute-start.14
  176.0 1.4 collective-permute-done.14.refs_2_
  177.4 0.7 collective-permute-done.15.refs_3_
  178.1 9.7 %shard_map.171 = (bf16[2,4,64,2048]{3,2,1,0:T(8,128)(2,1)}, f32[2,256]{1,0:T(2,128)S(1)}) custom-call(s32[9]{0:T(128)S(1)} %stack.42.place_ref, bf16[2,64,2048]{2,1,0:T(8,128)(2,1)S(1)} %collective-permute-done.12.refs_0_, bf16[2,64,2048]{2,1,0:T(8,128)(2,1)S(1)} %collective-permute-done.13.refs_1_, ...), custom_call_target="tpu_custom_call" | custom-call | flops 4294967296 | bytes 10485760 | tf_op jit(solution)/shard_map/pallas_call | solution.py:161
  188.0 13.4 %all_to_all.31 = f32[16,8,256]{2,1,0:T(8,128)S(1)} all-to-all(f32[16,8,256]{2,1,0:T(8,128)S(1)} %broadcast_in_dim.30), channel_id=1, replica_groups=mesh['y'=4,'core'=2,'x'=4,'z'=4] {'x','z'}, dimensions={0} | all-to-all | bytes 262144 | tf_op jit(solution)/shard_map/all_to_all | solution.py:278
  201.5 2.0 collective-permute-start.17
  203.5 1.1 fusion.27
  204.5 1.8 fusion.32
  206.3 0.9 collective-permute-done.18
  207.2 3.7 %collective-permute-start.19 = (f32[8,256]{1,0:T(8,128)S(1)}, f32[8,256]{1,0:T(8,128)S(1)}, u32[]{:S(2)}, u32[]{:S(2)}) collective-permute-start(f32[8,256]{1,0:T(8,128)S(1)} %add_add_fusion), channel_id=1, source_target_pairs={{16,0},{0,16},{17,1},{1,17},{18,2},{2,18},{19,3},{3,19},{20,4},{4,... | collective-permute-start | bytes 24584 | tf_op jit(solution)/shard_map/ppermute | solution.py:270
  210.8 0.8 collective-permute-done.19
  211.8 0.9 copy.38
  212.7 10.3 %shard_map.172 = bf16[4,8,64,2048]{3,2,1,0:T(8,128)(2,1)} custom-call(s32[9]{0:T(128)} %copy-done.4, bf16[2,4,64,2048]{3,2,1,0:T(8,128)(2,1)} %get-tuple-element.43.refs_0_, bf16[4,2,64,2048]{3,2,1,0:T(8,128)(2,1)} %get-tuple-element.44.refs_1_, bf16[4,2,64,2048]{3,2,1,0:T(8,128)(2,1)} %get-tuple-element.45.refs_2_, ...), custom_call_target="tpu_custom_call" | custom-call | flops 12582912 | bytes 16777216 | tf_op jit(solution)/shard_map/pallas_call | solution.py:233
  (91 shorter events, 4.5 us)
Async XLA Ops:
  7.2 89.6 %copy-start = (bf16[4,2048,128]{2,1,0:T(8,128)(2,1)S(1)}, bf16[4,2048,128]{2,1,0:T(8,128)(2,1)}, u32[]{:S(2)}) copy-start(bf16[4,2048,128]{2,1,0:T(8,128)(2,1)} %param.26) | copy-start | bytes 6291460
  7.2 56.9 %all-gather.5.cloned.1.call-start = ((), (), s32[]{:S(2)}) async-start(), calls=%async_computation.8 | async-start | bytes 7077888 | tf_op jit(solution)/shard_map/all_gather | solution.py:346
  7.9 28.1 %collective-permute-start = (bf16[2048,128]{1,0:T(8,128)(2,1)}, bf16[2048,128]{1,0:T(8,128)(2,1)S(1)}, u32[]{:S(2)}, u32[]{:S(2)}) collective-permute-start(bf16[2048,128]{1,0:T(8,128)(2,1)} %param.24), channel_id=1, source_target_pairs={{4,0},{8,4},{12,8},{0,12},{5,1},{9,5},{13,9},{1,13},{6,2},{10,6},{... | collective-permute-start | bytes 1572872 | tf_op jit(solution)/shard_map/ppermute | solution.py:270
  11.3 24.7 %collective-permute-start.1 = (bf16[2048,128]{1,0:T(8,128)(2,1)}, bf16[2048,128]{1,0:T(8,128)(2,1)S(1)}, u32[]{:S(2)}, u32[]{:S(2)}) collective-permute-start(bf16[2048,128]{1,0:T(8,128)(2,1)} %param.24), channel_id=1, source_target_pairs={{8,0},{12,4},{0,8},{4,12},{9,1},{13,5},{1,9},{5,13},{10,2},{14,6},... | collective-permute-start | bytes 1572872 | tf_op jit(solution)/shard_map/ppermute | solution.py:270
  11.8 26.4 %collective-permute-start.2 = (bf16[2048,128]{1,0:T(8,128)(2,1)}, bf16[2048,128]{1,0:T(8,128)(2,1)}, u32[]{:S(2)}, u32[]{:S(2)}) collective-permute-start(bf16[2048,128]{1,0:T(8,128)(2,1)} %param.24), channel_id=1, source_target_pairs={{12,0},{0,4},{4,8},{8,12},{13,1},{1,5},{5,9},{9,13},{14,2},{2,6},{... | collective-permute-start | bytes 1572872 | tf_op jit(solution)/shard_map/ppermute | solution.py:270
  14.7 2.2 copy-start.2
  16.9 0.9 copy-start.3
  17.8 17.8 %copy-start.6 = (bf16[2048,128]{1,0:T(8,128)(2,1)S(1)}, bf16[2048,128]{1,0:T(8,128)(2,1)}, u32[]{:S(2)}) copy-start(bf16[2048,128]{1,0:T(8,128)(2,1)} %param.24) | copy-start | bytes 1572868
  39.6 6.5 %copy-start.8 = (bf16[2048]{0:T(1024)(128)(2,1)S(1)}, bf16[2048]{0:T(1024)(128)(2,1)}, u32[]{:S(2)}) copy-start(bf16[2048]{0:T(1024)(128)(2,1)} %param.28) | copy-start | bytes 12292
  39.6 6.5 %copy-start.9 = (bf16[2048]{0:T(1024)(128)(2,1)S(1)}, bf16[2048]{0:T(1024)(128)(2,1)}, u32[]{:S(2)}) copy-start(bf16[2048]{0:T(1024)(128)(2,1)} %param.29) | copy-start | bytes 12292
  40.0 11.7 %copy-start.7 = (bf16[48,2048]{1,0:T(8,128)(2,1)S(1)}, bf16[48,2048]{1,0:T(8,128)(2,1)}, u32[]{:S(2)}) copy-start(bf16[48,2048]{1,0:T(8,128)(2,1)} %param.16) | copy-start | bytes 589828
  40.4 12.5 %copy-start.13 = (s32[1,4]{1,0:T(1,128)S(1)}, s32[1,4]{1,0:T(1,128)}, u32[]{:S(2)}) copy-start(s32[1,4]{1,0:T(1,128)} %param.22) | copy-start | bytes 52
  41.1 10.2 %all-to-all-start = ((bf16[4,48,512]{2,1,0:T(8,128)(2,1)}), bf16[4,48,512]{2,1,0:T(8,128)(2,1)S(1)}, u32[]{:S(2)}, u32[]{:S(2)}) async-start(bf16[4,48,512]{2,1,0:T(8,128)(2,1)} %bitcast.2), calls=%async_computation | async-start | bytes 393216 | tf_op jit(solution)/shard_map/all_to_all | solution.py:278
  46.1 62.4 %all-gather.3.cloned.1.call-start = ((), (), s32[]{:S(2)}) async-start(), calls=%async_computation.7 | async-start | bytes 3342336 | tf_op jit(solution)/shard_map/all_gather | solution.py:360
  66.5 7.9 %copy-start.10 = (bf16[2048]{0:T(1024)(128)(2,1)S(1)}, bf16[2048]{0:T(1024)(128)(2,1)}, u32[]{:S(2)}) copy-start(bf16[2048]{0:T(1024)(128)(2,1)} %param.30) | copy-start | bytes 12292
  66.5 7.9 %copy-start.11 = (bf16[2048]{0:T(1024)(128)(2,1)S(1)}, bf16[2048]{0:T(1024)(128)(2,1)}, u32[]{:S(2)}) copy-start(bf16[2048]{0:T(1024)(128)(2,1)} %param.31) | copy-start | bytes 12292
  70.9 11.5 %all-to-all-start.2 = ((bf16[16,4,2048]{2,1,0:T(4,128)(2,1)}), bf16[16,4,2048]{2,1,0:T(4,128)(2,1)S(1)}, u32[]{:S(2)}, u32[]{:S(2)}) async-start(bf16[16,4,2048]{2,1,0:T(4,128)(2,1)} %reshape.105), calls=%async_computation.2 | async-start | bytes 524288 | tf_op jit(solution)/shard_map/all_to_all | solution.py:278
  83.9 12.7 %all-to-all-start.3 = ((bf16[16,4,2048]{2,1,0:T(4,128)(2,1)}), bf16[16,4,2048]{2,1,0:T(4,128)(2,1)S(1)}, u32[]{:S(2)}, u32[]{:S(2)}) async-start(bf16[16,4,2048]{2,1,0:T(4,128)(2,1)} %broadcast_in_dim.24), calls=%async_computation.3 | async-start | bytes 524288 | tf_op jit(solution)/shard_map/all_to_all | solution.py:278
  98.5 24.5 %all-to-all-start.4 = ((bf16[16,4,64,128]{3,2,1,0:T(8,128)(2,1)}), bf16[16,4,64,128]{3,2,1,0:T(8,128)(2,1)S(1)}, u32[]{:S(2)}, u32[]{:S(2)}) async-start(bf16[16,4,64,128]{3,2,1,0:T(8,128)(2,1)} %broadcast_in_dim.25), calls=%async_computation.4 | async-start | bytes 2097152 | tf_op jit(solution)/shard_map/all_to_all | solution.py:278
  102.8 100.7 %reduce-scatter.2.cloned.1.call-start = ((), (), s32[]{:S(2)}) async-start(), calls=%async_computation.9 | async-start | bytes 3342336 | tf_op jit(solution)/shard_map/reduce_scatter | solution.py:377
  123.2 5.4 %copy-start.12 = (s32[128,2]{0,1:T(2,128)S(1)}, s32[128,2]{0,1:T(2,128)}, u32[]{:S(2)}) copy-start(s32[128,2]{0,1:T(2,128)} %param.23) | copy-start | bytes 3076
  123.2 5.6 %collective-permute-start.3 = (bf16[4,64,2048]{2,1,0:T(8,128)(2,1)S(1)}, bf16[4,64,2048]{2,1,0:T(8,128)(2,1)S(1)}, u32[]{:S(2)}, u32[]{:S(2)}) collective-permute-start(bf16[4,64,2048]{2,1,0:T(8,128)(2,1)S(1)} %copy_bitcast_fusion.refs_0_), channel_id=1, source_target_pairs={{16,0},{0,16},{17,1},{1,17},{18,2},{2,18},{19,3},{3,19},{20,4},{4,... | collective-permute-start | bytes 3145736 | tf_op jit(solution)/shard_map/ppermute | solution.py:270
  125.8 14.4 %collective-permute-start.4 = (bf16[2,64,2048]{2,1,0:T(8,128)(2,1)}, bf16[2,64,2048]{2,1,0:T(8,128)(2,1)S(1)}, u32[]{:S(2)}, u32[]{:S(2)}) collective-permute-start(bf16[2,64,2048]{2,1,0:T(8,128)(2,1)} %bitcast.108), channel_id=1, source_target_pairs={{32,0},{64,32},{96,64},{0,96},{33,1},{65,33},{97,65},{1,97},{34,2}... | collective-permute-start | bytes 1572872 | tf_op jit(solution)/shard_map/ppermute | solution.py:270
  128.6 14.8 %collective-permute-start.5 = (bf16[2,64,2048]{2,1,0:T(8,128)(2,1)}, bf16[2,64,2048]{2,1,0:T(8,128)(2,1)}, u32[]{:S(2)}, u32[]{:S(2)}) collective-permute-start(bf16[2,64,2048]{2,1,0:T(8,128)(2,1)} %bitcast.108), channel_id=1, source_target_pairs={{96,0},{0,32},{32,64},{64,96},{97,1},{1,33},{33,65},{65,97},{98,2}... | collective-permute-start | bytes 1572872 | tf_op jit(solution)/shard_map/ppermute | solution.py:270
  128.8 49.3 %copy-start.4 = (s32[9]{0:T(128)}, s32[9]{0:T(128)S(1)}, u32[]{:S(2)}) copy-start(s32[9]{0:T(128)S(1)} %stack.42.place_ref) | copy-start | bytes 112
  128.9 15.6 %copy-start.5 = (bf16[16,2,8,8,128]{4,3,2,1,0:T(8,128)(2,1)S(1)}, bf16[16,2,8,8,128]{4,3,2,1,0:T(8,128)(2,1)}, u32[]{:S(2)}) copy-start(bf16[16,2,8,8,128]{4,3,2,1,0:T(8,128)(2,1)} %get-tuple-element.52) | copy-start | bytes 1572868
  143.3 3.4 %collective-permute-start.6 = (bf16[2,64,2048]{2,1,0:T(8,128)(2,1)S(1)}, bf16[2,64,2048]{2,1,0:T(8,128)(2,1)S(1)}, u32[]{:S(2)}, u32[]{:S(2)}) collective-permute-start(bf16[2,64,2048]{2,1,0:T(8,128)(2,1)S(1)} %collective-permute-done.4.refs_0_), channel_id=1, source_target_pairs={{16,0},{0,16},{17,1},{1,17},{18,2},{2,18},{19,3},{3,19},{20,4},{4,... | collective-permute-start | bytes 1572872 | tf_op jit(solution)/shard_map/ppermute | solution.py:270
  144.5 2.5 %collective-permute-start.7 = (bf16[2,64,2048]{2,1,0:T(8,128)(2,1)}, bf16[2,64,2048]{2,1,0:T(8,128)(2,1)S(1)}, u32[]{:S(2)}, u32[]{:S(2)}) collective-permute-start(bf16[2,64,2048]{2,1,0:T(8,128)(2,1)} %collective-permute-done.5.refs_2_), channel_id=1, source_target_pairs={{16,0},{0,16},{17,1},{1,17},{18,2},{2,18},{19,3},{3,19},{20,4},{4,... | collective-permute-start | bytes 1572872 | tf_op jit(solution)/shard_map/ppermute | solution.py:270
  144.6 13.2 %collective-permute-start.8 = (bf16[2,64,2048]{2,1,0:T(8,128)(2,1)S(1)}, bf16[2,64,2048]{2,1,0:T(8,128)(2,1)S(1)}, u32[]{:S(2)}, u32[]{:S(2)}) collective-permute-start(bf16[2,64,2048]{2,1,0:T(8,128)(2,1)S(1)} %bitcast.118), channel_id=1, source_target_pairs={{32,0},{64,32},{96,64},{0,96},{33,1},{65,33},{97,65},{1,97},{34,2}... | collective-permute-start | bytes 1572872 | tf_op jit(solution)/shard_map/ppermute | solution.py:270
  144.7 14.2 %collective-permute-start.9 = (bf16[2,64,2048]{2,1,0:T(8,128)(2,1)S(1)}, bf16[2,64,2048]{2,1,0:T(8,128)(2,1)S(1)}, u32[]{:S(2)}, u32[]{:S(2)}) collective-permute-start(bf16[2,64,2048]{2,1,0:T(8,128)(2,1)S(1)} %bitcast.119), channel_id=1, source_target_pairs={{96,0},{0,32},{32,64},{64,96},{97,1},{1,33},{33,65},{65,97},{98,2}... | collective-permute-start | bytes 1572872 | tf_op jit(solution)/shard_map/ppermute | solution.py:270
  158.8 3.0 %collective-permute-start.10 = (bf16[2,64,2048]{2,1,0:T(8,128)(2,1)S(1)}, bf16[2,64,2048]{2,1,0:T(8,128)(2,1)S(1)}, u32[]{:S(2)}, u32[]{:S(2)}) collective-permute-start(bf16[2,64,2048]{2,1,0:T(8,128)(2,1)S(1)} %collective-permute-done.8.refs_0_), channel_id=1, source_target_pairs={{16,0},{0,16},{17,1},{1,17},{18,2},{2,18},{19,3},{3,19},{20,4},{4,... | collective-permute-start | bytes 1572872 | tf_op jit(solution)/shard_map/ppermute | solution.py:270
  160.3 2.3 collective-permute-start.11
  160.3 13.0 %collective-permute-start.12 = (bf16[2,64,2048]{2,1,0:T(8,128)(2,1)S(1)}, bf16[2,64,2048]{2,1,0:T(8,128)(2,1)S(1)}, u32[]{:S(2)}, u32[]{:S(2)}) collective-permute-start(bf16[2,64,2048]{2,1,0:T(8,128)(2,1)S(1)} %collective-permute-done.4.refs_0_), channel_id=1, source_target_pairs={{32,0},{64,32},{96,64},{0,96},{33,1},{65,33},{97,65},{1,97},{34,2}... | collective-permute-start | bytes 1572872 | tf_op jit(solution)/shard_map/ppermute | solution.py:270
  160.3 14.1 %collective-permute-start.13 = (bf16[2,64,2048]{2,1,0:T(8,128)(2,1)S(1)}, bf16[2,64,2048]{2,1,0:T(8,128)(2,1)S(1)}, u32[]{:S(2)}, u32[]{:S(2)}) collective-permute-start(bf16[2,64,2048]{2,1,0:T(8,128)(2,1)S(1)} %collective-permute-done.9.refs_2_), channel_id=1, source_target_pairs={{96,0},{0,32},{32,64},{64,96},{97,1},{1,33},{33,65},{65,97},{98,2}... | collective-permute-start | bytes 1572872 | tf_op jit(solution)/shard_map/ppermute | solution.py:270
  174.4 3.0 %collective-permute-start.14 = (bf16[2,64,2048]{2,1,0:T(8,128)(2,1)S(1)}, bf16[2,64,2048]{2,1,0:T(8,128)(2,1)S(1)}, u32[]{:S(2)}, u32[]{:S(2)}) collective-permute-start(bf16[2,64,2048]{2,1,0:T(8,128)(2,1)S(1)} %collective-permute-done.12.refs_0_), channel_id=1, source_target_pairs={{16,0},{0,16},{17,1},{1,17},{18,2},{2,18},{19,3},{3,19},{20,4},{4,... | collective-permute-start | bytes 1572872 | tf_op jit(solution)/shard_map/ppermute | solution.py:270
  175.8 2.3 collective-permute-start.15
  201.4 4.9 %collective-permute-start.16 = (f32[8,256]{1,0:T(8,128)S(1)}, f32[8,256]{1,0:T(8,128)S(1)}, u32[]{:S(2)}, u32[]{:S(2)}) collective-permute-start(f32[8,256]{1,0:T(8,128)S(1)} %reduce_sum.78), channel_id=1, source_target_pairs={{32,0},{64,32},{96,64},{0,96},{33,1},{65,33},{97,65},{1,97},{34,2}... | collective-permute-start | bytes 24584 | tf_op jit(solution)/shard_map/ppermute | solution.py:270
  201.5 4.8 %collective-permute-start.17 = (f32[8,256]{1,0:T(8,128)S(1)}, f32[8,256]{1,0:T(8,128)S(1)}, u32[]{:S(2)}, u32[]{:S(2)}) collective-permute-start(f32[8,256]{1,0:T(8,128)S(1)} %reduce_sum.78), channel_id=1, source_target_pairs={{64,0},{96,32},{0,64},{32,96},{65,1},{97,33},{1,65},{33,97},{66,2}... | collective-permute-start | bytes 24584 | tf_op jit(solution)/shard_map/ppermute | solution.py:270
  203.5 3.7 %collective-permute-start.18 = (f32[8,256]{1,0:T(8,128)S(1)}, f32[8,256]{1,0:T(8,128)S(1)}, u32[]{:S(2)}, u32[]{:S(2)}) collective-permute-start(f32[8,256]{1,0:T(8,128)S(1)} %reduce_sum.78), channel_id=1, source_target_pairs={{96,0},{0,32},{32,64},{64,96},{97,1},{1,33},{33,65},{65,97},{98,2}... | collective-permute-start | bytes 24584 | tf_op jit(solution)/shard_map/ppermute | solution.py:270
  207.2 4.5 %collective-permute-start.19 = (f32[8,256]{1,0:T(8,128)S(1)}, f32[8,256]{1,0:T(8,128)S(1)}, u32[]{:S(2)}, u32[]{:S(2)}) collective-permute-start(f32[8,256]{1,0:T(8,128)S(1)} %add_add_fusion), channel_id=1, source_target_pairs={{16,0},{0,16},{17,1},{1,17},{18,2},{2,18},{19,3},{3,19},{20,4},{4,... | collective-permute-start | bytes 24584 | tf_op jit(solution)/shard_map/ppermute | solution.py:270
  212.7 10.3 %copy-start.1 = (bf16[4,2048,128]{2,1,0:T(8,128)(2,1)S(1)}, bf16[4,2048,128]{2,1,0:T(8,128)(2,1)}, u32[]{:S(2)}) copy-start(bf16[4,2048,128]{2,1,0:T(8,128)(2,1)} %param.26) | copy-start | bytes 6291460
Sparse Core Ops, SparseCore 0:
  9.7 44.5 all-gather.4
  57.1 51.4 all-gather.2
  123.3 75.6 reduce-scatter.1

commit v11 on v10

--- a/solution.py
+++ b/solution.py
@@ -387,7 +387,7 @@
     low = drafts[:half]
     up_low, down_low = ring(low, "y", Y, 1), ring(low, "y", Y, 3)
     beside = ring(drafts, "core", CORE, 1)
-    high = after(drafts[half:], beside)
+    high = drafts[half:]
     up_high, down_high = ring(high, "y", Y, 1), ring(high, "y", Y, 3)
     table_a, totals_a = some_logits(
         0, (2, HEADS), place, [drafts, beside], pair, bounds, embedding

time: 231 us -> 231 us (level)
  no operation moved by 1% of the time
where the time goes in v11:
time: 231 us; the launch traced here: 230 us
  Pallas kernels  53.3 us (23%)
  waiting for transfers between devices  45.1 us (20%)
  starting transfers between devices  37.5 us (16%)
  blocking collectives  37.2 us (16%)
  matrix products  24.8 us (11%)
  between operations  14.8 us (6%)
  local copies, waits for them, and re-layouts  11.4 us (5%)
  other arithmetic  5.52 us (2%)
    pallas_call x4, Pallas kernels, some_logits(): pl.pallas_call(functools.partial(logits_kernel, first, parts), out_shape=...  38.9 us
    all_to_all x2, blocking collectives, swap(): return lax.all_to_all(copies, axes, split_axis=0, concat_axis=0, tiled=True)  23.4 us
    all_to_all x4, waiting for transfers between devices, swap(): return lax.all_to_all(copies, axes, split_axis=0, concat_axis=0, tiled=True)  22.3 us
    ppermute x20, starting transfers between devices, ring(): lax.ppermute(values, axis, [((i + shift) % size, i) for i in range(size)])  20.8 us
    ppermute x20, waiting for transfers between devices, ring(): lax.ppermute(values, axis, [((i + shift) % size, i) for i in range(size)])  16.5 us
    all_to_all x4, starting transfers between devices, swap(): return lax.all_to_all(copies, axes, split_axis=0, concat_axis=0, tiled=True)  16.4 us
    all_gather x1, blocking collectives, per_device(): group = lax.all_gather(attended, 'z', axis=0, tiled=True)  13.8 us
    dot_general x2, matrix products, unit_terms(): lax.dot_general(active, weights[2], (((1,), (1,)), ((), ())), preferred_e...  12.5 us
  transfers between devices with their start and end apart: 27, of which 19 were waited for; matrix products, arithmetic and copies ran while one was open for 16% of the time, Pallas kernels for 19%

profile of v11, /device:TPU:1, one launch (start us, length us, event | category | flops | bytes accessed | tf_op | source)
XLA Modules:
  0.0 229.5 jit_solution(5150458612421190937)
XLA Ops:
  7.2 0.7 all-gather.5.cloned.1.call-update
  7.9 3.4 %collective-permute-start = (bf16[2048,128]{1,0:T(8,128)(2,1)}, bf16[2048,128]{1,0:T(8,128)(2,1)S(1)}, u32[]{:S(2)}, u32[]{:S(2)}) collective-permute-start(bf16[2048,128]{1,0:T(8,128)(2,1)} %param.24), channel_id=1, source_target_pairs={{4,0},{8,4},{12,8},{0,12},{5,1},{9,5},{13,9},{1,13},{6,2},{10,6},{... | collective-permute-start | bytes 1572872 | tf_op jit(solution)/shard_map/ppermute | solution.py:270
  11.3 0.5 collective-permute-start.1
  11.8 0.6 collective-permute-start.2
  13.1 0.9 copy.48
  14.0 0.7 copy.33.parents_ref
  14.7 2.2 copy-done.2
  16.9 0.9 copy-done.3
  17.8 4.0 %shard_map.167 = bf16[48,2048]{1,0:T(8,128)(2,1)S(1)} custom-call(s32[1]{0:T(128)S(6)} %copy.49.length_ref, bf16[48,2048]{1,0:T(8,128)(2,1)S(1)} %copy-done.3, bf16[2,48,512]{2,1,0:T(8,128)(2,1)S(1)} %bitcast.110, s32[48,1]{1,0:T(8,128)S(1)} %copy.33.parents_ref, bf16[1,2,2,2048,256]{4,3,2,1,0:T(8,128)(2,1)S(1)} %copy-done.2, ...), custom_call_target="tpu_custom_call" | custom-call | flops 805306368 | bytes 4194304 | tf_op jit(solution)/shard_map/pallas_call | solution.py:78
  21.8 13.8 %all_gather.9 = bf16[192,2048]{1,0:T(8,128)(2,1)S(1)} all-gather(bf16[48,2048]{1,0:T(8,128)(2,1)S(1)} %shard_map.167), channel_id=1, replica_groups=mesh['y'=4,'core'=2,'x'=4,'z'=4] {'z'}, dimensions={0}, use_global_device_ids=true | all-gather | bytes 983040 | tf_op jit(solution)/shard_map/all_gather | solution.py:356
  36.0 2.2 collective-permute-done.2
  38.2 1.4 convolution_convert_fusion.4
  40.4 0.7 pad_maximum_fusion
  41.1 5.0 %all-to-all-start = ((bf16[4,48,512]{2,1,0:T(8,128)(2,1)}), bf16[4,48,512]{2,1,0:T(8,128)(2,1)S(1)}, u32[]{:S(2)}, u32[]{:S(2)}) async-start(bf16[4,48,512]{2,1,0:T(8,128)(2,1)} %bitcast.2), calls=%async_computation | async-start | bytes 393216 | tf_op jit(solution)/shard_map/all_to_all | solution.py:278
  46.1 5.2 %all-to-all-done = bf16[4,48,512]{2,1,0:T(8,128)(2,1)S(1)} async-done(((bf16[4,48,512]{2,1,0:T(8,128)(2,1)}), bf16[4,48,512]{2,1,0:T(8,128)(2,1)S(1)}, u32[]{:S(2)}, u32[]{:S(2)}) %all-to-all-start) | async-done | bytes 196640 | tf_op jit(solution)/shard_map/all_to_all | solution.py:278
  52.0 0.8 fusion.31
  52.8 1.1 convolution_convert_fusion.2
  54.1 9.9 %all_to_all.30 = bf16[16,4,2048]{2,1,0:T(4,128)(2,1)S(1)} all-to-all(bf16[16,4,2048]{2,1,0:T(4,128)(2,1)S(1)} %broadcast_in_dim.23), channel_id=1, replica_groups=mesh['y'=4,'core'=2,'x'=4,'z'=4] {'x','z'}, dimensions={0} | all-to-all | bytes 524288 | tf_op jit(solution)/shard_map/all_to_all | solution.py:278
  64.1 2.4 %fusion.39 = f32[64,512]{1,0:T(8,128)S(1)} fusion(bf16[64,2048]{1,0:T(8,128)(2,1)S(1)} %reshape.104, bf16[3,2048,512]{1,2,0:T(8,128)(2,1)} %all-gather.5.cloned.1.call-done), kind=kOutput, calls=%fused_computation.68 | convolution fusion | flops 134479872 | bytes 2490368 | tf_op jit(solution)/shard_map/dot_general | solution.py:315
  66.5 3.5 %convolution_convert_fusion.1 = bf16[64,2048]{1,0:T(8,128)(2,1)S(1)} fusion(bf16[3,2048,512]{1,2,0:T(8,128)(2,1)} %all-gather.5.cloned.1.call-done, f32[64,512]{1,0:T(8,128)S(1)} %fusion.39, bf16[64,2048]{1,0:T(8,128)(2,1)S(1)} %reshape.104), kind=kOutput, calls=%fused_computation.2 | convolution fusion | flops 268632064 | bytes 4849664 | tf_op jit(solution)/shard_map/dot_general | solution.py:318
  70.1 0.8 reshape.105
  70.9 3.6 %all-to-all-start.2 = ((bf16[16,4,2048]{2,1,0:T(4,128)(2,1)}), bf16[16,4,2048]{2,1,0:T(4,128)(2,1)S(1)}, u32[]{:S(2)}, u32[]{:S(2)}) async-start(bf16[16,4,2048]{2,1,0:T(4,128)(2,1)} %reshape.105), calls=%async_computation.2 | async-start | bytes 524288 | tf_op jit(solution)/shard_map/all_to_all | solution.py:278
  74.5 7.9 %all-to-all-done.2 = bf16[16,4,2048]{2,1,0:T(4,128)(2,1)S(1)} async-done(((bf16[16,4,2048]{2,1,0:T(4,128)(2,1)}), bf16[16,4,2048]{2,1,0:T(4,128)(2,1)S(1)}, u32[]{:S(2)}, u32[]{:S(2)}) %all-to-all-start.2) | async-done | bytes 262176 | tf_op jit(solution)/shard_map/all_to_all | solution.py:278
  83.1 0.8 broadcast_in_dim.24
  83.9 3.5 %all-to-all-start.3 = ((bf16[16,4,2048]{2,1,0:T(4,128)(2,1)}), bf16[16,4,2048]{2,1,0:T(4,128)(2,1)S(1)}, u32[]{:S(2)}, u32[]{:S(2)}) async-start(bf16[16,4,2048]{2,1,0:T(4,128)(2,1)} %broadcast_in_dim.24), calls=%async_computation.3 | async-start | bytes 524288 | tf_op jit(solution)/shard_map/all_to_all | solution.py:278
  87.4 9.2 %all-to-all-done.3 = bf16[16,4,2048]{2,1,0:T(4,128)(2,1)S(1)} async-done(((bf16[16,4,2048]{2,1,0:T(4,128)(2,1)}), bf16[16,4,2048]{2,1,0:T(4,128)(2,1)S(1)}, u32[]{:S(2)}, u32[]{:S(2)}) %all-to-all-start.3) | async-done | bytes 262176 | tf_op jit(solution)/shard_map/all_to_all | solution.py:278
  96.8 0.5 add_convert_fusion
  97.3 1.2 broadcast_in_dim.25
  98.5 4.3 %all-to-all-start.4 = ((bf16[16,4,64,128]{3,2,1,0:T(8,128)(2,1)}), bf16[16,4,64,128]{3,2,1,0:T(8,128)(2,1)S(1)}, u32[]{:S(2)}, u32[]{:S(2)}) async-start(bf16[16,4,64,128]{3,2,1,0:T(8,128)(2,1)} %broadcast_in_dim.25), calls=%async_computation.4 | async-start | bytes 2097152 | tf_op jit(solution)/shard_map/all_to_all | solution.py:278
  103.0 5.5 %all-gather.3.cloned.1.call-done = bf16[768,2048]{1,0:T(8,128)(2,1)} async-done(((bf16[48,2048]{1,0:T(8,128)(2,1)}), bf16[768,2048]{1,0:T(8,128)(2,1)}) %all-gather.3.cloned.1.call-update) | async-done | bytes 3145744 | tf_op jit(solution)/shard_map/all_gather | solution.py:360
  108.6 5.5 %fusion.4 = f32[768,512]{1,0:T(8,128)} fusion(bf16[768,2048]{1,0:T(8,128)(2,1)} %all-gather.3.cloned.1.call-done, bf16[3,2048,512]{1,2,0:T(8,128)(2,1)} %all-gather.5.cloned.1.call-done), kind=kOutput, calls=%fused_computation.12 | convolution fusion | flops 1610612736 | bytes 6815744 | tf_op jit(solution)/shard_map/dot_general | solution.py:315
  114.1 8.9 %convolution_convert_fusion = bf16[768,2048]{1,0:T(8,128)(2,1)} fusion(bf16[3,2048,512]{1,2,0:T(8,128)(2,1)} %all-gather.5.cloned.1.call-done, f32[768,512]{1,0:T(8,128)} %fusion.4, bf16[768,2048]{1,0:T(8,128)(2,1)} %all-gather.3.cloned.1.call-done), kind=kOutput, calls=%fused_computation | convolution fusion | flops 3226730496 | bytes 12058624 | tf_op jit(solution)/shard_map/dot_general | solution.py:318
  123.2 0.8 collective-permute-start.3
  124.0 0.9 slice_bitcast_fusion.19
  124.9 0.9 copy.47
  125.8 2.8 %collective-permute-start.4 = (bf16[2,64,2048]{2,1,0:T(8,128)(2,1)}, bf16[2,64,2048]{2,1,0:T(8,128)(2,1)S(1)}, u32[]{:S(2)}, u32[]{:S(2)}) collective-permute-start(bf16[2,64,2048]{2,1,0:T(8,128)(2,1)} %bitcast.108), channel_id=1, source_target_pairs={{32,0},{64,32},{96,64},{0,96},{33,1},{65,33},{97,65},{1,97},{34,2}... | collective-permute-start | bytes 1572872 | tf_op jit(solution)/shard_map/ppermute | solution.py:270
  128.9 9.7 %shard_map.168 = (bf16[2,4,64,2048]{3,2,1,0:T(8,128)(2,1)}, f32[2,256]{1,0:T(2,128)S(1)}) custom-call(s32[9]{0:T(128)S(1)} %stack.42.place_ref, bf16[4,64,2048]{2,1,0:T(8,128)(2,1)S(1)} %copy_bitcast_fusion.refs_0_, bf16[4,64,2048]{2,1,0:T(8,128)(2,1)S(1)} %collective-permute-done.3.refs_1_, s32[8,64,2]{2,1,0:T(8,128)S(1)} %bitcast.111, ...), custom_call_target="tpu_custom_call" | custom-call | flops 4294967296 | bytes 10485760 | tf_op jit(solution)/shard_map/pallas_call | solution.py:161
  138.5 1.7 collective-permute-done.4.refs_0_
  140.3 3.1 %collective-permute-done.5.refs_2_ = bf16[2,64,2048]{2,1,0:T(8,128)(2,1)} collective-permute-done((bf16[2,64,2048]{2,1,0:T(8,128)(2,1)}, bf16[2,64,2048]{2,1,0:T(8,128)(2,1)}, u32[]{:S(2)}, u32[]{:S(2)}) %collective-permute-start.5) | collective-permute-done | bytes 524320 | tf_op jit(solution)/shard_map/ppermute | solution.py:270
  143.3 1.1 collective-permute-start.6
  144.7 1.5 collective-permute-start.9
  146.1 0.6 collective-permute-done.6.refs_1_
  147.0 9.8 %shard_map.169 = (bf16[4,2,64,2048]{3,2,1,0:T(8,128)(2,1)}, f32[4,128]{1,0:T(4,128)S(1)}) custom-call(s32[9]{0:T(128)S(1)} %stack.42.place_ref, bf16[2,64,2048]{2,1,0:T(8,128)(2,1)S(1)} %collective-permute-done.4.refs_0_, bf16[2,64,2048]{2,1,0:T(8,128)(2,1)S(1)} %collective-permute-done.6.refs_1_, bf16[2,64,2048]{2,1,0:T(8,128)(2,1)} %collective-permute-done.5.refs_2_, ...), custom_call_target="tpu_custom_call" | custom-call | flops 4294967296 | bytes 10485760 | tf_op jit(solution)/shard_map/pallas_call | solution.py:161
  156.7 1.0 collective-permute-done.8.refs_0_
  157.7 1.1 collective-permute-done.9.refs_2_
  158.8 1.5 collective-permute-start.10
  160.3 1.5 collective-permute-start.13
  161.8 0.7 collective-permute-done.11.refs_3_
  162.6 9.8 %shard_map.170 = (bf16[4,2,64,2048]{3,2,1,0:T(8,128)(2,1)}, f32[4,128]{1,0:T(4,128)S(1)}) custom-call(s32[9]{0:T(128)S(1)} %stack.42.place_ref, bf16[2,64,2048]{2,1,0:T(8,128)(2,1)S(1)} %collective-permute-done.8.refs_0_, bf16[2,64,2048]{2,1,0:T(8,128)(2,1)S(1)} %collective-permute-done.10.refs_1_, bf16[2,64,2048]{2,1,0:T(8,128)(2,1)S(1)} %collective-permute-done.9.refs_2_, ...), custom_call_target="tpu_custom_call" | custom-call | flops 4294967296 | bytes 10485760 | tf_op jit(solution)/shard_map/pallas_call | solution.py:161
  172.4 1.0 collective-permute-done.12.refs_0_
  173.3 1.0 collective-permute-done.13.refs_1_
  174.4 1.5 collective-permute-start.14
  176.0 1.4 collective-permute-done.14.refs_2_
  177.4 0.7 collective-permute-done.15.refs_3_
  178.1 9.7 %shard_map.171 = (bf16[2,4,64,2048]{3,2,1,0:T(8,128)(2,1)}, f32[2,256]{1,0:T(2,128)S(1)}) custom-call(s32[9]{0:T(128)S(1)} %stack.42.place_ref, bf16[2,64,2048]{2,1,0:T(8,128)(2,1)S(1)} %collective-permute-done.12.refs_0_, bf16[2,64,2048]{2,1,0:T(8,128)(2,1)S(1)} %collective-permute-done.13.refs_1_, ...), custom_call_target="tpu_custom_call" | custom-call | flops 4294967296 | bytes 10485760 | tf_op jit(solution)/shard_map/pallas_call | solution.py:161
  188.0 13.4 %all_to_all.31 = f32[16,8,256]{2,1,0:T(8,128)S(1)} all-to-all(f32[16,8,256]{2,1,0:T(8,128)S(1)} %broadcast_in_dim.30), channel_id=1, replica_groups=mesh['y'=4,'core'=2,'x'=4,'z'=4] {'x','z'}, dimensions={0} | all-to-all | bytes 262144 | tf_op jit(solution)/shard_map/all_to_all | solution.py:278
  201.5 2.0 collective-permute-start.17
  203.5 1.1 fusion.27
  204.5 1.8 fusion.32
  206.3 0.9 collective-permute-done.18
  207.2 3.7 %collective-permute-start.19 = (f32[8,256]{1,0:T(8,128)S(1)}, f32[8,256]{1,0:T(8,128)S(1)}, u32[]{:S(2)}, u32[]{:S(2)}) collective-permute-start(f32[8,256]{1,0:T(8,128)S(1)} %add_add_fusion), channel_id=1, source_target_pairs={{16,0},{0,16},{17,1},{1,17},{18,2},{2,18},{19,3},{3,19},{20,4},{4,... | collective-permute-start | bytes 24584 | tf_op jit(solution)/shard_map/ppermute | solution.py:270
  210.8 0.8 collective-permute-done.19
  211.8 0.9 copy.38
  212.7 10.3 %shard_map.172 = bf16[4,8,64,2048]{3,2,1,0:T(8,128)(2,1)} custom-call(s32[9]{0:T(128)} %copy-done.4, bf16[2,4,64,2048]{3,2,1,0:T(8,128)(2,1)} %get-tuple-element.41.refs_0_, bf16[4,2,64,2048]{3,2,1,0:T(8,128)(2,1)} %get-tuple-element.42.refs_1_, bf16[4,2,64,2048]{3,2,1,0:T(8,128)(2,1)} %get-tuple-element.43.refs_2_, ...), custom_call_target="tpu_custom_call" | custom-call | flops 12582912 | bytes 16777216 | tf_op jit(solution)/shard_map/pallas_call | solution.py:233
  (91 shorter events, 4.5 us)
Async XLA Ops:
  7.2 89.6 %copy-start = (bf16[4,2048,128]{2,1,0:T(8,128)(2,1)S(1)}, bf16[4,2048,128]{2,1,0:T(8,128)(2,1)}, u32[]{:S(2)}) copy-start(bf16[4,2048,128]{2,1,0:T(8,128)(2,1)} %param.26) | copy-start | bytes 6291460
  7.2 56.9 %all-gather.5.cloned.1.call-start = ((), (), s32[]{:S(2)}) async-start(), calls=%async_computation.8 | async-start | bytes 7077888 | tf_op jit(solution)/shard_map/all_gather | solution.py:346
  7.9 28.1 %collective-permute-start = (bf16[2048,128]{1,0:T(8,128)(2,1)}, bf16[2048,128]{1,0:T(8,128)(2,1)S(1)}, u32[]{:S(2)}, u32[]{:S(2)}) collective-permute-start(bf16[2048,128]{1,0:T(8,128)(2,1)} %param.24), channel_id=1, source_target_pairs={{4,0},{8,4},{12,8},{0,12},{5,1},{9,5},{13,9},{1,13},{6,2},{10,6},{... | collective-permute-start | bytes 1572872 | tf_op jit(solution)/shard_map/ppermute | solution.py:270
  11.3 24.7 %collective-permute-start.1 = (bf16[2048,128]{1,0:T(8,128)(2,1)}, bf16[2048,128]{1,0:T(8,128)(2,1)S(1)}, u32[]{:S(2)}, u32[]{:S(2)}) collective-permute-start(bf16[2048,128]{1,0:T(8,128)(2,1)} %param.24), channel_id=1, source_target_pairs={{8,0},{12,4},{0,8},{4,12},{9,1},{13,5},{1,9},{5,13},{10,2},{14,6},... | collective-permute-start | bytes 1572872 | tf_op jit(solution)/shard_map/ppermute | solution.py:270
  11.8 26.4 %collective-permute-start.2 = (bf16[2048,128]{1,0:T(8,128)(2,1)}, bf16[2048,128]{1,0:T(8,128)(2,1)}, u32[]{:S(2)}, u32[]{:S(2)}) collective-permute-start(bf16[2048,128]{1,0:T(8,128)(2,1)} %param.24), channel_id=1, source_target_pairs={{12,0},{0,4},{4,8},{8,12},{13,1},{1,5},{5,9},{9,13},{14,2},{2,6},{... | collective-permute-start | bytes 1572872 | tf_op jit(solution)/shard_map/ppermute | solution.py:270
  14.7 2.2 copy-start.2
  16.9 0.9 copy-start.3
  17.8 17.8 %copy-start.6 = (bf16[2048,128]{1,0:T(8,128)(2,1)S(1)}, bf16[2048,128]{1,0:T(8,128)(2,1)}, u32[]{:S(2)}) copy-start(bf16[2048,128]{1,0:T(8,128)(2,1)} %param.24) | copy-start | bytes 1572868
  39.6 6.5 %copy-start.8 = (bf16[2048]{0:T(1024)(128)(2,1)S(1)}, bf16[2048]{0:T(1024)(128)(2,1)}, u32[]{:S(2)}) copy-start(bf16[2048]{0:T(1024)(128)(2,1)} %param.28) | copy-start | bytes 12292
  39.6 6.5 %copy-start.9 = (bf16[2048]{0:T(1024)(128)(2,1)S(1)}, bf16[2048]{0:T(1024)(128)(2,1)}, u32[]{:S(2)}) copy-start(bf16[2048]{0:T(1024)(128)(2,1)} %param.29) | copy-start | bytes 12292
  40.0 11.7 %copy-start.7 = (bf16[48,2048]{1,0:T(8,128)(2,1)S(1)}, bf16[48,2048]{1,0:T(8,128)(2,1)}, u32[]{:S(2)}) copy-start(bf16[48,2048]{1,0:T(8,128)(2,1)} %param.16) | copy-start | bytes 589828
  40.4 12.5 %copy-start.13 = (s32[1,4]{1,0:T(1,128)S(1)}, s32[1,4]{1,0:T(1,128)}, u32[]{:S(2)}) copy-start(s32[1,4]{1,0:T(1,128)} %param.22) | copy-start | bytes 52
  41.1 10.2 %all-to-all-start = ((bf16[4,48,512]{2,1,0:T(8,128)(2,1)}), bf16[4,48,512]{2,1,0:T(8,128)(2,1)S(1)}, u32[]{:S(2)}, u32[]{:S(2)}) async-start(bf16[4,48,512]{2,1,0:T(8,128)(2,1)} %bitcast.2), calls=%async_computation | async-start | bytes 393216 | tf_op jit(solution)/shard_map/all_to_all | solution.py:278
  46.1 62.4 %all-gather.3.cloned.1.call-start = ((), (), s32[]{:S(2)}) async-start(), calls=%async_computation.7 | async-start | bytes 3342336 | tf_op jit(solution)/shard_map/all_gather | solution.py:360
  66.5 7.9 %copy-start.10 = (bf16[2048]{0:T(1024)(128)(2,1)S(1)}, bf16[2048]{0:T(1024)(128)(2,1)}, u32[]{:S(2)}) copy-start(bf16[2048]{0:T(1024)(128)(2,1)} %param.30) | copy-start | bytes 12292
  66.5 7.9 %copy-start.11 = (bf16[2048]{0:T(1024)(128)(2,1)S(1)}, bf16[2048]{0:T(1024)(128)(2,1)}, u32[]{:S(2)}) copy-start(bf16[2048]{0:T(1024)(128)(2,1)} %param.31) | copy-start | bytes 12292
  70.9 11.5 %all-to-all-start.2 = ((bf16[16,4,2048]{2,1,0:T(4,128)(2,1)}), bf16[16,4,2048]{2,1,0:T(4,128)(2,1)S(1)}, u32[]{:S(2)}, u32[]{:S(2)}) async-start(bf16[16,4,2048]{2,1,0:T(4,128)(2,1)} %reshape.105), calls=%async_computation.2 | async-start | bytes 524288 | tf_op jit(solution)/shard_map/all_to_all | solution.py:278
  83.9 12.7 %all-to-all-start.3 = ((bf16[16,4,2048]{2,1,0:T(4,128)(2,1)}), bf16[16,4,2048]{2,1,0:T(4,128)(2,1)S(1)}, u32[]{:S(2)}, u32[]{:S(2)}) async-start(bf16[16,4,2048]{2,1,0:T(4,128)(2,1)} %broadcast_in_dim.24), calls=%async_computation.3 | async-start | bytes 524288 | tf_op jit(solution)/shard_map/all_to_all | solution.py:278
  98.5 24.5 %all-to-all-start.4 = ((bf16[16,4,64,128]{3,2,1,0:T(8,128)(2,1)}), bf16[16,4,64,128]{3,2,1,0:T(8,128)(2,1)S(1)}, u32[]{:S(2)}, u32[]{:S(2)}) async-start(bf16[16,4,64,128]{3,2,1,0:T(8,128)(2,1)} %broadcast_in_dim.25), calls=%async_computation.4 | async-start | bytes 2097152 | tf_op jit(solution)/shard_map/all_to_all | solution.py:278
  102.8 100.7 %reduce-scatter.2.cloned.1.call-start = ((), (), s32[]{:S(2)}) async-start(), calls=%async_computation.9 | async-start | bytes 3342336 | tf_op jit(solution)/shard_map/reduce_scatter | solution.py:377
  123.2 5.4 %copy-start.12 = (s32[128,2]{0,1:T(2,128)S(1)}, s32[128,2]{0,1:T(2,128)}, u32[]{:S(2)}) copy-start(s32[128,2]{0,1:T(2,128)} %param.23) | copy-start | bytes 3076
  123.2 5.6 %collective-permute-start.3 = (bf16[4,64,2048]{2,1,0:T(8,128)(2,1)S(1)}, bf16[4,64,2048]{2,1,0:T(8,128)(2,1)S(1)}, u32[]{:S(2)}, u32[]{:S(2)}) collective-permute-start(bf16[4,64,2048]{2,1,0:T(8,128)(2,1)S(1)} %copy_bitcast_fusion.refs_0_), channel_id=1, source_target_pairs={{16,0},{0,16},{17,1},{1,17},{18,2},{2,18},{19,3},{3,19},{20,4},{4,... | collective-permute-start | bytes 3145736 | tf_op jit(solution)/shard_map/ppermute | solution.py:270
  125.8 14.4 %collective-permute-start.4 = (bf16[2,64,2048]{2,1,0:T(8,128)(2,1)}, bf16[2,64,2048]{2,1,0:T(8,128)(2,1)S(1)}, u32[]{:S(2)}, u32[]{:S(2)}) collective-permute-start(bf16[2,64,2048]{2,1,0:T(8,128)(2,1)} %bitcast.108), channel_id=1, source_target_pairs={{32,0},{64,32},{96,64},{0,96},{33,1},{65,33},{97,65},{1,97},{34,2}... | collective-permute-start | bytes 1572872 | tf_op jit(solution)/shard_map/ppermute | solution.py:270
  128.6 14.8 %collective-permute-start.5 = (bf16[2,64,2048]{2,1,0:T(8,128)(2,1)}, bf16[2,64,2048]{2,1,0:T(8,128)(2,1)}, u32[]{:S(2)}, u32[]{:S(2)}) collective-permute-start(bf16[2,64,2048]{2,1,0:T(8,128)(2,1)} %bitcast.108), channel_id=1, source_target_pairs={{96,0},{0,32},{32,64},{64,96},{97,1},{1,33},{33,65},{65,97},{98,2}... | collective-permute-start | bytes 1572872 | tf_op jit(solution)/shard_map/ppermute | solution.py:270
  128.8 49.3 %copy-start.4 = (s32[9]{0:T(128)}, s32[9]{0:T(128)S(1)}, u32[]{:S(2)}) copy-start(s32[9]{0:T(128)S(1)} %stack.42.place_ref) | copy-start | bytes 112
  128.9 15.6 %copy-start.5 = (bf16[16,2,8,8,128]{4,3,2,1,0:T(8,128)(2,1)S(1)}, bf16[16,2,8,8,128]{4,3,2,1,0:T(8,128)(2,1)}, u32[]{:S(2)}) copy-start(bf16[16,2,8,8,128]{4,3,2,1,0:T(8,128)(2,1)} %get-tuple-element.50) | copy-start | bytes 1572868
  143.3 3.4 %collective-permute-start.6 = (bf16[2,64,2048]{2,1,0:T(8,128)(2,1)S(1)}, bf16[2,64,2048]{2,1,0:T(8,128)(2,1)S(1)}, u32[]{:S(2)}, u32[]{:S(2)}) collective-permute-start(bf16[2,64,2048]{2,1,0:T(8,128)(2,1)S(1)} %collective-permute-done.4.refs_0_), channel_id=1, source_target_pairs={{16,0},{0,16},{17,1},{1,17},{18,2},{2,18},{19,3},{3,19},{20,4},{4,... | collective-permute-start | bytes 1572872 | tf_op jit(solution)/shard_map/ppermute | solution.py:270
  144.5 2.5 %collective-permute-start.7 = (bf16[2,64,2048]{2,1,0:T(8,128)(2,1)}, bf16[2,64,2048]{2,1,0:T(8,128)(2,1)S(1)}, u32[]{:S(2)}, u32[]{:S(2)}) collective-permute-start(bf16[2,64,2048]{2,1,0:T(8,128)(2,1)} %collective-permute-done.5.refs_2_), channel_id=1, source_target_pairs={{16,0},{0,16},{17,1},{1,17},{18,2},{2,18},{19,3},{3,19},{20,4},{4,... | collective-permute-start | bytes 1572872 | tf_op jit(solution)/shard_map/ppermute | solution.py:270
  144.6 13.2 %collective-permute-start.8 = (bf16[2,64,2048]{2,1,0:T(8,128)(2,1)S(1)}, bf16[2,64,2048]{2,1,0:T(8,128)(2,1)S(1)}, u32[]{:S(2)}, u32[]{:S(2)}) collective-permute-start(bf16[2,64,2048]{2,1,0:T(8,128)(2,1)S(1)} %bitcast.118), channel_id=1, source_target_pairs={{32,0},{64,32},{96,64},{0,96},{33,1},{65,33},{97,65},{1,97},{34,2}... | collective-permute-start | bytes 1572872 | tf_op jit(solution)/shard_map/ppermute | solution.py:270
  144.7 14.2 %collective-permute-start.9 = (bf16[2,64,2048]{2,1,0:T(8,128)(2,1)S(1)}, bf16[2,64,2048]{2,1,0:T(8,128)(2,1)S(1)}, u32[]{:S(2)}, u32[]{:S(2)}) collective-permute-start(bf16[2,64,2048]{2,1,0:T(8,128)(2,1)S(1)} %bitcast.119), channel_id=1, source_target_pairs={{96,0},{0,32},{32,64},{64,96},{97,1},{1,33},{33,65},{65,97},{98,2}... | collective-permute-start | bytes 1572872 | tf_op jit(solution)/shard_map/ppermute | solution.py:270
  158.8 3.0 %collective-permute-start.10 = (bf16[2,64,2048]{2,1,0:T(8,128)(2,1)S(1)}, bf16[2,64,2048]{2,1,0:T(8,128)(2,1)S(1)}, u32[]{:S(2)}, u32[]{:S(2)}) collective-permute-start(bf16[2,64,2048]{2,1,0:T(8,128)(2,1)S(1)} %collective-permute-done.8.refs_0_), channel_id=1, source_target_pairs={{16,0},{0,16},{17,1},{1,17},{18,2},{2,18},{19,3},{3,19},{20,4},{4,... | collective-permute-start | bytes 1572872 | tf_op jit(solution)/shard_map/ppermute | solution.py:270
  160.3 2.3 collective-permute-start.11
  160.3 13.0 %collective-permute-start.12 = (bf16[2,64,2048]{2,1,0:T(8,128)(2,1)S(1)}, bf16[2,64,2048]{2,1,0:T(8,128)(2,1)S(1)}, u32[]{:S(2)}, u32[]{:S(2)}) collective-permute-start(bf16[2,64,2048]{2,1,0:T(8,128)(2,1)S(1)} %collective-permute-done.4.refs_0_), channel_id=1, source_target_pairs={{32,0},{64,32},{96,64},{0,96},{33,1},{65,33},{97,65},{1,97},{34,2}... | collective-permute-start | bytes 1572872 | tf_op jit(solution)/shard_map/ppermute | solution.py:270
  160.3 14.1 %collective-permute-start.13 = (bf16[2,64,2048]{2,1,0:T(8,128)(2,1)S(1)}, bf16[2,64,2048]{2,1,0:T(8,128)(2,1)S(1)}, u32[]{:S(2)}, u32[]{:S(2)}) collective-permute-start(bf16[2,64,2048]{2,1,0:T(8,128)(2,1)S(1)} %collective-permute-done.9.refs_2_), channel_id=1, source_target_pairs={{96,0},{0,32},{32,64},{64,96},{97,1},{1,33},{33,65},{65,97},{98,2}... | collective-permute-start | bytes 1572872 | tf_op jit(solution)/shard_map/ppermute | solution.py:270
  174.4 3.0 %collective-permute-start.14 = (bf16[2,64,2048]{2,1,0:T(8,128)(2,1)S(1)}, bf16[2,64,2048]{2,1,0:T(8,128)(2,1)S(1)}, u32[]{:S(2)}, u32[]{:S(2)}) collective-permute-start(bf16[2,64,2048]{2,1,0:T(8,128)(2,1)S(1)} %collective-permute-done.12.refs_0_), channel_id=1, source_target_pairs={{16,0},{0,16},{17,1},{1,17},{18,2},{2,18},{19,3},{3,19},{20,4},{4,... | collective-permute-start | bytes 1572872 | tf_op jit(solution)/shard_map/ppermute | solution.py:270
  175.8 2.3 collective-permute-start.15
  201.4 4.9 %collective-permute-start.16 = (f32[8,256]{1,0:T(8,128)S(1)}, f32[8,256]{1,0:T(8,128)S(1)}, u32[]{:S(2)}, u32[]{:S(2)}) collective-permute-start(f32[8,256]{1,0:T(8,128)S(1)} %reduce_sum.78), channel_id=1, source_target_pairs={{32,0},{64,32},{96,64},{0,96},{33,1},{65,33},{97,65},{1,97},{34,2}... | collective-permute-start | bytes 24584 | tf_op jit(solution)/shard_map/ppermute | solution.py:270
  201.5 4.8 %collective-permute-start.17 = (f32[8,256]{1,0:T(8,128)S(1)}, f32[8,256]{1,0:T(8,128)S(1)}, u32[]{:S(2)}, u32[]{:S(2)}) collective-permute-start(f32[8,256]{1,0:T(8,128)S(1)} %reduce_sum.78), channel_id=1, source_target_pairs={{64,0},{96,32},{0,64},{32,96},{65,1},{97,33},{1,65},{33,97},{66,2}... | collective-permute-start | bytes 24584 | tf_op jit(solution)/shard_map/ppermute | solution.py:270
  203.5 3.7 %collective-permute-start.18 = (f32[8,256]{1,0:T(8,128)S(1)}, f32[8,256]{1,0:T(8,128)S(1)}, u32[]{:S(2)}, u32[]{:S(2)}) collective-permute-start(f32[8,256]{1,0:T(8,128)S(1)} %reduce_sum.78), channel_id=1, source_target_pairs={{96,0},{0,32},{32,64},{64,96},{97,1},{1,33},{33,65},{65,97},{98,2}... | collective-permute-start | bytes 24584 | tf_op jit(solution)/shard_map/ppermute | solution.py:270
  207.2 4.5 %collective-permute-start.19 = (f32[8,256]{1,0:T(8,128)S(1)}, f32[8,256]{1,0:T(8,128)S(1)}, u32[]{:S(2)}, u32[]{:S(2)}) collective-permute-start(f32[8,256]{1,0:T(8,128)S(1)} %add_add_fusion), channel_id=1, source_target_pairs={{16,0},{0,16},{17,1},{1,17},{18,2},{2,18},{19,3},{3,19},{20,4},{4,... | collective-permute-start | bytes 24584 | tf_op jit(solution)/shard_map/ppermute | solution.py:270
  212.7 10.3 %copy-start.1 = (bf16[4,2048,128]{2,1,0:T(8,128)(2,1)S(1)}, bf16[4,2048,128]{2,1,0:T(8,128)(2,1)}, u32[]{:S(2)}) copy-start(bf16[4,2048,128]{2,1,0:T(8,128)(2,1)} %param.26) | copy-start | bytes 6291460
Sparse Core Ops, SparseCore 0:
  9.7 44.5 all-gather.4
  57.1 51.4 all-gather.2
  123.3 75.6 reduce-scatter.1
